TPU v7x, 32 devices: a whole 2x2x4 slice. The times are simulated.
32 devices in a mesh: dp: 4 (over y, x), ctx: 8 (over z, core).
Axes of the slice: x: 2, y: 2, z: 4, core: 2. Of those that a mesh axis runs over, the one named last changes fastest.
Arguments:
- hidden_in: bfloat16 [4, 2048, 2048], P('dp', 'ctx'), may hold values from -12.5 to 12.5
- seq_lengths: int32 [4, 8], replicated, may hold values from 0 to 1024, as said below
- qkv_weight: bfloat16 [2048, 6144], P(('dp', 'ctx')), may hold values from -0.125 to 0.125
- out_weight: bfloat16 [2048, 2048], P(('dp', 'ctx')), may hold values from -0.125 to 0.125
- in_weight: bfloat16 [2048, 16384], P(('dp', 'ctx')), may hold values from -0.125 to 0.125
- down_weight: bfloat16 [8192, 2048], P(('dp', 'ctx')), may hold values from -0.0625 to 0.0625
- norm_gains: float32 [4, 2048], replicated, may hold values from 0.25 to 1.75
- upstream: bfloat16 [4, 2048, 2048], P('dp', 'ctx'), may hold values from -6 to 6
Outputs:
- output: bfloat16 [4, 2048, 2048], P('dp', 'ctx')
- input_grad: float32 [4, 2048, 2048], P('dp', 'ctx')
- grad_qkv: float32 [2048, 6144], P(('dp', 'ctx'))
- grad_out: float32 [2048, 2048], P(('dp', 'ctx'))
- grad_in: float32 [2048, 16384], P(('dp', 'ctx'))
- grad_down: float32 [8192, 2048], P(('dp', 'ctx'))
- grad_gains: float32 [4, 2048], replicated
- rms_values: float32 [3], replicated
Inputs may be any that keep to these rules, and one draw needn't show every extreme that they name: `seq_lengths`: each row lists the lengths of its packed sequences in order, each from 256 to 1024, then zeros; a row's lengths add up to at most 2048 and the positions after them are padding. Every row holds at least one sequence, and some row of every draw holds one of exactly 1024.
All inputs are finite; a program needn't handle non-finite values.
Results may differ from a plain program's by a relative error of at most 0.015.
Values may be sent and summed in bfloat16 or wider, within the bound.
No kernel may reach another device: no remote copies, remote signals or barrier semaphores. Data moves between devices by JAX's collectives and lax.ppermute only.
A program may use at most 512 MiB of HBM per device.

v0:
```python
import jax
import jax.numpy as jnp
from jax import lax
from jax.sharding import PartitionSpec as P

D = 2048
HEADS = 16
HEAD_DIM = 128
FF = 8192
REACH = 4


norm_epsilon = 1e-06
rope_base = 500000.0
masked_score = -1e30


def from_behind(value, axis, steps):
    count = lax.axis_size(axis)
    first, last = (max(0, -steps), min(count, count - steps))
    return lax.ppermute(value, axis, [(source, source + steps) for source in range(first, last)])


def shortened(value):

    def short(part):
        return part.astype(jnp.bfloat16) if part.dtype == jnp.float32 else part

    return jax.tree.map(short, value)


def product(left_side, right_side):
    return jnp.dot(left_side, right_side, preferred_element_type=jnp.float32)


def product_left(left_side, right_side):
    return lax.dot_general(
        left_side, right_side, (((0,), (0,)), ((), ())), preferred_element_type=jnp.float32
    )


def product_right(left_side, right_side):
    return lax.dot_general(
        left_side, right_side, (((1,), (1,)), ((), ())), preferred_element_type=jnp.float32
    )


def weight_terms(term_fn, row_count):
    return lax.psum_scatter(
        term_fn(jnp.int32(0), row_count * lax.axis_size(("dp", "ctx"))),
        ("dp", "ctx"),
        scatter_dimension=0,
        tiled=True,
    )


def norm_forward(values, gain_row):
    factor = lax.rsqrt(jnp.mean(values * values, axis=-1, keepdims=True) + norm_epsilon)
    return (values * factor * gain_row, factor)


def norm_backward(values, factor, gain_row, incoming):
    weighted = incoming * gain_row
    mixing = jnp.mean(weighted * values, axis=-1, keepdims=True)
    return (
        factor * (weighted - values * factor * factor * mixing),
        jnp.sum(incoming * values * factor, axis=0),
    )


def rotate(values, offsets, direction):
    count_rows = values.shape[0]
    halfway = HEAD_DIM // 2
    inverse = rope_base ** (-2.0 * jnp.arange(halfway, dtype=jnp.float32) / HEAD_DIM)
    angles = offsets.astype(jnp.float32)[:, None] * inverse[None, :]
    cosine = jnp.cos(angles)[:, None, :]
    sine_part = direction * jnp.sin(angles)[:, None, :]
    split_heads = values.reshape(count_rows, HEADS, HEAD_DIM)
    leading = split_heads[..., :halfway]
    trailing = split_heads[..., halfway:]
    turned = jnp.concatenate(
        [leading * cosine - trailing * sine_part, trailing * cosine + leading * sine_part], axis=-1
    )
    return turned.reshape(count_rows, HEADS * HEAD_DIM)


def arrange(lengths, positions):
    finish = jnp.cumsum(lengths)
    has_ended = finish[None, :] <= positions[:, None]
    segment = jnp.sum(has_ended.astype(jnp.int32), axis=1)
    starts = jnp.sum(jnp.where(has_ended, lengths[None, :], 0), axis=1)
    return (segment, positions - starts, positions < finish[-1])


def gate_grads(hidden_grad, gate_part, up_part, sigmoid_gate):
    gate_grad = hidden_grad * up_part * sigmoid_gate * (1.0 + gate_part * (1.0 - sigmoid_gate))
    up_grad = hidden_grad * gate_part * sigmoid_gate
    return jnp.concatenate([gate_grad, up_grad], axis=1).astype(jnp.bfloat16)


def on_device(
    hidden_in, seq_lengths, qkv_weight, out_weight, in_weight, down_weight, norm_gains, upstream
):
    rows_here, piece_len, model_width = hidden_in.shape
    tokens = rows_here * piece_len
    span_keys = (REACH + 1) * piece_len
    piece_place = lax.axis_index("ctx")
    lengths = lax.dynamic_slice_in_dim(seq_lengths, lax.axis_index("dp") * rows_here, rows_here, 0)
    within = jnp.arange(piece_len, dtype=jnp.int32)
    scale_factor = HEAD_DIM ** (-0.5)

    def layout_at(back_steps):
        positions = (piece_place - back_steps) * piece_len + within
        segment, offsets, live_mask = jax.vmap(lambda row_lengths: arrange(row_lengths, positions))(
            lengths
        )
        return (segment, offsets, live_mask, jnp.broadcast_to(positions, (rows_here, piece_len)))

    layouts = [layout_at(back_steps) for back_steps in range(REACH + 1)]
    query_segment, query_offsets, query_live, query_positions = layouts[0]
    key_segment = jnp.concatenate(
        [layouts[REACH - block_index][0] for block_index in range(REACH + 1)], axis=1
    )
    key_positions = jnp.concatenate(
        [layouts[REACH - block_index][3] for block_index in range(REACH + 1)], axis=1
    )
    allowed = (
        (query_segment[:, :, None] == key_segment[:, None, :])
        & (key_positions[:, None, :] <= query_positions[:, :, None])
        & (key_positions[:, None, :] >= 0)
    )
    flat_offsets = query_offsets.reshape(tokens)
    flat_inputs = hidden_in.reshape(tokens, model_width)
    full_qkv, full_out = (
        lax.all_gather(qkv_weight, ("dp", "ctx"), axis=0, tiled=True),
        lax.all_gather(out_weight, ("dp", "ctx"), axis=0, tiled=True),
    )
    projected = product(flat_inputs, full_qkv)
    query_normed, query_factor = norm_forward(projected[:, :D], norm_gains[0])
    key_normed, key_factor = norm_forward(projected[:, D : 2 * D], norm_gains[1])
    query_low = rotate(query_normed, flat_offsets, 1.0).astype(jnp.bfloat16)
    key_low = rotate(key_normed, flat_offsets, 1.0).astype(jnp.bfloat16)
    value_low = projected[:, 2 * D :].astype(jnp.bfloat16)
    own_pair = (
        key_low.reshape(rows_here, piece_len, D),
        value_low.reshape(rows_here, piece_len, D),
    )
    kv_pieces = [own_pair]
    for back_steps in range(1, REACH + 1):
        kv_pieces.append(from_behind((own_pair[0], own_pair[1]), "ctx", back_steps))
    key_all = jnp.concatenate(
        [kv_pieces[REACH - block_index][0] for block_index in range(REACH + 1)], axis=1
    )
    value_all = jnp.concatenate(
        [kv_pieces[REACH - block_index][1] for block_index in range(REACH + 1)], axis=1
    )
    query_heads = query_low.reshape(rows_here, piece_len, HEADS, HEAD_DIM)
    key_heads = key_all.reshape(rows_here, span_keys, HEADS, HEAD_DIM)
    value_heads = value_all.reshape(rows_here, span_keys, HEADS, HEAD_DIM)

    def score_block():
        raw_scores = (
            jnp.einsum(
                "rqhd,rkhd->rhqk", query_heads, key_heads, preferred_element_type=jnp.float32
            )
            * scale_factor
        )
        return jnp.where(allowed[:, None], raw_scores, masked_score)

    scores = score_block()
    score_top = jnp.max(scores, axis=-1, keepdims=True)
    expanded = jnp.exp(scores - score_top)
    denominator = jnp.sum(expanded, axis=-1, keepdims=True)
    log_total = score_top + jnp.log(denominator)
    probs_low = (expanded / denominator).astype(jnp.bfloat16)
    attended_low = (
        jnp.einsum("rhqk,rkhd->rqhd", probs_low, value_heads, preferred_element_type=jnp.float32)
        .reshape(tokens, D)
        .astype(jnp.bfloat16)
    )
    branch = product(attended_low, full_out)
    branch_normed, branch_factor = norm_forward(branch, norm_gains[2])
    residual = flat_inputs.astype(jnp.float32) + branch_normed
    residual_low = residual.astype(jnp.bfloat16)
    full_in, full_down = (
        lax.all_gather(in_weight, ("dp", "ctx"), axis=0, tiled=True),
        lax.all_gather(down_weight, ("dp", "ctx"), axis=0, tiled=True),
    )
    gate_up = product(residual_low, full_in)
    unit_count = FF
    gate_part = gate_up[:, :unit_count]
    up_part = gate_up[:, unit_count:]
    sigmoid_gate = jax.nn.sigmoid(gate_part)
    hidden_low = (gate_part * sigmoid_gate * up_part).astype(jnp.bfloat16)
    second = product(hidden_low, full_down)
    second_normed, second_factor = norm_forward(second, norm_gains[3])
    result = residual + second_normed
    live_rows = query_live.reshape(tokens, 1).astype(jnp.float32)
    squares = jnp.stack(
        [
            jnp.sum(result * result * live_rows),
            jnp.sum(branch * branch * live_rows),
            jnp.sum(second * second * live_rows),
        ]
    )
    incoming = upstream.reshape(tokens, model_width).astype(jnp.float32)
    second_grad, second_gain_grad = norm_backward(second, second_factor, norm_gains[3], incoming)
    second_grad_low = second_grad.astype(jnp.bfloat16)
    back_in, back_down = (
        lax.all_gather(in_weight, ("dp", "ctx"), axis=0, tiled=True),
        lax.all_gather(down_weight, ("dp", "ctx"), axis=0, tiled=True),
    )
    hidden_grad = product_right(second_grad_low, back_down)

    def down_term(row_start, row_count):
        return product_left(hidden_low, second_grad_low)

    grad_down = weight_terms(down_term, down_weight.shape[0])
    gate_up_low = gate_grads(hidden_grad, gate_part, up_part, sigmoid_gate)
    residual_grad = incoming + product_right(gate_up_low, back_in)

    def in_term(row_start, row_count):
        return product_left(residual_low, gate_up_low)

    grad_in = weight_terms(in_term, in_weight.shape[0])
    branch_grad, branch_gain_grad = norm_backward(
        branch, branch_factor, norm_gains[2], residual_grad
    )
    branch_grad_low = branch_grad.astype(jnp.bfloat16)
    back_qkv, back_out = (
        lax.all_gather(qkv_weight, ("dp", "ctx"), axis=0, tiled=True),
        lax.all_gather(out_weight, ("dp", "ctx"), axis=0, tiled=True),
    )

    def out_term(row_start, row_count):
        return product_left(attended_low, branch_grad_low)

    grad_out = weight_terms(out_term, out_weight.shape[0])
    attended_grad = product_right(branch_grad_low, back_out).astype(jnp.bfloat16)
    probs = jnp.exp(score_block() - log_total)
    probs_again = probs.astype(jnp.bfloat16)
    grad_heads = attended_grad.reshape(rows_here, piece_len, HEADS, HEAD_DIM)
    prob_grad = jnp.einsum(
        "rqhd,rkhd->rhqk", grad_heads, value_heads, preferred_element_type=jnp.float32
    )
    row_inner = jnp.sum(probs * prob_grad, axis=-1, keepdims=True)
    score_grad = (probs * (prob_grad - row_inner)).astype(jnp.bfloat16)
    query_grad = (
        jnp.einsum(
            "rhqk,rkhd->rqhd", score_grad, key_heads, preferred_element_type=jnp.float32
        ).reshape(tokens, D)
        * scale_factor
    )
    key_grad_all = (
        jnp.einsum("rhqk,rqhd->rkhd", score_grad, query_heads, preferred_element_type=jnp.float32)
        * scale_factor
    )
    value_grad_all = jnp.einsum(
        "rhqk,rqhd->rkhd", probs_again, grad_heads, preferred_element_type=jnp.float32
    )
    key_blocks = key_grad_all.reshape(rows_here, REACH + 1, piece_len, D)
    value_blocks = value_grad_all.reshape(rows_here, REACH + 1, piece_len, D)

    def block_terms(back_steps):
        return (key_blocks[:, REACH - back_steps], value_blocks[:, REACH - back_steps])

    key_total, value_total = block_terms(0)
    for back_steps in range(1, REACH + 1):
        moved_key, moved_value = from_behind(shortened(block_terms(back_steps)), "ctx", -back_steps)
        key_total = key_total + moved_key
        value_total = value_total + moved_value
    query_raw_grad, query_gain_grad = norm_backward(
        projected[:, :D], query_factor, norm_gains[0], rotate(query_grad, flat_offsets, -1.0)
    )
    key_raw_grad, key_gain_grad = norm_backward(
        projected[:, D : 2 * D],
        key_factor,
        norm_gains[1],
        rotate(key_total.reshape(tokens, D), flat_offsets, -1.0),
    )
    projected_grad_low = jnp.concatenate(
        [query_raw_grad, key_raw_grad, value_total.reshape(tokens, D)], axis=1
    ).astype(jnp.bfloat16)

    def qkv_term(row_start, row_count):
        return product_left(flat_inputs, projected_grad_low)

    grad_qkv = weight_terms(qkv_term, qkv_weight.shape[0])
    input_grad = residual_grad + product_right(projected_grad_low, back_qkv)
    gain_sums, square_sums = lax.psum(
        (jnp.stack([query_gain_grad, key_gain_grad, branch_gain_grad, second_gain_grad]), squares),
        ("dp", "ctx"),
    )
    live_count = jnp.sum(seq_lengths).astype(jnp.float32)
    rms_values = jnp.sqrt(square_sums / (live_count * model_width))
    output = result.astype(jnp.bfloat16).reshape(rows_here, piece_len, model_width)
    return (
        output,
        input_grad.reshape(rows_here, piece_len, model_width),
        grad_qkv,
        grad_out,
        grad_in,
        grad_down,
        gain_sums,
        rms_values,
    )


def solution(mesh):
    return jax.shard_map(
        on_device,
        mesh=mesh,
        in_specs=(
            P("dp", "ctx", None),
            P(),
            P(("dp", "ctx"), None),
            P(("dp", "ctx"), None),
            P(("dp", "ctx"), None),
            P(("dp", "ctx"), None),
            P(),
            P("dp", "ctx", None),
        ),
        out_specs=(
            P("dp", "ctx", None),
            P("dp", "ctx", None),
            P(("dp", "ctx"), None),
            P(("dp", "ctx"), None),
            P(("dp", "ctx"), None),
            P(("dp", "ctx"), None),
            P(),
            P(),
        ),
        check_vma=False,
    )
```

profile of v0, /device:TPU:0, one launch (start us, length us, event | category | flops | bytes accessed | tf_op | source)
XLA Modules:
  0.0 4207.5 jit_solution(4384609367193629246)
XLA Ops:
  11.7 156.7 %all-gather.5.cloned.1.call-done = bf16[2048,6144]{1,0:T(8,128)(2,1)} async-done(((bf16[64,6144]{1,0:T(8,128)(2,1)}), bf16[2048,6144]{1,0:T(8,128)(2,1)}) %all-gather.5.cloned.1.call-update) | async-done | bytes 25165840 | tf_op jit(solution)/shard_map/all_gather | solution.py:135
  168.4 11.6 fusion.43
  192.3 4.4 collective-permute-start.4
  209.6 20.3 collective-permute-done.4
  229.9 54.6 %collective-permute-start.1 = (bf16[1,256,2048]{2,1,0:T(8,128)(2,1)}, bf16[1,256,2048]{2,1,0:T(8,128)(2,1)}, u32[]{:S(2)}, u32[]{:S(2)}) collective-permute-start(bf16[1,256,2048]{2,1,0:T(8,128)(2,1)} %slice_bitcast_fusion.10), channel_id=1, source_target_pairs={{0,3},{1,4},{2,5},{3,6},{4,7},{8,11},{9,12},{10,13},{11,14},{12,15... | collective-permute-start | bytes 3145736 | tf_op jit(solution)/shard_map/ppermute | solution.py:21
  284.5 38.9 collective-permute-start.2
  344.0 19.2 collective-permute-done.1
  365.5 42.7 %collective-permute-done.2 = bf16[1,256,2048]{2,1,0:T(8,128)(2,1)} collective-permute-done((bf16[1,256,2048]{2,1,0:T(8,128)(2,1)}, bf16[1,256,2048]{2,1,0:T(8,128)(2,1)}, u32[]{:S(2)}, u32[]{:S(2)}) %collective-permute-start.2) | collective-permute-done | bytes 1048608 | tf_op jit(solution)/shard_map/ppermute | solution.py:21
  421.3 9.8 fusion.57
  431.1 10.6 fusion
  441.8 9.3 fusion.37
  451.1 6.0 multiply_reduce_fusion.11
  458.5 294.1 %all-gather.9.cloned.1.call-done = bf16[2048,16384]{1,0:T(8,128)(2,1)} async-done(((bf16[64,16384]{1,0:T(8,128)(2,1)}), bf16[2048,16384]{1,0:T(8,128)(2,1)}) %all-gather.9.cloned.1.call-update) | async-done | bytes 67108880 | tf_op jit(solution)/shard_map/all_gather | solution.py:186
  752.6 31.2 fusion.61
  783.8 10.1 multiply_convert_fusion.3
  793.9 179.3 %all-gather.11.cloned.1.call-done = bf16[8192,2048]{1,0:T(8,128)(2,1)} async-done(((bf16[256,2048]{1,0:T(8,128)(2,1)}), bf16[8192,2048]{1,0:T(8,128)(2,1)}) %all-gather.11.cloned.1.call-update) | async-done | bytes 33554448 | tf_op jit(solution)/shard_map/all_gather | solution.py:187
  973.2 16.4 multiply_reduce_fusion.10
  993.0 23.5 multiply_convert_fusion.2
  1016.6 32.4 multiply_reduce_fusion.4
  1052.1 8.1 fusion.62
  1077.6 11.8 fusion.6
  1089.4 11.7 copy.251
  1101.1 11.5 reshape.982
  1112.6 7.3 convert.58
  1119.9 15.5 multiply_reduce_fusion
  1135.4 15.1 multiply_convert_fusion
  1150.6 3.8 copy-done
  1154.4 6.1 multiply_bitcast_fusion
  1160.6 11.7 copy.241
  1172.2 9.6 convert.56
  1181.9 9.9 slice_bitcast_fusion.4
  1200.8 4.3 multiply_bitcast_fusion.1
  1205.1 149.4 %collective-permute-done.11 = bf16[1,256,2048]{2,0,1:T(2,128)(2,1)S(1)} collective-permute-done((bf16[1,256,2048]{2,0,1:T(2,128)(2,1)}, bf16[1,256,2048]{2,0,1:T(2,128)(2,1)S(1)}, u32[]{:S(2)}, u32[]{:S(2)}) %collective-permute-start.11) | collective-permute-done | bytes 1048608 | tf_op jit(solution)/shard_map/ppermute | solution.py:21
  1358.4 8.4 convert_add_fusion.1
  1366.8 4.6 copy.246
  1372.5 3.1 copy.267
  1377.6 3.6 multiply_subtract_fusion.1
  1386.5 159.0 %collective-permute-done.15 = bf16[1,256,2048]{2,1,0:T(8,128)(2,1)} collective-permute-done((bf16[1,256,2048]{2,1,0:T(8,128)(2,1)}, bf16[1,256,2048]{2,1,0:T(8,128)(2,1)}, u32[]{:S(2)}, u32[]{:S(2)}) %collective-permute-start.15) | collective-permute-done | bytes 1048608 | tf_op jit(solution)/shard_map/ppermute | solution.py:21
  1545.5 4.7 fusion.41
  1550.3 20.6 convolution_bitcast_fusion
  1570.9 48.9 %copy.261 = f32[2048,6144]{1,0:T(8,128)} copy(f32[2048,6144]{0,1:T(8,128)} %convolution_bitcast_fusion) | data formatting | bytes 100663296
  1621.6 25.5 fusion.58
  1648.3 75.0 %fusion.9 = f32[2048,16384]{1,0:T(8,128)} fusion(bf16[256,2048]{1,0:T(8,128)(2,1)S(1)} %copy-done.15, bf16[256,8192]{1,0:T(8,128)(2,1)} %get-tuple-element.89, bf16[256,8192]{1,0:T(8,128)(2,1)} %get-tuple-element.88), kind=kOutput, calls=%fused_computation.19 | convolution fusion | flops 17196646400 | bytes 143654912 | tf_op jit(solution)/shard_map/dot_general | solution.py:37
  1727.2 73.8 %all-reduce.1 = (f32[4,2048]{1,0:T(4,128)}, f32[3]{0:T(128)S(1)}) all-reduce(f32[4,2048]{1,0:T(4,128)S(1)} %pad_maximum_fusion.12, f32[3]{0:T(128)S(1)} %pad_maximum_fusion.13), channel_id=1, replica_groups=mesh['dp'=4,'ctx'=8] {'dp','ctx'}, use_global_device_ids=true, to_apply=%region_26.27 | all-reduce | flops 8195 | bytes 65560 | tf_op jit(solution)/shard_map/psum | solution.py:290
  1801.5 14.7 fusion.15
  1816.3 267.4 %reduce-scatter.14.cloned.1.call-done = f32[64,6144]{1,0:T(8,128)} async-done(((f32[2048,6144]{1,0:T(8,128)}), f32[64,6144]{1,0:T(8,128)}) %reduce-scatter.14.cloned.1.call-update) | async-done | bytes 1572880
  2083.6 711.3 %reduce-scatter.12.cloned.1.call-done = f32[256,2048]{1,0:T(8,128)} async-done(((f32[8192,2048]{1,0:T(8,128)}), f32[256,2048]{1,0:T(8,128)}) %reduce-scatter.12.cloned.1.call-update) | async-done | bytes 2097168 | tf_op jit(solution)/shard_map/reduce_scatter | solution.py:49
  2794.9 1405.4 %reduce-scatter.16.cloned.1.call-done = f32[64,16384]{1,0:T(8,128)} async-done(((f32[2048,16384]{1,0:T(8,128)}), f32[64,16384]{1,0:T(8,128)}) %reduce-scatter.16.cloned.1.call-update) | async-done | bytes 4194320
  (274 shorter events, 118.3 us)
Async XLA Ops:
  7.2 161.3 %all-gather.5.cloned.1.call-start = ((), (), s32[]{:S(2)}) async-start(), calls=%async_computation.4 | async-start | bytes 25952256 | tf_op jit(solution)/shard_map/all_gather | solution.py:135
  7.9 160.5 %copy-start.12 = (bf16[1,256,2048]{2,1,0:T(8,128)(2,1)S(1)}, bf16[1,256,2048]{2,1,0:T(8,128)(2,1)}, u32[]{:S(2)}) copy-start(bf16[1,256,2048]{2,1,0:T(8,128)(2,1)} %param.8) | copy-start | bytes 3145732
  7.9 443.2 %all-gather.7.cloned.1.call-start = ((), (), s32[]{:S(2)}) async-start(), calls=%async_computation.5 | async-start | bytes 8650752 | tf_op jit(solution)/shard_map/all_gather | solution.py:136
  8.7 743.9 %all-gather.9.cloned.1.call-start = ((), (), s32[]{:S(2)}) async-start(), calls=%async_computation.6 | async-start | bytes 69206016 | tf_op jit(solution)/shard_map/all_gather | solution.py:186
  9.4 963.8 %all-gather.11.cloned.1.call-start = ((), (), s32[]{:S(2)}) async-start(), calls=%async_computation.7 | async-start | bytes 34603008 | tf_op jit(solution)/shard_map/all_gather | solution.py:187
  10.0 1806.3 %reduce-scatter.10.cloned.1.call-start = ((), (), s32[]{:S(2)}) async-start(), calls=%async_computation.8 | async-start | bytes 17301504 | tf_op jit(solution)/shard_map/reduce_scatter | solution.py:49
  11.6 173.1 %copy-start.33 = (f32[256,64]{1,0:T(8,128)}, f32[256,64]{1,0:T(8,128)S(1)}, u32[]{:S(2)}) copy-start(f32[256,64]{1,0:T(8,128)S(1)} %get-tuple-element.128) | copy-start | bytes 196612
  11.7 168.8 %copy-start.38 = (f32[1,2048]{1,0:T(1,128)}, f32[1,2048]{1,0:T(1,128)S(1)}, u32[]{:S(2)}) copy-start(f32[1,2048]{1,0:T(1,128)S(1)} %get-tuple-element.123) | copy-start | bytes 24580
  11.7 168.8 %copy-start.40 = (f32[1,2048]{1,0:T(1,128)}, f32[1,2048]{1,0:T(1,128)S(1)}, u32[]{:S(2)}) copy-start(f32[1,2048]{1,0:T(1,128)S(1)} %get-tuple-element.124) | copy-start | bytes 24580
  11.7 1004.9 %copy-start.42 = (f32[1,2048]{1,0:T(1,128)}, f32[1,2048]{1,0:T(1,128)S(1)}, u32[]{:S(2)}) copy-start(f32[1,2048]{1,0:T(1,128)S(1)} %get-tuple-element.125) | copy-start | bytes 24580
  187.5 233.8 %copy-start.2 = (bf16[256,16,64]{2,0,1:T(8,128)(2,1)}, bf16[256,16,64]{2,0,1:T(8,128)(2,1)S(1)}, u32[]{:S(2)}) copy-start(bf16[256,16,64]{2,0,1:T(8,128)(2,1)S(1)} %get-tuple-element.104) | copy-start | bytes 1572868
  187.5 233.8 %copy-start.4 = (bf16[256,16,64]{2,0,1:T(8,128)(2,1)}, bf16[256,16,64]{2,0,1:T(8,128)(2,1)S(1)}, u32[]{:S(2)}) copy-start(bf16[256,16,64]{2,0,1:T(8,128)(2,1)S(1)} %get-tuple-element.105) | copy-start | bytes 1572868
  192.3 37.6 collective-permute-start.4
  196.7 87.8 %collective-permute-start.5 = (bf16[1,256,2048]{1,2,0:T(8,128)(2,1)}, bf16[1,256,2048]{1,2,0:T(8,128)(2,1)}, u32[]{:S(2)}, u32[]{:S(2)}) collective-permute-start(bf16[1,256,2048]{1,2,0:T(8,128)(2,1)} %bitcast.244), channel_id=1, source_target_pairs={{0,3},{1,4},{2,5},{3,6},{4,7},{8,11},{9,12},{10,13},{11,14},{12,15... | collective-permute-start | bytes 3145736 | tf_op jit(solution)/shard_map/ppermute | solution.py:21
  199.6 123.8 %collective-permute-start.6 = (bf16[1,256,2048]{1,2,0:T(8,128)(2,1)}, bf16[1,256,2048]{1,2,0:T(8,128)(2,1)}, u32[]{:S(2)}, u32[]{:S(2)}) collective-permute-start(bf16[1,256,2048]{1,2,0:T(8,128)(2,1)} %bitcast.245), channel_id=1, source_target_pairs={{0,2},{1,3},{2,4},{3,5},{4,6},{5,7},{8,10},{9,11},{10,12},{11,13},... | collective-permute-start | bytes 3145736 | tf_op jit(solution)/shard_map/ppermute | solution.py:21
  202.3 137.0 %collective-permute-start.7 = (bf16[1,256,2048]{1,2,0:T(8,128)(2,1)}, bf16[1,256,2048]{1,2,0:T(8,128)(2,1)}, u32[]{:S(2)}, u32[]{:S(2)}) collective-permute-start(bf16[1,256,2048]{1,2,0:T(8,128)(2,1)} %bitcast.246), channel_id=1, source_target_pairs={{0,1},{1,2},{2,3},{3,4},{4,5},{5,6},{6,7},{8,9},{9,10},{10,11},{11... | collective-permute-start | bytes 3145736 | tf_op jit(solution)/shard_map/ppermute | solution.py:21
  207.4 134.3 %collective-permute-start = (bf16[1,256,2048]{2,1,0:T(8,128)(2,1)}, bf16[1,256,2048]{2,1,0:T(8,128)(2,1)}, u32[]{:S(2)}, u32[]{:S(2)}) collective-permute-start(bf16[1,256,2048]{2,1,0:T(8,128)(2,1)} %slice_bitcast_fusion.10), channel_id=1, source_target_pairs={{0,4},{1,5},{2,6},{3,7},{8,12},{9,13},{10,14},{11,15},{16,20},{17,... | collective-permute-start | bytes 3145736 | tf_op jit(solution)/shard_map/ppermute | solution.py:21
  229.9 133.3 %collective-permute-start.1 = (bf16[1,256,2048]{2,1,0:T(8,128)(2,1)}, bf16[1,256,2048]{2,1,0:T(8,128)(2,1)}, u32[]{:S(2)}, u32[]{:S(2)}) collective-permute-start(bf16[1,256,2048]{2,1,0:T(8,128)(2,1)} %slice_bitcast_fusion.10), channel_id=1, source_target_pairs={{0,3},{1,4},{2,5},{3,6},{4,7},{8,11},{9,12},{10,13},{11,14},{12,15... | collective-permute-start | bytes 3145736 | tf_op jit(solution)/shard_map/ppermute | solution.py:21
  284.5 123.6 %collective-permute-start.2 = (bf16[1,256,2048]{2,1,0:T(8,128)(2,1)}, bf16[1,256,2048]{2,1,0:T(8,128)(2,1)}, u32[]{:S(2)}, u32[]{:S(2)}) collective-permute-start(bf16[1,256,2048]{2,1,0:T(8,128)(2,1)} %slice_bitcast_fusion.10), channel_id=1, source_target_pairs={{0,2},{1,3},{2,4},{3,5},{4,6},{5,7},{8,10},{9,11},{10,12},{11,13},... | collective-permute-start | bytes 3145736 | tf_op jit(solution)/shard_map/ppermute | solution.py:21
  323.4 86.9 %collective-permute-start.3 = (bf16[1,256,2048]{2,1,0:T(8,128)(2,1)}, bf16[1,256,2048]{2,1,0:T(8,128)(2,1)}, u32[]{:S(2)}, u32[]{:S(2)}) collective-permute-start(bf16[1,256,2048]{2,1,0:T(8,128)(2,1)} %slice_bitcast_fusion.10), channel_id=1, source_target_pairs={{0,1},{1,2},{2,3},{3,4},{4,5},{5,6},{6,7},{8,9},{9,10},{10,11},{11... | collective-permute-start | bytes 3145736 | tf_op jit(solution)/shard_map/ppermute | solution.py:21
  973.2 17.7 copy-start.21
  989.6 26.9 copy-start.52
  993.0 23.5 copy-start.55
  1060.3 1023.3 %reduce-scatter.14.cloned.1.call-start = ((), (), s32[]{:S(2)}) async-start(), calls=%async_computation.10 | async-start | bytes 51904512
  1135.4 19.0 copy-start.3
  1135.4 19.0 copy-start.5
  1172.2 25.0 slice-start.7
  1172.2 25.0 slice-start.8
  1172.2 28.5 slice-start.9
  1181.8 18.9 slice-start
  1181.8 18.9 slice-start.1
  1181.8 18.9 slice-start.10
  1191.7 162.7 %collective-permute-start.11 = (bf16[1,256,2048]{2,0,1:T(2,128)(2,1)}, bf16[1,256,2048]{2,0,1:T(2,128)(2,1)S(1)}, u32[]{:S(2)}, u32[]{:S(2)}) collective-permute-start(bf16[1,256,2048]{2,0,1:T(2,128)(2,1)} %get-tuple-element.91), channel_id=1, source_target_pairs={{4,0},{5,1},{6,2},{7,3},{12,8},{13,9},{14,10},{15,11},{20,16},{21,... | collective-permute-start | bytes 3145736 | tf_op jit(solution)/shard_map/ppermute | solution.py:21
  1193.0 162.7 %collective-permute-start.10 = (bf16[1,256,2048]{2,0,1:T(2,128)(2,1)}, bf16[1,256,2048]{2,0,1:T(2,128)(2,1)S(1)}, u32[]{:S(2)}, u32[]{:S(2)}) collective-permute-start(bf16[1,256,2048]{2,0,1:T(2,128)(2,1)} %get-tuple-element.92), channel_id=1, source_target_pairs={{3,0},{4,1},{5,2},{6,3},{7,4},{11,8},{12,9},{13,10},{14,11},{15,12... | collective-permute-start | bytes 3145736 | tf_op jit(solution)/shard_map/ppermute | solution.py:21
  1194.5 162.6 %collective-permute-start.9 = (bf16[1,256,2048]{2,0,1:T(2,128)(2,1)}, bf16[1,256,2048]{2,0,1:T(2,128)(2,1)S(1)}, u32[]{:S(2)}, u32[]{:S(2)}) collective-permute-start(bf16[1,256,2048]{2,0,1:T(2,128)(2,1)} %get-tuple-element.93), channel_id=1, source_target_pairs={{2,0},{3,1},{4,2},{5,3},{6,4},{7,5},{10,8},{11,9},{12,10},{13,11},... | collective-permute-start | bytes 3145736 | tf_op jit(solution)/shard_map/ppermute | solution.py:21
  1195.9 162.4 %collective-permute-start.8 = (bf16[1,256,2048]{2,0,1:T(2,128)(2,1)}, bf16[1,256,2048]{2,0,1:T(2,128)(2,1)S(1)}, u32[]{:S(2)}, u32[]{:S(2)}) collective-permute-start(bf16[1,256,2048]{2,0,1:T(2,128)(2,1)} %get-tuple-element.90), channel_id=1, source_target_pairs={{1,0},{2,1},{3,2},{4,3},{5,4},{6,5},{7,6},{9,8},{10,9},{11,10},{12... | collective-permute-start | bytes 3145736 | tf_op jit(solution)/shard_map/ppermute | solution.py:21
  1199.4 346.1 %collective-permute-start.15 = (bf16[1,256,2048]{2,1,0:T(8,128)(2,1)}, bf16[1,256,2048]{2,1,0:T(8,128)(2,1)}, u32[]{:S(2)}, u32[]{:S(2)}) collective-permute-start(bf16[1,256,2048]{2,1,0:T(8,128)(2,1)} %get-tuple-element.99), channel_id=1, source_target_pairs={{4,0},{5,1},{6,2},{7,3},{12,8},{13,9},{14,10},{15,11},{20,16},{21,... | collective-permute-start | bytes 3145736 | tf_op jit(solution)/shard_map/ppermute | solution.py:21
  1354.5 191.1 %collective-permute-start.14 = (bf16[1,256,2048]{2,1,0:T(8,128)(2,1)}, bf16[1,256,2048]{2,1,0:T(8,128)(2,1)}, u32[]{:S(2)}, u32[]{:S(2)}) collective-permute-start(bf16[1,256,2048]{2,1,0:T(8,128)(2,1)} %get-tuple-element.100), channel_id=1, source_target_pairs={{3,0},{4,1},{5,2},{6,3},{7,4},{11,8},{12,9},{13,10},{14,11},{15,12... | collective-permute-start | bytes 3145736 | tf_op jit(solution)/shard_map/ppermute | solution.py:21
  1355.8 189.8 %collective-permute-start.13 = (bf16[1,256,2048]{2,1,0:T(8,128)(2,1)}, bf16[1,256,2048]{2,1,0:T(8,128)(2,1)}, u32[]{:S(2)}, u32[]{:S(2)}) collective-permute-start(bf16[1,256,2048]{2,1,0:T(8,128)(2,1)} %get-tuple-element.101), channel_id=1, source_target_pairs={{2,0},{3,1},{4,2},{5,3},{6,4},{7,5},{10,8},{11,9},{12,10},{13,11},... | collective-permute-start | bytes 3145736 | tf_op jit(solution)/shard_map/ppermute | solution.py:21
  1357.1 188.4 %collective-permute-start.12 = (bf16[1,256,2048]{2,1,0:T(8,128)(2,1)}, bf16[1,256,2048]{2,1,0:T(8,128)(2,1)}, u32[]{:S(2)}, u32[]{:S(2)}) collective-permute-start(bf16[1,256,2048]{2,1,0:T(8,128)(2,1)} %get-tuple-element.98), channel_id=1, source_target_pairs={{1,0},{2,1},{3,2},{4,3},{5,4},{6,5},{7,6},{9,8},{10,9},{11,10},{12... | collective-permute-start | bytes 3145736 | tf_op jit(solution)/shard_map/ppermute | solution.py:21
  1386.4 163.8 %copy-start.16 = (bf16[256,2048]{1,0:T(8,128)(2,1)}, bf16[256,2048]{1,0:T(8,128)(2,1)S(1)}, u32[]{:S(2)}) copy-start(bf16[256,2048]{1,0:T(8,128)(2,1)S(1)} %get-tuple-element.94) | copy-start | bytes 3145732
  1386.4 163.8 %copy-start.18 = (bf16[256,2048]{1,0:T(8,128)(2,1)}, bf16[256,2048]{1,0:T(8,128)(2,1)S(1)}, u32[]{:S(2)}) copy-start(bf16[256,2048]{1,0:T(8,128)(2,1)S(1)} %get-tuple-element.95) | copy-start | bytes 3145732
  1386.5 163.8 %copy-start.14 = (bf16[1,256,2048]{2,1,0:T(8,128)(2,1)S(1)}, bf16[1,256,2048]{2,1,0:T(8,128)(2,1)}, u32[]{:S(2)}) copy-start(bf16[1,256,2048]{2,1,0:T(8,128)(2,1)} %param.8) | copy-start | bytes 3145732
  1619.8 1175.2 %reduce-scatter.12.cloned.1.call-start = ((), (), s32[]{:S(2)}) async-start(), calls=%async_computation.9 | async-start | bytes 69206016 | tf_op jit(solution)/shard_map/reduce_scatter | solution.py:49
  1647.1 2553.3 %reduce-scatter.16.cloned.1.call-start = ((), (), s32[]{:S(2)}) async-start(), calls=%async_computation.11 | async-start | bytes 138412032
  1723.3 78.2 %copy-start.17 = (bf16[256,2048]{1,0:T(8,128)(2,1)S(1)}, bf16[256,2048]{1,0:T(8,128)(2,1)}, u32[]{:S(2)}) copy-start(bf16[256,2048]{1,0:T(8,128)(2,1)} %copy-done.16) | copy-start | bytes 3145732
  1723.3 78.2 %copy-start.19 = (bf16[256,2048]{1,0:T(8,128)(2,1)S(1)}, bf16[256,2048]{1,0:T(8,128)(2,1)}, u32[]{:S(2)}) copy-start(bf16[256,2048]{1,0:T(8,128)(2,1)} %copy-done.18) | copy-start | bytes 3145732
  1723.3 78.2 %copy-start.20 = (bf16[256,2048]{1,0:T(8,128)(2,1)S(1)}, bf16[256,2048]{1,0:T(8,128)(2,1)}, u32[]{:S(2)}) copy-start(bf16[256,2048]{1,0:T(8,128)(2,1)} %fusion.41) | copy-start | bytes 3145732
  (46 other events, 150.0 us)
Sparse Core Ops, SparseCore 0:
  11.0 157.3 all-gather.4
  171.4 122.7 all-gather.6
  297.3 455.2 all-gather.8
  755.4 217.7 all-gather.10
  1060.4 274.6 reduce-scatter.9
  1619.9 463.6 reduce-scatter.13
  2086.5 708.3 reduce-scatter.11
  2797.9 1402.4 reduce-scatter.15
where the time goes:
time: 4220 us; the launch traced here: 4210 us
  waiting for transfers between devices  3410 us (81%)
  matrix products  324 us (8%)
  local copies, waits for them, and re-layouts  173 us (4%)
  starting transfers between devices  122 us (3%)
  other arithmetic  91.5 us (2%)
  blocking collectives  73.8 us (2%)
    unnamed x10, waiting for transfers between devices  1680 us
    reduce_scatter x2, waiting for transfers between devices, weight_terms(): lax.psum_scatter(term_fn(jnp.int32(0), row_count * lax.axis_size(('dp', '...  711 us
    ppermute x16, waiting for transfers between devices, from_behind(): lax.ppermute(value, axis, [(source, source + steps) for source in range(f...  391 us
    all_gather x1, waiting for transfers between devices, on_device(): lax.all_gather(in_weight, ('dp', 'ctx'), axis=0, tiled=True)  294 us
    all_gather x1, waiting for transfers between devices, on_device(): lax.all_gather(down_weight, ('dp', 'ctx'), axis=0, tiled=True)  179 us
    all_gather x1, waiting for transfers between devices, on_device(): lax.all_gather(qkv_weight, ('dp', 'ctx'), axis=0, tiled=True)  157 us
    dot_general x4, matrix products, product_left(): lax.dot_general(left_side, right_side, (((0,), (0,)), ((), ())), preferre...  129 us
    ppermute x16, starting transfers between devices, from_behind(): lax.ppermute(value, axis, [(source, source + steps) for source in range(f...  121 us
  transfers between devices with their start and end apart: 24, of which 11 were waited for; matrix products, arithmetic and copies ran while one was open for 12% of the time, Pallas kernels for 0%

commit v1 on v0

v1 whole, which is shorter than its diff:
```python
import functools
import itertools

import jax
import jax.numpy as jnp
from jax import lax
from jax.experimental import pallas as pl
from jax.experimental.pallas import tpu as pltpu
from jax.sharding import Mesh
from jax.sharding import PartitionSpec as P

D = 2048
HEADS = 16
HEAD_DIM = 128
FF = 8192

norm_epsilon = 1e-06
rope_base = 500000.0
masked_score = -1e30
scale_factor = HEAD_DIM ** (-0.5)

AXES = ("dh", "dl", "zh", "zl", "c")
DATA = ("dh", "dl")
LINE = ("zh", "zl")
CTX = ("zh", "zl", "c")
MLP_CHIPS = ("zh", "zl")
MLP_DATA = tuple(a for a in AXES[:4] if a not in MLP_CHIPS)

BLOCK_Q = 512
BLOCK_K = 512

bf16 = jnp.bfloat16
f32 = jnp.float32


def sizes_of(axes):
    return tuple(lax.axis_size(a) for a in axes)


def offsets(axes):
    return list(itertools.product(*[range(n) for n in sizes_of(axes)]))


def linear(index, sizes):
    total = 0
    for i, n in zip(index, sizes):
        total = total * n + i
    return total


def shift(value, axes, steps):
    if not any(steps):
        return value
    sizes = sizes_of(axes)
    pairs = []
    for index in itertools.product(*[range(n) for n in sizes]):
        target = tuple((i + s) % n for i, s, n in zip(index, steps, sizes))
        pairs.append((linear(index, sizes), linear(target, sizes)))
    return lax.ppermute(value, axes, pairs)


def swap(value):
    return lax.ppermute(value, "c", [(0, 1), (1, 0)])


def place(axes, steps, sign=1):
    sizes = sizes_of(axes)
    here = [(lax.axis_index(a) + sign * s) % n for a, s, n in zip(axes, steps, sizes)]
    return linear(here, sizes)


def pick(value, index, axis=0):
    return lax.dynamic_index_in_dim(value, index, axis, keepdims=False)


def put(buffer, value, index):
    return lax.dynamic_update_slice_in_dim(buffer, value[None], index, 0)


def gather_groups(block, chips):
    same = [shift(block, chips, steps) for steps in offsets(chips)]
    return [(s, swap(s)) for s in same]


def scatter_sum(for_same, for_other):
    return for_same + swap(for_other.astype(bf16)).astype(f32)


def exchange(blocks, chips):
    core = lax.axis_index("c")
    got = swap(pick(blocks, 1 - core, 1))
    keep = pick(blocks, core, 1)
    first, second = jnp.where(core == 0, keep, got), jnp.where(core == 0, got, keep)
    pairs = jnp.stack([first, second], axis=1)
    result = jnp.zeros_like(pairs)
    for steps in offsets(chips):
        piece = shift(pick(pairs, place(chips, steps)), chips, steps)
        result = put(result, piece, place(chips, steps, -1))
    return result


def small_sum(value, axes):
    for axis in axes:
        if lax.axis_size(axis) == 2:
            value = value + lax.ppermute(value, axis, [(0, 1), (1, 0)])
        else:
            value = lax.psum(value, axis)
    return value


def product(left_side, right_side):
    return jnp.dot(left_side, right_side, preferred_element_type=f32)


def product_left(left_side, right_side):
    return lax.dot_general(
        left_side, right_side, (((0,), (0,)), ((), ())), preferred_element_type=f32
    )


def product_right(left_side, right_side):
    return lax.dot_general(
        left_side, right_side, (((1,), (1,)), ((), ())), preferred_element_type=f32
    )


def allowed_keys(shape, key_start, query_start, starts):
    key_place = key_start + lax.broadcasted_iota(jnp.int32, shape, 0)
    query_place = query_start + lax.broadcasted_iota(jnp.int32, shape, 1)
    return (key_place >= starts) & (key_place <= query_place)


def attend_kernel(low_ref, starts_ref, q_ref, k_ref, v_ref, out_ref, log_ref):
    block = pl.program_id(1)
    bq, bk = q_ref.shape[0], BLOCK_K
    queries, starts = q_ref[...], starts_ref[...]

    def step(j, carry):
        top, total, acc = carry
        rows = pl.ds(pl.multiple_of(j * bk, bk), bk)
        scores = product_right(k_ref[rows, :], queries) * scale_factor
        ok = allowed_keys(scores.shape, j * bk, block * bq, starts)
        scores = jnp.where(ok, scores, masked_score)
        new_top = jnp.maximum(top, jnp.max(scores, axis=0, keepdims=True))
        ratio = jnp.exp(top - new_top)
        expanded = jnp.exp(scores - new_top)
        total = total * ratio + jnp.sum(expanded, axis=0, keepdims=True)
        acc = acc * ratio + product_left(v_ref[rows, :], expanded.astype(bf16))
        return (new_top, total, acc)

    init = (
        jnp.full((1, bq), masked_score, f32),
        jnp.zeros((1, bq), f32),
        jnp.zeros((HEAD_DIM, bq), f32),
    )
    top, total, acc = lax.fori_loop(low_ref[block], (block * bq + bq) // bk, step, init)
    out_ref[...] = (acc / total).T
    log_ref[0] = top + jnp.log(total)


def attend(lows, starts, queries, keys, values):
    length, width = queries.shape
    heads, bq = width // HEAD_DIM, BLOCK_Q
    return pl.pallas_call(
        attend_kernel,
        grid_spec=pltpu.PrefetchScalarGridSpec(
            num_scalar_prefetch=1,
            grid=(heads, length // bq),
            in_specs=[
                pl.BlockSpec((1, bq), lambda h, i, low: (0, i)),
                pl.BlockSpec((bq, HEAD_DIM), lambda h, i, low: (i, h)),
                pl.BlockSpec((length, HEAD_DIM), lambda h, i, low: (0, h)),
                pl.BlockSpec((length, HEAD_DIM), lambda h, i, low: (0, h)),
            ],
            out_specs=[
                pl.BlockSpec((bq, HEAD_DIM), lambda h, i, low: (i, h)),
                pl.BlockSpec((1, 1, bq), lambda h, i, low: (h, 0, i)),
            ],
        ),
        out_shape=[
            jax.ShapeDtypeStruct((length, width), f32),
            jax.ShapeDtypeStruct((heads, 1, length), f32),
        ],
        compiler_params=pltpu.CompilerParams(vmem_limit_bytes=48 << 20),
        name="attend",
    )(lows, starts, queries, keys, values)


def attend_back_kernel(
    low_ref, starts_ref, q_ref, k_ref, v_ref, out_ref, log_ref, grad_ref, dq_ref, dk_ref, dv_ref
):
    length = q_ref.shape[0]
    bq, bk = BLOCK_Q, BLOCK_K
    dk_ref[...] = jnp.zeros_like(dk_ref)
    dv_ref[...] = jnp.zeros_like(dv_ref)

    def query_step(i, carry):
        queries_at = pl.ds(pl.multiple_of(i * bq, bq), bq)
        queries, grads = q_ref[queries_at, :], grad_ref[queries_at, :]
        starts = starts_ref[:, queries_at]
        log_total = log_ref[0, :, queries_at]
        inner = jnp.sum((grads.astype(f32) * out_ref[queries_at, :]).T, axis=0, keepdims=True)

        def step(j, acc):
            rows = pl.ds(pl.multiple_of(j * bk, bk), bk)
            keys = k_ref[rows, :]
            scores = product_right(keys, queries) * scale_factor
            ok = allowed_keys(scores.shape, j * bk, i * bq, starts)
            probs = jnp.where(ok, jnp.exp(scores - log_total), 0.0)
            dv_ref[rows, :] += product(probs.astype(bf16), grads)
            prob_grad = product_right(v_ref[rows, :], grads)
            score_grad = (probs * (prob_grad - inner)).astype(bf16)
            dk_ref[rows, :] += product(score_grad, queries) * scale_factor
            return acc + product_left(keys, score_grad)

        acc = lax.fori_loop(
            low_ref[i], (i * bq + bq) // bk, step, jnp.zeros((HEAD_DIM, bq), f32)
        )
        dq_ref[queries_at, :] = (acc * scale_factor).T
        return carry

    lax.fori_loop(0, length // bq, query_step, 0)


def attend_back(lows, starts, queries, keys, values, out, log_total, grads):
    length, width = queries.shape
    heads = width // HEAD_DIM
    column = pl.BlockSpec((length, HEAD_DIM), lambda h, low: (0, h))
    return pl.pallas_call(
        attend_back_kernel,
        grid_spec=pltpu.PrefetchScalarGridSpec(
            num_scalar_prefetch=1,
            grid=(heads,),
            in_specs=[
                pl.BlockSpec((1, length), lambda h, low: (0, 0)),
                column,
                column,
                column,
                column,
                pl.BlockSpec((1, 1, length), lambda h, low: (h, 0, 0)),
                column,
            ],
            out_specs=[column, column, column],
        ),
        out_shape=[jax.ShapeDtypeStruct((length, width), f32)] * 3,
        compiler_params=pltpu.CompilerParams(vmem_limit_bytes=56 << 20),
        name="attend_back",
    )(lows, starts, queries, keys, values, out, log_total, grads)


def norm_forward(values, gain_row):
    factor = lax.rsqrt(jnp.mean(values * values, axis=-1, keepdims=True) + norm_epsilon)
    return (values * factor * gain_row, factor)


def norm_backward(values, factor, gain_row, incoming):
    weighted = incoming * gain_row
    mixing = jnp.mean(weighted * values, axis=-1, keepdims=True)
    return (
        factor * (weighted - values * factor * factor * mixing),
        jnp.sum(incoming * values * factor, axis=0),
    )


def rotate(values, cosine, sine_part):
    count_rows, width = values.shape
    heads = values.reshape(count_rows, width // HEAD_DIM, HEAD_DIM)
    halfway = HEAD_DIM // 2
    turned = jnp.concatenate([heads[..., halfway:], heads[..., :halfway]], axis=-1)
    return (heads * cosine[:, None] + turned * sine_part[:, None]).reshape(count_rows, width)


def arrange(lengths, positions):
    finish = jnp.cumsum(lengths)
    has_ended = finish[None, :] <= positions[:, None]
    return jnp.sum(jnp.where(has_ended, lengths[None, :], 0), axis=1).astype(jnp.int32)


def to_natural(rows, chips, data):
    order = data + chips
    if order == AXES[:4]:
        return rows
    shaped = rows.reshape(sizes_of(order) + (-1,) + rows.shape[1:])
    back = tuple(order.index(a) for a in AXES[:4])
    return shaped.transpose(back + tuple(range(4, shaped.ndim))).reshape(rows.shape)


def from_natural(rows, chips, data):
    order = data + chips
    if order == AXES[:4]:
        return rows
    shaped = rows.reshape(sizes_of(AXES[:4]) + (-1,) + rows.shape[1:])
    perm = tuple(AXES.index(a) for a in order)
    return shaped.transpose(perm + tuple(range(4, shaped.ndim))).reshape(rows.shape)


def columns_out(weight):
    rows = weight.shape[0]
    shaped = weight.reshape((rows, 2) + sizes_of(AXES) + (-1,))
    where = {a: 2 + i for i, a in enumerate(AXES)}
    perm = [where[a] for a in MLP_CHIPS] + [where["c"], 0, 1] + [where[a] for a in MLP_DATA] + [7]
    chips = 1
    for a in MLP_CHIPS:
        chips *= lax.axis_size(a)
    return shaped.transpose(perm).reshape(chips, 2, rows, -1)


def columns_back(blocks):
    rows = blocks.shape[2]
    shape = sizes_of(MLP_CHIPS) + (2, rows, 2) + sizes_of(MLP_DATA) + (-1,)
    names = MLP_CHIPS + ("c", "rows", "half") + MLP_DATA + ("unit",)
    wanted = ("rows", "half") + AXES + ("unit",)
    perm = tuple(names.index(a) for a in wanted)
    return blocks.reshape(shape).transpose(perm).reshape(rows, -1)


def scatter_over(value, axes):
    return lax.psum_scatter(value.astype(bf16), axes, scatter_dimension=0, tiled=True)


def on_device(
    hidden_in, seq_lengths, qkv_weight, out_weight, in_weight, down_weight, norm_gains, upstream
):
    piece_len, model_width = hidden_in.shape[1:]
    line_sizes = sizes_of(LINE)
    line = line_sizes[0] * line_sizes[1]
    length = piece_len * line * 2
    width = D // (line * 2)
    core = lax.axis_index("c")
    ctx_place = linear([lax.axis_index(a) for a in CTX], sizes_of(CTX))
    data_place = linear([lax.axis_index(a) for a in DATA], sizes_of(DATA))
    line_place = linear([lax.axis_index(a) for a in LINE], line_sizes)
    lengths = lax.dynamic_index_in_dim(seq_lengths, data_place, 0, keepdims=False)
    places = jnp.arange(length, dtype=jnp.int32)
    starts = arrange(lengths, places)
    offset = (places - starts).astype(f32)
    lows = starts[::BLOCK_Q] // BLOCK_K
    starts_row = starts.reshape(1, length)
    inverse = rope_base ** (-2.0 * jnp.arange(HEAD_DIM // 2, dtype=f32) / HEAD_DIM)
    angles = offset[:, None] * inverse[None, :]
    cosine, sine_part = jnp.cos(angles), jnp.sin(angles)
    cosine = jnp.concatenate([cosine, cosine], axis=1)
    sine_part = jnp.concatenate([-sine_part, sine_part], axis=1)

    own_input = hidden_in.reshape(piece_len, model_width)

    row_count = qkv_weight.shape[0]
    qkv_blocks = qkv_weight.reshape(row_count, 3, line, 2, width).transpose(2, 3, 0, 1, 4)
    qkv_rows = exchange(qkv_blocks.reshape(line, 2, row_count, 3 * width), LINE)
    qkv_here = lax.all_gather(
        qkv_rows.reshape(-1, 3 * width), DATA, axis=0, tiled=True
    )

    full_input = jnp.zeros((line, 2, piece_len, model_width), bf16)
    for steps, (same, other) in zip(offsets(LINE), gather_groups(own_input, LINE)):
        at = place(LINE, steps, -1)
        full_input = lax.dynamic_update_slice(full_input, same[None, None], (at, core, 0, 0))
        full_input = lax.dynamic_update_slice(full_input, other[None, None], (at, 1 - core, 0, 0))
    full_input = full_input.reshape(length, model_width)

    out_line = jnp.zeros((line,) + out_weight.shape, bf16)
    for steps in offsets(LINE):
        out_line = put(out_line, shift(out_weight, LINE, steps), place(LINE, steps, -1))
    out_half = lax.all_gather(
        out_line.reshape(-1, D), DATA, axis=0, tiled=True
    ).reshape(-1, out_weight.shape[0], D)
    out_other = swap(out_half)
    out_full = jnp.stack(
        [jnp.where(core == 0, out_half, out_other), jnp.where(core == 0, out_other, out_half)],
        axis=1,
    ).reshape(D, D)

    in_rows = exchange(columns_out(in_weight), MLP_CHIPS)
    in_here = to_natural(
        lax.all_gather(in_rows.reshape(-1, in_rows.shape[-1]), MLP_DATA, axis=0, tiled=True),
        MLP_CHIPS,
        MLP_DATA,
    )
    down_here = lax.all_gather(down_weight, MLP_DATA, axis=0, tiled=True)
    units = down_here.shape[0]

    projected = product(full_input, qkv_here)
    q_raw, k_raw = projected[:, :width], projected[:, width : 2 * width]
    value_low = projected[:, 2 * width :].astype(bf16)
    squares = small_sum(
        jnp.stack([jnp.sum(q_raw * q_raw, axis=1), jnp.sum(k_raw * k_raw, axis=1)]), CTX
    )
    factors = lax.rsqrt(squares / D + norm_epsilon)
    q_factor, k_factor = factors[0][:, None], factors[1][:, None]
    gains_here = lax.dynamic_slice(norm_gains, (0, ctx_place * width), (2, width))
    query_low = rotate(q_raw * q_factor * gains_here[0], cosine, sine_part).astype(bf16)
    key_low = rotate(k_raw * k_factor * gains_here[1], cosine, sine_part).astype(bf16)
    head_out, log_total = attend(lows, starts_row, query_low, key_low, value_low)

    attended = exchange(head_out.astype(bf16).reshape(line, 2, piece_len, width), LINE)
    attended_low = attended.reshape(line * 2, piece_len, width).transpose(1, 0, 2)
    attended_low = attended_low.reshape(piece_len, D)
    branch = product(attended_low, out_full)
    branch_normed, branch_factor = norm_forward(branch, norm_gains[2])
    residual = own_input.astype(f32) + branch_normed
    residual_low = residual.astype(bf16)

    mlp_steps = offsets(MLP_CHIPS)
    residual_groups = [
        jnp.concatenate(pair, axis=0) for pair in gather_groups(residual_low, MLP_CHIPS)
    ]
    gate_ups, hidden_groups = [], []
    second = None
    for steps, rows in zip(mlp_steps, residual_groups):
        gate_up = product(rows, in_here)
        gate_part, up_part = gate_up[:, :units], gate_up[:, units:]
        hidden = (gate_part * jax.nn.sigmoid(gate_part) * up_part).astype(bf16)
        part = product(hidden, down_here)
        part = scatter_sum(part[:piece_len], part[piece_len:])
        if any(steps):
            back = tuple(-s for s in steps)
            part = shift(part.astype(bf16), MLP_CHIPS, back).astype(f32)
        second = part if second is None else second + part
        gate_ups.append(gate_up)
        hidden_groups.append(hidden)
    second_normed, second_factor = norm_forward(second, norm_gains[3])
    result = residual + second_normed
    live_places = ctx_place * piece_len + jnp.arange(piece_len, dtype=jnp.int32)
    live_rows = (live_places < jnp.sum(lengths)).astype(f32)[:, None]
    sums = jnp.stack(
        [
            jnp.sum(result * result * live_rows),
            jnp.sum(branch * branch * live_rows),
            jnp.sum(second * second * live_rows),
        ]
    )

    incoming = upstream.reshape(piece_len, model_width).astype(f32)
    second_grad, second_gain_grad = norm_backward(second, second_factor, norm_gains[3], incoming)
    second_grad_groups = [
        jnp.concatenate(pair, axis=0)
        for pair in gather_groups(second_grad.astype(bf16), MLP_CHIPS)
    ]
    gate_up_grads = []
    residual_grad = incoming
    for steps, rows, gate_up in zip(mlp_steps, second_grad_groups, gate_ups):
        hidden_grad = product_right(rows, down_here)
        gate_part, up_part = gate_up[:, :units], gate_up[:, units:]
        sigmoid_gate = jax.nn.sigmoid(gate_part)
        gate_grad = hidden_grad * up_part * sigmoid_gate * (1.0 + gate_part * (1.0 - sigmoid_gate))
        up_grad = hidden_grad * gate_part * sigmoid_gate
        gate_up_low = jnp.concatenate([gate_grad, up_grad], axis=1).astype(bf16)
        part = product_right(gate_up_low, in_here)
        part = scatter_sum(part[:piece_len], part[piece_len:])
        if any(steps):
            back = tuple(-s for s in steps)
            part = shift(part.astype(bf16), MLP_CHIPS, back).astype(f32)
        residual_grad = residual_grad + part
        gate_up_grads.append(gate_up_low)
    hidden_all = jnp.concatenate(hidden_groups, axis=0)
    second_grad_all = jnp.concatenate(second_grad_groups, axis=0)
    grad_down = scatter_over(product_left(hidden_all, second_grad_all), MLP_DATA).astype(f32)
    residual_all = jnp.concatenate(residual_groups, axis=0)
    gate_up_all = jnp.concatenate(gate_up_grads, axis=0)
    grad_in = from_natural(
        product_left(residual_all, gate_up_all).astype(bf16), MLP_CHIPS, MLP_DATA
    )
    grad_in = scatter_over(grad_in, MLP_DATA).reshape(in_rows.shape)
    grad_in = columns_back(exchange(grad_in, MLP_CHIPS)).astype(f32)

    branch_grad, branch_gain_grad = norm_backward(
        branch, branch_factor, norm_gains[2], residual_grad
    )
    branch_grad_low = branch_grad.astype(bf16)
    attended_grad = product_right(branch_grad_low, out_full).astype(bf16)
    attended_grad = attended_grad.reshape(piece_len, line, 2, width).transpose(1, 2, 0, 3)
    head_grad = exchange(attended_grad, LINE).reshape(length, width)

    out_grad = product_left(attended_low, branch_grad_low).reshape(-1, 2, out_weight.shape[0], D)
    out_grad = scatter_sum(pick(out_grad, core, 1), pick(out_grad, 1 - core, 1))
    out_grad = scatter_over(out_grad.reshape(D // 2, D), DATA).reshape((line,) + out_weight.shape)
    grad_out = None
    for steps in offsets(LINE):
        part = shift(pick(out_grad, place(LINE, steps)), LINE, steps).astype(f32)
        grad_out = part if grad_out is None else grad_out + part

    query_grad, key_grad, value_grad = attend_back(
        lows, starts_row, query_low, key_low, value_low, head_out, log_total, head_grad
    )
    query_turned = rotate(query_grad, cosine, -sine_part)
    key_turned = rotate(key_grad, cosine, -sine_part)
    query_weighted, key_weighted = query_turned * gains_here[0], key_turned * gains_here[1]
    mixing = small_sum(
        jnp.stack([jnp.sum(query_weighted * q_raw, axis=1), jnp.sum(key_weighted * k_raw, axis=1)]),
        CTX,
    )
    mixing = mixing / D
    query_mix, key_mix = mixing[0][:, None], mixing[1][:, None]
    query_raw_grad = q_factor * (query_weighted - q_raw * q_factor * q_factor * query_mix)
    key_raw_grad = k_factor * (key_weighted - k_raw * k_factor * k_factor * key_mix)
    query_gain_grad = jnp.sum(query_turned * q_raw * q_factor, axis=0)
    key_gain_grad = jnp.sum(key_turned * k_raw * k_factor, axis=0)
    projected_grad = jnp.concatenate([query_raw_grad, key_raw_grad, value_grad], axis=1)
    projected_grad = projected_grad.astype(bf16)

    grad_qkv = scatter_over(product_left(full_input, projected_grad), DATA)
    grad_qkv = exchange(grad_qkv.reshape(line, 2, row_count, 3 * width), LINE)
    grad_qkv = grad_qkv.reshape(line, 2, row_count, 3, width).transpose(2, 3, 0, 1, 4)
    grad_qkv = grad_qkv.reshape(row_count, 3 * D).astype(f32)

    input_grad = residual_grad
    grad_blocks = projected_grad.reshape(line, 2, piece_len, 3 * width)
    for steps in offsets(LINE)[::-1]:
        rows = pick(grad_blocks, place(LINE, steps))
        rows = jnp.concatenate([pick(rows, core), pick(rows, 1 - core)], axis=0)
        part = product_right(rows, qkv_here)
        part = scatter_sum(part[:piece_len], part[piece_len:])
        if any(steps):
            part = shift(part.astype(bf16), LINE, steps).astype(f32)
        input_grad = input_grad + part

    gain_rows = jnp.zeros((5, D), f32)
    gain_rows = lax.dynamic_update_slice(
        gain_rows, jnp.stack([query_gain_grad, key_gain_grad]), (0, ctx_place * width)
    )
    gain_rows = gain_rows.at[2].set(branch_gain_grad).at[3].set(second_gain_grad)
    gain_rows = gain_rows.at[4, :3].set(sums)
    gain_rows = small_sum(gain_rows, AXES)
    live_count = jnp.sum(seq_lengths).astype(f32)
    rms_values = jnp.sqrt(gain_rows[4, :3] / (live_count * model_width))
    return (
        result.astype(bf16)[None],
        input_grad[None],
        grad_qkv,
        grad_out,
        grad_in,
        grad_down,
        gain_rows[:4],
        rms_values,
    )


def solution(mesh):
    dp, ctx = mesh.shape["dp"], mesh.shape["ctx"]
    fine = Mesh(mesh.devices.reshape(2, dp // 2, 2, ctx // 4, 2), AXES)
    return jax.shard_map(
        on_device,
        mesh=fine,
        in_specs=(
            P(DATA, CTX, None),
            P(),
            P(AXES, None),
            P(AXES, None),
            P(AXES, None),
            P(AXES, None),
            P(),
            P(DATA, CTX, None),
        ),
        out_specs=(
            P(DATA, CTX, None),
            P(DATA, CTX, None),
            P(AXES, None),
            P(AXES, None),
            P(AXES, None),
            P(AXES, None),
            P(),
            P(),
        ),
        check_vma=False,
    )
```

time: 4220 us -> 1300 us (0.31)
  waiting for transfers between devices: 3410 us -> 628 us
  matrix products: 324 us -> 196 us
  blocking collectives: 73.8 us -> 0 us
    unnamed x10 -> x8, waiting for transfers between devices: 1680 us -> 0.13 us
    reduce_scatter x2 -> x4, waiting for transfers between devices: 711 us -> 0.01 us  [scatter_over(): lax.psum_scatter(value.astype(bf16), axes, scatter_dimension=0, tiled=True)]
    all_gather x4, waiting for transfers between devices: 630 us -> 0.03 us  [the longest x1 0.02 us: on_device(): down_here = lax.all_gather(down_weight, MLP_DATA, axis=0, tiled=True)]
    ppermute x16 -> x85, waiting for transfers between devices: 391 us -> 628 us  [the longest x42 519 us: shift(): return lax.ppermute(value, axes, pairs)]
    psum x1 -> x0, blocking collectives: 73.8 us -> none  [on_device(): lax.psum((jnp.stack([query_gain_grad, key_gain_grad, branch_gain_grad, se...]
    dot_general x10, matrix products: 122 us -> 57.3 us  [product(): return jnp.dot(left_side, right_side, preferred_element_type=f32)]
    dot_general x4, matrix products: 129 us -> 73 us  [product_left(): lax.dot_general(left_side, right_side, (((0,), (0,)), ((), ())), preferre...]
    unnamed x165 -> x221, local copies, waits for them, and re-layouts: 86.2 us -> 52.9 us
  transfers between devices with their start and end apart: 24 -> 93, of which waited for: 11 -> 39; matrix products, arithmetic and copies ran while one was open for 12% -> 27% of each run, Pallas kernels for 0% -> 1%
where the time goes in v1:
time: 1300 us; the launch traced here: 1290 us
  waiting for transfers between devices  628 us (48%)
  matrix products  196 us (15%)
  local copies, waits for them, and re-layouts  167 us (13%)
  starting transfers between devices  153 us (12%)
  other arithmetic  91 us (7%)
  Pallas kernels  37.2 us (3%)
  between operations  17.4 us (1%)
    ppermute x42, waiting for transfers between devices, shift(): return lax.ppermute(value, axes, pairs)  519 us
    ppermute x42, starting transfers between devices, shift(): return lax.ppermute(value, axes, pairs)  101 us
    ppermute x11, waiting for transfers between devices, small_sum(): value = value + lax.ppermute(value, axis, [(0, 1), (1, 0)])  95.6 us
    dot_general x4, matrix products, product_left(): lax.dot_general(left_side, right_side, (((0,), (0,)), ((), ())), preferre...  73 us
    dot_general x13, matrix products, product_right(): lax.dot_general(left_side, right_side, (((1,), (1,)), ((), ())), preferre...  65.6 us
    dot_general x10, matrix products, product(): return jnp.dot(left_side, right_side, preferred_element_type=f32)  57.3 us
    unnamed x221, local copies, waits for them, and re-layouts  52.9 us
    ppermute x11, starting transfers between devices, small_sum(): value = value + lax.ppermute(value, axis, [(0, 1), (1, 0)])  44 us
  transfers between devices with their start and end apart: 93, of which 39 were waited for; matrix products, arithmetic and copies ran while one was open for 27% of the time, Pallas kernels for 1%

profile of v1, /device:TPU:0, one launch (start us, length us, event | category | flops | bytes accessed | tf_op | source)
XLA Modules:
  0.0 1289.5 jit_solution(4377238191038559903)
XLA Ops:
  21.6 14.9 %collective-permute-done.9 = bf16[2,64,768]{2,1,0:T(8,128)(2,1)S(1)} collective-permute-done((bf16[2,64,768]{2,1,0:T(8,128)(2,1)S(1)}, bf16[2,64,768]{2,1,0:T(8,128)(2,1)S(1)}, u32[]{:S(2)}, u32[]{:S(2)}) %collective-permute-start.9) | collective-permute-done | bytes 196640 | tf_op jit(solution)/shard_map/ppermute | solution.py:59
  41.2 8.5 collective-permute-done.18
  49.8 13.3 %collective-permute-done.19 = bf16[64,2048]{1,0:T(8,128)(2,1)S(1)} collective-permute-done((bf16[64,2048]{1,0:T(8,128)(2,1)S(1)}, bf16[64,2048]{1,0:T(8,128)(2,1)S(1)}, u32[]{:S(2)}, u32[]{:S(2)}) %collective-permute-start.19) | collective-permute-done | bytes 262176 | tf_op jit(solution)/shard_map/ppermute | solution.py:59
  85.2 61.1 %collective-permute-done.24 = bf16[2,64,2048]{2,1,0:T(8,128)(2,1)} collective-permute-done((bf16[2,64,2048]{2,1,0:T(8,128)(2,1)}, bf16[2,64,2048]{2,1,0:T(8,128)(2,1)}, u32[]{:S(2)}, u32[]{:S(2)}) %collective-permute-start.24) | collective-permute-done | bytes 524320 | tf_op jit(solution)/shard_map/ppermute | solution.py:59
  151.4 11.9 collective-permute-done.26
  176.3 7.8 collective-permute-done.5
  196.5 10.0 fusion.233
  209.9 31.4 %collective-permute-start.11 = (f32[2,2048]{1,0:T(2,128)S(1)}, f32[2,2048]{1,0:T(2,128)S(1)}, u32[]{:S(2)}, u32[]{:S(2)}) collective-permute-start(f32[2,2048]{1,0:T(2,128)S(1)} %pad_maximum_fusion.4), channel_id=1, source_target_pairs={{0,4},{4,0},{1,5},{5,1},{2,6},{6,2},{3,7},{7,3},{8,12},{12,8},{9,1... | collective-permute-start | bytes 49160 | tf_op jit(solution)/shard_map/ppermute | solution.py:105
  259.4 8.0 fusion.227
  275.9 15.2 %attend.1 = (f32[2048,256]{1,0:T(8,128)S(1)}, f32[2,1,2048]{2,1,0:T(1,128)S(1)}) custom-call(s32[4]{0:T(128)S(1)} %and_select_fusion.low_ref, s32[1,2048]{1,0:T(1,128)S(1)} %bitcast.388, bf16[2048,256]{1,0:T(8,128)(2,1)S(1)} %get-tuple-element.117.q_ref, bf16[2048,256]{1,0:T(8,128)(2,1)S(1)} %get-tuple-element.116.k_ref, bf16[2048,256]{1,0:T(8,128)(2,1)S(1)} %slice.441.v_ref), custom_call_target="tpu_custom_call" | custom-call | tf_op jit(solution)/shard_map/attend/pallas_call | solution.py:164
  299.3 8.3 collective-permute-done.15
  307.6 10.4 collective-permute-done.16
  344.5 21.7 %collective-permute-done.36 = bf16[256,2048]{1,0:T(8,128)(2,1)S(1)} collective-permute-done((bf16[256,2048]{1,0:T(8,128)(2,1)S(1)}, bf16[256,2048]{1,0:T(8,128)(2,1)S(1)}, u32[]{:S(2)}, u32[]{:S(2)}) %collective-permute-start.36) | collective-permute-done | bytes 1048608 | tf_op jit(solution)/shard_map/ppermute | solution.py:59
  366.2 65.3 %collective-permute-done.32 = bf16[256,2048]{1,0:T(8,128)(2,1)S(1)} collective-permute-done((bf16[256,2048]{1,0:T(8,128)(2,1)S(1)}, bf16[256,2048]{1,0:T(8,128)(2,1)S(1)}, u32[]{:S(2)}, u32[]{:S(2)}) %collective-permute-start.32) | collective-permute-done | bytes 1048608 | tf_op jit(solution)/shard_map/ppermute | solution.py:59
  433.0 7.2 fusion.63
  448.1 7.7 fusion.67
  461.0 7.2 fusion.71
  471.6 7.4 fusion.75
  490.4 39.5 %collective-permute-done.31 = bf16[256,2048]{1,0:T(8,128)(2,1)S(1)} collective-permute-done((bf16[256,2048]{1,0:T(8,128)(2,1)S(1)}, bf16[256,2048]{1,0:T(8,128)(2,1)S(1)}, u32[]{:S(2)}, u32[]{:S(2)}) %collective-permute-start.31) | collective-permute-done | bytes 1048608 | tf_op jit(solution)/shard_map/ppermute | solution.py:59
  529.9 27.0 %collective-permute-done.35 = bf16[256,2048]{1,0:T(8,128)(2,1)S(1)} collective-permute-done((bf16[256,2048]{1,0:T(8,128)(2,1)S(1)}, bf16[256,2048]{1,0:T(8,128)(2,1)S(1)}, u32[]{:S(2)}, u32[]{:S(2)}) %collective-permute-start.35) | collective-permute-done | bytes 1048608 | tf_op jit(solution)/shard_map/ppermute | solution.py:59
  561.5 22.2 %collective-permute-start.42 = (bf16[256,2048]{1,0:T(8,128)(2,1)S(1)}, bf16[256,2048]{1,0:T(8,128)(2,1)}, u32[]{:S(2)}, u32[]{:S(2)}) collective-permute-start(bf16[256,2048]{1,0:T(8,128)(2,1)S(1)} %get-tuple-element.71), channel_id=1, source_target_pairs={{0,2},{2,0},{4,6},{6,4},{1,3},{3,1},{5,7},{7,5},{8,10},{10,8},{12,... | collective-permute-start | bytes 3145736 | tf_op jit(solution)/shard_map/ppermute | solution.py:59
  585.1 22.1 %collective-permute-done.42 = bf16[256,2048]{1,0:T(8,128)(2,1)} collective-permute-done((bf16[256,2048]{1,0:T(8,128)(2,1)S(1)}, bf16[256,2048]{1,0:T(8,128)(2,1)}, u32[]{:S(2)}, u32[]{:S(2)}) %collective-permute-start.42) | collective-permute-done | bytes 1048608 | tf_op jit(solution)/shard_map/ppermute | solution.py:59
  612.1 8.0 fusion.83
  621.9 9.8 collective-permute-done.50
  631.7 44.4 %collective-permute-done.46 = bf16[256,2048]{1,0:T(8,128)(2,1)} collective-permute-done((bf16[256,2048]{1,0:T(8,128)(2,1)S(1)}, bf16[256,2048]{1,0:T(8,128)(2,1)}, u32[]{:S(2)}, u32[]{:S(2)}) %collective-permute-start.46) | collective-permute-done | bytes 1048608 | tf_op jit(solution)/shard_map/ppermute | solution.py:59
  676.1 7.1 multiply_convert_fusion.8
  683.3 7.6 fusion.91
  691.6 6.6 multiply_convert_fusion.6
  698.2 7.9 fusion.99
  712.2 7.7 fusion.107
  729.1 39.2 %collective-permute-done.45 = bf16[256,2048]{1,0:T(8,128)(2,1)S(1)} collective-permute-done((bf16[256,2048]{1,0:T(8,128)(2,1)S(1)}, bf16[256,2048]{1,0:T(8,128)(2,1)S(1)}, u32[]{:S(2)}, u32[]{:S(2)}) %collective-permute-start.45) | collective-permute-done | bytes 1048608 | tf_op jit(solution)/shard_map/ppermute | solution.py:59
  768.3 26.4 %collective-permute-done.49 = bf16[256,2048]{1,0:T(8,128)(2,1)S(1)} collective-permute-done((bf16[256,2048]{1,0:T(8,128)(2,1)S(1)}, bf16[256,2048]{1,0:T(8,128)(2,1)S(1)}, u32[]{:S(2)}, u32[]{:S(2)}) %collective-permute-start.49) | collective-permute-done | bytes 1048608 | tf_op jit(solution)/shard_map/ppermute | solution.py:59
  811.5 22.2 %collective-permute-start.55 = (bf16[2,256,256]{2,1,0:T(8,128)(2,1)S(1)}, bf16[2,256,256]{2,1,0:T(8,128)(2,1)S(1)}, u32[]{:S(2)}, u32[]{:S(2)}) collective-permute-start(bf16[2,256,256]{2,1,0:T(8,128)(2,1)S(1)} %get-tuple-element.141), channel_id=1, source_target_pairs={{0,2},{2,0},{4,6},{6,4},{1,3},{3,1},{5,7},{7,5},{8,10},{10,8},{12,... | collective-permute-start | bytes 786440 | tf_op jit(solution)/shard_map/ppermute | solution.py:59
  836.1 8.6 collective-permute-done.55
  844.8 10.2 collective-permute-done.56
  856.0 22.0 %attend_back.1 = (f32[2048,256]{1,0:T(8,128)}, f32[2048,256]{1,0:T(8,128)}, f32[2048,256]{1,0:T(8,128)}) custom-call(s32[4]{0:T(128)} %copy-done.6, s32[1,2048]{1,0:T(1,128)} %bitcast.389, bf16[2048,256]{1,0:T(8,128)(2,1)} %copy-done.1, bf16[2048,256]{1,0:T(8,128)(2,1)} %copy-done, bf16[2048,256]{1,0:T(8,128)(2,1)} %copy-done.2, f32[2048,256]{1,0:T(8,128)} %copy-done.3, ...), custom_call_target="tpu_custom_call" | custom-call | tf_op jit(solution)/shard_map/attend_back/pallas_call | solution.py:229
  915.1 10.9 convolution_convert_fusion
  940.7 12.8 fusion.29
  968.4 45.7 %fusion.17 = bf16[2048,2048]{1,0:T(8,128)(2,1)} fusion(bf16[2048,2048]{1,0:T(8,128)(2,1)} %constant_dynamic-update-slice_fusion, bf16[512,1024]{1,0:T(8,128)(2,1)S(1)} %copy-done.99, bf16[512,1024]{1,0:T(8,128)(2,1)S(1)} %copy-done.98, bf16[512,1024]{1,0:T(8,128)(2,1)S(1)} %copy-done.96, bf16[512,1024]{1,0:T(8,128)(2,1)S(1)} %copy-done.94, ...), kind=kOutput, calls=%fused_computation.20 | convolution fusion | flops 17251172352 | bytes 25165824 | tf_op jit(solution)/shard_map/dot_general | solution.py:116
  1027.6 7.1 collective-permute-done.72
  1034.7 6.8 fusion.16
  1081.3 73.8 %collective-permute-done.82 = f32[5,2048]{1,0:T(8,128)S(1)} collective-permute-done((f32[5,2048]{1,0:T(8,128)S(1)}, f32[5,2048]{1,0:T(8,128)S(1)}, u32[]{:S(2)}, u32[]{:S(2)}) %collective-permute-start.82) | collective-permute-done | bytes 40992 | tf_op jit(solution)/shard_map/ppermute | solution.py:105
  1178.9 8.6 collective-permute-done.69
  1205.1 8.9 collective-permute-done.73
  1214.1 10.5 collective-permute-done.74
  1230.0 33.1 %collective-permute-done.78 = bf16[2,64,2048]{2,1,0:T(8,128)(2,1)S(1)} collective-permute-done((bf16[2,64,2048]{2,1,0:T(8,128)(2,1)S(1)}, bf16[2,64,2048]{2,1,0:T(8,128)(2,1)S(1)}, u32[]{:S(2)}, u32[]{:S(2)}) %collective-permute-start.78) | collective-permute-done | bytes 524320 | tf_op jit(solution)/shard_map/ppermute | solution.py:59
  1268.4 7.4 copy.84
  1275.9 6.4 reshape.371
  (572 shorter events, 384.1 us)
Async XLA Ops:
  7.2 189.4 %all-gather.5.cloned.1.call-start = ((), (), s32[]{:S(2)}) async-start(), calls=%async_computation.4 | async-start | bytes 3932160 | tf_op jit(solution)/shard_map/all_gather | solution.py:350
  37.4 221.5 %all-gather.7.cloned.1.call-start = ((), (), s32[]{:S(2)}) async-start(), calls=%async_computation.5 | async-start | bytes 5242880 | tf_op jit(solution)/shard_map/all_gather | solution.py:364
  37.6 25.6 %collective-permute-start.20 = (bf16[64,2048]{1,0:T(8,128)(2,1)S(1)}, bf16[64,2048]{1,0:T(8,128)(2,1)S(1)}, u32[]{:S(2)}, u32[]{:S(2)}) collective-permute-start(bf16[64,2048]{1,0:T(8,128)(2,1)S(1)} %copy-done.68), channel_id=1, source_target_pairs={{0,6},{2,4},{4,2},{6,0},{1,7},{3,5},{5,3},{7,1},{8,14},{10,12},{12... | collective-permute-start | bytes 786440 | tf_op jit(solution)/shard_map/ppermute | solution.py:59
  64.2 367.9 %all-gather.9.cloned.1.call-start = ((), (), s32[]{:S(2)}) async-start(), calls=%async_computation.6 | async-start | bytes 10485760 | tf_op jit(solution)/shard_map/all_gather | solution.py:375
  75.4 100.4 %collective-permute-start.3 = (bf16[256,2048]{1,0:T(8,128)(2,1)S(1)}, bf16[256,2048]{1,0:T(8,128)(2,1)}, u32[]{:S(2)}, u32[]{:S(2)}) collective-permute-start(bf16[256,2048]{1,0:T(8,128)(2,1)S(1)} %bitcast.402), channel_id=1, source_target_pairs={{0,4},{2,6},{4,0},{6,2},{1,5},{3,7},{5,1},{7,3},{8,12},{10,14},{12... | collective-permute-start | bytes 3145736 | tf_op jit(solution)/shard_map/ppermute | solution.py:59
  75.4 95.0 %collective-permute-start.1 = (bf16[256,2048]{1,0:T(8,128)(2,1)S(1)}, bf16[256,2048]{1,0:T(8,128)(2,1)}, u32[]{:S(2)}, u32[]{:S(2)}) collective-permute-start(bf16[256,2048]{1,0:T(8,128)(2,1)S(1)} %bitcast.403), channel_id=1, source_target_pairs={{0,2},{2,0},{4,6},{6,4},{1,3},{3,1},{5,7},{7,5},{8,10},{10,8},{12,... | collective-permute-start | bytes 3145736 | tf_op jit(solution)/shard_map/ppermute | solution.py:59
  78.3 105.8 %collective-permute-start = (bf16[256,2048]{1,0:T(8,128)(2,1)S(1)}, bf16[256,2048]{1,0:T(8,128)(2,1)}, u32[]{:S(2)}, u32[]{:S(2)}) collective-permute-start(bf16[256,2048]{1,0:T(8,128)(2,1)S(1)} %bitcast.404), channel_id=1, source_target_pairs={{0,1},{1,0},{2,3},{3,2},{4,5},{5,4},{6,7},{7,6},{8,9},{9,8},{10,11... | collective-permute-start | bytes 3145736 | tf_op jit(solution)/shard_map/ppermute | solution.py:63
  81.1 65.2 %collective-permute-start.24 = (bf16[2,64,2048]{2,1,0:T(8,128)(2,1)}, bf16[2,64,2048]{2,1,0:T(8,128)(2,1)}, u32[]{:S(2)}, u32[]{:S(2)}) collective-permute-start(bf16[2,64,2048]{2,1,0:T(8,128)(2,1)} %get-tuple-element.124), channel_id=1, source_target_pairs={{0,2},{2,0},{4,6},{6,4},{1,3},{3,1},{5,7},{7,5},{8,10},{10,8},{12,... | collective-permute-start | bytes 1572872 | tf_op jit(solution)/shard_map/ppermute | solution.py:59
  82.7 66.2 %collective-permute-start.25 = (bf16[2,64,2048]{2,1,0:T(8,128)(2,1)}, bf16[2,64,2048]{2,1,0:T(8,128)(2,1)S(1)}, u32[]{:S(2)}, u32[]{:S(2)}) collective-permute-start(bf16[2,64,2048]{2,1,0:T(8,128)(2,1)} %get-tuple-element.125), channel_id=1, source_target_pairs={{0,4},{2,6},{4,0},{6,2},{1,5},{3,7},{5,1},{7,3},{8,12},{10,14},{12... | collective-permute-start | bytes 1572872 | tf_op jit(solution)/shard_map/ppermute | solution.py:59
  148.9 35.1 %collective-permute-start.5 = (bf16[256,2048]{1,0:T(8,128)(2,1)S(1)}, bf16[256,2048]{1,0:T(8,128)(2,1)}, u32[]{:S(2)}, u32[]{:S(2)}) collective-permute-start(bf16[256,2048]{1,0:T(8,128)(2,1)S(1)} %bitcast.405), channel_id=1, source_target_pairs={{0,6},{2,4},{4,2},{6,0},{1,7},{3,5},{5,3},{7,1},{8,14},{10,12},{12... | collective-permute-start | bytes 3145736 | tf_op jit(solution)/shard_map/ppermute | solution.py:59
  164.7 278.2 %all-gather.11.cloned.1.call-start = ((), (), s32[]{:S(2)}) async-start(), calls=%async_computation.7 | async-start | bytes 5242880 | tf_op jit(solution)/shard_map/all_gather | solution.py:379
  209.9 33.8 %collective-permute-start.11 = (f32[2,2048]{1,0:T(2,128)S(1)}, f32[2,2048]{1,0:T(2,128)S(1)}, u32[]{:S(2)}, u32[]{:S(2)}) collective-permute-start(f32[2,2048]{1,0:T(2,128)S(1)} %pad_maximum_fusion.4), channel_id=1, source_target_pairs={{0,4},{4,0},{1,5},{5,1},{2,6},{6,2},{3,7},{7,3},{8,12},{12,8},{9,1... | collective-permute-start | bytes 49160 | tf_op jit(solution)/shard_map/ppermute | solution.py:105
  258.9 59.8 %collective-permute-start.21 = (bf16[16,64,2048]{2,1,0:T(8,128)(2,1)}, bf16[16,64,2048]{2,1,0:T(8,128)(2,1)}, u32[]{:S(2)}, u32[]{:S(2)}) collective-permute-start(bf16[16,64,2048]{2,1,0:T(8,128)(2,1)} %bitcast.413), channel_id=1, source_target_pairs={{0,1},{1,0},{2,3},{3,2},{4,5},{5,4},{6,7},{7,6},{8,9},{9,8},{10,11... | collective-permute-start | bytes 12582920 | tf_op jit(solution)/shard_map/ppermute | solution.py:63
  292.5 869.4 %reduce-scatter.5.cloned.1.call-start = ((), (), s32[]{:S(2)}) async-start(), calls=%async_computation.8 | async-start | bytes 3932160 | tf_op jit(solution)/shard_map/reduce_scatter | solution.py:318
  338.2 28.0 %collective-permute-start.36 = (bf16[256,2048]{1,0:T(8,128)(2,1)S(1)}, bf16[256,2048]{1,0:T(8,128)(2,1)S(1)}, u32[]{:S(2)}, u32[]{:S(2)}) collective-permute-start(bf16[256,2048]{1,0:T(8,128)(2,1)S(1)} %get-tuple-element.73), channel_id=1, source_target_pairs={{0,6},{2,4},{4,2},{6,0},{1,7},{3,5},{5,3},{7,1},{8,14},{10,12},{12... | collective-permute-start | bytes 3145736 | tf_op jit(solution)/shard_map/ppermute | solution.py:59
  340.8 90.8 %collective-permute-start.32 = (bf16[256,2048]{1,0:T(8,128)(2,1)S(1)}, bf16[256,2048]{1,0:T(8,128)(2,1)S(1)}, u32[]{:S(2)}, u32[]{:S(2)}) collective-permute-start(bf16[256,2048]{1,0:T(8,128)(2,1)S(1)} %get-tuple-element.73), channel_id=1, source_target_pairs={{0,4},{2,6},{4,0},{6,2},{1,5},{3,7},{5,1},{7,3},{8,12},{10,14},{12... | collective-permute-start | bytes 3145736 | tf_op jit(solution)/shard_map/ppermute | solution.py:59
  344.5 87.1 %collective-permute-start.28 = (bf16[256,2048]{1,0:T(8,128)(2,1)S(1)}, bf16[256,2048]{1,0:T(8,128)(2,1)}, u32[]{:S(2)}, u32[]{:S(2)}) collective-permute-start(bf16[256,2048]{1,0:T(8,128)(2,1)S(1)} %get-tuple-element.73), channel_id=1, source_target_pairs={{0,2},{2,0},{4,6},{6,4},{1,3},{3,1},{5,7},{7,5},{8,10},{10,8},{12,... | collective-permute-start | bytes 3145736 | tf_op jit(solution)/shard_map/ppermute | solution.py:59
  344.5 87.6 %collective-permute-start.22 = (bf16[256,2048]{1,0:T(8,128)(2,1)S(1)}, bf16[256,2048]{1,0:T(8,128)(2,1)S(1)}, u32[]{:S(2)}, u32[]{:S(2)}) collective-permute-start(bf16[256,2048]{1,0:T(8,128)(2,1)S(1)} %get-tuple-element.73), channel_id=1, source_target_pairs={{0,1},{1,0},{2,3},{3,2},{4,5},{5,4},{6,7},{7,6},{8,9},{9,8},{10,11... | collective-permute-start | bytes 3145736 | tf_op jit(solution)/shard_map/ppermute | solution.py:63
  366.2 105.3 %collective-permute-start.37 = (bf16[256,2048]{1,0:T(8,128)(2,1)S(1)}, bf16[256,2048]{1,0:T(8,128)(2,1)}, u32[]{:S(2)}, u32[]{:S(2)}) collective-permute-start(bf16[256,2048]{1,0:T(8,128)(2,1)S(1)} %collective-permute-done.36), channel_id=1, source_target_pairs={{0,1},{1,0},{2,3},{3,2},{4,5},{5,4},{6,7},{7,6},{8,9},{9,8},{10,11... | collective-permute-start | bytes 3145736 | tf_op jit(solution)/shard_map/ppermute | solution.py:63
  431.6 29.5 %collective-permute-start.33 = (bf16[256,2048]{1,0:T(8,128)(2,1)S(1)}, bf16[256,2048]{1,0:T(8,128)(2,1)}, u32[]{:S(2)}, u32[]{:S(2)}) collective-permute-start(bf16[256,2048]{1,0:T(8,128)(2,1)S(1)} %collective-permute-done.32), channel_id=1, source_target_pairs={{0,1},{1,0},{2,3},{3,2},{4,5},{5,4},{6,7},{7,6},{8,9},{9,8},{10,11... | collective-permute-start | bytes 3145736 | tf_op jit(solution)/shard_map/ppermute | solution.py:63
  448.0 42.4 %collective-permute-start.27 = (bf16[256,2048]{1,0:T(8,128)(2,1)S(1)}, bf16[256,2048]{1,0:T(8,128)(2,1)S(1)}, u32[]{:S(2)}, u32[]{:S(2)}) collective-permute-start(bf16[256,2048]{1,0:T(8,128)(2,1)S(1)} %slice.440), channel_id=1, source_target_pairs={{0,1},{1,0},{2,3},{3,2},{4,5},{5,4},{6,7},{7,6},{8,9},{9,8},{10,11... | collective-permute-start | bytes 3145736 | tf_op jit(solution)/shard_map/ppermute | solution.py:63
  460.5 23.7 %collective-permute-start.30 = (bf16[256,2048]{1,0:T(8,128)(2,1)S(1)}, bf16[256,2048]{1,0:T(8,128)(2,1)S(1)}, u32[]{:S(2)}, u32[]{:S(2)}) collective-permute-start(bf16[256,2048]{1,0:T(8,128)(2,1)S(1)} %slice.439), channel_id=1, source_target_pairs={{0,1},{1,0},{2,3},{3,2},{4,5},{5,4},{6,7},{7,6},{8,9},{9,8},{10,11... | collective-permute-start | bytes 3145736 | tf_op jit(solution)/shard_map/ppermute | solution.py:63
  484.5 45.4 %collective-permute-start.31 = (bf16[256,2048]{1,0:T(8,128)(2,1)S(1)}, bf16[256,2048]{1,0:T(8,128)(2,1)S(1)}, u32[]{:S(2)}, u32[]{:S(2)}) collective-permute-start(bf16[256,2048]{1,0:T(8,128)(2,1)S(1)} %fusion.59), channel_id=1, source_target_pairs={{0,2},{2,0},{4,6},{6,4},{1,3},{3,1},{5,7},{7,5},{8,10},{10,8},{12,... | collective-permute-start | bytes 3145736 | tf_op jit(solution)/shard_map/ppermute | solution.py:59
  484.9 72.0 %collective-permute-start.35 = (bf16[256,2048]{1,0:T(8,128)(2,1)S(1)}, bf16[256,2048]{1,0:T(8,128)(2,1)S(1)}, u32[]{:S(2)}, u32[]{:S(2)}) collective-permute-start(bf16[256,2048]{1,0:T(8,128)(2,1)S(1)} %fusion.58), channel_id=1, source_target_pairs={{0,4},{2,6},{4,0},{6,2},{1,5},{3,7},{5,1},{7,3},{8,12},{10,14},{12... | collective-permute-start | bytes 3145736 | tf_op jit(solution)/shard_map/ppermute | solution.py:59
  486.8 70.1 %collective-permute-start.39 = (bf16[256,2048]{1,0:T(8,128)(2,1)S(1)}, bf16[256,2048]{1,0:T(8,128)(2,1)S(1)}, u32[]{:S(2)}, u32[]{:S(2)}) collective-permute-start(bf16[256,2048]{1,0:T(8,128)(2,1)S(1)} %fusion.57), channel_id=1, source_target_pairs={{0,6},{2,4},{4,2},{6,0},{1,7},{3,5},{5,3},{7,1},{8,14},{10,12},{12... | collective-permute-start | bytes 3145736 | tf_op jit(solution)/shard_map/ppermute | solution.py:59
  561.5 45.8 %collective-permute-start.42 = (bf16[256,2048]{1,0:T(8,128)(2,1)S(1)}, bf16[256,2048]{1,0:T(8,128)(2,1)}, u32[]{:S(2)}, u32[]{:S(2)}) collective-permute-start(bf16[256,2048]{1,0:T(8,128)(2,1)S(1)} %get-tuple-element.71), channel_id=1, source_target_pairs={{0,2},{2,0},{4,6},{6,4},{1,3},{3,1},{5,7},{7,5},{8,10},{10,8},{12,... | collective-permute-start | bytes 3145736 | tf_op jit(solution)/shard_map/ppermute | solution.py:59
  583.6 48.1 %collective-permute-start.50 = (bf16[256,2048]{1,0:T(8,128)(2,1)S(1)}, bf16[256,2048]{1,0:T(8,128)(2,1)S(1)}, u32[]{:S(2)}, u32[]{:S(2)}) collective-permute-start(bf16[256,2048]{1,0:T(8,128)(2,1)S(1)} %get-tuple-element.71), channel_id=1, source_target_pairs={{0,6},{2,4},{4,2},{6,0},{1,7},{3,5},{5,3},{7,1},{8,14},{10,12},{12... | collective-permute-start | bytes 3145736 | tf_op jit(solution)/shard_map/ppermute | solution.py:59
  585.1 91.1 %collective-permute-start.46 = (bf16[256,2048]{1,0:T(8,128)(2,1)S(1)}, bf16[256,2048]{1,0:T(8,128)(2,1)}, u32[]{:S(2)}, u32[]{:S(2)}) collective-permute-start(bf16[256,2048]{1,0:T(8,128)(2,1)S(1)} %get-tuple-element.71), channel_id=1, source_target_pairs={{0,4},{2,6},{4,0},{6,2},{1,5},{3,7},{5,1},{7,3},{8,12},{10,14},{12... | collective-permute-start | bytes 3145736 | tf_op jit(solution)/shard_map/ppermute | solution.py:59
  607.2 68.9 %collective-permute-start.43 = (bf16[256,2048]{1,0:T(8,128)(2,1)}, bf16[256,2048]{1,0:T(8,128)(2,1)}, u32[]{:S(2)}, u32[]{:S(2)}) collective-permute-start(bf16[256,2048]{1,0:T(8,128)(2,1)} %collective-permute-done.42), channel_id=1, source_target_pairs={{0,1},{1,0},{2,3},{3,2},{4,5},{5,4},{6,7},{7,6},{8,9},{9,8},{10,11... | collective-permute-start | bytes 3145736 | tf_op jit(solution)/shard_map/ppermute | solution.py:63
  621.4 107.7 %collective-permute-start.41 = (bf16[256,2048]{1,0:T(8,128)(2,1)}, bf16[256,2048]{1,0:T(8,128)(2,1)}, u32[]{:S(2)}, u32[]{:S(2)}) collective-permute-start(bf16[256,2048]{1,0:T(8,128)(2,1)} %slice.436), channel_id=1, source_target_pairs={{0,1},{1,0},{2,3},{3,2},{4,5},{5,4},{6,7},{7,6},{8,9},{9,8},{10,11... | collective-permute-start | bytes 3145736 | tf_op jit(solution)/shard_map/ppermute | solution.py:63
  631.7 75.2 %collective-permute-start.51 = (bf16[256,2048]{1,0:T(8,128)(2,1)S(1)}, bf16[256,2048]{1,0:T(8,128)(2,1)}, u32[]{:S(2)}, u32[]{:S(2)}) collective-permute-start(bf16[256,2048]{1,0:T(8,128)(2,1)S(1)} %collective-permute-done.50), channel_id=1, source_target_pairs={{0,1},{1,0},{2,3},{3,2},{4,5},{5,4},{6,7},{7,6},{8,9},{9,8},{10,11... | collective-permute-start | bytes 3145736 | tf_op jit(solution)/shard_map/ppermute | solution.py:63
  691.0 30.9 %collective-permute-start.44 = (bf16[256,2048]{1,0:T(8,128)(2,1)S(1)}, bf16[256,2048]{1,0:T(8,128)(2,1)S(1)}, u32[]{:S(2)}, u32[]{:S(2)}) collective-permute-start(bf16[256,2048]{1,0:T(8,128)(2,1)S(1)} %slice.435), channel_id=1, source_target_pairs={{0,1},{1,0},{2,3},{3,2},{4,5},{5,4},{6,7},{7,6},{8,9},{9,8},{10,11... | collective-permute-start | bytes 3145736 | tf_op jit(solution)/shard_map/ppermute | solution.py:63
  722.2 46.1 %collective-permute-start.45 = (bf16[256,2048]{1,0:T(8,128)(2,1)S(1)}, bf16[256,2048]{1,0:T(8,128)(2,1)S(1)}, u32[]{:S(2)}, u32[]{:S(2)}) collective-permute-start(bf16[256,2048]{1,0:T(8,128)(2,1)S(1)} %fusion.56), channel_id=1, source_target_pairs={{0,2},{2,0},{4,6},{6,4},{1,3},{3,1},{5,7},{7,5},{8,10},{10,8},{12,... | collective-permute-start | bytes 3145736 | tf_op jit(solution)/shard_map/ppermute | solution.py:59
  722.6 72.0 %collective-permute-start.49 = (bf16[256,2048]{1,0:T(8,128)(2,1)S(1)}, bf16[256,2048]{1,0:T(8,128)(2,1)S(1)}, u32[]{:S(2)}, u32[]{:S(2)}) collective-permute-start(bf16[256,2048]{1,0:T(8,128)(2,1)S(1)} %fusion.55), channel_id=1, source_target_pairs={{0,4},{2,6},{4,0},{6,2},{1,5},{3,7},{5,1},{7,3},{8,12},{10,14},{12... | collective-permute-start | bytes 3145736 | tf_op jit(solution)/shard_map/ppermute | solution.py:59
  727.2 67.4 %collective-permute-start.53 = (bf16[256,2048]{1,0:T(8,128)(2,1)S(1)}, bf16[256,2048]{1,0:T(8,128)(2,1)S(1)}, u32[]{:S(2)}, u32[]{:S(2)}) collective-permute-start(bf16[256,2048]{1,0:T(8,128)(2,1)S(1)} %fusion.54), channel_id=1, source_target_pairs={{0,6},{2,4},{4,2},{6,0},{1,7},{3,5},{5,3},{7,1},{8,14},{10,12},{12... | collective-permute-start | bytes 3145736 | tf_op jit(solution)/shard_map/ppermute | solution.py:59
  811.5 33.3 %collective-permute-start.55 = (bf16[2,256,256]{2,1,0:T(8,128)(2,1)S(1)}, bf16[2,256,256]{2,1,0:T(8,128)(2,1)S(1)}, u32[]{:S(2)}, u32[]{:S(2)}) collective-permute-start(bf16[2,256,256]{2,1,0:T(8,128)(2,1)S(1)} %get-tuple-element.141), channel_id=1, source_target_pairs={{0,2},{2,0},{4,6},{6,4},{1,3},{3,1},{5,7},{7,5},{8,10},{10,8},{12,... | collective-permute-start | bytes 786440 | tf_op jit(solution)/shard_map/ppermute | solution.py:59
  926.0 243.0 %reduce-scatter.11.cloned.1.call-start = ((), (), s32[]{:S(2)}) async-start(), calls=%async_computation.11 | async-start | bytes 5242880 | tf_op jit(solution)/shard_map/reduce_scatter | solution.py:318
  953.6 222.9 %reduce-scatter.9.cloned.1.call-start = ((), (), s32[]{:S(2)}) async-start(), calls=%async_computation.10 | async-start | bytes 10485760 | tf_op jit(solution)/shard_map/reduce_scatter | solution.py:318
  1014.1 183.7 %reduce-scatter.7.cloned.1.call-start = ((), (), s32[]{:S(2)}) async-start(), calls=%async_computation.9 | async-start | bytes 5242880 | tf_op jit(solution)/shard_map/reduce_scatter | solution.py:318
  1054.3 110.0 %collective-permute-start.67 = (bf16[256,2048]{1,0:T(8,128)(2,1)}, bf16[256,2048]{1,0:T(8,128)(2,1)S(1)}, u32[]{:S(2)}, u32[]{:S(2)}) collective-permute-start(bf16[256,2048]{1,0:T(8,128)(2,1)} %slice.429), channel_id=1, source_target_pairs={{0,1},{1,0},{2,3},{3,2},{4,5},{5,4},{6,7},{7,6},{8,9},{9,8},{10,11... | collective-permute-start | bytes 3145736 | tf_op jit(solution)/shard_map/ppermute | solution.py:63
  1058.1 106.1 %collective-permute-start.62 = (bf16[256,2048]{1,0:T(8,128)(2,1)}, bf16[256,2048]{1,0:T(8,128)(2,1)}, u32[]{:S(2)}, u32[]{:S(2)}) collective-permute-start(bf16[256,2048]{1,0:T(8,128)(2,1)} %fusion.53), channel_id=1, source_target_pairs={{0,6},{2,4},{4,2},{6,0},{1,7},{3,5},{5,3},{7,1},{8,14},{10,12},{12... | collective-permute-start | bytes 3145736 | tf_op jit(solution)/shard_map/ppermute | solution.py:59
  1061.3 102.9 %collective-permute-start.66 = (bf16[256,2048]{1,0:T(8,128)(2,1)}, bf16[256,2048]{1,0:T(8,128)(2,1)}, u32[]{:S(2)}, u32[]{:S(2)}) collective-permute-start(bf16[256,2048]{1,0:T(8,128)(2,1)} %fusion.51), channel_id=1, source_target_pairs={{0,2},{2,0},{4,6},{6,4},{1,3},{3,1},{5,7},{7,5},{8,10},{10,8},{12,... | collective-permute-start | bytes 3145736 | tf_op jit(solution)/shard_map/ppermute | solution.py:59
  1063.8 100.5 %collective-permute-start.64 = (bf16[256,2048]{1,0:T(8,128)(2,1)}, bf16[256,2048]{1,0:T(8,128)(2,1)}, u32[]{:S(2)}, u32[]{:S(2)}) collective-permute-start(bf16[256,2048]{1,0:T(8,128)(2,1)} %fusion.52), channel_id=1, source_target_pairs={{0,4},{2,6},{4,0},{6,2},{1,5},{3,7},{5,1},{7,3},{8,12},{10,14},{12... | collective-permute-start | bytes 3145736 | tf_op jit(solution)/shard_map/ppermute | solution.py:59
  1079.6 75.5 %collective-permute-start.82 = (f32[5,2048]{1,0:T(8,128)S(1)}, f32[5,2048]{1,0:T(8,128)S(1)}, u32[]{:S(2)}, u32[]{:S(2)}) collective-permute-start(f32[5,2048]{1,0:T(8,128)S(1)} %add.763), channel_id=1, source_target_pairs={{0,4},{4,0},{1,5},{5,1},{2,6},{6,2},{3,7},{7,3},{8,12},{12,8},{9,1... | collective-permute-start | bytes 122888 | tf_op jit(solution)/shard_map/ppermute | solution.py:105
  1178.8 23.8 %collective-permute-start.76 = (bf16[4,64,2048]{2,1,0:T(8,128)(2,1)}, bf16[4,64,2048]{2,1,0:T(8,128)(2,1)}, u32[]{:S(2)}, u32[]{:S(2)}) collective-permute-start(bf16[4,64,2048]{2,1,0:T(8,128)(2,1)} %dynamic-slice_bitcast_fusion), channel_id=1, source_target_pairs={{0,1},{1,0},{2,3},{3,2},{4,5},{5,4},{6,7},{7,6},{8,9},{9,8},{10,11... | collective-permute-start | bytes 3145736 | tf_op jit(solution)/shard_map/ppermute | solution.py:63
  1204.1 25.9 %collective-permute-start.77 = (bf16[2,64,2048]{2,1,0:T(8,128)(2,1)S(1)}, bf16[2,64,2048]{2,1,0:T(8,128)(2,1)S(1)}, u32[]{:S(2)}, u32[]{:S(2)}) collective-permute-start(bf16[2,64,2048]{2,1,0:T(8,128)(2,1)S(1)} %get-tuple-element.110), channel_id=1, source_target_pairs={{0,2},{2,0},{4,6},{6,4},{1,3},{3,1},{5,7},{7,5},{8,10},{10,8},{12,... | collective-permute-start | bytes 1572872 | tf_op jit(solution)/shard_map/ppermute | solution.py:59
  1226.5 36.7 %collective-permute-start.78 = (bf16[2,64,2048]{2,1,0:T(8,128)(2,1)S(1)}, bf16[2,64,2048]{2,1,0:T(8,128)(2,1)S(1)}, u32[]{:S(2)}, u32[]{:S(2)}) collective-permute-start(bf16[2,64,2048]{2,1,0:T(8,128)(2,1)S(1)} %get-tuple-element.111), channel_id=1, source_target_pairs={{0,4},{2,6},{4,0},{6,2},{1,5},{3,7},{5,1},{7,3},{8,12},{10,14},{12... | collective-permute-start | bytes 1572872 | tf_op jit(solution)/shard_map/ppermute | solution.py:59
  1226.8 36.4 %collective-permute-start.79 = (bf16[2,64,2048]{2,1,0:T(8,128)(2,1)S(1)}, bf16[2,64,2048]{2,1,0:T(8,128)(2,1)S(1)}, u32[]{:S(2)}, u32[]{:S(2)}) collective-permute-start(bf16[2,64,2048]{2,1,0:T(8,128)(2,1)S(1)} %get-tuple-element.109), channel_id=1, source_target_pairs={{0,6},{2,4},{4,2},{6,0},{1,7},{3,5},{5,3},{7,1},{8,14},{10,12},{12... | collective-permute-start | bytes 1572872 | tf_op jit(solution)/shard_map/ppermute | solution.py:59
  (149 other events, 2389.8 us)
Sparse Core Ops, SparseCore 0:
  37.5 44.2 all-gather.4
  83.7 52.6 all-gather.6
  164.8 116.6 all-gather.8
  292.7 51.0 all-gather.10
  926.1 41.7 reduce-scatter.4
  970.7 52.6 reduce-scatter.10
  1026.8 87.8 reduce-scatter.8
  1117.6 52.6 reduce-scatter.6

commit v2 on v1

v2 whole, which is shorter than its diff:
```python
import itertools

import jax
import jax.numpy as jnp
import numpy as np
from jax import lax
from jax.experimental import pallas as pl
from jax.experimental.pallas import tpu as pltpu
from jax.sharding import Mesh
from jax.sharding import PartitionSpec as P

D = 2048
HEADS = 16
HEAD_DIM = 128
FF = 8192

norm_epsilon = 1e-06
rope_base = 500000.0
masked_score = -1e30
scale_factor = HEAD_DIM ** (-0.5)

AXES = ("dh", "dl", "zh", "zl", "c")
DATA = ("dh", "dl")
LINE = ("zh", "zl")
CTX = ("zh", "zl", "c")

BLOCK_Q = 512
BLOCK_K = 512

bf16 = jnp.bfloat16
f32 = jnp.float32


def sizes_of(axes):
    return tuple(lax.axis_size(a) for a in axes)


def offsets(axes):
    return list(itertools.product(*[range(n) for n in sizes_of(axes)]))


def linear(index, sizes):
    total = 0
    for i, n in zip(index, sizes):
        total = total * n + i
    return total


def shift(value, axes, steps):
    if not any(steps):
        return value
    sizes = sizes_of(axes)
    pairs = []
    for index in itertools.product(*[range(n) for n in sizes]):
        target = tuple((i + s) % n for i, s, n in zip(index, steps, sizes))
        pairs.append((linear(index, sizes), linear(target, sizes)))
    return lax.ppermute(value, axes, pairs)


def swap(value):
    return lax.ppermute(value, "c", [(0, 1), (1, 0)])


def place(axes, steps, sign=1):
    sizes = sizes_of(axes)
    here = [(lax.axis_index(a) + sign * s) % n for a, s, n in zip(axes, steps, sizes)]
    return linear(here, sizes)


def pick(value, index, axis=0):
    return lax.dynamic_index_in_dim(value, index, axis, keepdims=False)


def put(buffer, value, index):
    return lax.dynamic_update_slice_in_dim(buffer, value[None], index, 0)


def together(*values):
    return lax.optimization_barrier(values)


def line_order(count):
    return np.array(
        [sorted(range(count), key=lambda j: (abs(i - j), j != i ^ 1)) for i in range(count)],
        dtype=np.int32,
    )


class Line:
    def __init__(self, axes):
        self.axes = axes
        sizes = sizes_of(axes)
        self.count = sizes[0] * sizes[1]
        self.place = linear([lax.axis_index(a) for a in axes], sizes)
        self.order = line_order(self.count)

    def served(self, k):
        return jnp.asarray(self.order[:, k])[self.place]

    def hop(self, value, step, keep=lambda i: True):
        pairs = [
            (i, i + step) for i in range(self.count) if 0 <= i + step < self.count and keep(i)
        ]
        return lax.ppermute(value, self.axes, pairs)

    def choose(self, options, wanted):
        used = sorted({w for w in wanted if w is not None})
        value = options[used[0]]
        for w in used[1:]:
            mask = np.array([v == w for v in wanted])
            value = jnp.where(jnp.asarray(mask)[self.place], options[w], value)
        return value

    def gather(self, block, work, extra=None, plan=None):
        plan = plan or [[k] for k in range(self.count)]
        options, results, tied, arrived, swapped = {}, [], [], [], [None]
        for slot in range(self.count):
            if slot:
                wanted = []
                for i in range(self.count):
                    j = self.order[i, slot]
                    wanted.append((1, i - j) if j < i else (-1, j - i))
                arrived.append(self.choose(options, wanted))
            else:
                arrived.append(block)
            moved = ()
            if slot + 1 < self.count:
                moved = tuple(
                    self.hop(options[(step, slot)] if slot else block, step) for step in (1, -1)
                )
            other = swap(arrived[slot])
            done = [work(k, arrived[k], swapped[k]) for k in plan[slot]]
            more = extra(slot, tied) if extra else ()
            moved, other, done, more = together(moved, other, done, more)
            if moved:
                options[(1, slot + 1)], options[(-1, slot + 1)] = moved
            swapped.append(other)
            tied.append(more)
            results += done
        results.append(work(self.count, None, swapped[self.count]))
        return results, tied

    def scatter(self, parts, fill=None):
        count = self.count
        made = {count - 1: parts(count - 1)}
        last = {1: None, -1: None}
        tied = []
        for slot in range(1, count):
            far = count - slot
            moved = []
            for step in (1, -1):
                wanted = []
                for i in range(count):
                    j = i + step * far
                    wanted.append(int(np.argmax(self.order[i] == j)) if 0 <= j < count else None)
                value = self.choose(made, wanted)
                if last[step] is not None:
                    value = value + last[step].astype(f32)
                keep = lambda i: 0 <= i + step * far < count
                moved.append(self.hop(value.astype(bf16), step, keep))
            done = parts(far - 1)
            more = fill(slot, tied) if fill else ()
            moved, done, more = together(moved, done, more)
            tied.append(more)
            made[far - 1] = done
            last[1], last[-1] = moved
        return made[0] + last[1].astype(f32) + last[-1].astype(f32), tied


def scatter_sum(for_same, for_other):
    return for_same.astype(f32) + swap(for_other.astype(bf16)).astype(f32)


def exchange_cores(blocks):
    core = lax.axis_index("c")
    got = swap(pick(blocks, 1 - core, 1))
    return by_core(pick(blocks, core, 1), got)


def by_core(mine, other):
    shape = (mine.shape[0], 2) + mine.shape[1:]
    here = lax.broadcasted_iota(jnp.int32, shape, 1) == lax.axis_index("c")
    return jnp.where(here, mine[:, None], other[:, None])


def exchange_chips(pairs, chips):
    result = jnp.zeros_like(pairs)
    for steps in offsets(chips):
        piece = shift(pick(pairs, place(chips, steps)), chips, steps)
        result = put(result, piece, place(chips, steps, -1))
    return result


def exchange(blocks, chips):
    return exchange_chips(exchange_cores(blocks), chips)


def small_sum(value, axes):
    for axis in axes:
        if lax.axis_size(axis) == 2:
            value = value + lax.ppermute(value, axis, [(0, 1), (1, 0)])
        else:
            value = lax.psum(value, axis)
    return value


def product(left_side, right_side):
    return jnp.dot(left_side, right_side, preferred_element_type=f32)


def product_left(left_side, right_side):
    return lax.dot_general(
        left_side, right_side, (((0,), (0,)), ((), ())), preferred_element_type=f32
    )


def product_right(left_side, right_side):
    return lax.dot_general(
        left_side, right_side, (((1,), (1,)), ((), ())), preferred_element_type=f32
    )


def allowed_keys(shape, key_start, query_start, starts):
    key_place = key_start + lax.broadcasted_iota(jnp.int32, shape, 0)
    query_place = query_start + lax.broadcasted_iota(jnp.int32, shape, 1)
    return (key_place >= starts) & (key_place <= query_place)


def attend_kernel(low_ref, starts_ref, q_ref, k_ref, v_ref, out_ref, log_ref):
    block = pl.program_id(1)
    bq, bk = q_ref.shape[0], BLOCK_K
    queries, starts = q_ref[...], starts_ref[...]

    def step(j, carry):
        top, total, acc = carry
        rows = pl.ds(pl.multiple_of(j * bk, bk), bk)
        scores = product_right(k_ref[rows, :], queries) * scale_factor
        ok = allowed_keys(scores.shape, j * bk, block * bq, starts)
        scores = jnp.where(ok, scores, masked_score)
        new_top = jnp.maximum(top, jnp.max(scores, axis=0, keepdims=True))
        ratio = jnp.exp(top - new_top)
        expanded = jnp.exp(scores - new_top)
        total = total * ratio + jnp.sum(expanded, axis=0, keepdims=True)
        acc = acc * ratio + product_left(v_ref[rows, :], expanded.astype(bf16))
        return (new_top, total, acc)

    init = (
        jnp.full((1, bq), masked_score, f32),
        jnp.zeros((1, bq), f32),
        jnp.zeros((HEAD_DIM, bq), f32),
    )
    top, total, acc = lax.fori_loop(low_ref[block], (block * bq + bq) // bk, step, init)
    out_ref[...] = (acc / total).T
    log_ref[0] = top + jnp.log(total)


def attend(lows, starts, queries, keys, values):
    length, width = queries.shape
    heads, bq = width // HEAD_DIM, BLOCK_Q
    return pl.pallas_call(
        attend_kernel,
        grid_spec=pltpu.PrefetchScalarGridSpec(
            num_scalar_prefetch=1,
            grid=(heads, length // bq),
            in_specs=[
                pl.BlockSpec((1, bq), lambda h, i, low: (0, i)),
                pl.BlockSpec((bq, HEAD_DIM), lambda h, i, low: (i, h)),
                pl.BlockSpec((length, HEAD_DIM), lambda h, i, low: (0, h)),
                pl.BlockSpec((length, HEAD_DIM), lambda h, i, low: (0, h)),
            ],
            out_specs=[
                pl.BlockSpec((bq, HEAD_DIM), lambda h, i, low: (i, h)),
                pl.BlockSpec((1, 1, bq), lambda h, i, low: (h, 0, i)),
            ],
        ),
        out_shape=[
            jax.ShapeDtypeStruct((length, width), f32),
            jax.ShapeDtypeStruct((heads, 1, length), f32),
        ],
        compiler_params=pltpu.CompilerParams(vmem_limit_bytes=48 << 20),
        name="attend",
    )(lows, starts, queries, keys, values)


def attend_back_kernel(
    low_ref, starts_ref, q_ref, k_ref, v_ref, out_ref, log_ref, grad_ref, dq_ref, dk_ref, dv_ref
):
    length = q_ref.shape[0]
    bq, bk = BLOCK_Q, BLOCK_K
    dk_ref[...] = jnp.zeros_like(dk_ref)
    dv_ref[...] = jnp.zeros_like(dv_ref)

    def query_step(i, carry):
        queries_at = pl.ds(pl.multiple_of(i * bq, bq), bq)
        queries, grads = q_ref[queries_at, :], grad_ref[queries_at, :]
        starts = starts_ref[:, queries_at]
        log_total = log_ref[0, :, queries_at]
        inner = jnp.sum((grads.astype(f32) * out_ref[queries_at, :]).T, axis=0, keepdims=True)

        def step(j, acc):
            rows = pl.ds(pl.multiple_of(j * bk, bk), bk)
            keys = k_ref[rows, :]
            scores = product_right(keys, queries) * scale_factor
            ok = allowed_keys(scores.shape, j * bk, i * bq, starts)
            probs = jnp.where(ok, jnp.exp(scores - log_total), 0.0)
            dv_ref[rows, :] += product(probs.astype(bf16), grads)
            prob_grad = product_right(v_ref[rows, :], grads)
            score_grad = (probs * (prob_grad - inner)).astype(bf16)
            dk_ref[rows, :] += product(score_grad, queries) * scale_factor
            return acc + product_left(keys, score_grad)

        acc = lax.fori_loop(
            low_ref[i], (i * bq + bq) // bk, step, jnp.zeros((HEAD_DIM, bq), f32)
        )
        dq_ref[queries_at, :] = (acc * scale_factor).T
        return carry

    lax.fori_loop(0, length // bq, query_step, 0)


def attend_back(lows, starts, queries, keys, values, out, log_total, grads):
    length, width = queries.shape
    heads = width // HEAD_DIM
    column = pl.BlockSpec((length, HEAD_DIM), lambda h, low: (0, h))
    return pl.pallas_call(
        attend_back_kernel,
        grid_spec=pltpu.PrefetchScalarGridSpec(
            num_scalar_prefetch=1,
            grid=(heads,),
            in_specs=[
                pl.BlockSpec((1, length), lambda h, low: (0, 0)),
                column,
                column,
                column,
                column,
                pl.BlockSpec((1, 1, length), lambda h, low: (h, 0, 0)),
                column,
            ],
            out_specs=[column, column, column],
        ),
        out_shape=[jax.ShapeDtypeStruct((length, width), f32)] * 3,
        compiler_params=pltpu.CompilerParams(vmem_limit_bytes=56 << 20),
        name="attend_back",
    )(lows, starts, queries, keys, values, out, log_total, grads)


def spread_kernel(in_ref, out_ref):
    unit = out_ref.shape[2]
    for k in range(out_ref.shape[0]):
        out_ref[k] = in_ref[:, k * unit : (k + 1) * unit]


def spread(weight, groups, owners):
    rows, columns = weight.shape
    unit = columns // (groups * owners)
    if unit % 128:
        shaped = weight.reshape(rows, groups, owners, unit).transpose(2, 0, 1, 3)
        return shaped.reshape(owners, rows, groups * unit)
    return pl.pallas_call(
        spread_kernel,
        grid=(groups,),
        in_specs=[pl.BlockSpec((rows, owners * unit), lambda g: (0, g))],
        out_specs=pl.BlockSpec((owners, rows, unit), lambda g: (0, 0, g)),
        out_shape=jax.ShapeDtypeStruct((owners, rows, groups * unit), weight.dtype),
        name="spread",
    )(weight)


def collect_kernel(in_ref, out_ref):
    unit = in_ref.shape[2]
    for k in range(in_ref.shape[0]):
        out_ref[:, k * unit : (k + 1) * unit] = in_ref[k].astype(f32)


def collect(blocks, groups):
    owners, rows, columns = blocks.shape
    unit = columns // groups
    if unit % 128:
        shaped = blocks.reshape(owners, rows, groups, unit).transpose(1, 2, 0, 3)
        return shaped.reshape(rows, groups * owners * unit).astype(f32)
    return pl.pallas_call(
        collect_kernel,
        grid=(groups,),
        in_specs=[pl.BlockSpec((owners, rows, unit), lambda g: (0, 0, g))],
        out_specs=pl.BlockSpec((rows, owners * unit), lambda g: (0, g)),
        out_shape=jax.ShapeDtypeStruct((rows, groups * owners * unit), f32),
        name="collect",
    )(blocks)


def columns_of(row):
    return jnp.broadcast_to(row, (HEAD_DIM, row.shape[1])).T


def halves_swapped(values):
    return pltpu.roll(values, HEAD_DIM // 2, 1)


def project_kernel(in_ref, weight_ref, out_ref, square_ref):
    width = out_ref.shape[1] // 3
    out = product(in_ref[...], weight_ref[...])
    out_ref[...] = out
    for part in range(2):
        total = None
        for h in range(0, width, HEAD_DIM):
            raw = out[:, part * width + h : part * width + h + HEAD_DIM]
            total = raw * raw if total is None else total + raw * raw
        square_ref[part : part + 1, :] = jnp.sum(total.T, axis=0, keepdims=True)


def project(inputs, weight):
    length, depth = inputs.shape
    columns = weight.shape[1]
    return pl.pallas_call(
        project_kernel,
        grid=(length // 256,),
        in_specs=[row_block(depth, 256), whole_block(depth, columns)],
        out_specs=[row_block(columns, 256), lane_block(2, 256)],
        out_shape=[
            jax.ShapeDtypeStruct((length, columns), f32),
            jax.ShapeDtypeStruct((2, length), f32),
        ],
        compiler_params=pltpu.CompilerParams(vmem_limit_bytes=32 << 20),
        name="project",
    )(inputs, weight)


def turn_kernel(proj_ref, factor_ref, gain_ref, cos_ref, sin_ref, q_ref, k_ref, v_ref):
    width = q_ref.shape[1]
    cosine, sine_part = cos_ref[...], sin_ref[...]
    for part, out in enumerate((q_ref, k_ref)):
        factor = columns_of(factor_ref[part : part + 1, :])
        for h in range(0, width, HEAD_DIM):
            raw = proj_ref[:, part * width + h : part * width + h + HEAD_DIM]
            normed = raw * factor * gain_ref[part : part + 1, h : h + HEAD_DIM]
            turned = normed * cosine + halves_swapped(normed) * sine_part
            out[:, h : h + HEAD_DIM] = turned.astype(bf16)
    v_ref[...] = proj_ref[:, 2 * width :].astype(bf16)


def row_block(columns, rows=512):
    return pl.BlockSpec((rows, columns), lambda i: (i, 0))


def lane_block(lines, rows=512):
    return pl.BlockSpec((lines, rows), lambda i: (0, i))


def whole_block(*shape):
    return pl.BlockSpec(shape, lambda i: (0,) * len(shape))


def turn(projected, factors, gains, cosine, sine_part):
    length, columns = projected.shape
    width = columns // 3
    return pl.pallas_call(
        turn_kernel,
        grid=(length // 512,),
        in_specs=[
            row_block(columns),
            lane_block(2),
            whole_block(2, width),
            row_block(HEAD_DIM),
            row_block(HEAD_DIM),
        ],
        out_specs=[row_block(width)] * 3,
        out_shape=[jax.ShapeDtypeStruct((length, width), bf16)] * 3,
        name="turn",
    )(projected, factors, gains, cosine, sine_part)


def unturn_kernel(
    dq_ref, dk_ref, proj_ref, factor_ref, gain_ref, cos_ref, sin_ref, out_ref, mix_ref, sum_ref
):
    width = dq_ref.shape[1]
    cosine, sine_part = cos_ref[...], sin_ref[...]

    @pl.when(pl.program_id(0) == 0)
    def _():
        sum_ref[...] = jnp.zeros_like(sum_ref)

    for part, grad_ref in enumerate((dq_ref, dk_ref)):
        factor = columns_of(factor_ref[part : part + 1, :])
        mixed = None
        for h in range(0, width, HEAD_DIM):
            at = part * width + h
            grad = grad_ref[:, h : h + HEAD_DIM]
            turned = grad * cosine - halves_swapped(grad) * sine_part
            raw = proj_ref[:, at : at + HEAD_DIM]
            sums = jnp.sum(turned * raw * factor, axis=0, keepdims=True)
            sum_ref[part : part + 1, h : h + HEAD_DIM] += sums
            weighted = turned * gain_ref[part : part + 1, h : h + HEAD_DIM]
            out_ref[:, at : at + HEAD_DIM] = weighted
            mixed = weighted * raw if mixed is None else mixed + weighted * raw
        mix_ref[part : part + 1, :] = jnp.sum(mixed.T, axis=0, keepdims=True)


def unturn(query_grad, key_grad, projected, factors, gains, cosine, sine_part):
    length, width = query_grad.shape
    return pl.pallas_call(
        unturn_kernel,
        grid=(length // 512,),
        in_specs=[
            row_block(width),
            row_block(width),
            row_block(3 * width),
            lane_block(2),
            whole_block(2, width),
            row_block(HEAD_DIM),
            row_block(HEAD_DIM),
        ],
        out_specs=[row_block(2 * width), lane_block(2), whole_block(2, width)],
        out_shape=[
            jax.ShapeDtypeStruct((length, 2 * width), f32),
            jax.ShapeDtypeStruct((2, length), f32),
            jax.ShapeDtypeStruct((2, width), f32),
        ],
        name="unturn",
    )(query_grad, key_grad, projected, factors, gains, cosine, sine_part)


def finish_kernel(weighted_ref, proj_ref, factor_ref, mix_ref, dv_ref, out_ref):
    width = dv_ref.shape[1]
    for part in range(2):
        factor = columns_of(factor_ref[part : part + 1, :])
        mixing = columns_of(mix_ref[part : part + 1, :])
        for h in range(0, width, HEAD_DIM):
            at = pl.ds(part * width + h, HEAD_DIM)
            grad = weighted_ref[:, at] - proj_ref[:, at] * factor * factor * mixing
            out_ref[:, at] = (factor * grad).astype(bf16)
    out_ref[:, 2 * width :] = dv_ref[...].astype(bf16)


def finish(weighted, projected, factors, mixing, value_grad):
    length, width = value_grad.shape
    return pl.pallas_call(
        finish_kernel,
        grid=(length // 512,),
        in_specs=[
            row_block(2 * width),
            row_block(3 * width),
            lane_block(2),
            lane_block(2),
            row_block(width),
        ],
        out_specs=row_block(3 * width),
        out_shape=jax.ShapeDtypeStruct((length, 3 * width), bf16),
        name="finish",
    )(weighted, projected, factors, mixing, value_grad)


def norm_forward(values, gain_row):
    factor = lax.rsqrt(jnp.mean(values * values, axis=-1, keepdims=True) + norm_epsilon)
    return (values * factor * gain_row, factor)


def norm_backward(values, factor, gain_row, incoming):
    weighted = incoming * gain_row
    mixing = jnp.mean(weighted * values, axis=-1, keepdims=True)
    return (
        factor * (weighted - values * factor * factor * mixing),
        jnp.sum(incoming * values * factor, axis=0),
    )


def arrange(lengths, positions):
    finish = jnp.cumsum(lengths)
    has_ended = finish[None, :] <= positions[:, None]
    return jnp.sum(jnp.where(has_ended, lengths[None, :], 0), axis=1).astype(jnp.int32)


def scatter_over(value, axes):
    return lax.psum_scatter(value.astype(bf16), axes, scatter_dimension=0, tiled=True)


def on_device(
    hidden_in, seq_lengths, qkv_weight, out_weight, in_weight, down_weight, norm_gains, upstream
):
    piece_len, model_width = hidden_in.shape[1:]
    line_sizes = sizes_of(LINE)
    line = line_sizes[0] * line_sizes[1]
    length = piece_len * line * 2
    width = D // (line * 2)
    core = lax.axis_index("c")
    ctx_place = linear([lax.axis_index(a) for a in CTX], sizes_of(CTX))
    data_place = linear([lax.axis_index(a) for a in DATA], sizes_of(DATA))
    line_place = linear([lax.axis_index(a) for a in LINE], line_sizes)
    lengths = lax.dynamic_index_in_dim(seq_lengths, data_place, 0, keepdims=False)
    places = jnp.arange(length, dtype=jnp.int32)
    starts = arrange(lengths, places)
    offset = (places - starts).astype(f32)
    lows = starts[::BLOCK_Q] // BLOCK_K
    starts_row = starts.reshape(1, length)
    inverse = rope_base ** (-2.0 * jnp.arange(HEAD_DIM // 2, dtype=f32) / HEAD_DIM)
    angles = offset[:, None] * inverse[None, :]
    cosine, sine_part = jnp.cos(angles), jnp.sin(angles)
    cosine = jnp.concatenate([cosine, cosine], axis=1)
    sine_part = jnp.concatenate([-sine_part, sine_part], axis=1)

    own_input = hidden_in.reshape(piece_len, model_width)

    row = Line(LINE)

    row_count = qkv_weight.shape[0]
    owners = line * 2
    data_count = sizes_of(DATA)[0] * sizes_of(DATA)[1]
    buffer = [jnp.zeros((line, 2, piece_len, model_width), bf16)]

    def keep_input(k, same, other):
        for at_core, block, at in ((core, same, k), (1 - core, other, k - 1)):
            if block is not None:
                buffer[0] = lax.dynamic_update_slice(
                    buffer[0], block[None, None], (row.served(at), at_core, 0, 0)
                )
        return ()

    def weights_step(slot, tied):
        if slot == 0:
            blocks = spread(qkv_weight, 3, owners)
            return (exchange(blocks.reshape(line, 2, row_count, 3 * width), LINE),)
        if slot == 1:
            down = lax.all_gather(down_weight, DATA, axis=0, tiled=True)
            out_line = jnp.zeros((line,) + out_weight.shape, bf16)
            for steps in offsets(LINE):
                out_line = put(out_line, shift(out_weight, LINE, steps), place(LINE, steps, -1))
            return (down, out_line)
        if slot == 2:
            blocks = spread(in_weight, 2 * data_count, owners)
            return (exchange_cores(blocks.reshape((line, 2) + blocks.shape[1:])),)
        if slot == line - 1:
            return tied[2]
        return ()

    _, tied = row.gather(own_input, keep_input, weights_step)
    full_input = buffer[0].reshape(length, model_width)
    qkv_here = lax.all_gather(tied[0][0].reshape(-1, 3 * width), DATA, axis=0, tiled=True)
    down_here, out_line = tied[1]
    units = down_here.shape[0]
    out_half = lax.all_gather(out_line.reshape(-1, D), DATA, axis=0, tiled=True)
    in_rows = exchange_chips(tied[line - 1][0], LINE)

    projected, squares = project(full_input, qkv_here)
    factors = lax.rsqrt(small_sum(squares, CTX) / D + norm_epsilon)
    gains_here = lax.dynamic_slice(norm_gains, (0, ctx_place * width), (2, width))
    query_low, key_low, value_low = turn(projected, factors, gains_here, cosine, sine_part)
    head_out, log_total = attend(lows, starts_row, query_low, key_low, value_low)
    head_out, in_rows = together(head_out, in_rows)
    in_here = lax.all_gather(in_rows.reshape(-1, in_rows.shape[-1]), DATA, axis=0, tiled=True)

    pairs = exchange_cores(head_out.astype(bf16).reshape(line, 2, piece_len, width))
    pairs, out_half = together(pairs, out_half)
    attended = exchange_chips(pairs, LINE)
    out_half = out_half.reshape(-1, out_weight.shape[0], D)
    out_full = by_core(out_half, swap(out_half)).reshape(D, D)
    attended_low = attended.reshape(line * 2, piece_len, width).transpose(1, 0, 2)
    attended_low = attended_low.reshape(piece_len, D)
    branch = product(attended_low, out_full)
    branch_normed, branch_factor = norm_forward(branch, norm_gains[2])
    residual = own_input.astype(f32) + branch_normed
    residual_low = residual.astype(bf16)

    def rows_of(same, other):
        return jnp.concatenate([b for b in (same, other) if b is not None], axis=0)

    def chip_sums(results):
        def parts(k):
            return scatter_sum(results[k][-1][:piece_len], results[k + 1][-1][-piece_len:])

        return parts

    def forward_chip(k, same, other):
        rows = rows_of(same, other)
        gate_up = product(rows, in_here)
        gate_part, up_part = gate_up[:, :units], gate_up[:, units:]
        hidden = (gate_part * jax.nn.sigmoid(gate_part) * up_part).astype(bf16)
        return rows, gate_up, hidden, product(hidden, down_here).astype(bf16)

    plan = [[], [], [0, 1, 2]] + [[k] for k in range(3, line)]
    forward, _ = row.gather(residual_low, forward_chip, plan=plan)
    second, _ = row.scatter(chip_sums(forward))
    second_normed, second_factor = norm_forward(second, norm_gains[3])
    result = residual + second_normed
    live_places = ctx_place * piece_len + jnp.arange(piece_len, dtype=jnp.int32)
    live_rows = (live_places < jnp.sum(lengths)).astype(f32)[:, None]
    sums = jnp.stack(
        [
            jnp.sum(result * result * live_rows),
            jnp.sum(branch * branch * live_rows),
            jnp.sum(second * second * live_rows),
        ]
    )

    incoming = upstream.reshape(piece_len, model_width).astype(f32)
    second_grad, second_gain_grad = norm_backward(second, second_factor, norm_gains[3], incoming)

    def backward_chip(k, same, other):
        rows = rows_of(same, other)
        gate_up = forward[k][1]
        hidden_grad = product_right(rows, down_here)
        gate_part, up_part = gate_up[:, :units], gate_up[:, units:]
        sigmoid_gate = jax.nn.sigmoid(gate_part)
        gate_grad = hidden_grad * up_part * sigmoid_gate * (1.0 + gate_part * (1.0 - sigmoid_gate))
        up_grad = hidden_grad * gate_part * sigmoid_gate
        gate_up_low = jnp.concatenate([gate_grad, up_grad], axis=1).astype(bf16)
        return rows, gate_up_low, product_right(gate_up_low, in_here).astype(bf16)

    backward, _ = row.gather(second_grad.astype(bf16), backward_chip)

    def weight_grads(slot, tied):
        if slot == 1:
            gate_up_all = jnp.concatenate([b[1] for b in backward], axis=0)
            residual_all = jnp.concatenate([f[0] for f in forward], axis=0)
            return (product_left(residual_all, gate_up_all).astype(bf16),)
        if slot == 2:
            hidden_all = jnp.concatenate([f[2] for f in forward], axis=0)
            second_grad_all = jnp.concatenate([b[0] for b in backward], axis=0)
            return (product_left(hidden_all, second_grad_all).astype(bf16),)
        return ()

    residual_part, tied = row.scatter(chip_sums(backward), weight_grads)
    grad_in, grad_down = tied[0][0], tied[1][0]
    residual_grad = incoming + residual_part
    grad_in = scatter_over(grad_in, DATA).reshape(in_rows.shape)
    grad_down = scatter_over(grad_down, DATA).astype(f32)

    branch_grad, branch_gain_grad = norm_backward(
        branch, branch_factor, norm_gains[2], residual_grad
    )
    branch_grad_low = branch_grad.astype(bf16)
    attended_grad = product_right(branch_grad_low, out_full).astype(bf16)
    attended_grad = attended_grad.reshape(piece_len, line, 2, width).transpose(1, 2, 0, 3)
    pairs, branch_grad_low = together(exchange_cores(attended_grad), branch_grad_low)
    head_grad = exchange_chips(pairs, LINE).reshape(length, width)

    out_grad = product_left(attended_low, branch_grad_low).astype(bf16)
    out_grad = out_grad.reshape(-1, 2, out_weight.shape[0], D)
    out_keep, out_got = pick(out_grad, core, 1), swap(pick(out_grad, 1 - core, 1))
    in_pairs = exchange_cores(grad_in.reshape((line, 2) + in_rows.shape[2:]))
    head_grad, in_pairs = together(head_grad, in_pairs)
    grad_in = exchange_chips(in_pairs, LINE)

    query_grad, key_grad, value_grad = attend_back(
        lows, starts_row, query_low, key_low, value_low, head_out, log_total, head_grad
    )
    query_grad, out_keep = together(query_grad, out_keep)
    out_grad = (out_keep.astype(f32) + out_got.astype(f32)).astype(bf16).reshape(D // 2, D)
    out_grad = scatter_over(out_grad, DATA).reshape((line,) + out_weight.shape)
    weighted, mixing, gain_grads = unturn(
        query_grad, key_grad, projected, factors, gains_here, cosine, sine_part
    )
    mixing, grad_down = together(mixing, grad_down)
    mixing = small_sum(mixing, CTX) / D
    projected_grad = finish(weighted, projected, factors, mixing, value_grad)

    grad_blocks = projected_grad.reshape(line, 2, piece_len, 3 * width)

    later = []

    def input_chip(k):
        rows = pick(grad_blocks, row.served(k))
        rows = jnp.concatenate([pick(rows, core), pick(rows, 1 - core)], axis=0)
        part = product_right(rows, qkv_here).astype(bf16)
        part = scatter_sum(part[:piece_len], part[piece_len:])
        if not later:
            part, grads = together(part, projected_grad)
            later.append(grads)
        return part

    gain_rows = jnp.zeros((5, D), f32)
    gain_rows = lax.dynamic_update_slice(gain_rows, gain_grads, (0, ctx_place * width))
    gain_rows = gain_rows.at[2].set(branch_gain_grad).at[3].set(second_gain_grad)
    gain_rows = gain_rows.at[4, :3].set(sums)

    def last_grads(slot, tied):
        if slot == 1:
            part = product_left(full_input, later[0]).astype(bf16)
            return (part, small_sum(gain_rows, AXES[2:]), out_grad, grad_in)
        if slot == 2:
            return (scatter_over(tied[0][0], DATA), small_sum(tied[0][1], AXES[:2]))
        if slot == line - 1:
            blocks = tied[1][0].reshape(line, 2, row_count, 3 * width)
            return (exchange_cores(blocks),)
        return ()

    input_part, tied = row.scatter(input_chip, last_grads)
    (_, _, out_grad, grad_in), (_, gain_rows), (grad_qkv,) = tied[0], tied[1], tied[line - 2]
    input_grad = residual_grad + input_part
    grad_in = collect(grad_in.reshape((owners,) + grad_in.shape[2:]), 2 * data_count)
    grad_qkv = exchange_chips(grad_qkv, LINE)
    grad_qkv = collect(grad_qkv.reshape(owners, row_count, 3 * width), 3)
    grad_out = None
    for steps in offsets(LINE):
        part = shift(pick(out_grad, place(LINE, steps)), LINE, steps).astype(f32)
        grad_out = part if grad_out is None else grad_out + part

    live_count = jnp.sum(seq_lengths).astype(f32)
    rms_values = jnp.sqrt(gain_rows[4, :3] / (live_count * model_width))
    return (
        result.astype(bf16)[None],
        input_grad[None],
        grad_qkv,
        grad_out,
        grad_in,
        grad_down,
        gain_rows[:4],
        rms_values,
    )


def solution(mesh):
    dp, ctx = mesh.shape["dp"], mesh.shape["ctx"]
    fine = Mesh(mesh.devices.reshape(2, dp // 2, 2, ctx // 4, 2), AXES)
    return jax.shard_map(
        on_device,
        mesh=fine,
        in_specs=(
            P(DATA, CTX, None),
            P(),
            P(AXES, None),
            P(AXES, None),
            P(AXES, None),
            P(AXES, None),
            P(),
            P(DATA, CTX, None),
        ),
        out_specs=(
            P(DATA, CTX, None),
            P(DATA, CTX, None),
            P(AXES, None),
            P(AXES, None),
            P(AXES, None),
            P(AXES, None),
            P(),
            P(),
        ),
        check_vma=False,
    )
```

time: 1300 us -> 1040 us (0.80)
  waiting for transfers between devices: 628 us -> 324 us
  other arithmetic: 91 us -> 143 us
  Pallas kernels: 37.2 us -> 83.3 us
  local copies, waits for them, and re-layouts: 167 us -> 125 us
  matrix products: 196 us -> 158 us
  starting transfers between devices: 153 us -> 174 us
    ppermute x42 -> x24, waiting for transfers between devices: 519 us -> 90.4 us  [shift(): return lax.ppermute(value, axes, pairs)]
    ppermute x0 -> x36, waiting for transfers between devices: none -> 196 us  [hop(): return lax.ppermute(value, self.axes, pairs)]
    ppermute x0 -> x36, starting transfers between devices: none -> 105 us  [hop(): return lax.ppermute(value, self.axes, pairs)]
    ppermute x11, waiting for transfers between devices: 95.6 us -> 26 us  [small_sum(): value = value + lax.ppermute(value, axis, [(0, 1), (1, 0)])]
    ppermute x42 -> x24, starting transfers between devices: 101 us -> 46.9 us  [shift(): return lax.ppermute(value, axes, pairs)]
    pallas_call x0 -> x8, Pallas kernels: none -> 48.5 us  [the longest x1 10.3 us: project(): pl.pallas_call(project_kernel, grid=(length // 256,), in_specs=[row_block...]
    select_n x0 -> x14, other arithmetic: none -> 30.2 us  [the longest x8 15.9 us: by_core(): return jnp.where(here, mine[:, None], other[:, None])]
    ppermute x11, starting transfers between devices: 44 us -> 15.3 us  [small_sum(): value = value + lax.ppermute(value, axis, [(0, 1), (1, 0)])]
  transfers between devices with their start and end apart: 93 -> 111, of which waited for: 39 -> 40; matrix products, arithmetic and copies ran while one was open for 27% -> 35% of each run, Pallas kernels for 1% -> 8%
where the time goes in v2:
time: 1040 us; the launch traced here: 1030 us
  waiting for transfers between devices  324 us (31%)
  starting transfers between devices  174 us (17%)
  matrix products  158 us (15%)
  other arithmetic  143 us (14%)
  local copies, waits for them, and re-layouts  125 us (12%)
  Pallas kernels  83.3 us (8%)
  between operations  23.1 us (2%)
    ppermute x36, waiting for transfers between devices, hop(): return lax.ppermute(value, self.axes, pairs)  196 us
    ppermute x36, starting transfers between devices, hop(): return lax.ppermute(value, self.axes, pairs)  105 us
    ppermute x24, waiting for transfers between devices, shift(): return lax.ppermute(value, axes, pairs)  90.4 us
    dot_general x15, matrix products, product_right(): lax.dot_general(left_side, right_side, (((1,), (1,)), ((), ())), preferre...  69.2 us
    unnamed x202, local copies, waits for them, and re-layouts  51 us
    dot_general x4, matrix products, product_left(): lax.dot_general(left_side, right_side, (((0,), (0,)), ((), ())), preferre...  47.6 us
    ppermute x24, starting transfers between devices, shift(): return lax.ppermute(value, axes, pairs)  46.9 us
    dot_general x11, matrix products, product(): return jnp.dot(left_side, right_side, preferred_element_type=f32)  41.4 us
  transfers between devices with their start and end apart: 111, of which 40 were waited for; matrix products, arithmetic and copies ran while one was open for 35% of the time, Pallas kernels for 8%

profile of v2, /device:TPU:0, one launch (start us, length us, event | category | flops | bytes accessed | tf_op | source)
XLA Modules:
  0.0 1030.9 jit_solution(1390712932032618729)
XLA Ops:
  27.4 26.0 %collective-permute-done.4 = bf16[2,64,768]{2,1,0:T(8,128)(2,1)} collective-permute-done((bf16[2,64,768]{2,1,0:T(8,128)(2,1)}, bf16[2,64,768]{2,1,0:T(8,128)(2,1)}, u32[]{:S(2)}, u32[]{:S(2)}) %collective-permute-start.4) | collective-permute-done | bytes 196640 | tf_op jit(solution)/shard_map/ppermute | solution.py:57
  56.0 5.7 collective-permute-done.6
  109.3 13.9 %collective-permute-done.7 = bf16[256,2048]{1,0:T(8,128)(2,1)S(1)} collective-permute-done((bf16[256,2048]{1,0:T(8,128)(2,1)S(1)}, bf16[256,2048]{1,0:T(8,128)(2,1)S(1)}, u32[]{:S(2)}, u32[]{:S(2)}) %collective-permute-start.7) | collective-permute-done | bytes 1048608 | tf_op jit(solution)/shard_map/ppermute | solution.py:104
  142.1 11.0 %collective-permute-done.13 = bf16[256,2048]{1,0:T(8,128)(2,1)} collective-permute-done((bf16[256,2048]{1,0:T(8,128)(2,1)}, bf16[256,2048]{1,0:T(8,128)(2,1)}, u32[]{:S(2)}, u32[]{:S(2)}) %collective-permute-start.13) | collective-permute-done | bytes 1048608 | tf_op jit(solution)/shard_map/ppermute | solution.py:104
  172.7 10.3 %project.1 = (f32[2048,768]{1,0:T(8,128)S(1)}, f32[2,2048]{1,0:T(2,128)S(1)}) custom-call(bf16[2048,2048]{1,0:T(8,128)(2,1)} %bitcast.36.in_ref, bf16[2048,768]{1,0:T(8,128)(2,1)S(1)} %copy-done.5), custom_call_target="tpu_custom_call" | custom-call | tf_op jit(solution)/shard_map/project/pallas_call | solution.py:414
  198.9 6.4 turn.1
  209.0 13.7 %attend.1 = (f32[2048,256]{1,0:T(8,128)S(1)}, f32[2,1,2048]{2,1,0:T(1,128)S(1)}) custom-call(s32[4]{0:T(128)S(1)} %and_select_fusion.low_ref, s32[1,2048]{1,0:T(1,128)S(1)} %bitcast.268, bf16[2048,256]{1,0:T(8,128)(2,1)S(1)} %copy-done.2, bf16[2048,256]{1,0:T(8,128)(2,1)S(1)} %copy-done.3, bf16[2048,256]{1,0:T(8,128)(2,1)S(1)} %copy-done.4), custom_call_target="tpu_custom_call" | custom-call | tf_op jit(solution)/shard_map/attend/pallas_call | solution.py:260
  225.5 8.8 collective-permute-done.22
  241.4 9.6 collective-permute-start.25
  253.5 7.8 collective-permute-done.25
  261.3 11.0 %collective-permute-done.26 = bf16[2,256,256]{2,1,0:T(8,128)(2,1)S(1)} collective-permute-done((bf16[2,256,256]{2,1,0:T(8,128)(2,1)S(1)}, bf16[2,256,256]{2,1,0:T(8,128)(2,1)S(1)}, u32[]{:S(2)}, u32[]{:S(2)}) %collective-permute-start.26) | collective-permute-done | bytes 262176 | tf_op jit(solution)/shard_map/ppermute | solution.py:57
  281.4 7.2 collective-permute-start.29
  290.0 20.5 %collective-permute-done.29 = bf16[256,2048]{1,0:T(8,128)(2,1)S(1)} collective-permute-done((bf16[256,2048]{1,0:T(8,128)(2,1)S(1)}, bf16[256,2048]{1,0:T(8,128)(2,1)S(1)}, u32[]{:S(2)}, u32[]{:S(2)}) %collective-permute-start.29) | collective-permute-done | bytes 1048608 | tf_op jit(solution)/shard_map/ppermute | solution.py:104
  320.7 17.2 %collective-permute-done.32 = bf16[256,2048]{1,0:T(8,128)(2,1)} collective-permute-done((bf16[256,2048]{1,0:T(8,128)(2,1)S(1)}, bf16[256,2048]{1,0:T(8,128)(2,1)}, u32[]{:S(2)}, u32[]{:S(2)}) %collective-permute-start.32) | collective-permute-done | bytes 1048608 | tf_op jit(solution)/shard_map/ppermute | solution.py:104
  353.9 5.9 fusion.45
  370.4 5.8 fusion.42
  387.8 7.2 fusion.41
  401.8 5.7 fusion.46
  421.2 18.2 %collective-permute-done.40 = bf16[256,2048]{1,0:T(8,128)(2,1)S(1)} collective-permute-done((bf16[256,2048]{1,0:T(8,128)(2,1)S(1)}, bf16[256,2048]{1,0:T(8,128)(2,1)S(1)}, u32[]{:S(2)}, u32[]{:S(2)}) %collective-permute-start.40) | collective-permute-done | bytes 1048608 | tf_op jit(solution)/shard_map/ppermute | solution.py:104
  451.4 16.4 %collective-permute-done.43 = bf16[256,2048]{1,0:T(8,128)(2,1)S(1)} collective-permute-done((bf16[256,2048]{1,0:T(8,128)(2,1)S(1)}, bf16[256,2048]{1,0:T(8,128)(2,1)S(1)}, u32[]{:S(2)}, u32[]{:S(2)}) %collective-permute-start.43) | collective-permute-done | bytes 1048608 | tf_op jit(solution)/shard_map/ppermute | solution.py:104
  469.8 6.5 collective-permute-start.46
  481.9 15.2 %collective-permute-done.46 = bf16[256,2048]{1,0:T(8,128)(2,1)S(1)} collective-permute-done((bf16[256,2048]{1,0:T(8,128)(2,1)S(1)}, bf16[256,2048]{1,0:T(8,128)(2,1)S(1)}, u32[]{:S(2)}, u32[]{:S(2)}) %collective-permute-start.46) | collective-permute-done | bytes 1048608 | tf_op jit(solution)/shard_map/ppermute | solution.py:104
  510.1 6.7 convolution_convert_fusion.18
  516.9 10.1 collective-permute-done.49
  543.4 9.9 convolution_convert_fusion.13
  571.6 9.6 convolution_convert_fusion.12
  595.5 8.5 convolution_convert_fusion.11
  609.0 5.7 convolution_convert_fusion.17
  627.0 22.1 %convolution_convert_fusion.1 = bf16[2048,2048]{1,0:T(8,128)(2,1)} fusion(bf16[2048,2048]{1,0:T(8,128)(2,1)S(1)} %bitcast.297, bf16[2048,2048]{1,0:T(8,128)(2,1)} %fusion.26), kind=kOutput, calls=%fused_computation.4 | convolution fusion | flops 17184063488 | bytes 25165824 | tf_op jit(solution)/shard_map/dot_general | solution.py:212
  673.0 12.4 %convolution_convert_fusion.2 = bf16[1024,2048]{1,0:T(8,128)(2,1)} fusion(bf16[2048,1024]{1,0:T(8,128)(2,1)} %get-tuple-element.305, bf16[2048,2048]{1,0:T(8,128)(2,1)S(1)} %constant_dynamic-update-slice_fusion.14), kind=kOutput, calls=%fused_computation.7 | convolution fusion | flops 8592031744 | bytes 16777216 | tf_op jit(solution)/shard_map/dot_general | solution.py:212
  687.7 6.8 collective-permute-done.63
  705.7 7.9 bitcast_select_fusion
  716.8 9.0 collective-permute-done.66
  730.9 5.8 multiply_reduce_fusion.3
  759.7 6.5 collective-permute-done.70
  766.1 10.5 %collective-permute-done.71 = bf16[2,256,256]{2,1,0:T(8,128)(2,1)S(1)} collective-permute-done((bf16[2,256,256]{2,1,0:T(8,128)(2,1)S(1)}, bf16[2,256,256]{2,1,0:T(8,128)(2,1)S(1)}, u32[]{:S(2)}, u32[]{:S(2)}) %collective-permute-start.71) | collective-permute-done | bytes 262176 | tf_op jit(solution)/shard_map/ppermute | solution.py:57
  777.7 21.1 %attend_back.1 = (f32[2048,256]{1,0:T(8,128)}, f32[2048,256]{1,0:T(8,128)}, f32[2048,256]{1,0:T(8,128)}) custom-call(s32[4]{0:T(128)} %copy-done.9, s32[1,2048]{1,0:T(1,128)} %bitcast.269, bf16[2048,256]{1,0:T(8,128)(2,1)} %get-tuple-element.184.q_ref, bf16[2048,256]{1,0:T(8,128)(2,1)} %get-tuple-element.185.k_ref, ...), custom_call_target="tpu_custom_call" | custom-call | tf_op jit(solution)/shard_map/attend_back/pallas_call | solution.py:325
  798.9 6.5 add_convert_fusion
  808.3 7.3 unturn.1
  815.5 5.9 collective-permute-start.74
  838.5 7.1 finish.1
  851.3 18.6 %collective-permute-done.82 = f32[5,2048]{1,0:T(8,128)} collective-permute-done((f32[5,2048]{1,0:T(8,128)}, f32[5,2048]{1,0:T(8,128)}, u32[]{:S(2)}, u32[]{:S(2)}) %collective-permute-start.82) | collective-permute-done | bytes 40992 | tf_op jit(solution)/shard_map/ppermute | solution.py:201
  883.6 7.5 collective-permute-start.78
  892.7 10.8 %convolution_convert_fusion.3 = bf16[2048,768]{1,0:T(8,128)(2,1)} fusion(bf16[2048,2048]{1,0:T(8,128)(2,1)} %bitcast.36.in_ref, bf16[2048,768]{1,0:T(8,128)(2,1)S(1)} %copy-done.22), kind=kOutput, calls=%fused_computation.8 | convolution fusion | flops 6444023808 | bytes 14680064 | tf_op jit(solution)/shard_map/dot_general | solution.py:212
  948.1 6.0 collect.3
  964.9 13.9 %collective-permute-start.93 = (bf16[256,2048]{1,0:T(8,128)(2,1)S(1)}, bf16[256,2048]{1,0:T(8,128)(2,1)S(1)}, u32[]{:S(2)}, u32[]{:S(2)}) collective-permute-start(bf16[256,2048]{1,0:T(8,128)(2,1)S(1)} %get-tuple-element.328), channel_id=1, source_target_pairs={{0,2},{2,4},{4,6},{1,3},{3,5},{5,7},{8,10},{10,12},{12,14},{9,11},... | collective-permute-start | bytes 3145736 | tf_op jit(solution)/shard_map/ppermute | solution.py:104
  992.1 8.4 collective-permute-done.94
  1011.8 7.9 collective-permute-done.98
  (599 shorter events, 505.4 us)
Async XLA Ops:
  7.2 121.2 %all-gather.5.cloned.1.call-start = ((), (), s32[]{:S(2)}) async-start(), calls=%async_computation.4 | async-start | bytes 5242880 | tf_op jit(solution)/shard_map/all_gather | solution.py:622
  7.9 162.9 %all-gather.7.cloned.1.call-start = ((), (), s32[]{:S(2)}) async-start(), calls=%async_computation.5 | async-start | bytes 3932160 | tf_op jit(solution)/shard_map/all_gather | solution.py:636
  13.2 49.3 %collective-permute-start = (bf16[256,2048]{1,0:T(8,128)(2,1)S(1)}, bf16[256,2048]{1,0:T(8,128)(2,1)S(1)}, u32[]{:S(2)}, u32[]{:S(2)}) collective-permute-start(bf16[256,2048]{1,0:T(8,128)(2,1)S(1)} %bitcast.279), channel_id=1, source_target_pairs={{0,2},{2,4},{4,6},{1,3},{3,5},{5,7},{8,10},{10,12},{12,14},{9,11},... | collective-permute-start | bytes 3145736 | tf_op jit(solution)/shard_map/ppermute | solution.py:104
  17.7 44.7 %collective-permute-start.1 = (bf16[256,2048]{1,0:T(8,128)(2,1)S(1)}, bf16[256,2048]{1,0:T(8,128)(2,1)S(1)}, u32[]{:S(2)}, u32[]{:S(2)}) collective-permute-start(bf16[256,2048]{1,0:T(8,128)(2,1)S(1)} %bitcast.280), channel_id=1, source_target_pairs={{2,0},{4,2},{6,4},{3,1},{5,3},{7,5},{10,8},{12,10},{14,12},{11,9},... | collective-permute-start | bytes 3145736 | tf_op jit(solution)/shard_map/ppermute | solution.py:104
  19.0 43.4 %collective-permute-start.2 = (bf16[256,2048]{1,0:T(8,128)(2,1)S(1)}, bf16[256,2048]{1,0:T(8,128)(2,1)}, u32[]{:S(2)}, u32[]{:S(2)}) collective-permute-start(bf16[256,2048]{1,0:T(8,128)(2,1)S(1)} %bitcast.281), channel_id=1, source_target_pairs={{0,1},{1,0},{2,3},{3,2},{4,5},{5,4},{6,7},{7,6},{8,9},{9,8},{10,11... | collective-permute-start | bytes 3145736 | tf_op jit(solution)/shard_map/ppermute | solution.py:61
  22.3 31.1 %collective-permute-start.4 = (bf16[2,64,768]{2,1,0:T(8,128)(2,1)}, bf16[2,64,768]{2,1,0:T(8,128)(2,1)}, u32[]{:S(2)}, u32[]{:S(2)}) collective-permute-start(bf16[2,64,768]{2,1,0:T(8,128)(2,1)} %get-tuple-element.384), channel_id=1, source_target_pairs={{0,2},{2,0},{4,6},{6,4},{1,3},{3,1},{5,7},{7,5},{8,10},{10,8},{12,... | collective-permute-start | bytes 589832 | tf_op jit(solution)/shard_map/ppermute | solution.py:57
  24.8 30.5 %collective-permute-start.5 = (bf16[2,64,768]{2,1,0:T(8,128)(2,1)}, bf16[2,64,768]{2,1,0:T(8,128)(2,1)S(1)}, u32[]{:S(2)}, u32[]{:S(2)}) collective-permute-start(bf16[2,64,768]{2,1,0:T(8,128)(2,1)} %get-tuple-element.383), channel_id=1, source_target_pairs={{0,4},{2,6},{4,0},{6,2},{1,5},{3,7},{5,1},{7,3},{8,12},{10,14},{12... | collective-permute-start | bytes 589832 | tf_op jit(solution)/shard_map/ppermute | solution.py:57
  62.5 178.5 %all-gather.9.cloned.1.call-start = ((), (), s32[]{:S(2)}) async-start(), calls=%async_computation.6 | async-start | bytes 5242880 | tf_op jit(solution)/shard_map/all_gather | solution.py:639
  62.6 33.0 %collective-permute-start.10 = (bf16[64,2048]{1,0:T(8,128)(2,1)S(1)}, bf16[64,2048]{1,0:T(8,128)(2,1)}, u32[]{:S(2)}, u32[]{:S(2)}) collective-permute-start(bf16[64,2048]{1,0:T(8,128)(2,1)S(1)} %copy-done.64), channel_id=1, source_target_pairs={{0,2},{2,0},{4,6},{6,4},{1,3},{3,1},{5,7},{7,5},{8,10},{10,8},{12,... | collective-permute-start | bytes 786440 | tf_op jit(solution)/shard_map/ppermute | solution.py:57
  65.1 38.3 %collective-permute-start.11 = (bf16[64,2048]{1,0:T(8,128)(2,1)S(1)}, bf16[64,2048]{1,0:T(8,128)(2,1)}, u32[]{:S(2)}, u32[]{:S(2)}) collective-permute-start(bf16[64,2048]{1,0:T(8,128)(2,1)S(1)} %copy-done.64), channel_id=1, source_target_pairs={{0,4},{2,6},{4,0},{6,2},{1,5},{3,7},{5,1},{7,3},{8,12},{10,14},{12... | collective-permute-start | bytes 786440 | tf_op jit(solution)/shard_map/ppermute | solution.py:57
  65.2 40.1 %collective-permute-start.12 = (bf16[64,2048]{1,0:T(8,128)(2,1)S(1)}, bf16[64,2048]{1,0:T(8,128)(2,1)}, u32[]{:S(2)}, u32[]{:S(2)}) collective-permute-start(bf16[64,2048]{1,0:T(8,128)(2,1)S(1)} %copy-done.64), channel_id=1, source_target_pairs={{0,6},{2,4},{4,2},{6,0},{1,7},{3,5},{5,3},{7,1},{8,14},{10,12},{12... | collective-permute-start | bytes 786440 | tf_op jit(solution)/shard_map/ppermute | solution.py:57
  76.5 61.5 %collective-permute-start.16 = (bf16[4,64,2048]{2,1,0:T(8,128)(2,1)}, bf16[4,64,2048]{2,1,0:T(8,128)(2,1)}, u32[]{:S(2)}, u32[]{:S(2)}) collective-permute-start(bf16[4,64,2048]{2,1,0:T(8,128)(2,1)} %get-tuple-element.360), channel_id=1, source_target_pairs={{0,1},{1,0},{2,3},{3,2},{4,5},{5,4},{6,7},{7,6},{8,9},{9,8},{10,11... | collective-permute-start | bytes 3145736 | tf_op jit(solution)/shard_map/ppermute | solution.py:61
  100.2 27.2 %collective-permute-start.8 = (bf16[256,2048]{1,0:T(8,128)(2,1)S(1)}, bf16[256,2048]{1,0:T(8,128)(2,1)S(1)}, u32[]{:S(2)}, u32[]{:S(2)}) collective-permute-start(bf16[256,2048]{1,0:T(8,128)(2,1)S(1)} %collective-permute-done.1), channel_id=1, source_target_pairs={{2,0},{4,2},{6,4},{3,1},{5,3},{7,5},{10,8},{12,10},{14,12},{11,9},... | collective-permute-start | bytes 3145736 | tf_op jit(solution)/shard_map/ppermute | solution.py:104
  131.5 26.7 %collective-permute-start.14 = (bf16[256,2048]{1,0:T(8,128)(2,1)}, bf16[256,2048]{1,0:T(8,128)(2,1)}, u32[]{:S(2)}, u32[]{:S(2)}) collective-permute-start(bf16[256,2048]{1,0:T(8,128)(2,1)} %copy-done.42), channel_id=1, source_target_pairs={{2,0},{4,2},{6,4},{3,1},{5,3},{7,5},{10,8},{12,10},{14,12},{11,9},... | collective-permute-start | bytes 3145736 | tf_op jit(solution)/shard_map/ppermute | solution.py:104
  132.8 221.1 %all-gather.11.cloned.1.call-start = ((), (), s32[]{:S(2)}) async-start(), calls=%async_computation.7 | async-start | bytes 10485760 | tf_op jit(solution)/shard_map/all_gather | solution.py:648
  193.2 30.1 %collective-permute-start.21 = (bf16[2,64,2048]{2,1,0:T(8,128)(2,1)}, bf16[2,64,2048]{2,1,0:T(8,128)(2,1)}, u32[]{:S(2)}, u32[]{:S(2)}) collective-permute-start(bf16[2,64,2048]{2,1,0:T(8,128)(2,1)} %get-tuple-element.357), channel_id=1, source_target_pairs={{0,2},{2,0},{4,6},{6,4},{1,3},{3,1},{5,7},{7,5},{8,10},{10,8},{12,... | collective-permute-start | bytes 1572872 | tf_op jit(solution)/shard_map/ppermute | solution.py:57
  195.9 38.5 %collective-permute-start.22 = (bf16[2,64,2048]{2,1,0:T(8,128)(2,1)}, bf16[2,64,2048]{2,1,0:T(8,128)(2,1)}, u32[]{:S(2)}, u32[]{:S(2)}) collective-permute-start(bf16[2,64,2048]{2,1,0:T(8,128)(2,1)} %get-tuple-element.356), channel_id=1, source_target_pairs={{0,4},{2,6},{4,0},{6,2},{1,5},{3,7},{5,1},{7,3},{8,12},{10,14},{12... | collective-permute-start | bytes 1572872 | tf_op jit(solution)/shard_map/ppermute | solution.py:57
  195.9 40.3 %collective-permute-start.23 = (bf16[2,64,2048]{2,1,0:T(8,128)(2,1)}, bf16[2,64,2048]{2,1,0:T(8,128)(2,1)}, u32[]{:S(2)}, u32[]{:S(2)}) collective-permute-start(bf16[2,64,2048]{2,1,0:T(8,128)(2,1)} %get-tuple-element.355), channel_id=1, source_target_pairs={{0,6},{2,4},{4,2},{6,0},{1,7},{3,5},{5,3},{7,1},{8,14},{10,12},{12... | collective-permute-start | bytes 1572872 | tf_op jit(solution)/shard_map/ppermute | solution.py:57
  238.1 514.8 %reduce-scatter.5.cloned.1.call-start = ((), (), s32[]{:S(2)}) async-start(), calls=%async_computation.8 | async-start | bytes 10485760 | tf_op jit(solution)/shard_map/reduce_scatter | solution.py:573
  241.0 31.9 %collective-permute-start.28 = (bf16[16,64,2048]{2,1,0:T(8,128)(2,1)}, bf16[16,64,2048]{2,1,0:T(8,128)(2,1)}, u32[]{:S(2)}, u32[]{:S(2)}) collective-permute-start(bf16[16,64,2048]{2,1,0:T(8,128)(2,1)} %bitcast.272), channel_id=1, source_target_pairs={{0,1},{1,0},{2,3},{3,2},{4,5},{5,4},{6,7},{7,6},{8,9},{9,8},{10,11... | collective-permute-start | bytes 12582920 | tf_op jit(solution)/shard_map/ppermute | solution.py:61
  281.4 29.1 %collective-permute-start.29 = (bf16[256,2048]{1,0:T(8,128)(2,1)S(1)}, bf16[256,2048]{1,0:T(8,128)(2,1)S(1)}, u32[]{:S(2)}, u32[]{:S(2)}) collective-permute-start(bf16[256,2048]{1,0:T(8,128)(2,1)S(1)} %fusion.12), channel_id=1, source_target_pairs={{0,2},{2,4},{4,6},{1,3},{3,5},{5,7},{8,10},{10,12},{12,14},{9,11},... | collective-permute-start | bytes 3145736 | tf_op jit(solution)/shard_map/ppermute | solution.py:104
  343.1 37.6 %collective-permute-start.35 = (bf16[256,2048]{1,0:T(8,128)(2,1)}, bf16[256,2048]{1,0:T(8,128)(2,1)}, u32[]{:S(2)}, u32[]{:S(2)}) collective-permute-start(bf16[256,2048]{1,0:T(8,128)(2,1)} %collective-permute-done.32), channel_id=1, source_target_pairs={{0,2},{2,4},{4,6},{1,3},{3,5},{5,7},{8,10},{10,12},{12,14},{9,11},... | collective-permute-start | bytes 3145736 | tf_op jit(solution)/shard_map/ppermute | solution.py:104
  345.4 35.3 %collective-permute-start.36 = (bf16[256,2048]{1,0:T(8,128)(2,1)}, bf16[256,2048]{1,0:T(8,128)(2,1)}, u32[]{:S(2)}, u32[]{:S(2)}) collective-permute-start(bf16[256,2048]{1,0:T(8,128)(2,1)} %collective-permute-done.33), channel_id=1, source_target_pairs={{2,0},{4,2},{6,4},{3,1},{5,3},{7,5},{10,8},{12,10},{14,12},{11,9},... | collective-permute-start | bytes 3145736 | tf_op jit(solution)/shard_map/ppermute | solution.py:104
  351.0 29.7 %collective-permute-start.37 = (bf16[256,2048]{1,0:T(8,128)(2,1)}, bf16[256,2048]{1,0:T(8,128)(2,1)}, u32[]{:S(2)}, u32[]{:S(2)}) collective-permute-start(bf16[256,2048]{1,0:T(8,128)(2,1)} %select_select_fusion.3), channel_id=1, source_target_pairs={{0,1},{1,0},{2,3},{3,2},{4,5},{5,4},{6,7},{7,6},{8,9},{9,8},{10,11... | collective-permute-start | bytes 3145736 | tf_op jit(solution)/shard_map/ppermute | solution.py:61
  419.1 30.7 %collective-permute-start.45 = (bf16[256,2048]{1,0:T(8,128)(2,1)S(1)}, bf16[256,2048]{1,0:T(8,128)(2,1)}, u32[]{:S(2)}, u32[]{:S(2)}) collective-permute-start(bf16[256,2048]{1,0:T(8,128)(2,1)S(1)} %slice.198), channel_id=1, source_target_pairs={{0,1},{1,0},{2,3},{3,2},{4,5},{5,4},{6,7},{7,6},{8,9},{9,8},{10,11... | collective-permute-start | bytes 3145736 | tf_op jit(solution)/shard_map/ppermute | solution.py:61
  419.2 61.0 %collective-permute-start.48 = (bf16[256,2048]{1,0:T(8,128)(2,1)S(1)}, bf16[256,2048]{1,0:T(8,128)(2,1)}, u32[]{:S(2)}, u32[]{:S(2)}) collective-permute-start(bf16[256,2048]{1,0:T(8,128)(2,1)S(1)} %slice.199), channel_id=1, source_target_pairs={{0,1},{1,0},{2,3},{3,2},{4,5},{5,4},{6,7},{7,6},{8,9},{9,8},{10,11... | collective-permute-start | bytes 3145736 | tf_op jit(solution)/shard_map/ppermute | solution.py:61
  469.8 27.3 %collective-permute-start.46 = (bf16[256,2048]{1,0:T(8,128)(2,1)S(1)}, bf16[256,2048]{1,0:T(8,128)(2,1)S(1)}, u32[]{:S(2)}, u32[]{:S(2)}) collective-permute-start(bf16[256,2048]{1,0:T(8,128)(2,1)S(1)} %get-tuple-element.334), channel_id=1, source_target_pairs={{0,2},{2,4},{4,6},{1,3},{3,5},{5,7},{8,10},{10,12},{12,14},{9,11},... | collective-permute-start | bytes 3145736 | tf_op jit(solution)/shard_map/ppermute | solution.py:104
  619.1 30.0 %collective-permute-start.62 = (bf16[256,2048]{1,0:T(8,128)(2,1)}, bf16[256,2048]{1,0:T(8,128)(2,1)}, u32[]{:S(2)}, u32[]{:S(2)}) collective-permute-start(bf16[256,2048]{1,0:T(8,128)(2,1)} %slice.211), channel_id=1, source_target_pairs={{0,1},{1,0},{2,3},{3,2},{4,5},{5,4},{6,7},{7,6},{8,9},{9,8},{10,11... | collective-permute-start | bytes 3145736 | tf_op jit(solution)/shard_map/ppermute | solution.py:61
  623.1 29.2 %collective-permute-start.60 = (bf16[256,2048]{1,0:T(8,128)(2,1)}, bf16[256,2048]{1,0:T(8,128)(2,1)}, u32[]{:S(2)}, u32[]{:S(2)}) collective-permute-start(bf16[256,2048]{1,0:T(8,128)(2,1)} %fusion.11), channel_id=1, source_target_pairs={{0,2},{1,3},{8,10},{9,11},{16,18},{17,19},{24,26},{25,27}} | collective-permute-start | bytes 3145736 | tf_op jit(solution)/shard_map/ppermute | solution.py:104
  625.4 27.0 %collective-permute-start.61 = (bf16[256,2048]{1,0:T(8,128)(2,1)}, bf16[256,2048]{1,0:T(8,128)(2,1)}, u32[]{:S(2)}, u32[]{:S(2)}) collective-permute-start(bf16[256,2048]{1,0:T(8,128)(2,1)} %fusion.11), channel_id=1, source_target_pairs={{6,4},{7,5},{14,12},{15,13},{22,20},{23,21},{30,28},{31,29}} | collective-permute-start | bytes 3145736 | tf_op jit(solution)/shard_map/ppermute | solution.py:104
  652.4 153.1 %reduce-scatter.7.cloned.1.call-start = ((), (), s32[]{:S(2)}) async-start(), calls=%async_computation.9 | async-start | bytes 5242880 | tf_op jit(solution)/shard_map/reduce_scatter | solution.py:573
  656.6 57.0 %collective-permute-start.68 = (bf16[256,2048]{1,0:T(8,128)(2,1)}, bf16[256,2048]{1,0:T(8,128)(2,1)}, u32[]{:S(2)}, u32[]{:S(2)}) collective-permute-start(bf16[256,2048]{1,0:T(8,128)(2,1)} %slice.214), channel_id=1, source_target_pairs={{0,1},{1,0},{2,3},{3,2},{4,5},{5,4},{6,7},{7,6},{8,9},{9,8},{10,11... | collective-permute-start | bytes 3145736 | tf_op jit(solution)/shard_map/ppermute | solution.py:61
  699.0 26.8 %collective-permute-start.66 = (bf16[256,2048]{1,0:T(8,128)(2,1)}, bf16[256,2048]{1,0:T(8,128)(2,1)}, u32[]{:S(2)}, u32[]{:S(2)}) collective-permute-start(bf16[256,2048]{1,0:T(8,128)(2,1)} %get-tuple-element.332), channel_id=1, source_target_pairs={{0,2},{2,4},{4,6},{1,3},{3,5},{5,7},{8,10},{10,12},{12,14},{9,11},... | collective-permute-start | bytes 3145736 | tf_op jit(solution)/shard_map/ppermute | solution.py:104
  716.5 195.8 %reduce-scatter.9.cloned.1.call-start = ((), (), s32[]{:S(2)}) async-start(), calls=%async_computation.10 | async-start | bytes 5242880 | tf_op jit(solution)/shard_map/reduce_scatter | solution.py:573
  752.8 46.1 %collective-permute-start.84 = (bf16[16,64,2048]{2,1,0:T(8,128)(2,1)}, bf16[16,64,2048]{2,1,0:T(8,128)(2,1)}, u32[]{:S(2)}, u32[]{:S(2)}) collective-permute-start(bf16[16,64,2048]{2,1,0:T(8,128)(2,1)} %get-tuple-element.315), channel_id=1, source_target_pairs={{0,1},{1,0},{2,3},{3,2},{4,5},{5,4},{6,7},{7,6},{8,9},{9,8},{10,11... | collective-permute-start | bytes 12582920 | tf_op jit(solution)/shard_map/ppermute | solution.py:61
  805.4 155.7 %reduce-scatter.11.cloned.1.call-start = ((), (), s32[]{:S(2)}) async-start(), calls=%async_computation.11 | async-start | bytes 3932160 | tf_op jit(solution)/shard_map/reduce_scatter | solution.py:573
  831.6 43.5 %collective-permute-start.85 = (bf16[2,64,2048]{2,1,0:T(8,128)(2,1)}, bf16[2,64,2048]{2,1,0:T(8,128)(2,1)}, u32[]{:S(2)}, u32[]{:S(2)}) collective-permute-start(bf16[2,64,2048]{2,1,0:T(8,128)(2,1)} %get-tuple-element.351), channel_id=1, source_target_pairs={{0,2},{2,0},{4,6},{6,4},{1,3},{3,1},{5,7},{7,5},{8,10},{10,8},{12,... | collective-permute-start | bytes 1572872 | tf_op jit(solution)/shard_map/ppermute | solution.py:57
  833.8 43.2 %collective-permute-start.86 = (bf16[2,64,2048]{2,1,0:T(8,128)(2,1)}, bf16[2,64,2048]{2,1,0:T(8,128)(2,1)}, u32[]{:S(2)}, u32[]{:S(2)}) collective-permute-start(bf16[2,64,2048]{2,1,0:T(8,128)(2,1)} %get-tuple-element.350), channel_id=1, source_target_pairs={{0,4},{2,6},{4,0},{6,2},{1,5},{3,7},{5,1},{7,3},{8,12},{10,14},{12... | collective-permute-start | bytes 1572872 | tf_op jit(solution)/shard_map/ppermute | solution.py:57
  834.2 44.6 %collective-permute-start.87 = (bf16[2,64,2048]{2,1,0:T(8,128)(2,1)}, bf16[2,64,2048]{2,1,0:T(8,128)(2,1)}, u32[]{:S(2)}, u32[]{:S(2)}) collective-permute-start(bf16[2,64,2048]{2,1,0:T(8,128)(2,1)} %get-tuple-element.349), channel_id=1, source_target_pairs={{0,6},{2,4},{4,2},{6,0},{1,7},{3,5},{5,3},{7,1},{8,14},{10,12},{12... | collective-permute-start | bytes 1572872 | tf_op jit(solution)/shard_map/ppermute | solution.py:57
  836.8 33.1 %collective-permute-start.82 = (f32[5,2048]{1,0:T(8,128)}, f32[5,2048]{1,0:T(8,128)}, u32[]{:S(2)}, u32[]{:S(2)}) collective-permute-start(f32[5,2048]{1,0:T(8,128)} %add.837), channel_id=1, source_target_pairs={{0,2},{2,0},{1,3},{3,1},{4,6},{6,4},{5,7},{7,5},{8,10},{10,8},{9,1... | collective-permute-start | bytes 122888 | tf_op jit(solution)/shard_map/ppermute | solution.py:201
  851.2 29.6 %collective-permute-start.77 = (bf16[256,2048]{1,0:T(8,128)(2,1)S(1)}, bf16[256,2048]{1,0:T(8,128)(2,1)S(1)}, u32[]{:S(2)}, u32[]{:S(2)}) collective-permute-start(bf16[256,2048]{1,0:T(8,128)(2,1)S(1)} %slice.236), channel_id=1, source_target_pairs={{0,1},{1,0},{2,3},{3,2},{4,5},{5,4},{6,7},{7,6},{8,9},{9,8},{10,11... | collective-permute-start | bytes 3145736 | tf_op jit(solution)/shard_map/ppermute | solution.py:61
  874.0 29.5 %collective-permute-start.80 = (bf16[256,2048]{1,0:T(8,128)(2,1)}, bf16[256,2048]{1,0:T(8,128)(2,1)}, u32[]{:S(2)}, u32[]{:S(2)}) collective-permute-start(bf16[256,2048]{1,0:T(8,128)(2,1)} %slice.238), channel_id=1, source_target_pairs={{0,1},{1,0},{2,3},{3,2},{4,5},{5,4},{6,7},{7,6},{8,9},{9,8},{10,11... | collective-permute-start | bytes 3145736 | tf_op jit(solution)/shard_map/ppermute | solution.py:61
  883.6 28.8 %collective-permute-start.78 = (bf16[256,2048]{1,0:T(8,128)(2,1)}, bf16[256,2048]{1,0:T(8,128)(2,1)}, u32[]{:S(2)}, u32[]{:S(2)}) collective-permute-start(bf16[256,2048]{1,0:T(8,128)(2,1)} %convert_element_type.389), channel_id=1, source_target_pairs={{0,2},{1,3},{8,10},{9,11},{16,18},{17,19},{24,26},{25,27}} | collective-permute-start | bytes 3145736 | tf_op jit(solution)/shard_map/ppermute | solution.py:104
  925.9 30.4 %collective-permute-start.88 = (bf16[256,2048]{1,0:T(8,128)(2,1)}, bf16[256,2048]{1,0:T(8,128)(2,1)S(1)}, u32[]{:S(2)}, u32[]{:S(2)}) collective-permute-start(bf16[256,2048]{1,0:T(8,128)(2,1)} %get-tuple-element.330), channel_id=1, source_target_pairs={{0,2},{2,4},{1,3},{3,5},{8,10},{10,12},{9,11},{11,13},{16,18},{18,... | collective-permute-start | bytes 3145736 | tf_op jit(solution)/shard_map/ppermute | solution.py:104
  944.2 36.0 %collective-permute-start.102 = (bf16[64,2048]{1,0:T(8,128)(2,1)}, bf16[64,2048]{1,0:T(8,128)(2,1)}, u32[]{:S(2)}, u32[]{:S(2)}) collective-permute-start(bf16[64,2048]{1,0:T(8,128)(2,1)} %get-tuple-element.362), channel_id=1, source_target_pairs={{0,6},{2,4},{4,2},{6,0},{1,7},{3,5},{5,3},{7,1},{8,14},{10,12},{12... | collective-permute-start | bytes 786440 | tf_op jit(solution)/shard_map/ppermute | solution.py:57
  948.1 35.5 %collective-permute-start.101 = (bf16[64,2048]{1,0:T(8,128)(2,1)}, bf16[64,2048]{1,0:T(8,128)(2,1)}, u32[]{:S(2)}, u32[]{:S(2)}) collective-permute-start(bf16[64,2048]{1,0:T(8,128)(2,1)} %get-tuple-element.363), channel_id=1, source_target_pairs={{0,4},{2,6},{4,0},{6,2},{1,5},{3,7},{5,1},{7,3},{8,12},{10,14},{12... | collective-permute-start | bytes 786440 | tf_op jit(solution)/shard_map/ppermute | solution.py:57
  954.8 28.9 %collective-permute-start.100 = (bf16[64,2048]{1,0:T(8,128)(2,1)S(1)}, bf16[64,2048]{1,0:T(8,128)(2,1)}, u32[]{:S(2)}, u32[]{:S(2)}) collective-permute-start(bf16[64,2048]{1,0:T(8,128)(2,1)S(1)} %get-tuple-element.361), channel_id=1, source_target_pairs={{0,2},{2,0},{4,6},{6,4},{1,3},{3,1},{5,7},{7,5},{8,10},{10,8},{12,... | collective-permute-start | bytes 786440 | tf_op jit(solution)/shard_map/ppermute | solution.py:57
  964.9 27.2 %collective-permute-start.93 = (bf16[256,2048]{1,0:T(8,128)(2,1)S(1)}, bf16[256,2048]{1,0:T(8,128)(2,1)S(1)}, u32[]{:S(2)}, u32[]{:S(2)}) collective-permute-start(bf16[256,2048]{1,0:T(8,128)(2,1)S(1)} %get-tuple-element.328), channel_id=1, source_target_pairs={{0,2},{2,4},{4,6},{1,3},{3,5},{5,7},{8,10},{10,12},{12,14},{9,11},... | collective-permute-start | bytes 3145736 | tf_op jit(solution)/shard_map/ppermute | solution.py:104
  (155 other events, 2092.6 us)
Sparse Core Ops, SparseCore 0:
  9.9 55.3 all-gather.4
  67.1 44.0 all-gather.6
  132.9 53.0 all-gather.8
  238.3 94.7 all-gather.10
  652.5 84.6 reduce-scatter.4
  740.3 52.6 reduce-scatter.6
  805.5 56.3 reduce-scatter.8
  912.5 48.4 reduce-scatter.10

commit v3 on v2

--- a/solution.py
+++ b/solution.py
@@ -111,8 +111,9 @@
             value = jnp.where(jnp.asarray(mask)[self.place], options[w], value)
         return value
 
-    def gather(self, block, work, extra=None, plan=None):
-        plan = plan or [[k] for k in range(self.count)]
+    def gather(self, block, work, extra=None, plan=None, late=False):
+        plan = plan or [[k] for k in range(self.count - 1)]
+        plan = plan + [[]]
         options, results, tied, arrived, swapped = {}, [], [], [], [None]
         for slot in range(self.count):
             if slot:
@@ -137,8 +138,17 @@
             swapped.append(other)
             tied.append(more)
             results += done
-        results.append(work(self.count, None, swapped[self.count]))
+        last = self.count - 1
+        results.append(work(last, arrived[last], swapped[self.count]))
+        if not late:
+            results.append(work(self.count, None, swapped[last]))
+        else:
+            results.append(lambda gate: self.later(work, swapped[last], gate))
         return results, tied
+
+    def later(self, work, block, gate):
+        gate, block = together(gate, block)
+        return gate, lambda: work(self.count, None, block)
 
     def scatter(self, parts, fill=None):
         count = self.count
@@ -155,7 +165,7 @@
                     wanted.append(int(np.argmax(self.order[i] == j)) if 0 <= j < count else None)
                 value = self.choose(made, wanted)
                 if last[step] is not None:
-                    value = value + last[step].astype(f32)
+                    value = value.astype(f32) + last[step].astype(f32)
                 keep = lambda i: 0 <= i + step * far < count
                 moved.append(self.hop(value.astype(bf16), step, keep))
             done = parts(far - 1)
@@ -164,17 +174,21 @@
             tied.append(more)
             made[far - 1] = done
             last[1], last[-1] = moved
-        return made[0] + last[1].astype(f32) + last[-1].astype(f32), tied
+        total = made[0].astype(f32) + last[1].astype(f32) + last[-1].astype(f32)
+        return total, tied
 
 
 def scatter_sum(for_same, for_other):
-    return for_same.astype(f32) + swap(for_other.astype(bf16)).astype(f32)
+    return (for_same.astype(f32) + swap(for_other.astype(bf16)).astype(f32)).astype(bf16)
+
+
+def cores_start(blocks):
+    core = lax.axis_index("c")
+    return pick(blocks, core, 1), swap(pick(blocks, 1 - core, 1))
 
 
 def exchange_cores(blocks):
-    core = lax.axis_index("c")
-    got = swap(pick(blocks, 1 - core, 1))
-    return by_core(pick(blocks, core, 1), got)
+    return by_core(*cores_start(blocks))
 
 
 def by_core(mine, other):
@@ -183,12 +197,47 @@
     return jnp.where(here, mine[:, None], other[:, None])
 
 
+def assemble_kernel(*refs):
+    out_ref = refs[-1]
+    for i, piece in enumerate(refs[1:-1]):
+
+        @pl.when(pl.program_id(0) == i)
+        def _(piece=piece):
+            out_ref[0] = piece[...]
+
+
+def assemble(pieces, places):
+    shape = pieces[0].shape
+    block = pl.BlockSpec(shape, lambda i, places: (0,) * len(shape))
+    return pl.pallas_call(
+        assemble_kernel,
+        grid_spec=pltpu.PrefetchScalarGridSpec(
+            num_scalar_prefetch=1,
+            grid=(len(pieces),),
+            in_specs=[block] * len(pieces),
+            out_specs=pl.BlockSpec((1,) + shape, lambda i, places: (places[i],) + (0,) * len(shape)),
+        ),
+        out_shape=jax.ShapeDtypeStruct((len(pieces),) + shape, pieces[0].dtype),
+        compiler_params=pltpu.CompilerParams(vmem_limit_bytes=32 << 20),
+        cost_estimate=cost(2),
+        name="assemble",
+    )(jnp.stack(places).astype(jnp.int32), *pieces)
+
+
+def shifts(value_for, chips):
+    return tuple(shift(value_for(steps), chips, steps) for steps in offsets(chips))
+
+
+def by_source(pieces, chips):
+    return assemble(pieces, [place(chips, steps, -1) for steps in offsets(chips)])
+
+
+def chips_start(pairs, chips):
+    return shifts(lambda steps: pick(pairs, place(chips, steps)), chips)
+
+
 def exchange_chips(pairs, chips):
-    result = jnp.zeros_like(pairs)
-    for steps in offsets(chips):
-        piece = shift(pick(pairs, place(chips, steps)), chips, steps)
-        result = put(result, piece, place(chips, steps, -1))
-    return result
+    return by_source(chips_start(pairs, chips), chips)
 
 
 def exchange(blocks, chips):
@@ -217,6 +266,14 @@
 def product_right(left_side, right_side):
     return lax.dot_general(
         left_side, right_side, (((1,), (1,)), ((), ())), preferred_element_type=f32
+    )
+
+
+def cost(microseconds):
+    return pl.CostEstimate(
+        flops=int(microseconds * 1.0e9),
+        transcendentals=0,
+        bytes_accessed=int(microseconds * 3.0e6),
     )
 
 
@@ -278,6 +335,7 @@
             jax.ShapeDtypeStruct((heads, 1, length), f32),
         ],
         compiler_params=pltpu.CompilerParams(vmem_limit_bytes=48 << 20),
+        cost_estimate=cost(16),
         name="attend",
     )(lows, starts, queries, keys, values)
 
@@ -340,6 +398,7 @@
         ),
         out_shape=[jax.ShapeDtypeStruct((length, width), f32)] * 3,
         compiler_params=pltpu.CompilerParams(vmem_limit_bytes=56 << 20),
+        cost_estimate=cost(26),
         name="attend_back",
     )(lows, starts, queries, keys, values, out, log_total, grads)
 
@@ -362,6 +421,7 @@
         in_specs=[pl.BlockSpec((rows, owners * unit), lambda g: (0, g))],
         out_specs=pl.BlockSpec((owners, rows, unit), lambda g: (0, 0, g)),
         out_shape=jax.ShapeDtypeStruct((owners, rows, groups * unit), weight.dtype),
+        cost_estimate=cost(4),
         name="spread",
     )(weight)
 
@@ -384,6 +444,7 @@
         in_specs=[pl.BlockSpec((owners, rows, unit), lambda g: (0, 0, g))],
         out_specs=pl.BlockSpec((rows, owners * unit), lambda g: (0, g)),
         out_shape=jax.ShapeDtypeStruct((rows, groups * owners * unit), f32),
+        cost_estimate=cost(5),
         name="collect",
     )(blocks)
 
@@ -421,8 +482,34 @@
             jax.ShapeDtypeStruct((2, length), f32),
         ],
         compiler_params=pltpu.CompilerParams(vmem_limit_bytes=32 << 20),
+        cost_estimate=cost(10),
         name="project",
     )(inputs, weight)
+
+
+def join_kernel(core_ref, full_ref, got_ref, out_ref):
+    out_ref[...] = (full_ref[:, 0].astype(f32) + got_ref[...].astype(f32)).astype(bf16)
+
+
+def join(full, got):
+    count, _, rows, columns = full.shape
+    step = 4 if count % 4 == 0 else 1
+    part = pl.BlockSpec((step, rows, columns), lambda i, core: (i, 0, 0))
+    return pl.pallas_call(
+        join_kernel,
+        grid_spec=pltpu.PrefetchScalarGridSpec(
+            num_scalar_prefetch=1,
+            grid=(count // step,),
+            in_specs=[
+                pl.BlockSpec((step, 1, rows, columns), lambda i, core: (i, core[0], 0, 0)),
+                part,
+            ],
+            out_specs=part,
+        ),
+        out_shape=jax.ShapeDtypeStruct((count, rows, columns), bf16),
+        cost_estimate=cost(4),
+        name="join",
+    )(lax.axis_index("c").astype(jnp.int32).reshape(1), full, got)
 
 
 def turn_kernel(proj_ref, factor_ref, gain_ref, cos_ref, sin_ref, q_ref, k_ref, v_ref):
@@ -465,6 +552,7 @@
         ],
         out_specs=[row_block(width)] * 3,
         out_shape=[jax.ShapeDtypeStruct((length, width), bf16)] * 3,
+        cost_estimate=cost(6),
         name="turn",
     )(projected, factors, gains, cosine, sine_part)
 
@@ -515,6 +603,7 @@
             jax.ShapeDtypeStruct((2, length), f32),
             jax.ShapeDtypeStruct((2, width), f32),
         ],
+        cost_estimate=cost(7),
         name="unturn",
     )(query_grad, key_grad, projected, factors, gains, cosine, sine_part)
 
@@ -545,6 +634,7 @@
         ],
         out_specs=row_block(3 * width),
         out_shape=jax.ShapeDtypeStruct((length, 3 * width), bf16),
+        cost_estimate=cost(7),
         name="finish",
     )(weighted, projected, factors, mixing, value_grad)
 
@@ -607,7 +697,8 @@
     buffer = [jnp.zeros((line, 2, piece_len, model_width), bf16)]
 
     def keep_input(k, same, other):
-        for at_core, block, at in ((core, same, k), (1 - core, other, k - 1)):
+        of_other = k if k == line - 1 else k - 1 if k < line else line - 2
+        for at_core, block, at in ((core, same, k), (1 - core, other, of_other)):
             if block is not None:
                 buffer[0] = lax.dynamic_update_slice(
                     buffer[0], block[None, None], (row.served(at), at_core, 0, 0)
@@ -617,41 +708,44 @@
     def weights_step(slot, tied):
         if slot == 0:
             blocks = spread(qkv_weight, 3, owners)
-            return (exchange(blocks.reshape(line, 2, row_count, 3 * width), LINE),)
+            blocks = exchange_cores(blocks.reshape(line, 2, row_count, 3 * width))
+            return (blocks, in_weight)
         if slot == 1:
             down = lax.all_gather(down_weight, DATA, axis=0, tiled=True)
-            out_line = jnp.zeros((line,) + out_weight.shape, bf16)
-            for steps in offsets(LINE):
-                out_line = put(out_line, shift(out_weight, LINE, steps), place(LINE, steps, -1))
-            return (down, out_line)
-        if slot == 2:
-            blocks = spread(in_weight, 2 * data_count, owners)
-            return (exchange_cores(blocks.reshape((line, 2) + blocks.shape[1:])),)
+            blocks = spread(tied[0][1], 2 * data_count, owners)
+            in_cores = cores_start(blocks.reshape((line, 2) + blocks.shape[1:]))
+            return (exchange_chips(tied[0][0], LINE), down, in_cores)
         if slot == line - 1:
-            return tied[2]
+            return (out_weight, tied[1][2])
         return ()
 
     _, tied = row.gather(own_input, keep_input, weights_step)
     full_input = buffer[0].reshape(length, model_width)
-    qkv_here = lax.all_gather(tied[0][0].reshape(-1, 3 * width), DATA, axis=0, tiled=True)
-    down_here, out_line = tied[1]
+    qkv_here = lax.all_gather(tied[1][0].reshape(-1, 3 * width), DATA, axis=0, tiled=True)
+    down_here = tied[1][1]
     units = down_here.shape[0]
+    out_shuffled, (in_keep, in_got) = tied[line - 1]
+    out_pieces = shifts(lambda steps: out_shuffled, LINE)
+
+    projected, squares = project(full_input, qkv_here)
+    squares, out_pieces, in_got = together(squares, out_pieces, in_got)
+    out_line = by_source(out_pieces, LINE)
     out_half = lax.all_gather(out_line.reshape(-1, D), DATA, axis=0, tiled=True)
-    in_rows = exchange_chips(tied[line - 1][0], LINE)
-
-    projected, squares = project(full_input, qkv_here)
+    in_pieces = chips_start(by_core(in_keep, in_got), LINE)
     factors = lax.rsqrt(small_sum(squares, CTX) / D + norm_epsilon)
     gains_here = lax.dynamic_slice(norm_gains, (0, ctx_place * width), (2, width))
     query_low, key_low, value_low = turn(projected, factors, gains_here, cosine, sine_part)
     head_out, log_total = attend(lows, starts_row, query_low, key_low, value_low)
-    head_out, in_rows = together(head_out, in_rows)
+
+    head_out, in_pieces, out_half = together(head_out, in_pieces, out_half)
+    blocks = head_out.astype(bf16).reshape(line, 2, piece_len, width)
+    keep, got = cores_start(blocks)
+    out_half = out_half.reshape(-1, out_weight.shape[0], D)
+    out_other = swap(out_half)
+    in_rows = by_source(in_pieces, LINE)
     in_here = lax.all_gather(in_rows.reshape(-1, in_rows.shape[-1]), DATA, axis=0, tiled=True)
-
-    pairs = exchange_cores(head_out.astype(bf16).reshape(line, 2, piece_len, width))
-    pairs, out_half = together(pairs, out_half)
-    attended = exchange_chips(pairs, LINE)
-    out_half = out_half.reshape(-1, out_weight.shape[0], D)
-    out_full = by_core(out_half, swap(out_half)).reshape(D, D)
+    attended = exchange_chips(by_core(keep, got), LINE)
+    out_full = by_core(out_half, out_other).reshape(D, D)
     attended_low = attended.reshape(line * 2, piece_len, width).transpose(1, 0, 2)
     attended_low = attended_low.reshape(piece_len, D)
     branch = product(attended_low, out_full)
@@ -664,7 +758,15 @@
 
     def chip_sums(results):
         def parts(k):
-            return scatter_sum(results[k][-1][:piece_len], results[k + 1][-1][-piece_len:])
+            same = results[k][-1][:piece_len]
+            if k == line - 1:
+                got = swap(results[k][-1][piece_len:])
+                if callable(results[line]):
+                    got, results[line] = results[line](got)
+                return (same.astype(f32) + got.astype(f32)).astype(bf16)
+            if k == line - 2 and callable(results[line]):
+                results[line] = results[line]()
+            return scatter_sum(same, results[line if k == line - 2 else k + 1][-1][-piece_len:])
 
         return parts
 
@@ -673,11 +775,21 @@
         gate_up = product(rows, in_here)
         gate_part, up_part = gate_up[:, :units], gate_up[:, units:]
         hidden = (gate_part * jax.nn.sigmoid(gate_part) * up_part).astype(bf16)
-        return rows, gate_up, hidden, product(hidden, down_here).astype(bf16)
-
-    plan = [[], [], [0, 1, 2]] + [[k] for k in range(3, line)]
+        return rows, gate_up.astype(bf16), hidden, product(hidden, down_here).astype(bf16)
+
+    plan = [[], [0], [1, 2]] + [[k] for k in range(3, line - 1)]
     forward, _ = row.gather(residual_low, forward_chip, plan=plan)
-    second, _ = row.scatter(chip_sums(forward))
+    def join_rows(slot, tied):
+        if slot == 1:
+            return ([f[0] for f in forward], [f[2] for f in forward])
+        if slot == 2:
+            return (jnp.concatenate(tied[0][0], axis=0), tied[0][1])
+        if slot == 3:
+            return (jnp.concatenate(tied[1][1], axis=0),)
+        return ()
+
+    second, tied = row.scatter(chip_sums(forward), join_rows)
+    residual_all, hidden_all = tied[1][0], tied[2][0]
     second_normed, second_factor = norm_forward(second, norm_gains[3])
     result = residual + second_normed
     live_places = ctx_place * piece_len + jnp.arange(piece_len, dtype=jnp.int32)
@@ -695,7 +807,7 @@
 
     def backward_chip(k, same, other):
         rows = rows_of(same, other)
-        gate_up = forward[k][1]
+        gate_up = forward[k][1].astype(f32)
         hidden_grad = product_right(rows, down_here)
         gate_part, up_part = gate_up[:, :units], gate_up[:, units:]
         sigmoid_gate = jax.nn.sigmoid(gate_part)
@@ -709,11 +821,10 @@
     def weight_grads(slot, tied):
         if slot == 1:
             gate_up_all = jnp.concatenate([b[1] for b in backward], axis=0)
-            residual_all = jnp.concatenate([f[0] for f in forward], axis=0)
-            return (product_left(residual_all, gate_up_all).astype(bf16),)
+            grads = product_left(residual_all, gate_up_all).astype(bf16)
+            return (grads, [b[0] for b in backward])
         if slot == 2:
-            hidden_all = jnp.concatenate([f[2] for f in forward], axis=0)
-            second_grad_all = jnp.concatenate([b[0] for b in backward], axis=0)
+            second_grad_all = jnp.concatenate(tied[0][1], axis=0)
             return (product_left(hidden_all, second_grad_all).astype(bf16),)
         return ()
 
@@ -721,7 +832,7 @@
     grad_in, grad_down = tied[0][0], tied[1][0]
     residual_grad = incoming + residual_part
     grad_in = scatter_over(grad_in, DATA).reshape(in_rows.shape)
-    grad_down = scatter_over(grad_down, DATA).astype(f32)
+    grad_down = scatter_over(grad_down, DATA)
 
     branch_grad, branch_gain_grad = norm_backward(
         branch, branch_factor, norm_gains[2], residual_grad
@@ -729,29 +840,32 @@
     branch_grad_low = branch_grad.astype(bf16)
     attended_grad = product_right(branch_grad_low, out_full).astype(bf16)
     attended_grad = attended_grad.reshape(piece_len, line, 2, width).transpose(1, 2, 0, 3)
-    pairs, branch_grad_low = together(exchange_cores(attended_grad), branch_grad_low)
-    head_grad = exchange_chips(pairs, LINE).reshape(length, width)
-
+    keep, give = pick(attended_grad, core, 1), pick(attended_grad, 1 - core, 1)
+    give, branch_grad_low = together(give, branch_grad_low)
     out_grad = product_left(attended_low, branch_grad_low).astype(bf16)
     out_grad = out_grad.reshape(-1, 2, out_weight.shape[0], D)
-    out_keep, out_got = pick(out_grad, core, 1), swap(pick(out_grad, 1 - core, 1))
-    in_pairs = exchange_cores(grad_in.reshape((line, 2) + in_rows.shape[2:]))
-    head_grad, in_pairs = together(head_grad, in_pairs)
-    grad_in = exchange_chips(in_pairs, LINE)
+    got, out_grad, grad_in = together(swap(give), out_grad, grad_in)
+    pieces = chips_start(by_core(keep, got), LINE)
+    in_keep, in_got = cores_start(grad_in.reshape((line, 2) + in_rows.shape[2:]))
+    out_got = swap(pick(out_grad, 1 - core, 1))
+    pieces, in_got, out_got = together(pieces, in_got, out_got)
+    head_grad = by_source(pieces, LINE).reshape(length, width)
+    in_pieces = chips_start(by_core(in_keep, in_got), LINE)
+    out_grad = join(out_grad, out_got)
+    head_grad, out_grad = together(head_grad, out_grad)
+    out_grad = scatter_over(out_grad.reshape(D // 2, D), DATA)
+    out_grad = out_grad.reshape((line,) + out_weight.shape)
 
     query_grad, key_grad, value_grad = attend_back(
         lows, starts_row, query_low, key_low, value_low, head_out, log_total, head_grad
     )
-    query_grad, out_keep = together(query_grad, out_keep)
-    out_grad = (out_keep.astype(f32) + out_got.astype(f32)).astype(bf16).reshape(D // 2, D)
-    out_grad = scatter_over(out_grad, DATA).reshape((line,) + out_weight.shape)
     weighted, mixing, gain_grads = unturn(
         query_grad, key_grad, projected, factors, gains_here, cosine, sine_part
     )
-    mixing, grad_down = together(mixing, grad_down)
+    mixing, in_pieces = together(mixing, in_pieces)
     mixing = small_sum(mixing, CTX) / D
     projected_grad = finish(weighted, projected, factors, mixing, value_grad)
-
+    projected_grad, grad_down = together(projected_grad, grad_down)
     grad_blocks = projected_grad.reshape(line, 2, piece_len, 3 * width)
 
     later = []
@@ -762,37 +876,44 @@
         part = product_right(rows, qkv_here).astype(bf16)
         part = scatter_sum(part[:piece_len], part[piece_len:])
         if not later:
-            part, grads = together(part, projected_grad)
-            later.append(grads)
+            later.extend(together(part, projected_grad))
+            part = later[0]
         return part
 
-    gain_rows = jnp.zeros((5, D), f32)
-    gain_rows = lax.dynamic_update_slice(gain_rows, gain_grads, (0, ctx_place * width))
-    gain_rows = gain_rows.at[2].set(branch_gain_grad).at[3].set(second_gain_grad)
-    gain_rows = gain_rows.at[4, :3].set(sums)
+    def step(rows, axis):
+        if lax.axis_size(axis) == 2:
+            return (rows, lax.ppermute(rows, axis, [(0, 1), (1, 0)]))
+        return (lax.psum(rows, axis),)
 
     def last_grads(slot, tied):
         if slot == 1:
-            part = product_left(full_input, later[0]).astype(bf16)
-            return (part, small_sum(gain_rows, AXES[2:]), out_grad, grad_in)
+            grads = product_left(full_input, later[1]).astype(bf16)
+            return (grads, gain_grads, chips_start(out_grad, LINE))
         if slot == 2:
-            return (scatter_over(tied[0][0], DATA), small_sum(tied[0][1], AXES[:2]))
+            rows = jnp.zeros((5, D), f32)
+            rows = lax.dynamic_update_slice(rows, tied[0][1], (0, ctx_place * width))
+            rows = rows.at[2].set(branch_gain_grad).at[3].set(second_gain_grad)
+            rows = rows.at[4, :3].set(sums)
+            return (scatter_over(tied[0][0], DATA), step(rows, "c"))
         if slot == line - 1:
             blocks = tied[1][0].reshape(line, 2, row_count, 3 * width)
-            return (exchange_cores(blocks),)
+            rows = step(sum(tied[1][1]), "zl")
+            return (cores_start(blocks), rows, in_pieces, grad_down)
         return ()
 
     input_part, tied = row.scatter(input_chip, last_grads)
-    (_, _, out_grad, grad_in), (_, gain_rows), (grad_qkv,) = tied[0], tied[1], tied[line - 2]
+    qkv_cores, gain_rows, in_pieces, grad_down = tied[line - 2]
+    out_pieces = tied[0][2]
+    qkv_pieces = chips_start(by_core(*qkv_cores), LINE)
+    gain_rows = small_sum(sum(gain_rows), ("zh", "dl", "dh"))
     input_grad = residual_grad + input_part
+    grad_in = by_source(in_pieces, LINE)
     grad_in = collect(grad_in.reshape((owners,) + grad_in.shape[2:]), 2 * data_count)
-    grad_qkv = exchange_chips(grad_qkv, LINE)
+    grad_down = grad_down.astype(f32)
+    grad_out = sum(piece.astype(f32) for piece in out_pieces)
+    qkv_pieces, grad_in, grad_down = together(qkv_pieces, grad_in, grad_down)
+    grad_qkv = by_source(qkv_pieces, LINE)
     grad_qkv = collect(grad_qkv.reshape(owners, row_count, 3 * width), 3)
-    grad_out = None
-    for steps in offsets(LINE):
-        part = shift(pick(out_grad, place(LINE, steps)), LINE, steps).astype(f32)
-        grad_out = part if grad_out is None else grad_out + part
-
     live_count = jnp.sum(seq_lengths).astype(f32)
     rms_values = jnp.sqrt(gain_rows[4, :3] / (live_count * model_width))
     return (

time: 1040 us -> 1030 us (level)
  local copies, waits for them, and re-layouts: 125 us -> 85.7 us
  Pallas kernels: 83.3 us -> 98.7 us
  other arithmetic: 143 us -> 129 us
    ppermute x36, waiting for transfers between devices: 196 us -> 172 us  [hop(): return lax.ppermute(value, self.axes, pairs)]
    dynamic_update_slice x24 -> x1, local copies, waits for them, and re-layouts: 21.7 us -> 0.01 us  [last_grads(): rows = lax.dynamic_update_slice(rows, tied[0][1], (0, ctx_place * width))]
    ppermute x0 -> x2, waiting for transfers between devices: none -> 20.9 us  [step(): return (rows, lax.ppermute(rows, axis, [(0, 1), (1, 0)]))]
    add x11 -> x3, other arithmetic: 21.3 us -> 0.94 us  [the longest x1 0.92 us: on_device(): grad_out = sum((piece.astype(f32) for piece in out_pieces))]
    pallas_call x0 -> x8, Pallas kernels: none -> 15.6 us  [the longest x7 9.16 us: assemble(): pl.pallas_call(assemble_kernel, grid_spec=pltpu.PrefetchScalarGridSpec(nu...]
    ppermute x24, waiting for transfers between devices: 90.4 us -> 102 us  [shift(): return lax.ppermute(value, axes, pairs)]
    dot_general x11, matrix products: 41.4 us -> 51.9 us  [product(): return jnp.dot(left_side, right_side, preferred_element_type=f32)]
    ppermute x11 -> x9, starting transfers between devices: 15.3 us -> 25.5 us  [small_sum(): value = value + lax.ppermute(value, axis, [(0, 1), (1, 0)])]
  transfers between devices with their start and end apart: 111 -> 111, of which waited for: 40 -> 49; matrix products, arithmetic and copies ran while one was open for 35% -> 31% of each run, Pallas kernels for 8% -> 9%
where the time goes in v3:
time: 1030 us; the launch traced here: 1020 us
  waiting for transfers between devices  333 us (32%)
  starting transfers between devices  182 us (18%)
  matrix products  167 us (16%)
  other arithmetic  129 us (13%)
  Pallas kernels  98.7 us (10%)
  local copies, waits for them, and re-layouts  85.7 us (8%)
  between operations  23.3 us (2%)
    ppermute x36, waiting for transfers between devices, hop(): return lax.ppermute(value, self.axes, pairs)  172 us
    ppermute x24, waiting for transfers between devices, shift(): return lax.ppermute(value, axes, pairs)  102 us
    ppermute x36, starting transfers between devices, hop(): return lax.ppermute(value, self.axes, pairs)  99.9 us
    dot_general x15, matrix products, product_right(): lax.dot_general(left_side, right_side, (((1,), (1,)), ((), ())), preferre...  64.5 us
    dot_general x11, matrix products, product(): return jnp.dot(left_side, right_side, preferred_element_type=f32)  51.9 us
    dot_general x4, matrix products, product_left(): lax.dot_general(left_side, right_side, (((0,), (0,)), ((), ())), preferre...  50.7 us
    ppermute x24, starting transfers between devices, shift(): return lax.ppermute(value, axes, pairs)  45.8 us
    unnamed x207, local copies, waits for them, and re-layouts  41.7 us
  transfers between devices with their start and end apart: 111, of which 49 were waited for; matrix products, arithmetic and copies ran while one was open for 31% of the time, Pallas kernels for 9%

profile of v3, /device:TPU:0, one launch (start us, length us, event | category | flops | bytes accessed | tf_op | source)
XLA Modules:
  0.0 1018.3 jit_solution(3677851673021420177)
XLA Ops:
  29.5 6.2 collective-permute-done
  59.7 14.3 %collective-permute-done.7.refs_2_ = bf16[2,64,768]{2,1,0:T(8,128)(2,1)S(1)} collective-permute-done((bf16[2,64,768]{2,1,0:T(8,128)(2,1)S(1)}, bf16[2,64,768]{2,1,0:T(8,128)(2,1)S(1)}, u32[]{:S(2)}, u32[]{:S(2)}) %collective-permute-start.7) | collective-permute-done | bytes 196640 | tf_op jit(solution)/shard_map/ppermute | solution.py:57
  74.3 9.0 collective-permute-done.8.refs_3_
  109.1 7.1 collective-permute-done.11
  137.4 10.5 %project.1 = (f32[2048,768]{1,0:T(8,128)S(1)}, f32[2,2048]{1,0:T(2,128)S(1)}) custom-call(bf16[2048,2048]{1,0:T(8,128)(2,1)} %bitcast.34.in_ref, bf16[2048,768]{1,0:T(8,128)(2,1)S(1)} %copy-done.3), custom_call_target="tpu_custom_call" | custom-call | flops 10000000000 | bytes 30000000 | tf_op jit(solution)/shard_map/project/pallas_call | solution.py:475
  160.3 6.6 collective-permute-start.18
  178.8 6.4 turn.1
  189.0 13.8 %attend.1 = (f32[2048,256]{1,0:T(8,128)S(1)}, f32[2,1,2048]{2,1,0:T(1,128)S(1)}) custom-call(s32[4]{0:T(128)S(1)} %and_select_fusion.low_ref, s32[1,2048]{1,0:T(1,128)S(1)} %bitcast.239, bf16[2048,256]{1,0:T(8,128)(2,1)S(1)} %copy-done.12, bf16[2048,256]{1,0:T(8,128)(2,1)S(1)} %copy-done.13, bf16[2048,256]{1,0:T(8,128)(2,1)S(1)} %copy-done.14), custom_call_target="tpu_custom_call" | custom-call | flops 16000000000 | bytes 48000000 | tf_op jit(solution)/shard_map/attend/pallas_call | solution.py:317
  203.3 10.3 %collective-permute-done.22.refs_3_ = bf16[2,64,2048]{2,1,0:T(8,128)(2,1)} collective-permute-done((bf16[2,64,2048]{2,1,0:T(8,128)(2,1)}, bf16[2,64,2048]{2,1,0:T(8,128)(2,1)}, u32[]{:S(2)}, u32[]{:S(2)}) %collective-permute-start.22) | collective-permute-done | bytes 524320 | tf_op jit(solution)/shard_map/ppermute | solution.py:57
  217.9 6.8 collective-permute-done.24
  224.9 11.1 %collective-permute-start.25 = (bf16[2,256,256]{2,1,0:T(8,128)(2,1)S(1)}, bf16[2,256,256]{2,1,0:T(8,128)(2,1)S(1)}, u32[]{:S(2)}, u32[]{:S(2)}) collective-permute-start(bf16[2,256,256]{2,1,0:T(8,128)(2,1)S(1)} %get-tuple-element.477), channel_id=1, source_target_pairs={{0,2},{2,0},{4,6},{6,4},{1,3},{3,1},{5,7},{7,5},{8,10},{10,8},{12,... | collective-permute-start | bytes 786440 | tf_op jit(solution)/shard_map/ppermute | solution.py:57
  239.1 9.2 collective-permute-done.25.refs_2_
  248.3 9.1 collective-permute-done.26.refs_3_
  267.2 8.2 collective-permute-start.29
  276.7 19.6 %collective-permute-done.29 = bf16[256,2048]{1,0:T(8,128)(2,1)} collective-permute-done((bf16[256,2048]{1,0:T(8,128)(2,1)S(1)}, bf16[256,2048]{1,0:T(8,128)(2,1)}, u32[]{:S(2)}, u32[]{:S(2)}) %collective-permute-start.29) | collective-permute-done | bytes 1048608 | tf_op jit(solution)/shard_map/ppermute | solution.py:104
  337.0 7.2 fusion.62
  347.2 7.3 fusion.63
  361.7 7.1 convert_convert_fusion.1
  368.8 10.4 %convert_convert_fusion = (f32[512,2048]{1,0:T(8,128)}, f32[512,2048]{1,0:T(8,128)S(1)}) fusion(bf16[2048,2048]{1,0:T(8,128)(2,1)} %all-gather.11.cloned.1.call-done, bf16[256,2048]{1,0:T(8,128)(2,1)S(1)} %collective-permute-done.38, bf16[256,2048]{1,0:T(8,128)(2,1)S(1)} %select_select_fusion.2), kind=kOutput, calls=%fused_computation.84 | convolution fusion | flops 4301258752 | bytes 18874368 | tf_op jit(solution)/shard_map/dot_general | solution.py:257
  399.2 21.0 %collective-permute-done.40 = bf16[256,2048]{1,0:T(8,128)(2,1)S(1)} collective-permute-done((bf16[256,2048]{1,0:T(8,128)(2,1)S(1)}, bf16[256,2048]{1,0:T(8,128)(2,1)S(1)}, u32[]{:S(2)}, u32[]{:S(2)}) %collective-permute-start.40) | collective-permute-done | bytes 1048608 | tf_op jit(solution)/shard_map/ppermute | solution.py:104
  429.3 19.3 %collective-permute-done.43 = bf16[256,2048]{1,0:T(8,128)(2,1)S(1)} collective-permute-done((bf16[256,2048]{1,0:T(8,128)(2,1)S(1)}, bf16[256,2048]{1,0:T(8,128)(2,1)S(1)}, u32[]{:S(2)}, u32[]{:S(2)}) %collective-permute-start.43) | collective-permute-done | bytes 1048608 | tf_op jit(solution)/shard_map/ppermute | solution.py:104
  450.7 7.7 collective-permute-start.46
  460.7 18.2 %collective-permute-done.46 = bf16[256,2048]{1,0:T(8,128)(2,1)S(1)} collective-permute-done((bf16[256,2048]{1,0:T(8,128)(2,1)S(1)}, bf16[256,2048]{1,0:T(8,128)(2,1)S(1)}, u32[]{:S(2)}, u32[]{:S(2)}) %collective-permute-start.46) | collective-permute-done | bytes 1048608 | tf_op jit(solution)/shard_map/ppermute | solution.py:104
  492.1 6.8 convolution_convert_fusion.18
  498.8 9.7 collective-permute-done.49
  523.5 9.1 convolution_convert_fusion.13
  549.6 9.3 convolution_convert_fusion.12
  576.3 8.2 convolution_convert_fusion.11
  585.1 6.7 convolution_convert_fusion.17
  602.5 23.7 %convolution_convert_fusion.1 = bf16[2048,2048]{1,0:T(8,128)(2,1)} fusion(bf16[2048,2048]{1,0:T(8,128)(2,1)} %copy-done.65, bf16[2048,2048]{1,0:T(8,128)(2,1)} %fusion.41), kind=kOutput, calls=%fused_computation.3 | convolution fusion | flops 17184063488 | bytes 25165824 | tf_op jit(solution)/shard_map/dot_general | solution.py:261
  652.3 11.0 %convolution_convert_fusion.2 = bf16[1024,2048]{1,0:T(8,128)(2,1)} fusion(bf16[2048,1024]{1,0:T(8,128)(2,1)S(1)} %copy-done.70, bf16[2048,2048]{1,0:T(8,128)(2,1)S(1)} %constant_dynamic-update-slice_fusion.13), kind=kOutput, calls=%fused_computation.5 | convolution fusion | flops 8592031744 | bytes 16777216 | tf_op jit(solution)/shard_map/dot_general | solution.py:261
  672.1 6.8 collective-permute-start.66
  680.6 7.6 bitcast_select_fusion
  690.8 9.7 collective-permute-done.66
  734.7 7.7 collective-permute-done.70.refs_2_
  742.4 9.4 collective-permute-done.71.refs_3_
  755.6 6.4 join.1
  771.2 20.4 %attend_back.1 = (f32[2048,256]{1,0:T(8,128)}, f32[2048,256]{1,0:T(8,128)}, f32[2048,256]{1,0:T(8,128)}) custom-call(s32[4]{0:T(128)} %copy-done.10, s32[1,2048]{1,0:T(1,128)} %bitcast.240, bf16[2048,256]{1,0:T(8,128)(2,1)} %get-tuple-element.244.q_ref, bf16[2048,256]{1,0:T(8,128)(2,1)} %get-tuple-element.245.k_ref, ...), custom_call_target="tpu_custom_call" | custom-call | flops 25999998976 | bytes 78000000 | tf_op jit(solution)/shard_map/attend_back/pallas_call | solution.py:383
  791.5 7.6 unturn.1
  799.1 7.6 collective-permute-done.76.refs_3_
  806.8 9.8 collective-permute-start.78
  825.9 7.1 finish.1
  850.0 10.4 %convolution_convert_fusion.3 = bf16[2048,768]{1,0:T(8,128)(2,1)} fusion(bf16[2048,2048]{1,0:T(8,128)(2,1)} %bitcast.34.in_ref, bf16[2048,768]{1,0:T(8,128)(2,1)S(1)} %copy-done.33), kind=kOutput, calls=%fused_computation.6 | convolution fusion | flops 6444023808 | bytes 14680064 | tf_op jit(solution)/shard_map/dot_general | solution.py:261
  881.9 8.4 collective-permute-done.87
  901.0 6.2 add_convert_fusion.4
  919.9 11.6 %collective-permute-done.88 = bf16[256,2048]{1,0:T(8,128)(2,1)} collective-permute-done((bf16[256,2048]{1,0:T(8,128)(2,1)}, bf16[256,2048]{1,0:T(8,128)(2,1)}, u32[]{:S(2)}, u32[]{:S(2)}) %collective-permute-start.88) | collective-permute-done | bytes 1048608 | tf_op jit(solution)/shard_map/ppermute | solution.py:104
  948.5 20.9 %collective-permute-done.96 = f32[5,2048]{1,0:T(8,128)S(1)} collective-permute-done((f32[5,2048]{1,0:T(8,128)S(1)}, f32[5,2048]{1,0:T(8,128)S(1)}, u32[]{:S(2)}, u32[]{:S(2)}) %collective-permute-start.96) | collective-permute-done | bytes 40992 | tf_op jit(solution)/shard_map/ppermute | solution.py:885
  977.5 14.2 %collective-permute-done.100 = f32[5,2048]{1,0:T(8,128)S(1)} collective-permute-done((f32[5,2048]{1,0:T(8,128)S(1)}, f32[5,2048]{1,0:T(8,128)S(1)}, u32[]{:S(2)}, u32[]{:S(2)}) %collective-permute-start.100) | collective-permute-done | bytes 40992 | tf_op jit(solution)/shard_map/ppermute | solution.py:250
  (585 shorter events, 492.7 us)
Async XLA Ops:
  7.2 85.7 %all-gather.5.cloned.1.call-start = ((), (), s32[]{:S(2)}) async-start(), calls=%async_computation.4 | async-start | bytes 5242880 | tf_op jit(solution)/shard_map/all_gather | solution.py:714
  7.9 127.6 %all-gather.7.cloned.1.call-start = ((), (), s32[]{:S(2)}) async-start(), calls=%async_computation.5 | async-start | bytes 3932160 | tf_op jit(solution)/shard_map/all_gather | solution.py:724
  8.0 27.7 %collective-permute-start = (bf16[256,2048]{1,0:T(8,128)(2,1)}, bf16[256,2048]{1,0:T(8,128)(2,1)S(1)}, u32[]{:S(2)}, u32[]{:S(2)}) collective-permute-start(bf16[256,2048]{1,0:T(8,128)(2,1)} %bitcast.253), channel_id=1, source_target_pairs={{0,2},{2,4},{4,6},{1,3},{3,5},{5,7},{8,10},{10,12},{12,14},{9,11},... | collective-permute-start | bytes 3145736 | tf_op jit(solution)/shard_map/ppermute | solution.py:104
  13.0 26.8 %collective-permute-start.1 = (bf16[256,2048]{1,0:T(8,128)(2,1)}, bf16[256,2048]{1,0:T(8,128)(2,1)}, u32[]{:S(2)}, u32[]{:S(2)}) collective-permute-start(bf16[256,2048]{1,0:T(8,128)(2,1)} %bitcast.254), channel_id=1, source_target_pairs={{2,0},{4,2},{6,4},{3,1},{5,3},{7,5},{10,8},{12,10},{14,12},{11,9},... | collective-permute-start | bytes 3145736 | tf_op jit(solution)/shard_map/ppermute | solution.py:104
  14.3 25.5 %collective-permute-start.2 = (bf16[256,2048]{1,0:T(8,128)(2,1)}, bf16[256,2048]{1,0:T(8,128)(2,1)}, u32[]{:S(2)}, u32[]{:S(2)}) collective-permute-start(bf16[256,2048]{1,0:T(8,128)(2,1)} %bitcast.255), channel_id=1, source_target_pairs={{0,1},{1,0},{2,3},{3,2},{4,5},{5,4},{6,7},{7,6},{8,9},{9,8},{10,11... | collective-permute-start | bytes 3145736 | tf_op jit(solution)/shard_map/ppermute | solution.py:61
  39.8 53.0 %collective-permute-start.4 = (bf16[256,2048]{1,0:T(8,128)(2,1)S(1)}, bf16[256,2048]{1,0:T(8,128)(2,1)}, u32[]{:S(2)}, u32[]{:S(2)}) collective-permute-start(bf16[256,2048]{1,0:T(8,128)(2,1)S(1)} %collective-permute-done), channel_id=1, source_target_pairs={{0,2},{2,4},{4,6},{1,3},{3,5},{5,7},{8,10},{10,12},{12,14},{9,11},... | collective-permute-start | bytes 3145736 | tf_op jit(solution)/shard_map/ppermute | solution.py:104
  44.2 48.6 %collective-permute-start.5 = (bf16[256,2048]{1,0:T(8,128)(2,1)}, bf16[256,2048]{1,0:T(8,128)(2,1)}, u32[]{:S(2)}, u32[]{:S(2)}) collective-permute-start(bf16[256,2048]{1,0:T(8,128)(2,1)} %collective-permute-done.1), channel_id=1, source_target_pairs={{2,0},{4,2},{6,4},{3,1},{5,3},{7,5},{10,8},{12,10},{14,12},{11,9},... | collective-permute-start | bytes 3145736 | tf_op jit(solution)/shard_map/ppermute | solution.py:104
  49.1 43.7 %collective-permute-start.6 = (bf16[256,2048]{1,0:T(8,128)(2,1)}, bf16[256,2048]{1,0:T(8,128)(2,1)}, u32[]{:S(2)}, u32[]{:S(2)}) collective-permute-start(bf16[256,2048]{1,0:T(8,128)(2,1)} %get-tuple-element.420), channel_id=1, source_target_pairs={{0,1},{1,0},{2,3},{3,2},{4,5},{5,4},{6,7},{7,6},{8,9},{9,8},{10,11... | collective-permute-start | bytes 3145736 | tf_op jit(solution)/shard_map/ppermute | solution.py:61
  57.6 35.2 %collective-permute-start.10 = (bf16[4,64,2048]{2,1,0:T(8,128)(2,1)}, bf16[4,64,2048]{2,1,0:T(8,128)(2,1)}, u32[]{:S(2)}, u32[]{:S(2)}) collective-permute-start(bf16[4,64,2048]{2,1,0:T(8,128)(2,1)} %get-tuple-element.463), channel_id=1, source_target_pairs={{0,1},{1,0},{2,3},{3,2},{4,5},{5,4},{6,7},{7,6},{8,9},{9,8},{10,11... | collective-permute-start | bytes 3145736 | tf_op jit(solution)/shard_map/ppermute | solution.py:61
  92.9 120.8 %all-gather.9.cloned.1.call-start = ((), (), s32[]{:S(2)}) async-start(), calls=%async_computation.6 | async-start | bytes 5242880 | tf_op jit(solution)/shard_map/all_gather | solution.py:733
  152.6 162.4 %all-gather.11.cloned.1.call-start = ((), (), s32[]{:S(2)}) async-start(), calls=%async_computation.7 | async-start | bytes 10485760 | tf_op jit(solution)/shard_map/all_gather | solution.py:746
  173.7 29.6 %collective-permute-start.21 = (bf16[2,64,2048]{2,1,0:T(8,128)(2,1)}, bf16[2,64,2048]{2,1,0:T(8,128)(2,1)S(1)}, u32[]{:S(2)}, u32[]{:S(2)}) collective-permute-start(bf16[2,64,2048]{2,1,0:T(8,128)(2,1)} %get-tuple-element.461), channel_id=1, source_target_pairs={{0,2},{2,0},{4,6},{6,4},{1,3},{3,1},{5,7},{7,5},{8,10},{10,8},{12,... | collective-permute-start | bytes 1572872 | tf_op jit(solution)/shard_map/ppermute | solution.py:57
  175.1 38.5 %collective-permute-start.22 = (bf16[2,64,2048]{2,1,0:T(8,128)(2,1)}, bf16[2,64,2048]{2,1,0:T(8,128)(2,1)}, u32[]{:S(2)}, u32[]{:S(2)}) collective-permute-start(bf16[2,64,2048]{2,1,0:T(8,128)(2,1)} %get-tuple-element.460), channel_id=1, source_target_pairs={{0,4},{2,6},{4,0},{6,2},{1,5},{3,7},{5,1},{7,3},{8,12},{10,14},{12... | collective-permute-start | bytes 1572872 | tf_op jit(solution)/shard_map/ppermute | solution.py:57
  176.7 36.9 %collective-permute-start.23 = (bf16[2,64,2048]{2,1,0:T(8,128)(2,1)}, bf16[2,64,2048]{2,1,0:T(8,128)(2,1)}, u32[]{:S(2)}, u32[]{:S(2)}) collective-permute-start(bf16[2,64,2048]{2,1,0:T(8,128)(2,1)} %get-tuple-element.459), channel_id=1, source_target_pairs={{0,6},{2,4},{4,2},{6,0},{1,7},{3,5},{5,3},{7,1},{8,14},{10,12},{12... | collective-permute-start | bytes 1572872 | tf_op jit(solution)/shard_map/ppermute | solution.py:57
  217.0 507.6 %reduce-scatter.5.cloned.1.call-start = ((), (), s32[]{:S(2)}) async-start(), calls=%async_computation.8 | async-start | bytes 10485760 | tf_op jit(solution)/shard_map/reduce_scatter | solution.py:663
  217.0 41.6 %collective-permute-start.28 = (bf16[16,64,2048]{2,1,0:T(8,128)(2,1)}, bf16[16,64,2048]{2,1,0:T(8,128)(2,1)}, u32[]{:S(2)}, u32[]{:S(2)}) collective-permute-start(bf16[16,64,2048]{2,1,0:T(8,128)(2,1)} %bitcast.247), channel_id=1, source_target_pairs={{0,1},{1,0},{2,3},{3,2},{4,5},{5,4},{6,7},{7,6},{8,9},{9,8},{10,11... | collective-permute-start | bytes 12582920 | tf_op jit(solution)/shard_map/ppermute | solution.py:61
  267.2 29.1 %collective-permute-start.29 = (bf16[256,2048]{1,0:T(8,128)(2,1)S(1)}, bf16[256,2048]{1,0:T(8,128)(2,1)}, u32[]{:S(2)}, u32[]{:S(2)}) collective-permute-start(bf16[256,2048]{1,0:T(8,128)(2,1)S(1)} %fusion.20), channel_id=1, source_target_pairs={{0,2},{2,4},{4,6},{1,3},{3,5},{5,7},{8,10},{10,12},{12,14},{9,11},... | collective-permute-start | bytes 3145736 | tf_op jit(solution)/shard_map/ppermute | solution.py:104
  275.4 26.1 %collective-permute-start.30 = (bf16[256,2048]{1,0:T(8,128)(2,1)S(1)}, bf16[256,2048]{1,0:T(8,128)(2,1)}, u32[]{:S(2)}, u32[]{:S(2)}) collective-permute-start(bf16[256,2048]{1,0:T(8,128)(2,1)S(1)} %fusion.20), channel_id=1, source_target_pairs={{2,0},{4,2},{6,4},{3,1},{5,3},{7,5},{10,8},{12,10},{14,12},{11,9},... | collective-permute-start | bytes 3145736 | tf_op jit(solution)/shard_map/ppermute | solution.py:104
  276.7 24.8 %collective-permute-start.31 = (bf16[256,2048]{1,0:T(8,128)(2,1)S(1)}, bf16[256,2048]{1,0:T(8,128)(2,1)S(1)}, u32[]{:S(2)}, u32[]{:S(2)}) collective-permute-start(bf16[256,2048]{1,0:T(8,128)(2,1)S(1)} %fusion.20), channel_id=1, source_target_pairs={{0,1},{1,0},{2,3},{3,2},{4,5},{5,4},{6,7},{7,6},{8,9},{9,8},{10,11... | collective-permute-start | bytes 3145736 | tf_op jit(solution)/shard_map/ppermute | solution.py:61
  305.5 25.1 %collective-permute-start.33 = (bf16[256,2048]{1,0:T(8,128)(2,1)}, bf16[256,2048]{1,0:T(8,128)(2,1)}, u32[]{:S(2)}, u32[]{:S(2)}) collective-permute-start(bf16[256,2048]{1,0:T(8,128)(2,1)} %collective-permute-done.30), channel_id=1, source_target_pairs={{2,0},{4,2},{6,4},{3,1},{5,3},{7,5},{10,8},{12,10},{14,12},{11,9},... | collective-permute-start | bytes 3145736 | tf_op jit(solution)/shard_map/ppermute | solution.py:104
  330.7 28.4 %collective-permute-start.35 = (bf16[256,2048]{1,0:T(8,128)(2,1)}, bf16[256,2048]{1,0:T(8,128)(2,1)S(1)}, u32[]{:S(2)}, u32[]{:S(2)}) collective-permute-start(bf16[256,2048]{1,0:T(8,128)(2,1)} %collective-permute-done.32), channel_id=1, source_target_pairs={{0,2},{2,4},{4,6},{1,3},{3,5},{5,7},{8,10},{10,12},{12,14},{9,11},... | collective-permute-start | bytes 3145736 | tf_op jit(solution)/shard_map/ppermute | solution.py:104
  332.3 26.8 %collective-permute-start.36 = (bf16[256,2048]{1,0:T(8,128)(2,1)}, bf16[256,2048]{1,0:T(8,128)(2,1)S(1)}, u32[]{:S(2)}, u32[]{:S(2)}) collective-permute-start(bf16[256,2048]{1,0:T(8,128)(2,1)} %collective-permute-done.33), channel_id=1, source_target_pairs={{2,0},{4,2},{6,4},{3,1},{5,3},{7,5},{10,8},{12,10},{14,12},{11,9},... | collective-permute-start | bytes 3145736 | tf_op jit(solution)/shard_map/ppermute | solution.py:104
  388.9 71.0 %collective-permute-start.48 = (bf16[256,2048]{1,0:T(8,128)(2,1)S(1)}, bf16[256,2048]{1,0:T(8,128)(2,1)S(1)}, u32[]{:S(2)}, u32[]{:S(2)}) collective-permute-start(bf16[256,2048]{1,0:T(8,128)(2,1)S(1)} %slice.203), channel_id=1, source_target_pairs={{0,1},{1,0},{2,3},{3,2},{4,5},{5,4},{6,7},{7,6},{8,9},{9,8},{10,11... | collective-permute-start | bytes 3145736 | tf_op jit(solution)/shard_map/ppermute | solution.py:61
  391.8 28.4 %collective-permute-start.40 = (bf16[256,2048]{1,0:T(8,128)(2,1)S(1)}, bf16[256,2048]{1,0:T(8,128)(2,1)S(1)}, u32[]{:S(2)}, u32[]{:S(2)}) collective-permute-start(bf16[256,2048]{1,0:T(8,128)(2,1)S(1)} %add_convert_fusion.23), channel_id=1, source_target_pairs={{0,2},{1,3},{8,10},{9,11},{16,18},{17,19},{24,26},{25,27}} | collective-permute-start | bytes 3145736 | tf_op jit(solution)/shard_map/ppermute | solution.py:104
  422.4 26.1 %collective-permute-start.43 = (bf16[256,2048]{1,0:T(8,128)(2,1)S(1)}, bf16[256,2048]{1,0:T(8,128)(2,1)S(1)}, u32[]{:S(2)}, u32[]{:S(2)}) collective-permute-start(bf16[256,2048]{1,0:T(8,128)(2,1)S(1)} %get-tuple-element.458), channel_id=1, source_target_pairs={{0,2},{2,4},{1,3},{3,5},{8,10},{10,12},{9,11},{11,13},{16,18},{18,... | collective-permute-start | bytes 3145736 | tf_op jit(solution)/shard_map/ppermute | solution.py:104
  450.7 28.2 %collective-permute-start.46 = (bf16[256,2048]{1,0:T(8,128)(2,1)S(1)}, bf16[256,2048]{1,0:T(8,128)(2,1)S(1)}, u32[]{:S(2)}, u32[]{:S(2)}) collective-permute-start(bf16[256,2048]{1,0:T(8,128)(2,1)S(1)} %get-tuple-element.456), channel_id=1, source_target_pairs={{0,2},{2,4},{4,6},{1,3},{3,5},{5,7},{8,10},{10,12},{12,14},{9,11},... | collective-permute-start | bytes 3145736 | tf_op jit(solution)/shard_map/ppermute | solution.py:104
  458.4 24.7 %collective-permute-start.47 = (bf16[256,2048]{1,0:T(8,128)(2,1)S(1)}, bf16[256,2048]{1,0:T(8,128)(2,1)S(1)}, u32[]{:S(2)}, u32[]{:S(2)}) collective-permute-start(bf16[256,2048]{1,0:T(8,128)(2,1)S(1)} %get-tuple-element.455), channel_id=1, source_target_pairs={{2,0},{4,2},{6,4},{3,1},{5,3},{7,5},{10,8},{12,10},{14,12},{11,9},... | collective-permute-start | bytes 3145736 | tf_op jit(solution)/shard_map/ppermute | solution.py:104
  591.8 37.4 %collective-permute-start.62 = (bf16[256,2048]{1,0:T(8,128)(2,1)}, bf16[256,2048]{1,0:T(8,128)(2,1)}, u32[]{:S(2)}, u32[]{:S(2)}) collective-permute-start(bf16[256,2048]{1,0:T(8,128)(2,1)} %convolution_convert_fusion.17), channel_id=1, source_target_pairs={{0,1},{1,0},{2,3},{3,2},{4,5},{5,4},{6,7},{7,6},{8,9},{9,8},{10,11... | collective-permute-start | bytes 3145736 | tf_op jit(solution)/shard_map/ppermute | solution.py:61
  597.3 33.5 %collective-permute-start.60 = (bf16[256,2048]{1,0:T(8,128)(2,1)}, bf16[256,2048]{1,0:T(8,128)(2,1)}, u32[]{:S(2)}, u32[]{:S(2)}) collective-permute-start(bf16[256,2048]{1,0:T(8,128)(2,1)} %add_convert_fusion.15), channel_id=1, source_target_pairs={{0,2},{1,3},{8,10},{9,11},{16,18},{17,19},{24,26},{25,27}} | collective-permute-start | bytes 3145736 | tf_op jit(solution)/shard_map/ppermute | solution.py:104
  600.4 30.4 %collective-permute-start.61 = (bf16[256,2048]{1,0:T(8,128)(2,1)}, bf16[256,2048]{1,0:T(8,128)(2,1)}, u32[]{:S(2)}, u32[]{:S(2)}) collective-permute-start(bf16[256,2048]{1,0:T(8,128)(2,1)} %add_convert_fusion.15), channel_id=1, source_target_pairs={{6,4},{7,5},{14,12},{15,13},{22,20},{23,21},{30,28},{31,29}} | collective-permute-start | bytes 3145736 | tf_op jit(solution)/shard_map/ppermute | solution.py:104
  630.8 202.1 %reduce-scatter.7.cloned.1.call-start = ((), (), s32[]{:S(2)}) async-start(), calls=%async_computation.9 | async-start | bytes 5242880 | tf_op jit(solution)/shard_map/reduce_scatter | solution.py:663
  633.8 54.3 %collective-permute-start.68 = (bf16[256,2048]{1,0:T(8,128)(2,1)}, bf16[256,2048]{1,0:T(8,128)(2,1)}, u32[]{:S(2)}, u32[]{:S(2)}) collective-permute-start(bf16[256,2048]{1,0:T(8,128)(2,1)} %slice.220), channel_id=1, source_target_pairs={{0,1},{1,0},{2,3},{3,2},{4,5},{5,4},{6,7},{7,6},{8,9},{9,8},{10,11... | collective-permute-start | bytes 3145736 | tf_op jit(solution)/shard_map/ppermute | solution.py:61
  641.9 24.8 %collective-permute-start.63 = (bf16[256,2048]{1,0:T(8,128)(2,1)}, bf16[256,2048]{1,0:T(8,128)(2,1)}, u32[]{:S(2)}, u32[]{:S(2)}) collective-permute-start(bf16[256,2048]{1,0:T(8,128)(2,1)} %get-tuple-element.454), channel_id=1, source_target_pairs={{0,2},{2,4},{1,3},{3,5},{8,10},{10,12},{9,11},{11,13},{16,18},{18,... | collective-permute-start | bytes 3145736 | tf_op jit(solution)/shard_map/ppermute | solution.py:104
  672.1 28.5 %collective-permute-start.66 = (bf16[256,2048]{1,0:T(8,128)(2,1)}, bf16[256,2048]{1,0:T(8,128)(2,1)}, u32[]{:S(2)}, u32[]{:S(2)}) collective-permute-start(bf16[256,2048]{1,0:T(8,128)(2,1)} %get-tuple-element.452), channel_id=1, source_target_pairs={{0,2},{2,4},{4,6},{1,3},{3,5},{5,7},{8,10},{10,12},{12,14},{9,11},... | collective-permute-start | bytes 3145736 | tf_op jit(solution)/shard_map/ppermute | solution.py:104
  678.9 26.7 %collective-permute-start.67 = (bf16[256,2048]{1,0:T(8,128)(2,1)}, bf16[256,2048]{1,0:T(8,128)(2,1)}, u32[]{:S(2)}, u32[]{:S(2)}) collective-permute-start(bf16[256,2048]{1,0:T(8,128)(2,1)} %get-tuple-element.451), channel_id=1, source_target_pairs={{2,0},{4,2},{6,4},{3,1},{5,3},{7,5},{10,8},{12,10},{14,12},{11,9},... | collective-permute-start | bytes 3145736 | tf_op jit(solution)/shard_map/ppermute | solution.py:104
  690.8 169.6 %reduce-scatter.9.cloned.1.call-start = ((), (), s32[]{:S(2)}) async-start(), calls=%async_computation.10 | async-start | bytes 5242880 | tf_op jit(solution)/shard_map/reduce_scatter | solution.py:663
  763.3 35.8 %collective-permute-start.75 = (bf16[2,64,2048]{2,1,0:T(8,128)(2,1)}, bf16[2,64,2048]{2,1,0:T(8,128)(2,1)S(1)}, u32[]{:S(2)}, u32[]{:S(2)}) collective-permute-start(bf16[2,64,2048]{2,1,0:T(8,128)(2,1)} %get-tuple-element.447), channel_id=1, source_target_pairs={{0,2},{2,0},{4,6},{6,4},{1,3},{3,1},{5,7},{7,5},{8,10},{10,8},{12,... | collective-permute-start | bytes 1572872 | tf_op jit(solution)/shard_map/ppermute | solution.py:57
  768.5 38.2 %collective-permute-start.76 = (bf16[2,64,2048]{2,1,0:T(8,128)(2,1)S(1)}, bf16[2,64,2048]{2,1,0:T(8,128)(2,1)S(1)}, u32[]{:S(2)}, u32[]{:S(2)}) collective-permute-start(bf16[2,64,2048]{2,1,0:T(8,128)(2,1)S(1)} %get-tuple-element.446), channel_id=1, source_target_pairs={{0,4},{2,6},{4,0},{6,2},{1,5},{3,7},{5,1},{7,3},{8,12},{10,14},{12... | collective-permute-start | bytes 1572872 | tf_op jit(solution)/shard_map/ppermute | solution.py:57
  768.5 38.2 %collective-permute-start.77 = (bf16[2,64,2048]{2,1,0:T(8,128)(2,1)S(1)}, bf16[2,64,2048]{2,1,0:T(8,128)(2,1)S(1)}, u32[]{:S(2)}, u32[]{:S(2)}) collective-permute-start(bf16[2,64,2048]{2,1,0:T(8,128)(2,1)S(1)} %get-tuple-element.445), channel_id=1, source_target_pairs={{0,6},{2,4},{4,2},{6,0},{1,7},{3,5},{5,3},{7,1},{8,14},{10,12},{12... | collective-permute-start | bytes 1572872 | tf_op jit(solution)/shard_map/ppermute | solution.py:57
  770.9 162.6 %reduce-scatter.11.cloned.1.call-start = ((), (), s32[]{:S(2)}) async-start(), calls=%async_computation.11 | async-start | bytes 3932160 | tf_op jit(solution)/shard_map/reduce_scatter | solution.py:663
  842.9 27.8 %collective-permute-start.82 = (bf16[256,2048]{1,0:T(8,128)(2,1)}, bf16[256,2048]{1,0:T(8,128)(2,1)}, u32[]{:S(2)}, u32[]{:S(2)}) collective-permute-start(bf16[256,2048]{1,0:T(8,128)(2,1)} %add_convert_fusion.7), channel_id=1, source_target_pairs={{0,2},{1,3},{8,10},{9,11},{16,18},{17,19},{24,26},{25,27}} | collective-permute-start | bytes 3145736 | tf_op jit(solution)/shard_map/ppermute | solution.py:104
  864.7 25.5 %collective-permute-start.87 = (bf16[64,2048]{1,0:T(8,128)(2,1)S(1)}, bf16[64,2048]{1,0:T(8,128)(2,1)S(1)}, u32[]{:S(2)}, u32[]{:S(2)}) collective-permute-start(bf16[64,2048]{1,0:T(8,128)(2,1)S(1)} %get-tuple-element.465), channel_id=1, source_target_pairs={{0,6},{2,4},{4,2},{6,0},{1,7},{3,5},{5,3},{7,1},{8,14},{10,12},{12... | collective-permute-start | bytes 786440 | tf_op jit(solution)/shard_map/ppermute | solution.py:57
  915.6 27.5 %collective-permute-start.94 = (bf16[256,2048]{1,0:T(8,128)(2,1)}, bf16[256,2048]{1,0:T(8,128)(2,1)}, u32[]{:S(2)}, u32[]{:S(2)}) collective-permute-start(bf16[256,2048]{1,0:T(8,128)(2,1)} %slice.262), channel_id=1, source_target_pairs={{0,1},{1,0},{2,3},{3,2},{4,5},{5,4},{6,7},{7,6},{8,9},{9,8},{10,11... | collective-permute-start | bytes 3145736 | tf_op jit(solution)/shard_map/ppermute | solution.py:61
  937.7 31.7 %collective-permute-start.92 = (bf16[256,2048]{1,0:T(8,128)(2,1)S(1)}, bf16[256,2048]{1,0:T(8,128)(2,1)S(1)}, u32[]{:S(2)}, u32[]{:S(2)}) collective-permute-start(bf16[256,2048]{1,0:T(8,128)(2,1)S(1)} %get-tuple-element.442), channel_id=1, source_target_pairs={{0,2},{2,4},{4,6},{1,3},{3,5},{5,7},{8,10},{10,12},{12,14},{9,11},... | collective-permute-start | bytes 3145736 | tf_op jit(solution)/shard_map/ppermute | solution.py:104
  941.4 28.1 %collective-permute-start.93 = (bf16[256,2048]{1,0:T(8,128)(2,1)S(1)}, bf16[256,2048]{1,0:T(8,128)(2,1)S(1)}, u32[]{:S(2)}, u32[]{:S(2)}) collective-permute-start(bf16[256,2048]{1,0:T(8,128)(2,1)S(1)} %get-tuple-element.441), channel_id=1, source_target_pairs={{2,0},{4,2},{6,4},{3,1},{5,3},{7,5},{10,8},{12,10},{14,12},{11,9},... | collective-permute-start | bytes 3145736 | tf_op jit(solution)/shard_map/ppermute | solution.py:104
  969.6 36.7 %collective-permute-start.97 = (bf16[2,64,768]{2,1,0:T(8,128)(2,1)S(1)}, bf16[2,64,768]{2,1,0:T(8,128)(2,1)S(1)}, u32[]{:S(2)}, u32[]{:S(2)}) collective-permute-start(bf16[2,64,768]{2,1,0:T(8,128)(2,1)S(1)} %get-tuple-element.483), channel_id=1, source_target_pairs={{0,2},{2,0},{4,6},{6,4},{1,3},{3,1},{5,7},{7,5},{8,10},{10,8},{12,... | collective-permute-start | bytes 589832 | tf_op jit(solution)/shard_map/ppermute | solution.py:57
  969.7 36.7 %collective-permute-start.98 = (bf16[2,64,768]{2,1,0:T(8,128)(2,1)S(1)}, bf16[2,64,768]{2,1,0:T(8,128)(2,1)S(1)}, u32[]{:S(2)}, u32[]{:S(2)}) collective-permute-start(bf16[2,64,768]{2,1,0:T(8,128)(2,1)S(1)} %get-tuple-element.482), channel_id=1, source_target_pairs={{0,4},{2,6},{4,0},{6,2},{1,5},{3,7},{5,1},{7,3},{8,12},{10,14},{12... | collective-permute-start | bytes 589832 | tf_op jit(solution)/shard_map/ppermute | solution.py:57
  972.1 34.2 %collective-permute-start.99 = (bf16[2,64,768]{2,1,0:T(8,128)(2,1)S(1)}, bf16[2,64,768]{2,1,0:T(8,128)(2,1)S(1)}, u32[]{:S(2)}, u32[]{:S(2)}) collective-permute-start(bf16[2,64,768]{2,1,0:T(8,128)(2,1)S(1)} %get-tuple-element.481), channel_id=1, source_target_pairs={{0,6},{2,4},{4,2},{6,0},{1,7},{3,5},{5,3},{7,1},{8,14},{10,12},{12... | collective-permute-start | bytes 589832 | tf_op jit(solution)/shard_map/ppermute | solution.py:57
  (158 other events, 2050.7 us)
Sparse Core Ops, SparseCore 0:
  9.8 55.3 all-gather.4
  93.0 42.4 all-gather.6
  152.7 56.9 all-gather.8
  217.1 97.8 all-gather.10
  630.9 85.0 reduce-scatter.4
  719.2 52.6 reduce-scatter.6
  774.8 52.6 reduce-scatter.8
  891.1 42.3 reduce-scatter.10

commit v4 on v3

--- a/solution.py
+++ b/solution.py
@@ -1,3 +1,4 @@
+import functools
 import itertools
 
 import jax
@@ -111,10 +112,11 @@
             value = jnp.where(jnp.asarray(mask)[self.place], options[w], value)
         return value
 
-    def gather(self, block, work, extra=None, plan=None, late=False):
-        plan = plan or [[k] for k in range(self.count - 1)]
-        plan = plan + [[]]
-        options, results, tied, arrived, swapped = {}, [], [], [], [None]
+    def gather(self, block, work, extra=None, plan=None, swaps=None):
+        last = self.count - 1
+        plan = plan or [[k] for k in range(last)] + [[]]
+        swaps = swaps or [[k] for k in range(last + 1)]
+        options, results, tied, arrived, other = {}, [], [], [], {-1: None}
         for slot in range(self.count):
             if slot:
                 wanted = []
@@ -125,54 +127,57 @@
             else:
                 arrived.append(block)
             moved = ()
-            if slot + 1 < self.count:
+            if slot < last:
                 moved = tuple(
                     self.hop(options[(step, slot)] if slot else block, step) for step in (1, -1)
                 )
-            other = swap(arrived[slot])
-            done = [work(k, arrived[k], swapped[k]) for k in plan[slot]]
+            swapped = [swap(arrived[k]) for k in swaps[slot]]
+            done = [work(k, arrived[k], other[k - 1]) for k in plan[slot]]
             more = extra(slot, tied) if extra else ()
-            moved, other, done, more = together(moved, other, done, more)
+            moved, swapped, done, more = together(moved, swapped, done, more)
             if moved:
                 options[(1, slot + 1)], options[(-1, slot + 1)] = moved
-            swapped.append(other)
+            other.update(zip(swaps[slot], swapped))
             tied.append(more)
             results += done
-        last = self.count - 1
-        results.append(work(last, arrived[last], swapped[self.count]))
-        if not late:
-            results.append(work(self.count, None, swapped[last]))
-        else:
-            results.append(lambda gate: self.later(work, swapped[last], gate))
+        results.append(work(last, arrived[last], other[last]))
+        results.append(work(self.count, None, other[last - 1]))
         return results, tied
 
-    def later(self, work, block, gate):
-        gate, block = together(gate, block)
-        return gate, lambda: work(self.count, None, block)
-
-    def scatter(self, parts, fill=None):
+    def hop_values(self, made, far, last):
+        wanted = {}
+        for step in (1, -1):
+            wanted[step] = []
+            for i in range(self.count):
+                j = i + step * far
+                known = 0 <= j < self.count
+                wanted[step].append(int(np.argmax(self.order[i] == j)) if known else None)
+        values = []
+        for step in (1, -1):
+            value = self.choose(made, wanted[step])
+            if last[step] is not None:
+                value = value.astype(f32) + last[step].astype(f32)
+            values.append(value.astype(bf16))
+        return values
+
+    def scatter(self, parts, fill=None, plan=None):
         count = self.count
+        plan = plan or [[k] for k in range(count - 2, -1, -1)]
         made = {count - 1: parts(count - 1)}
         last = {1: None, -1: None}
         tied = []
         for slot in range(1, count):
             far = count - slot
+            values = self.hop_values(made, far, last)
             moved = []
-            for step in (1, -1):
-                wanted = []
-                for i in range(count):
-                    j = i + step * far
-                    wanted.append(int(np.argmax(self.order[i] == j)) if 0 <= j < count else None)
-                value = self.choose(made, wanted)
-                if last[step] is not None:
-                    value = value.astype(f32) + last[step].astype(f32)
+            for step, value in zip((1, -1), values):
                 keep = lambda i: 0 <= i + step * far < count
-                moved.append(self.hop(value.astype(bf16), step, keep))
-            done = parts(far - 1)
+                moved.append(self.hop(value, step, keep))
+            done = [parts(k) for k in plan[slot - 1]]
             more = fill(slot, tied) if fill else ()
             moved, done, more = together(moved, done, more)
             tied.append(more)
-            made[far - 1] = done
+            made.update(zip(plan[slot - 1], done))
             last[1], last[-1] = moved
         total = made[0].astype(f32) + last[1].astype(f32) + last[-1].astype(f32)
         return total, tied
@@ -507,7 +512,7 @@
             out_specs=part,
         ),
         out_shape=jax.ShapeDtypeStruct((count, rows, columns), bf16),
-        cost_estimate=cost(4),
+        cost_estimate=cost(1),
         name="join",
     )(lax.axis_index("c").astype(jnp.int32).reshape(1), full, got)
 
@@ -552,7 +557,7 @@
         ],
         out_specs=[row_block(width)] * 3,
         out_shape=[jax.ShapeDtypeStruct((length, width), bf16)] * 3,
-        cost_estimate=cost(6),
+        cost_estimate=cost(1),
         name="turn",
     )(projected, factors, gains, cosine, sine_part)
 
@@ -603,7 +608,7 @@
             jax.ShapeDtypeStruct((2, length), f32),
             jax.ShapeDtypeStruct((2, width), f32),
         ],
-        cost_estimate=cost(7),
+        cost_estimate=cost(1),
         name="unturn",
     )(query_grad, key_grad, projected, factors, gains, cosine, sine_part)
 
@@ -634,9 +639,157 @@
         ],
         out_specs=row_block(3 * width),
         out_shape=jax.ShapeDtypeStruct((length, 3 * width), bf16),
-        cost_estimate=cost(7),
+        cost_estimate=cost(1),
         name="finish",
     )(weighted, projected, factors, mixing, value_grad)
+
+
+UNITS = 512
+COLUMNS = 1024
+
+
+class Steps:
+    def __init__(self, units):
+        self.first, self.second = units // UNITS, D // COLUMNS
+        self.count = self.first + self.second
+
+    def unit(self, i):
+        return jnp.minimum(i, self.first - 1)
+
+    def column(self, i):
+        return jnp.maximum(i - self.first, 0)
+
+
+def feed_call(kernel, name, blocks, chip, length, specs, weights, widths, held):
+    count, piece = len(blocks), blocks[0].shape[0]
+    rows, steps = piece * count, Steps(weights[1].shape[0])
+    inputs, outputs, scratch = specs(steps, rows, chip)
+    held = list(held or ())
+    in_specs = [pl.BlockSpec((piece, D), lambda i: (0, 0))] * count + [s for s, _ in inputs]
+    first = len(in_specs)
+    part = pl.BlockSpec((piece, COLUMNS), lambda i: (0, steps.column(i)))
+    results = pl.pallas_call(
+        functools.partial(kernel, steps.first, count, len(held)),
+        grid=(steps.count,),
+        in_specs=in_specs + [pl.BlockSpec(memory_space=pl.ANY)] * len(held),
+        out_specs=outputs + [part] * count,
+        out_shape=[jax.ShapeDtypeStruct((length, w), bf16) for w in widths]
+        + [jax.ShapeDtypeStruct((piece, D), bf16)] * count,
+        scratch_shapes=[pltpu.VMEM((rows, D), bf16)]
+        + [pltpu.VMEM((rows, width), bf16) for width in scratch],
+        input_output_aliases={first + i: i for i in range(len(held))},
+        cost_estimate=cost(1),
+        compiler_params=pltpu.CompilerParams(vmem_limit_bytes=40 << 20),
+        name=name,
+    )(*blocks, *[array for _, array in inputs], *held)
+    return list(results[: len(widths)]), tuple(results[len(widths) :])
+
+
+def feed(blocks, chip, length, weights, held):
+    units = weights[1].shape[0]
+
+    def specs(steps, rows, chip):
+        by_unit = pl.BlockSpec((rows, UNITS), lambda i: (chip, steps.unit(i)))
+        inputs = [
+            (pl.BlockSpec((D, UNITS), lambda i: (0, steps.unit(i))), weights[0]),
+            (pl.BlockSpec((D, UNITS), lambda i: (0, steps.first + steps.unit(i))), weights[0]),
+            (pl.BlockSpec((units, COLUMNS), lambda i: (0, steps.column(i))), weights[1]),
+        ]
+        rows_out = pl.BlockSpec((rows, D // steps.first), lambda i: (chip, steps.unit(i)))
+        return inputs, [rows_out, by_unit, by_unit, by_unit], [units]
+
+    widths = (D, units, units, units)
+    return feed_call(feed_kernel, "feed", blocks, chip, length, specs, weights, widths, held)
+
+
+def feed_back(blocks, chip, length, gate_all, up_all, weights, held):
+    units = weights[1].shape[0]
+
+    def specs(steps, rows, chip):
+        by_unit = pl.BlockSpec((rows, UNITS), lambda i: (chip, steps.unit(i)))
+        inputs = [
+            (by_unit, gate_all),
+            (by_unit, up_all),
+            (pl.BlockSpec((UNITS, D), lambda i: (steps.unit(i), 0)), weights[1]),
+            (pl.BlockSpec((COLUMNS, 2 * units), lambda i: (steps.column(i), 0)), weights[0]),
+        ]
+        rows_out = pl.BlockSpec((rows, D // steps.first), lambda i: (chip, steps.unit(i)))
+        grads = pl.BlockSpec((rows, 2 * units // steps.second), lambda i: (chip, steps.column(i)))
+        return inputs, [rows_out, grads], [2 * units]
+
+    widths = (D, 2 * units)
+    return feed_call(
+        feed_back_kernel, "feed_back", blocks, chip, length, specs, weights, widths, held
+    )
+
+
+def chunk(step, size, offset=0):
+    return pl.ds(pl.multiple_of(step * size, size) + offset, size)
+
+
+def take_rows(block_refs, rows, rows_out):
+    step = pl.program_id(0)
+
+    @pl.when(step == 0)
+    def _():
+        piece = block_refs[0].shape[0]
+        for i, block in enumerate(block_refs):
+            rows[i * piece : (i + 1) * piece, :] = block[...]
+
+    size = rows_out.shape[1]
+    rows_out[...] = rows[:, chunk(step, size)]
+
+
+def give_parts(part, part_refs):
+    piece = part_refs[0].shape[0]
+    for i, out in enumerate(part_refs):
+        out[...] = part[i * piece : (i + 1) * piece].astype(bf16)
+
+
+def feed_kernel(first, count, held, *refs):
+    block_refs, (gate_w, up_w, down_w) = refs[:count], refs[count : count + 3]
+    outs = refs[count + 3 + held :]
+    rows_out, gate_out, up_out, hidden_out = outs[:4]
+    part_refs, (rows, all_hidden) = outs[4 : 4 + count], outs[4 + count :]
+    step = pl.program_id(0)
+
+    @pl.when(step < first)
+    def _():
+        take_rows(block_refs, rows, rows_out)
+        gate, up = product(rows[...], gate_w[...]), product(rows[...], up_w[...])
+        hidden = (gate * jax.nn.sigmoid(gate) * up).astype(bf16)
+        gate_out[...], up_out[...] = gate.astype(bf16), up.astype(bf16)
+        hidden_out[...] = hidden
+        all_hidden[:, chunk(step, UNITS)] = hidden
+
+    @pl.when(step >= first)
+    def _():
+        give_parts(product(all_hidden[...], down_w[...]), part_refs)
+
+
+def feed_back_kernel(first, count, held, *refs):
+    block_refs, (gate_in, up_in, down_w, in_w) = refs[:count], refs[count : count + 4]
+    outs = refs[count + 4 + held :]
+    rows_out, grads_out = outs[:2]
+    part_refs, (rows, grads) = outs[2 : 2 + count], outs[2 + count :]
+    units = grads.shape[1] // 2
+    step = pl.program_id(0)
+
+    @pl.when(step < first)
+    def _():
+        take_rows(block_refs, rows, rows_out)
+        hidden_grad = product_right(rows[...], down_w[...])
+        gate, up = gate_in[...].astype(f32), up_in[...].astype(f32)
+        sigmoid_gate = jax.nn.sigmoid(gate)
+        gate_grad = hidden_grad * up * sigmoid_gate * (1.0 + gate * (1.0 - sigmoid_gate))
+        grads[:, chunk(step, UNITS)] = gate_grad.astype(bf16)
+        grads[:, chunk(step, UNITS, units)] = (hidden_grad * gate * sigmoid_gate).astype(bf16)
+
+    @pl.when(step >= first)
+    def _():
+        size = grads_out.shape[1]
+        grads_out[...] = grads[:, chunk(step - first, size)]
+        give_parts(product_right(grads[...], in_w[...]), part_refs)
 
 
 def norm_forward(values, gain_row):
@@ -682,10 +835,12 @@
     lows = starts[::BLOCK_Q] // BLOCK_K
     starts_row = starts.reshape(1, length)
     inverse = rope_base ** (-2.0 * jnp.arange(HEAD_DIM // 2, dtype=f32) / HEAD_DIM)
-    angles = offset[:, None] * inverse[None, :]
-    cosine, sine_part = jnp.cos(angles), jnp.sin(angles)
-    cosine = jnp.concatenate([cosine, cosine], axis=1)
-    sine_part = jnp.concatenate([-sine_part, sine_part], axis=1)
+
+    def tables(offset):
+        angles = offset[:, None] * inverse[None, :]
+        cosine, sine_part = jnp.cos(angles), jnp.sin(angles)
+        cosine = jnp.concatenate([cosine, cosine], axis=1)
+        return cosine, jnp.concatenate([-sine_part, sine_part], axis=1)
 
     own_input = hidden_in.reshape(piece_len, model_width)
 
@@ -709,20 +864,24 @@
         if slot == 0:
             blocks = spread(qkv_weight, 3, owners)
             blocks = exchange_cores(blocks.reshape(line, 2, row_count, 3 * width))
-            return (blocks, in_weight)
+            return (blocks, in_weight, offset)
         if slot == 1:
             down = lax.all_gather(down_weight, DATA, axis=0, tiled=True)
             blocks = spread(tied[0][1], 2 * data_count, owners)
-            in_cores = cores_start(blocks.reshape((line, 2) + blocks.shape[1:]))
-            return (exchange_chips(tied[0][0], LINE), down, in_cores)
+            return (chips_start(tied[0][0], LINE), down, blocks, tables(tied[0][2]))
+        if slot == 2:
+            return cores_start(tied[1][2].reshape((line, 2) + tied[1][2].shape[1:]))
         if slot == line - 1:
-            return (out_weight, tied[1][2])
+            return (out_weight, tied[2])
         return ()
 
-    _, tied = row.gather(own_input, keep_input, weights_step)
+    plan = [[0], [1], []] + [[slot - 1] for slot in range(3, line)]
+    swaps = [[0], [], [1, 2]] + [[k] for k in range(3, line)]
+    _, tied = row.gather(own_input, keep_input, weights_step, plan, swaps)
     full_input = buffer[0].reshape(length, model_width)
-    qkv_here = lax.all_gather(tied[1][0].reshape(-1, 3 * width), DATA, axis=0, tiled=True)
-    down_here = tied[1][1]
+    qkv_rows = by_source(tied[1][0], LINE).reshape(-1, 3 * width)
+    qkv_here = lax.all_gather(qkv_rows, DATA, axis=0, tiled=True)
+    down_here, (cosine, sine_part) = tied[1][1], tied[1][3]
     units = down_here.shape[0]
     out_shuffled, (in_keep, in_got) = tied[line - 1]
     out_pieces = shifts(lambda steps: out_shuffled, LINE)
@@ -737,15 +896,16 @@
     query_low, key_low, value_low = turn(projected, factors, gains_here, cosine, sine_part)
     head_out, log_total = attend(lows, starts_row, query_low, key_low, value_low)
 
-    head_out, in_pieces, out_half = together(head_out, in_pieces, out_half)
     blocks = head_out.astype(bf16).reshape(line, 2, piece_len, width)
     keep, got = cores_start(blocks)
+    got, in_pieces, out_half = together(got, in_pieces, out_half)
     out_half = out_half.reshape(-1, out_weight.shape[0], D)
     out_other = swap(out_half)
     in_rows = by_source(in_pieces, LINE)
     in_here = lax.all_gather(in_rows.reshape(-1, in_rows.shape[-1]), DATA, axis=0, tiled=True)
-    attended = exchange_chips(by_core(keep, got), LINE)
     out_full = by_core(out_half, out_other).reshape(D, D)
+    pieces, out_full = together(chips_start(by_core(keep, got), LINE), out_full)
+    attended = by_source(pieces, LINE)
     attended_low = attended.reshape(line * 2, piece_len, width).transpose(1, 0, 2)
     attended_low = attended_low.reshape(piece_len, D)
     branch = product(attended_low, out_full)
@@ -753,43 +913,32 @@
     residual = own_input.astype(f32) + branch_normed
     residual_low = residual.astype(bf16)
 
-    def rows_of(same, other):
-        return jnp.concatenate([b for b in (same, other) if b is not None], axis=0)
-
     def chip_sums(results):
         def parts(k):
-            same = results[k][-1][:piece_len]
             if k == line - 1:
-                got = swap(results[k][-1][piece_len:])
-                if callable(results[line]):
-                    got, results[line] = results[line](got)
-                return (same.astype(f32) + got.astype(f32)).astype(bf16)
-            if k == line - 2 and callable(results[line]):
-                results[line] = results[line]()
-            return scatter_sum(same, results[line if k == line - 2 else k + 1][-1][-piece_len:])
+                other = results[k][1]
+            else:
+                other = results[line][0] if k == line - 2 else results[k + 1][1]
+            return scatter_sum(results[k][0], other)
 
         return parts
 
+    def window_of(k):
+        return 2 * line - 2 if k == 0 else 2 * line - 1 if k == line else k - 1
+
+    held = {}
+
     def forward_chip(k, same, other):
-        rows = rows_of(same, other)
-        gate_up = product(rows, in_here)
-        gate_part, up_part = gate_up[:, :units], gate_up[:, units:]
-        hidden = (gate_part * jax.nn.sigmoid(gate_part) * up_part).astype(bf16)
-        return rows, gate_up.astype(bf16), hidden, product(hidden, down_here).astype(bf16)
-
-    plan = [[], [0], [1, 2]] + [[k] for k in range(3, line - 1)]
+        blocks = [b for b in (same, other) if b is not None]
+        held["forward"], parts = feed(
+            blocks, window_of(k), length, (in_here, down_here), held.get("forward")
+        )
+        return parts
+
+    plan = [[], [0], [1, 2]] + [[k] for k in range(3, line - 1)] + [[]]
     forward, _ = row.gather(residual_low, forward_chip, plan=plan)
-    def join_rows(slot, tied):
-        if slot == 1:
-            return ([f[0] for f in forward], [f[2] for f in forward])
-        if slot == 2:
-            return (jnp.concatenate(tied[0][0], axis=0), tied[0][1])
-        if slot == 3:
-            return (jnp.concatenate(tied[1][1], axis=0),)
-        return ()
-
-    second, tied = row.scatter(chip_sums(forward), join_rows)
-    residual_all, hidden_all = tied[1][0], tied[2][0]
+    residual_all, gate_all, up_all, hidden_all = held["forward"]
+    second, _ = row.scatter(chip_sums(forward))
     second_normed, second_factor = norm_forward(second, norm_gains[3])
     result = residual + second_normed
     live_places = ctx_place * piece_len + jnp.arange(piece_len, dtype=jnp.int32)
@@ -806,25 +955,20 @@
     second_grad, second_gain_grad = norm_backward(second, second_factor, norm_gains[3], incoming)
 
     def backward_chip(k, same, other):
-        rows = rows_of(same, other)
-        gate_up = forward[k][1].astype(f32)
-        hidden_grad = product_right(rows, down_here)
-        gate_part, up_part = gate_up[:, :units], gate_up[:, units:]
-        sigmoid_gate = jax.nn.sigmoid(gate_part)
-        gate_grad = hidden_grad * up_part * sigmoid_gate * (1.0 + gate_part * (1.0 - sigmoid_gate))
-        up_grad = hidden_grad * gate_part * sigmoid_gate
-        gate_up_low = jnp.concatenate([gate_grad, up_grad], axis=1).astype(bf16)
-        return rows, gate_up_low, product_right(gate_up_low, in_here).astype(bf16)
+        blocks = [b for b in (same, other) if b is not None]
+        held["backward"], parts = feed_back(
+            blocks, window_of(k), length, gate_all, up_all, (in_here, down_here),
+            held.get("backward"),
+        )
+        return parts
 
     backward, _ = row.gather(second_grad.astype(bf16), backward_chip)
+    second_grad_all, gate_up_grads = held["backward"]
 
     def weight_grads(slot, tied):
         if slot == 1:
-            gate_up_all = jnp.concatenate([b[1] for b in backward], axis=0)
-            grads = product_left(residual_all, gate_up_all).astype(bf16)
-            return (grads, [b[0] for b in backward])
+            return (product_left(residual_all, gate_up_grads).astype(bf16),)
         if slot == 2:
-            second_grad_all = jnp.concatenate(tied[0][1], axis=0)
             return (product_left(hidden_all, second_grad_all).astype(bf16),)
         return ()
 
@@ -832,7 +976,6 @@
     grad_in, grad_down = tied[0][0], tied[1][0]
     residual_grad = incoming + residual_part
     grad_in = scatter_over(grad_in, DATA).reshape(in_rows.shape)
-    grad_down = scatter_over(grad_down, DATA)
 
     branch_grad, branch_gain_grad = norm_backward(
         branch, branch_factor, norm_gains[2], residual_grad
@@ -862,10 +1005,11 @@
     weighted, mixing, gain_grads = unturn(
         query_grad, key_grad, projected, factors, gains_here, cosine, sine_part
     )
-    mixing, in_pieces = together(mixing, in_pieces)
+    mixing, in_pieces, grad_down = together(mixing, in_pieces, grad_down)
+    grad_down = scatter_over(grad_down, DATA)
     mixing = small_sum(mixing, CTX) / D
     projected_grad = finish(weighted, projected, factors, mixing, value_grad)
-    projected_grad, grad_down = together(projected_grad, grad_down)
+    projected_grad, out_pieces = together(projected_grad, chips_start(out_grad, LINE))
     grad_blocks = projected_grad.reshape(line, 2, piece_len, 3 * width)
 
     later = []
@@ -887,31 +1031,29 @@
 
     def last_grads(slot, tied):
         if slot == 1:
-            grads = product_left(full_input, later[1]).astype(bf16)
-            return (grads, gain_grads, chips_start(out_grad, LINE))
+            return (product_left(full_input, later[1]).astype(bf16), gain_grads)
         if slot == 2:
             rows = jnp.zeros((5, D), f32)
             rows = lax.dynamic_update_slice(rows, tied[0][1], (0, ctx_place * width))
             rows = rows.at[2].set(branch_gain_grad).at[3].set(second_gain_grad)
             rows = rows.at[4, :3].set(sums)
-            return (scatter_over(tied[0][0], DATA), step(rows, "c"))
+            return (scatter_over(tied[0][0], DATA), step(rows, "c"), grad_down)
         if slot == line - 1:
             blocks = tied[1][0].reshape(line, 2, row_count, 3 * width)
-            rows = step(sum(tied[1][1]), "zl")
-            return (cores_start(blocks), rows, in_pieces, grad_down)
+            return (cores_start(blocks), step(sum(tied[1][1]), "zl"), in_pieces, tied[1][2])
         return ()
 
-    input_part, tied = row.scatter(input_chip, last_grads)
+    plan = [[line - 2, line - 3]] + [[k] for k in range(line - 4, -1, -1)] + [[]]
+    input_part, tied = row.scatter(input_chip, last_grads, plan)
     qkv_cores, gain_rows, in_pieces, grad_down = tied[line - 2]
-    out_pieces = tied[0][2]
     qkv_pieces = chips_start(by_core(*qkv_cores), LINE)
-    gain_rows = small_sum(sum(gain_rows), ("zh", "dl", "dh"))
+    gain_rows, qkv_pieces = together(step(sum(gain_rows), "zh"), qkv_pieces)
+    gain_rows = small_sum(sum(gain_rows), ("dl", "dh"))
     input_grad = residual_grad + input_part
     grad_in = by_source(in_pieces, LINE)
     grad_in = collect(grad_in.reshape((owners,) + grad_in.shape[2:]), 2 * data_count)
     grad_down = grad_down.astype(f32)
     grad_out = sum(piece.astype(f32) for piece in out_pieces)
-    qkv_pieces, grad_in, grad_down = together(qkv_pieces, grad_in, grad_down)
     grad_qkv = by_source(qkv_pieces, LINE)
     grad_qkv = collect(grad_qkv.reshape(owners, row_count, 3 * width), 3)
     live_count = jnp.sum(seq_lengths).astype(f32)

time: 1030 us -> 1010 us (0.981)
  Pallas kernels: 98.7 us -> 208 us
  matrix products: 167 us -> 68.5 us
  local copies, waits for them, and re-layouts: 85.7 us -> 60.6 us
  other arithmetic: 129 us -> 107 us
  waiting for transfers between devices: 333 us -> 344 us
    pallas_call x0 -> x10, Pallas kernels: none -> 113 us  [feed_call(): pl.pallas_call(functools.partial(kernel, steps.first, count, len(held)),...]
    dot_general x15 -> x5, matrix products: 64.5 us -> 11.8 us  [product_right(): lax.dot_general(left_side, right_side, (((1,), (1,)), ((), ())), preferre...]
    dot_general x11 -> x1, matrix products: 51.9 us -> 6.21 us  [product(): return jnp.dot(left_side, right_side, preferred_element_type=f32)]
    ppermute x36, waiting for transfers between devices: 172 us -> 215 us  [hop(): return lax.ppermute(value, self.axes, pairs)]
    ppermute x24, waiting for transfers between devices: 102 us -> 66.3 us  [shift(): return lax.ppermute(value, axes, pairs)]
    unnamed x207 -> x152, local copies, waits for them, and re-layouts: 41.7 us -> 20.6 us
    ppermute x9 -> x8, waiting for transfers between devices: 21.6 us -> 7.43 us  [small_sum(): value = value + lax.ppermute(value, axis, [(0, 1), (1, 0)])]
    all_gather x1, waiting for transfers between devices: 3.31 us -> 14.2 us  [on_device(): lax.all_gather(in_rows.reshape(-1, in_rows.shape[-1]), DATA, axis=0, tile...]
  transfers between devices with their start and end apart: 111 -> 111, of which waited for: 49 -> 47; matrix products, arithmetic and copies ran while one was open for 31% -> 19% of each run, Pallas kernels for 9% -> 17%
where the time goes in v4:
time: 1010 us; the launch traced here: 999 us
  waiting for transfers between devices  344 us (34%)
  Pallas kernels  208 us (21%)
  starting transfers between devices  189 us (19%)
  other arithmetic  107 us (11%)
  matrix products  68.5 us (7%)
  local copies, waits for them, and re-layouts  60.6 us (6%)
  between operations  22.7 us (2%)
    ppermute x36, waiting for transfers between devices, hop(): return lax.ppermute(value, self.axes, pairs)  215 us
    pallas_call x10, Pallas kernels, feed_call(): pl.pallas_call(functools.partial(kernel, steps.first, count, len(held)),...  113 us
    ppermute x36, starting transfers between devices, hop(): return lax.ppermute(value, self.axes, pairs)  107 us
    ppermute x24, waiting for transfers between devices, shift(): return lax.ppermute(value, axes, pairs)  66.3 us
    dot_general x4, matrix products, product_left(): lax.dot_general(left_side, right_side, (((0,), (0,)), ((), ())), preferre...  50.5 us
    ppermute x24, starting transfers between devices, shift(): return lax.ppermute(value, axes, pairs)  47.3 us
    convert_element_type x6, other arithmetic, hop_values(): values.append(value.astype(bf16))  26.3 us
    ppermute x8, starting transfers between devices, small_sum(): value = value + lax.ppermute(value, axis, [(0, 1), (1, 0)])  24.1 us
  transfers between devices with their start and end apart: 111, of which 47 were waited for; matrix products, arithmetic and copies ran while one was open for 19% of the time, Pallas kernels for 17%

profile of v4, /device:TPU:0, one launch (start us, length us, event | category | flops | bytes accessed | tf_op | source)
XLA Modules:
  0.0 998.8 jit_solution(12002548261674167274)
XLA Ops:
  65.1 10.1 %collective-permute-done.4 = bf16[256,2048]{1,0:T(8,128)(2,1)} collective-permute-done((bf16[256,2048]{1,0:T(8,128)(2,1)S(1)}, bf16[256,2048]{1,0:T(8,128)(2,1)}, u32[]{:S(2)}, u32[]{:S(2)}) %collective-permute-start.4) | collective-permute-done | bytes 1048608 | tf_op jit(solution)/shard_map/ppermute | solution.py:105
  87.0 8.2 collective-permute-start.9
  97.7 18.2 %collective-permute-done.10 = bf16[256,2048]{1,0:T(8,128)(2,1)} collective-permute-done((bf16[256,2048]{1,0:T(8,128)(2,1)}, bf16[256,2048]{1,0:T(8,128)(2,1)}, u32[]{:S(2)}, u32[]{:S(2)}) %collective-permute-start.10) | collective-permute-done | bytes 1048608 | tf_op jit(solution)/shard_map/ppermute | solution.py:105
  138.9 10.3 %project.1 = (f32[2048,768]{1,0:T(8,128)S(1)}, f32[2,2048]{1,0:T(2,128)S(1)}) custom-call(bf16[2048,2048]{1,0:T(8,128)(2,1)} %bitcast.34.in_ref, bf16[2048,768]{1,0:T(8,128)(2,1)S(1)} %copy-done.5), custom_call_target="tpu_custom_call" | custom-call | flops 10000000000 | bytes 30000000 | tf_op jit(solution)/shard_map/project/pallas_call | solution.py:480
  154.5 6.3 collective-permute-start.18
  172.7 6.4 turn.1
  182.7 12.2 %attend.1 = (f32[2048,256]{1,0:T(8,128)S(1)}, f32[2,1,2048]{2,1,0:T(1,128)S(1)}) custom-call(s32[4]{0:T(128)S(1)} %and_select_fusion.low_ref, s32[1,2048]{1,0:T(1,128)S(1)} %bitcast.208, bf16[2048,256]{1,0:T(8,128)(2,1)S(1)} %copy-done.7, bf16[2048,256]{1,0:T(8,128)(2,1)S(1)} %copy-done.8, bf16[2048,256]{1,0:T(8,128)(2,1)S(1)} %copy-done.9), custom_call_target="tpu_custom_call" | custom-call | flops 16000000000 | bytes 48000000 | tf_op jit(solution)/shard_map/attend/pallas_call | solution.py:322
  196.3 11.8 %collective-permute-done.23.refs_3_ = bf16[2,64,2048]{2,1,0:T(8,128)(2,1)S(1)} collective-permute-done((bf16[2,64,2048]{2,1,0:T(8,128)(2,1)}, bf16[2,64,2048]{2,1,0:T(8,128)(2,1)S(1)}, u32[]{:S(2)}, u32[]{:S(2)}) %collective-permute-start.23) | collective-permute-done | bytes 524320 | tf_op jit(solution)/shard_map/ppermute | solution.py:58
  213.9 8.3 collective-permute-start.25
  224.7 6.7 bitcast_select_fusion
  234.3 9.2 collective-permute-done.26.refs_3_
  252.4 8.3 collective-permute-start.29
  262.1 19.7 %collective-permute-done.29 = bf16[256,2048]{1,0:T(8,128)(2,1)} collective-permute-done((bf16[256,2048]{1,0:T(8,128)(2,1)S(1)}, bf16[256,2048]{1,0:T(8,128)(2,1)}, u32[]{:S(2)}, u32[]{:S(2)}) %collective-permute-start.29) | collective-permute-done | bytes 1048608 | tf_op jit(solution)/shard_map/ppermute | solution.py:105
  293.7 14.2 %all-gather.11.cloned.1.call-done.refs_1_.refs_2_.refs_3_.refs_4_.refs_5_ = bf16[2048,2048]{1,0:T(8,128)(2,1)} async-done(((bf16[512,2048]{1,0:T(8,128)(2,1)}), bf16[2048,2048]{1,0:T(8,128)(2,1)}) %all-gather.11.cloned.1.call-update) | async-done | bytes 8388624 | tf_op jit(solution)/shard_map/all_gather | solution.py:905
  307.9 8.9 feed.5
  326.6 12.1 %feed.6 = (bf16[2048,2048]{1,0:T(8,128)(2,1)}, bf16[2048,1024]{1,0:T(8,128)(2,1)S(1)}, bf16[2048,1024]{1,0:T(8,128)(2,1)S(1)}, bf16[2048,1024]{1,0:T(8,128)(2,1)...) custom-call(bf16[256,2048]{1,0:T(8,128)(2,1)S(1)} %broadcast_select_, ...), custom_call_target="tpu_custom_call", output_to_operand_aliasing={{0}: (5, {}), {1}: (6, {}), {2}: (7, {}), {3}: (8, {})} | custom-call | flops 1000000000 | bytes 3000000 | tf_op jit(solution)/shard_map/feed/pallas_call | solution.py:671
  338.6 12.9 %feed.7 = (bf16[2048,2048]{1,0:T(8,128)(2,1)}, bf16[2048,1024]{1,0:T(8,128)(2,1)S(1)}, bf16[2048,1024]{1,0:T(8,128)(2,1)S(1)}, bf16[2048,1024]{1,0:T(8,128)(2,1)...) custom-call(bf16[256,2048]{1,0:T(8,128)(2,1)S(1)} %select_select_fus, ...), custom_call_target="tpu_custom_call", output_to_operand_aliasing={{0}: (5, {}), {1}: (6, {}), {2}: (7, {}), {3}: (8, {})} | custom-call | flops 1000000000 | bytes 3000000 | tf_op jit(solution)/shard_map/feed/pallas_call | solution.py:671
  357.2 12.0 %feed.8 = (bf16[2048,2048]{1,0:T(8,128)(2,1)}, bf16[2048,1024]{1,0:T(8,128)(2,1)S(1)}, bf16[2048,1024]{1,0:T(8,128)(2,1)S(1)}, bf16[2048,1024]{1,0:T(8,128)(2,1)...) custom-call(bf16[256,2048]{1,0:T(8,128)(2,1)S(1)} %select_select_fus, ...), custom_call_target="tpu_custom_call", output_to_operand_aliasing={{0}: (5, {}), {1}: (6, {}), {2}: (7, {}), {3}: (8, {})} | custom-call | flops 1000000000 | bytes 3000000 | tf_op jit(solution)/shard_map/feed/pallas_call | solution.py:671
  369.4 8.9 feed.9
  386.1 20.7 %collective-permute-done.40 = bf16[256,2048]{1,0:T(8,128)(2,1)S(1)} collective-permute-done((bf16[256,2048]{1,0:T(8,128)(2,1)S(1)}, bf16[256,2048]{1,0:T(8,128)(2,1)S(1)}, u32[]{:S(2)}, u32[]{:S(2)}) %collective-permute-start.40) | collective-permute-done | bytes 1048608 | tf_op jit(solution)/shard_map/ppermute | solution.py:105
  414.6 20.6 %collective-permute-done.43 = bf16[256,2048]{1,0:T(8,128)(2,1)S(1)} collective-permute-done((bf16[256,2048]{1,0:T(8,128)(2,1)S(1)}, bf16[256,2048]{1,0:T(8,128)(2,1)S(1)}, u32[]{:S(2)}, u32[]{:S(2)}) %collective-permute-start.43) | collective-permute-done | bytes 1048608 | tf_op jit(solution)/shard_map/ppermute | solution.py:105
  437.3 7.7 collective-permute-start.46
  447.3 18.2 %collective-permute-done.46 = bf16[256,2048]{1,0:T(8,128)(2,1)S(1)} collective-permute-done((bf16[256,2048]{1,0:T(8,128)(2,1)S(1)}, bf16[256,2048]{1,0:T(8,128)(2,1)S(1)}, u32[]{:S(2)}, u32[]{:S(2)}) %collective-permute-start.46) | collective-permute-done | bytes 1048608 | tf_op jit(solution)/shard_map/ppermute | solution.py:105
  476.7 9.4 feed_back.5
  486.1 8.9 collective-permute-done.49
  503.4 12.9 %feed_back.6 = (bf16[2048,2048]{1,0:T(8,128)(2,1)}, bf16[2048,2048]{1,0:T(8,128)(2,1)}, bf16[256,2048]{1,0:T(8,128)(2,1)S(1)}, bf16[256,2048]{1,0:T(8,128)(2,1)S(1)}) custom-call(bf16[256,2048]{1,0:T(8,128)(2,1)S(1)} %broadcast_select_fusion.4.refs_0_, ...), custom_call_target="tpu_custom_call", output_to_operand_aliasing={{0}: (6, {}), {1}: (7, {})} | custom-call | flops 1000000000 | bytes 3000000 | tf_op jit(solution)/shard_map/feed_back/pallas_call | solution.py:671
  516.3 8.8 collective-permute-done.52
  535.2 12.9 %feed_back.7 = (bf16[2048,2048]{1,0:T(8,128)(2,1)}, bf16[2048,2048]{1,0:T(8,128)(2,1)}, bf16[256,2048]{1,0:T(8,128)(2,1)S(1)}, bf16[256,2048]{1,0:T(8,128)(2,1)S(1)}) custom-call(bf16[256,2048]{1,0:T(8,128)(2,1)S(1)} %select_select_fusion.1.refs_0_, ...), custom_call_target="tpu_custom_call", output_to_operand_aliasing={{0}: (6, {}), {1}: (7, {})} | custom-call | flops 1000000000 | bytes 3000000 | tf_op jit(solution)/shard_map/feed_back/pallas_call | solution.py:671
  549.1 7.6 collective-permute-done.55
  565.7 12.8 %feed_back.8 = (bf16[2048,2048]{1,0:T(8,128)(2,1)}, bf16[2048,2048]{1,0:T(8,128)(2,1)}, bf16[256,2048]{1,0:T(8,128)(2,1)S(1)}, bf16[256,2048]{1,0:T(8,128)(2,1)S(1)}) custom-call(bf16[256,2048]{1,0:T(8,128)(2,1)S(1)} %select_select_fusion.refs_0_, ...), custom_call_target="tpu_custom_call", output_to_operand_aliasing={{0}: (6, {}), {1}: (7, {})} | custom-call | flops 1000000000 | bytes 3000000 | tf_op jit(solution)/shard_map/feed_back/pallas_call | solution.py:671
  578.7 9.8 feed_back.9
  596.7 21.3 %convolution_convert_fusion.1 = bf16[2048,2048]{1,0:T(8,128)(2,1)} fusion(bf16[2048,2048]{1,0:T(8,128)(2,1)S(1)} %bitcast.214, bf16[2048,2048]{1,0:T(8,128)(2,1)} %get-tuple-element.375), kind=kOutput, calls=%fused_computation.2 | convolution fusion | flops 17184063488 | bytes 25165824 | tf_op jit(solution)/shard_map/dot_general | solution.py:266
  622.3 6.3 add_convert_fusion.12
  632.6 13.1 %convolution_convert_fusion.2 = bf16[1024,2048]{1,0:T(8,128)(2,1)} fusion(bf16[2048,1024]{1,0:T(8,128)(2,1)S(1)} %copy-done.19, bf16[2048,2048]{1,0:T(8,128)(2,1)} %get-tuple-element.382), kind=kOutput, calls=%fused_computation.4 | convolution fusion | flops 8592031744 | bytes 16777216 | tf_op jit(solution)/shard_map/dot_general | solution.py:266
  666.6 18.0 %collective-permute-done.66 = bf16[256,2048]{1,0:T(8,128)(2,1)S(1)} collective-permute-done((bf16[256,2048]{1,0:T(8,128)(2,1)S(1)}, bf16[256,2048]{1,0:T(8,128)(2,1)S(1)}, u32[]{:S(2)}, u32[]{:S(2)}) %collective-permute-start.66) | collective-permute-done | bytes 1048608 | tf_op jit(solution)/shard_map/ppermute | solution.py:105
  715.2 8.4 collective-permute-done.70.refs_2_
  723.7 10.1 %collective-permute-done.71.refs_3_ = bf16[2,256,256]{2,1,0:T(8,128)(2,1)S(1)} collective-permute-done((bf16[2,256,256]{2,1,0:T(8,128)(2,1)S(1)}, bf16[2,256,256]{2,1,0:T(8,128)(2,1)S(1)}, u32[]{:S(2)}, u32[]{:S(2)}) %collective-permute-start.71) | collective-permute-done | bytes 262176 | tf_op jit(solution)/shard_map/ppermute | solution.py:58
  754.0 18.3 %attend_back.1 = (f32[2048,256]{1,0:T(8,128)}, f32[2048,256]{1,0:T(8,128)}, f32[2048,256]{1,0:T(8,128)}) custom-call(s32[4]{0:T(128)} %copy-done.17, s32[1,2048]{1,0:T(1,128)} %bitcast.209, bf16[2048,256]{1,0:T(8,128)(2,1)} %get-tuple-element.277.q_ref, bf16[2048,256]{1,0:T(8,128)(2,1)} %get-tuple-element.278.k_ref, ...), custom_call_target="tpu_custom_call" | custom-call | flops 25999998976 | bytes 78000000 | tf_op jit(solution)/shard_map/attend_back/pallas_call | solution.py:388
  772.3 7.4 unturn.1
  779.7 10.2 %collective-permute-done.76.refs_3_ = bf16[2,64,2048]{2,1,0:T(8,128)(2,1)S(1)} collective-permute-done((bf16[2,64,2048]{2,1,0:T(8,128)(2,1)S(1)}, bf16[2,64,2048]{2,1,0:T(8,128)(2,1)S(1)}, u32[]{:S(2)}, u32[]{:S(2)}) %collective-permute-start.76) | collective-permute-done | bytes 524320 | tf_op jit(solution)/shard_map/ppermute | solution.py:58
  790.6 9.5 collective-permute-start.78
  813.4 7.4 finish.1
  821.4 10.3 %collective-permute-done.82 = bf16[64,2048]{1,0:T(8,128)(2,1)} collective-permute-done((bf16[64,2048]{1,0:T(8,128)(2,1)S(1)}, bf16[64,2048]{1,0:T(8,128)(2,1)}, u32[]{:S(2)}, u32[]{:S(2)}) %collective-permute-start.82) | collective-permute-done | bytes 262176 | tf_op jit(solution)/shard_map/ppermute | solution.py:58
  845.2 8.3 collective-permute-start.85
  855.5 10.5 %convolution_convert_fusion.3 = bf16[2048,768]{1,0:T(8,128)(2,1)} fusion(bf16[2048,2048]{1,0:T(8,128)(2,1)} %bitcast.34.in_ref, bf16[2048,768]{1,0:T(8,128)(2,1)S(1)} %copy-done.28), kind=kOutput, calls=%fused_computation.5 | convolution fusion | flops 6444023808 | bytes 14680064 | tf_op jit(solution)/shard_map/dot_general | solution.py:266
  899.4 14.7 %collective-permute-done.89 = bf16[256,2048]{1,0:T(8,128)(2,1)} collective-permute-done((bf16[256,2048]{1,0:T(8,128)(2,1)}, bf16[256,2048]{1,0:T(8,128)(2,1)}, u32[]{:S(2)}, u32[]{:S(2)}) %collective-permute-start.89) | collective-permute-done | bytes 1048608 | tf_op jit(solution)/shard_map/ppermute | solution.py:105
  914.1 6.8 reduce-scatter.9.cloned.1.call-done
  938.4 19.4 %collective-permute-done.96 = f32[5,2048]{1,0:T(8,128)S(1)} collective-permute-done((f32[5,2048]{1,0:T(8,128)S(1)}, f32[5,2048]{1,0:T(8,128)S(1)}, u32[]{:S(2)}, u32[]{:S(2)}) %collective-permute-start.96) | collective-permute-done | bytes 40992 | tf_op jit(solution)/shard_map/ppermute | solution.py:1029
  (493 shorter events, 421.3 us)
Async XLA Ops:
  7.2 70.2 %all-gather.5.cloned.1.call-start = ((), (), s32[]{:S(2)}) async-start(), calls=%async_computation.4 | async-start | bytes 5242880 | tf_op jit(solution)/shard_map/all_gather | solution.py:869
  7.9 129.1 %all-gather.7.cloned.1.call-start = ((), (), s32[]{:S(2)}) async-start(), calls=%async_computation.5 | async-start | bytes 3932160 | tf_op jit(solution)/shard_map/all_gather | solution.py:883
  7.9 27.7 %collective-permute-start = (bf16[256,2048]{1,0:T(8,128)(2,1)}, bf16[256,2048]{1,0:T(8,128)(2,1)S(1)}, u32[]{:S(2)}, u32[]{:S(2)}) collective-permute-start(bf16[256,2048]{1,0:T(8,128)(2,1)} %bitcast.223), channel_id=1, source_target_pairs={{0,2},{2,4},{4,6},{1,3},{3,5},{5,7},{8,10},{10,12},{12,14},{9,11},... | collective-permute-start | bytes 3145736 | tf_op jit(solution)/shard_map/ppermute | solution.py:105
  13.0 26.7 %collective-permute-start.1 = (bf16[256,2048]{1,0:T(8,128)(2,1)}, bf16[256,2048]{1,0:T(8,128)(2,1)S(1)}, u32[]{:S(2)}, u32[]{:S(2)}) collective-permute-start(bf16[256,2048]{1,0:T(8,128)(2,1)} %bitcast.224), channel_id=1, source_target_pairs={{2,0},{4,2},{6,4},{3,1},{5,3},{7,5},{10,8},{12,10},{14,12},{11,9},... | collective-permute-start | bytes 3145736 | tf_op jit(solution)/shard_map/ppermute | solution.py:105
  14.3 25.4 %collective-permute-start.2 = (bf16[256,2048]{1,0:T(8,128)(2,1)}, bf16[256,2048]{1,0:T(8,128)(2,1)}, u32[]{:S(2)}, u32[]{:S(2)}) collective-permute-start(bf16[256,2048]{1,0:T(8,128)(2,1)} %bitcast.225), channel_id=1, source_target_pairs={{0,1},{1,0},{2,3},{3,2},{4,5},{5,4},{6,7},{7,6},{8,9},{9,8},{10,11... | collective-permute-start | bytes 3145736 | tf_op jit(solution)/shard_map/ppermute | solution.py:62
  44.2 31.0 %collective-permute-start.4 = (bf16[256,2048]{1,0:T(8,128)(2,1)S(1)}, bf16[256,2048]{1,0:T(8,128)(2,1)}, u32[]{:S(2)}, u32[]{:S(2)}) collective-permute-start(bf16[256,2048]{1,0:T(8,128)(2,1)S(1)} %collective-permute-done), channel_id=1, source_target_pairs={{0,2},{2,4},{4,6},{1,3},{3,5},{5,7},{8,10},{10,12},{12,14},{9,11},... | collective-permute-start | bytes 3145736 | tf_op jit(solution)/shard_map/ppermute | solution.py:105
  47.7 29.6 %collective-permute-start.5 = (bf16[256,2048]{1,0:T(8,128)(2,1)S(1)}, bf16[256,2048]{1,0:T(8,128)(2,1)}, u32[]{:S(2)}, u32[]{:S(2)}) collective-permute-start(bf16[256,2048]{1,0:T(8,128)(2,1)S(1)} %collective-permute-done.1), channel_id=1, source_target_pairs={{2,0},{4,2},{6,4},{3,1},{5,3},{7,5},{10,8},{12,10},{14,12},{11,9},... | collective-permute-start | bytes 3145736 | tf_op jit(solution)/shard_map/ppermute | solution.py:105
  65.1 32.6 %collective-permute-start.11 = (bf16[256,2048]{1,0:T(8,128)(2,1)}, bf16[256,2048]{1,0:T(8,128)(2,1)}, u32[]{:S(2)}, u32[]{:S(2)}) collective-permute-start(bf16[256,2048]{1,0:T(8,128)(2,1)} %get-tuple-element.472), channel_id=1, source_target_pairs={{0,1},{1,0},{2,3},{3,2},{4,5},{5,4},{6,7},{7,6},{8,9},{9,8},{10,11... | collective-permute-start | bytes 3145736 | tf_op jit(solution)/shard_map/ppermute | solution.py:62
  79.4 131.5 %all-gather.9.cloned.1.call-start = ((), (), s32[]{:S(2)}) async-start(), calls=%async_computation.6 | async-start | bytes 5242880 | tf_op jit(solution)/shard_map/all_gather | solution.py:892
  85.7 30.2 %collective-permute-start.10 = (bf16[256,2048]{1,0:T(8,128)(2,1)}, bf16[256,2048]{1,0:T(8,128)(2,1)}, u32[]{:S(2)}, u32[]{:S(2)}) collective-permute-start(bf16[256,2048]{1,0:T(8,128)(2,1)} %collective-permute-done.5), channel_id=1, source_target_pairs={{2,0},{4,2},{6,4},{3,1},{5,3},{7,5},{10,8},{12,10},{14,12},{11,9},... | collective-permute-start | bytes 3145736 | tf_op jit(solution)/shard_map/ppermute | solution.py:105
  87.0 30.1 %collective-permute-start.9 = (bf16[256,2048]{1,0:T(8,128)(2,1)}, bf16[256,2048]{1,0:T(8,128)(2,1)}, u32[]{:S(2)}, u32[]{:S(2)}) collective-permute-start(bf16[256,2048]{1,0:T(8,128)(2,1)} %collective-permute-done.4), channel_id=1, source_target_pairs={{0,2},{2,4},{4,6},{1,3},{3,5},{5,7},{8,10},{10,12},{12,14},{9,11},... | collective-permute-start | bytes 3145736 | tf_op jit(solution)/shard_map/ppermute | solution.py:105
  154.1 153.8 %all-gather.11.cloned.1.call-start = ((), (), s32[]{:S(2)}) async-start(), calls=%async_computation.7 | async-start | bytes 10485760 | tf_op jit(solution)/shard_map/all_gather | solution.py:905
  167.7 28.6 %collective-permute-start.22 = (bf16[2,64,2048]{2,1,0:T(8,128)(2,1)}, bf16[2,64,2048]{2,1,0:T(8,128)(2,1)S(1)}, u32[]{:S(2)}, u32[]{:S(2)}) collective-permute-start(bf16[2,64,2048]{2,1,0:T(8,128)(2,1)} %get-tuple-element.503), channel_id=1, source_target_pairs={{0,2},{2,0},{4,6},{6,4},{1,3},{3,1},{5,7},{7,5},{8,10},{10,8},{12,... | collective-permute-start | bytes 1572872 | tf_op jit(solution)/shard_map/ppermute | solution.py:58
  169.7 38.4 %collective-permute-start.23 = (bf16[2,64,2048]{2,1,0:T(8,128)(2,1)}, bf16[2,64,2048]{2,1,0:T(8,128)(2,1)S(1)}, u32[]{:S(2)}, u32[]{:S(2)}) collective-permute-start(bf16[2,64,2048]{2,1,0:T(8,128)(2,1)} %get-tuple-element.502), channel_id=1, source_target_pairs={{0,4},{2,6},{4,0},{6,2},{1,5},{3,7},{5,1},{7,3},{8,12},{10,14},{12... | collective-permute-start | bytes 1572872 | tf_op jit(solution)/shard_map/ppermute | solution.py:58
  170.6 37.5 %collective-permute-start.24 = (bf16[2,64,2048]{2,1,0:T(8,128)(2,1)}, bf16[2,64,2048]{2,1,0:T(8,128)(2,1)S(1)}, u32[]{:S(2)}, u32[]{:S(2)}) collective-permute-start(bf16[2,64,2048]{2,1,0:T(8,128)(2,1)} %get-tuple-element.501), channel_id=1, source_target_pairs={{0,6},{2,4},{4,2},{6,0},{1,7},{3,5},{5,3},{7,1},{8,14},{10,12},{12... | collective-permute-start | bytes 1572872 | tf_op jit(solution)/shard_map/ppermute | solution.py:58
  213.4 493.3 %reduce-scatter.5.cloned.1.call-start = ((), (), s32[]{:S(2)}) async-start(), calls=%async_computation.8 | async-start | bytes 10485760 | tf_op jit(solution)/shard_map/reduce_scatter | solution.py:816
  252.4 29.4 %collective-permute-start.29 = (bf16[256,2048]{1,0:T(8,128)(2,1)S(1)}, bf16[256,2048]{1,0:T(8,128)(2,1)}, u32[]{:S(2)}, u32[]{:S(2)}) collective-permute-start(bf16[256,2048]{1,0:T(8,128)(2,1)S(1)} %fusion.7.refs_0_), channel_id=1, source_target_pairs={{0,2},{2,4},{4,6},{1,3},{3,5},{5,7},{8,10},{10,12},{12,14},{9,11},... | collective-permute-start | bytes 3145736 | tf_op jit(solution)/shard_map/ppermute | solution.py:105
  260.7 26.3 %collective-permute-start.30 = (bf16[256,2048]{1,0:T(8,128)(2,1)S(1)}, bf16[256,2048]{1,0:T(8,128)(2,1)}, u32[]{:S(2)}, u32[]{:S(2)}) collective-permute-start(bf16[256,2048]{1,0:T(8,128)(2,1)S(1)} %fusion.7.refs_0_), channel_id=1, source_target_pairs={{2,0},{4,2},{6,4},{3,1},{5,3},{7,5},{10,8},{12,10},{14,12},{11,9},... | collective-permute-start | bytes 3145736 | tf_op jit(solution)/shard_map/ppermute | solution.py:105
  288.9 27.9 %collective-permute-start.34 = (bf16[256,2048]{1,0:T(8,128)(2,1)S(1)}, bf16[256,2048]{1,0:T(8,128)(2,1)}, u32[]{:S(2)}, u32[]{:S(2)}) collective-permute-start(bf16[256,2048]{1,0:T(8,128)(2,1)S(1)} %broadcast_select_fusion.5.refs_0_), channel_id=1, source_target_pairs={{0,1},{1,0},{2,3},{3,2},{4,5},{5,4},{6,7},{7,6},{8,9},{9,8},{10,11... | collective-permute-start | bytes 3145736 | tf_op jit(solution)/shard_map/ppermute | solution.py:62
  289.0 27.8 %collective-permute-start.32 = (bf16[256,2048]{1,0:T(8,128)(2,1)}, bf16[256,2048]{1,0:T(8,128)(2,1)}, u32[]{:S(2)}, u32[]{:S(2)}) collective-permute-start(bf16[256,2048]{1,0:T(8,128)(2,1)} %collective-permute-done.29), channel_id=1, source_target_pairs={{0,2},{2,4},{4,6},{1,3},{3,5},{5,7},{8,10},{10,12},{12,14},{9,11},... | collective-permute-start | bytes 3145736 | tf_op jit(solution)/shard_map/ppermute | solution.py:105
  292.4 27.5 %collective-permute-start.33 = (bf16[256,2048]{1,0:T(8,128)(2,1)}, bf16[256,2048]{1,0:T(8,128)(2,1)}, u32[]{:S(2)}, u32[]{:S(2)}) collective-permute-start(bf16[256,2048]{1,0:T(8,128)(2,1)} %collective-permute-done.30), channel_id=1, source_target_pairs={{2,0},{4,2},{6,4},{3,1},{5,3},{7,5},{10,8},{12,10},{14,12},{11,9},... | collective-permute-start | bytes 3145736 | tf_op jit(solution)/shard_map/ppermute | solution.py:105
  323.3 28.3 %collective-permute-start.37 = (bf16[256,2048]{1,0:T(8,128)(2,1)S(1)}, bf16[256,2048]{1,0:T(8,128)(2,1)S(1)}, u32[]{:S(2)}, u32[]{:S(2)}) collective-permute-start(bf16[256,2048]{1,0:T(8,128)(2,1)S(1)} %select_select_fusion.3.refs_0_), channel_id=1, source_target_pairs={{0,1},{1,0},{2,3},{3,2},{4,5},{5,4},{6,7},{7,6},{8,9},{9,8},{10,11... | collective-permute-start | bytes 3145736 | tf_op jit(solution)/shard_map/ppermute | solution.py:62
  323.4 28.2 %collective-permute-start.35 = (bf16[256,2048]{1,0:T(8,128)(2,1)}, bf16[256,2048]{1,0:T(8,128)(2,1)S(1)}, u32[]{:S(2)}, u32[]{:S(2)}) collective-permute-start(bf16[256,2048]{1,0:T(8,128)(2,1)} %collective-permute-done.32), channel_id=1, source_target_pairs={{0,2},{2,4},{4,6},{1,3},{3,5},{5,7},{8,10},{10,12},{12,14},{9,11},... | collective-permute-start | bytes 3145736 | tf_op jit(solution)/shard_map/ppermute | solution.py:105
  324.9 27.5 %collective-permute-start.36 = (bf16[256,2048]{1,0:T(8,128)(2,1)}, bf16[256,2048]{1,0:T(8,128)(2,1)S(1)}, u32[]{:S(2)}, u32[]{:S(2)}) collective-permute-start(bf16[256,2048]{1,0:T(8,128)(2,1)} %collective-permute-done.33), channel_id=1, source_target_pairs={{2,0},{4,2},{6,4},{3,1},{5,3},{7,5},{10,8},{12,10},{14,12},{11,9},... | collective-permute-start | bytes 3145736 | tf_op jit(solution)/shard_map/ppermute | solution.py:105
  379.1 27.7 %collective-permute-start.40 = (bf16[256,2048]{1,0:T(8,128)(2,1)S(1)}, bf16[256,2048]{1,0:T(8,128)(2,1)S(1)}, u32[]{:S(2)}, u32[]{:S(2)}) collective-permute-start(bf16[256,2048]{1,0:T(8,128)(2,1)S(1)} %add_convert_fusion.23), channel_id=1, source_target_pairs={{0,2},{1,3},{8,10},{9,11},{16,18},{17,19},{24,26},{25,27}} | collective-permute-start | bytes 3145736 | tf_op jit(solution)/shard_map/ppermute | solution.py:105
  385.7 28.6 %collective-permute-start.45 = (bf16[256,2048]{1,0:T(8,128)(2,1)S(1)}, bf16[256,2048]{1,0:T(8,128)(2,1)S(1)}, u32[]{:S(2)}, u32[]{:S(2)}) collective-permute-start(bf16[256,2048]{1,0:T(8,128)(2,1)S(1)} %get-tuple-element.337), channel_id=1, source_target_pairs={{0,1},{1,0},{2,3},{3,2},{4,5},{5,4},{6,7},{7,6},{8,9},{9,8},{10,11... | collective-permute-start | bytes 3145736 | tf_op jit(solution)/shard_map/ppermute | solution.py:62
  408.9 26.3 %collective-permute-start.43 = (bf16[256,2048]{1,0:T(8,128)(2,1)S(1)}, bf16[256,2048]{1,0:T(8,128)(2,1)S(1)}, u32[]{:S(2)}, u32[]{:S(2)}) collective-permute-start(bf16[256,2048]{1,0:T(8,128)(2,1)S(1)} %get-tuple-element.500), channel_id=1, source_target_pairs={{0,2},{2,4},{1,3},{3,5},{8,10},{10,12},{9,11},{11,13},{16,18},{18,... | collective-permute-start | bytes 3145736 | tf_op jit(solution)/shard_map/ppermute | solution.py:105
  414.1 32.8 %collective-permute-start.48 = (bf16[256,2048]{1,0:T(8,128)(2,1)S(1)}, bf16[256,2048]{1,0:T(8,128)(2,1)S(1)}, u32[]{:S(2)}, u32[]{:S(2)}) collective-permute-start(bf16[256,2048]{1,0:T(8,128)(2,1)S(1)} %get-tuple-element.342), channel_id=1, source_target_pairs={{0,1},{1,0},{2,3},{3,2},{4,5},{5,4},{6,7},{7,6},{8,9},{9,8},{10,11... | collective-permute-start | bytes 3145736 | tf_op jit(solution)/shard_map/ppermute | solution.py:62
  437.3 28.3 %collective-permute-start.46 = (bf16[256,2048]{1,0:T(8,128)(2,1)S(1)}, bf16[256,2048]{1,0:T(8,128)(2,1)S(1)}, u32[]{:S(2)}, u32[]{:S(2)}) collective-permute-start(bf16[256,2048]{1,0:T(8,128)(2,1)S(1)} %get-tuple-element.498), channel_id=1, source_target_pairs={{0,2},{2,4},{4,6},{1,3},{3,5},{5,7},{8,10},{10,12},{12,14},{9,11},... | collective-permute-start | bytes 3145736 | tf_op jit(solution)/shard_map/ppermute | solution.py:105
  502.1 27.2 %collective-permute-start.53 = (bf16[256,2048]{1,0:T(8,128)(2,1)S(1)}, bf16[256,2048]{1,0:T(8,128)(2,1)S(1)}, u32[]{:S(2)}, u32[]{:S(2)}) collective-permute-start(bf16[256,2048]{1,0:T(8,128)(2,1)S(1)} %collective-permute-done.50), channel_id=1, source_target_pairs={{2,0},{4,2},{6,4},{3,1},{5,3},{7,5},{10,8},{12,10},{14,12},{11,9},... | collective-permute-start | bytes 3145736 | tf_op jit(solution)/shard_map/ppermute | solution.py:105
  533.7 27.2 %collective-permute-start.56 = (bf16[256,2048]{1,0:T(8,128)(2,1)S(1)}, bf16[256,2048]{1,0:T(8,128)(2,1)S(1)}, u32[]{:S(2)}, u32[]{:S(2)}) collective-permute-start(bf16[256,2048]{1,0:T(8,128)(2,1)S(1)} %collective-permute-done.53), channel_id=1, source_target_pairs={{2,0},{4,2},{6,4},{3,1},{5,3},{7,5},{10,8},{12,10},{14,12},{11,9},... | collective-permute-start | bytes 3145736 | tf_op jit(solution)/shard_map/ppermute | solution.py:105
  588.6 29.4 %collective-permute-start.62 = (bf16[256,2048]{1,0:T(8,128)(2,1)}, bf16[256,2048]{1,0:T(8,128)(2,1)}, u32[]{:S(2)}, u32[]{:S(2)}) collective-permute-start(bf16[256,2048]{1,0:T(8,128)(2,1)} %get-tuple-element.373), channel_id=1, source_target_pairs={{0,1},{1,0},{2,3},{3,2},{4,5},{5,4},{6,7},{7,6},{8,9},{9,8},{10,11... | collective-permute-start | bytes 3145736 | tf_op jit(solution)/shard_map/ppermute | solution.py:62
  591.5 29.1 %collective-permute-start.60 = (bf16[256,2048]{1,0:T(8,128)(2,1)}, bf16[256,2048]{1,0:T(8,128)(2,1)}, u32[]{:S(2)}, u32[]{:S(2)}) collective-permute-start(bf16[256,2048]{1,0:T(8,128)(2,1)} %add_convert_fusion.15), channel_id=1, source_target_pairs={{0,2},{1,3},{8,10},{9,11},{16,18},{17,19},{24,26},{25,27}} | collective-permute-start | bytes 3145736 | tf_op jit(solution)/shard_map/ppermute | solution.py:105
  594.7 25.9 %collective-permute-start.61 = (bf16[256,2048]{1,0:T(8,128)(2,1)}, bf16[256,2048]{1,0:T(8,128)(2,1)}, u32[]{:S(2)}, u32[]{:S(2)}) collective-permute-start(bf16[256,2048]{1,0:T(8,128)(2,1)} %add_convert_fusion.15), channel_id=1, source_target_pairs={{6,4},{7,5},{14,12},{15,13},{22,20},{23,21},{30,28},{31,29}} | collective-permute-start | bytes 3145736 | tf_op jit(solution)/shard_map/ppermute | solution.py:105
  620.6 186.3 %reduce-scatter.7.cloned.1.call-start = ((), (), s32[]{:S(2)}) async-start(), calls=%async_computation.9 | async-start | bytes 5242880 | tf_op jit(solution)/shard_map/reduce_scatter | solution.py:816
  621.8 43.1 %collective-permute-start.68 = (bf16[256,2048]{1,0:T(8,128)(2,1)S(1)}, bf16[256,2048]{1,0:T(8,128)(2,1)}, u32[]{:S(2)}, u32[]{:S(2)}) collective-permute-start(bf16[256,2048]{1,0:T(8,128)(2,1)S(1)} %copy-done.11), channel_id=1, source_target_pairs={{0,1},{1,0},{2,3},{3,2},{4,5},{5,4},{6,7},{7,6},{8,9},{9,8},{10,11... | collective-permute-start | bytes 3145736 | tf_op jit(solution)/shard_map/ppermute | solution.py:62
  657.6 27.0 %collective-permute-start.66 = (bf16[256,2048]{1,0:T(8,128)(2,1)S(1)}, bf16[256,2048]{1,0:T(8,128)(2,1)S(1)}, u32[]{:S(2)}, u32[]{:S(2)}) collective-permute-start(bf16[256,2048]{1,0:T(8,128)(2,1)S(1)} %get-tuple-element.494), channel_id=1, source_target_pairs={{0,2},{2,4},{4,6},{1,3},{3,5},{5,7},{8,10},{10,12},{12,14},{9,11},... | collective-permute-start | bytes 3145736 | tf_op jit(solution)/shard_map/ppermute | solution.py:105
  743.9 155.5 %reduce-scatter.11.cloned.1.call-start = ((), (), s32[]{:S(2)}) async-start(), calls=%async_computation.11 | async-start | bytes 5242880 | tf_op jit(solution)/shard_map/reduce_scatter | solution.py:816
  746.3 33.4 %collective-permute-start.75 = (bf16[2,64,2048]{2,1,0:T(8,128)(2,1)}, bf16[2,64,2048]{2,1,0:T(8,128)(2,1)S(1)}, u32[]{:S(2)}, u32[]{:S(2)}) collective-permute-start(bf16[2,64,2048]{2,1,0:T(8,128)(2,1)} %get-tuple-element.489), channel_id=1, source_target_pairs={{0,2},{2,0},{4,6},{6,4},{1,3},{3,1},{5,7},{7,5},{8,10},{10,8},{12,... | collective-permute-start | bytes 1572872 | tf_op jit(solution)/shard_map/ppermute | solution.py:58
  751.7 38.2 %collective-permute-start.76 = (bf16[2,64,2048]{2,1,0:T(8,128)(2,1)S(1)}, bf16[2,64,2048]{2,1,0:T(8,128)(2,1)S(1)}, u32[]{:S(2)}, u32[]{:S(2)}) collective-permute-start(bf16[2,64,2048]{2,1,0:T(8,128)(2,1)S(1)} %get-tuple-element.488), channel_id=1, source_target_pairs={{0,4},{2,6},{4,0},{6,2},{1,5},{3,7},{5,1},{7,3},{8,12},{10,14},{12... | collective-permute-start | bytes 1572872 | tf_op jit(solution)/shard_map/ppermute | solution.py:58
  751.7 38.2 %collective-permute-start.77 = (bf16[2,64,2048]{2,1,0:T(8,128)(2,1)S(1)}, bf16[2,64,2048]{2,1,0:T(8,128)(2,1)S(1)}, u32[]{:S(2)}, u32[]{:S(2)}) collective-permute-start(bf16[2,64,2048]{2,1,0:T(8,128)(2,1)S(1)} %get-tuple-element.487), channel_id=1, source_target_pairs={{0,6},{2,4},{4,2},{6,0},{1,7},{3,5},{5,3},{7,1},{8,14},{10,12},{12... | collective-permute-start | bytes 1572872 | tf_op jit(solution)/shard_map/ppermute | solution.py:58
  789.9 130.9 %reduce-scatter.9.cloned.1.call-start = ((), (), s32[]{:S(2)}) async-start(), calls=%async_computation.10 | async-start | bytes 3932160 | tf_op jit(solution)/shard_map/reduce_scatter | solution.py:816
  839.9 26.0 %collective-permute-start.88 = (bf16[256,2048]{1,0:T(8,128)(2,1)}, bf16[256,2048]{1,0:T(8,128)(2,1)S(1)}, u32[]{:S(2)}, u32[]{:S(2)}) collective-permute-start(bf16[256,2048]{1,0:T(8,128)(2,1)} %slice.108), channel_id=1, source_target_pairs={{0,1},{1,0},{2,3},{3,2},{4,5},{5,4},{6,7},{7,6},{8,9},{9,8},{10,11... | collective-permute-start | bytes 3145736 | tf_op jit(solution)/shard_map/ppermute | solution.py:62
  845.2 30.3 %collective-permute-start.85 = (bf16[256,2048]{1,0:T(8,128)(2,1)}, bf16[256,2048]{1,0:T(8,128)(2,1)}, u32[]{:S(2)}, u32[]{:S(2)}) collective-permute-start(bf16[256,2048]{1,0:T(8,128)(2,1)} %add_convert_fusion.7), channel_id=1, source_target_pairs={{0,2},{1,3},{8,10},{9,11},{16,18},{17,19},{24,26},{25,27}} | collective-permute-start | bytes 3145736 | tf_op jit(solution)/shard_map/ppermute | solution.py:105
  886.6 27.4 %collective-permute-start.89 = (bf16[256,2048]{1,0:T(8,128)(2,1)}, bf16[256,2048]{1,0:T(8,128)(2,1)}, u32[]{:S(2)}, u32[]{:S(2)}) collective-permute-start(bf16[256,2048]{1,0:T(8,128)(2,1)} %get-tuple-element.486), channel_id=1, source_target_pairs={{0,2},{2,4},{1,3},{3,5},{8,10},{10,12},{9,11},{11,13},{16,18},{18,... | collective-permute-start | bytes 3145736 | tf_op jit(solution)/shard_map/ppermute | solution.py:105
  926.2 31.6 %collective-permute-start.93 = (bf16[256,2048]{1,0:T(8,128)(2,1)}, bf16[256,2048]{1,0:T(8,128)(2,1)S(1)}, u32[]{:S(2)}, u32[]{:S(2)}) collective-permute-start(bf16[256,2048]{1,0:T(8,128)(2,1)} %get-tuple-element.484), channel_id=1, source_target_pairs={{0,2},{2,4},{4,6},{1,3},{3,5},{5,7},{8,10},{10,12},{12,14},{9,11},... | collective-permute-start | bytes 3145736 | tf_op jit(solution)/shard_map/ppermute | solution.py:105
  929.6 28.2 %collective-permute-start.94 = (bf16[256,2048]{1,0:T(8,128)(2,1)}, bf16[256,2048]{1,0:T(8,128)(2,1)}, u32[]{:S(2)}, u32[]{:S(2)}) collective-permute-start(bf16[256,2048]{1,0:T(8,128)(2,1)} %get-tuple-element.483), channel_id=1, source_target_pairs={{2,0},{4,2},{6,4},{3,1},{5,3},{7,5},{10,8},{12,10},{14,12},{11,9},... | collective-permute-start | bytes 3145736 | tf_op jit(solution)/shard_map/ppermute | solution.py:105
  932.2 25.5 %collective-permute-start.96 = (f32[5,2048]{1,0:T(8,128)S(1)}, f32[5,2048]{1,0:T(8,128)S(1)}, u32[]{:S(2)}, u32[]{:S(2)}) collective-permute-start(f32[5,2048]{1,0:T(8,128)S(1)} %add.747), channel_id=1, source_target_pairs={{0,2},{2,0},{1,3},{3,1},{4,6},{6,4},{5,7},{7,5},{8,10},{10,8},{9,1... | collective-permute-start | bytes 122888 | tf_op jit(solution)/shard_map/ppermute | solution.py:1029
  (138 other events, 2372.7 us)
Sparse Core Ops, SparseCore 0:
  9.8 55.3 all-gather.4
  79.5 48.4 all-gather.6
  154.3 56.6 all-gather.8
  213.5 94.3 all-gather.10
  620.7 84.8 reduce-scatter.4
  744.0 55.3 reduce-scatter.6
  802.4 52.6 reduce-scatter.10
  875.7 45.1 reduce-scatter.8

commit v5 on v4

--- a/solution.py
+++ b/solution.py
@@ -165,7 +165,7 @@
         plan = plan or [[k] for k in range(count - 2, -1, -1)]
         made = {count - 1: parts(count - 1)}
         last = {1: None, -1: None}
-        tied = []
+        tied = self.tied = []
         for slot in range(1, count):
             far = count - slot
             values = self.hop_values(made, far, last)
@@ -223,7 +223,7 @@
             out_specs=pl.BlockSpec((1,) + shape, lambda i, places: (places[i],) + (0,) * len(shape)),
         ),
         out_shape=jax.ShapeDtypeStruct((len(pieces),) + shape, pieces[0].dtype),
-        compiler_params=pltpu.CompilerParams(vmem_limit_bytes=32 << 20),
+        compiler_params=pltpu.CompilerParams(vmem_limit_bytes=18 << 20),
         cost_estimate=cost(2),
         name="assemble",
     )(jnp.stack(places).astype(jnp.int32), *pieces)
@@ -316,8 +316,13 @@
     log_ref[0] = top + jnp.log(total)
 
 
+def in_hbm(*arrays):
+    return tuple(pltpu.with_memory_space_constraint(a, pltpu.HBM) for a in arrays)
+
+
 def attend(lows, starts, queries, keys, values):
     length, width = queries.shape
+    queries, keys, values = in_hbm(queries, keys, values)
     heads, bq = width // HEAD_DIM, BLOCK_Q
     return pl.pallas_call(
         attend_kernel,
@@ -336,10 +341,10 @@
             ],
         ),
         out_shape=[
-            jax.ShapeDtypeStruct((length, width), f32),
+            pltpu.HBM((length, width), f32),
             jax.ShapeDtypeStruct((heads, 1, length), f32),
         ],
-        compiler_params=pltpu.CompilerParams(vmem_limit_bytes=48 << 20),
+        compiler_params=pltpu.CompilerParams(vmem_limit_bytes=16 << 20),
         cost_estimate=cost(16),
         name="attend",
     )(lows, starts, queries, keys, values)
@@ -401,8 +406,8 @@
             ],
             out_specs=[column, column, column],
         ),
-        out_shape=[jax.ShapeDtypeStruct((length, width), f32)] * 3,
-        compiler_params=pltpu.CompilerParams(vmem_limit_bytes=56 << 20),
+        out_shape=[pltpu.HBM((length, width), f32)] * 3,
+        compiler_params=pltpu.CompilerParams(vmem_limit_bytes=28 << 20),
         cost_estimate=cost(26),
         name="attend_back",
     )(lows, starts, queries, keys, values, out, log_total, grads)
@@ -483,10 +488,10 @@
         in_specs=[row_block(depth, 256), whole_block(depth, columns)],
         out_specs=[row_block(columns, 256), lane_block(2, 256)],
         out_shape=[
-            jax.ShapeDtypeStruct((length, columns), f32),
+            pltpu.HBM((length, columns), f32),
             jax.ShapeDtypeStruct((2, length), f32),
         ],
-        compiler_params=pltpu.CompilerParams(vmem_limit_bytes=32 << 20),
+        compiler_params=pltpu.CompilerParams(vmem_limit_bytes=18 << 20),
         cost_estimate=cost(10),
         name="project",
     )(inputs, weight)
@@ -556,7 +561,7 @@
             row_block(HEAD_DIM),
         ],
         out_specs=[row_block(width)] * 3,
-        out_shape=[jax.ShapeDtypeStruct((length, width), bf16)] * 3,
+        out_shape=[pltpu.HBM((length, width), bf16)] * 3,
         cost_estimate=cost(1),
         name="turn",
     )(projected, factors, gains, cosine, sine_part)
@@ -590,6 +595,7 @@
 
 def unturn(query_grad, key_grad, projected, factors, gains, cosine, sine_part):
     length, width = query_grad.shape
+    query_grad, key_grad, projected = in_hbm(query_grad, key_grad, projected)
     return pl.pallas_call(
         unturn_kernel,
         grid=(length // 512,),
@@ -604,7 +610,7 @@
         ],
         out_specs=[row_block(2 * width), lane_block(2), whole_block(2, width)],
         out_shape=[
-            jax.ShapeDtypeStruct((length, 2 * width), f32),
+            pltpu.HBM((length, 2 * width), f32),
             jax.ShapeDtypeStruct((2, length), f32),
             jax.ShapeDtypeStruct((2, width), f32),
         ],
@@ -644,152 +650,73 @@
     )(weighted, projected, factors, mixing, value_grad)
 
 
-UNITS = 512
-COLUMNS = 1024
-
-
-class Steps:
-    def __init__(self, units):
-        self.first, self.second = units // UNITS, D // COLUMNS
-        self.count = self.first + self.second
-
-    def unit(self, i):
-        return jnp.minimum(i, self.first - 1)
-
-    def column(self, i):
-        return jnp.maximum(i - self.first, 0)
-
-
-def feed_call(kernel, name, blocks, chip, length, specs, weights, widths, held):
+def take_rows(block_refs, rows_out):
+    for i, block in enumerate(block_refs):
+
+        @pl.when(pl.program_id(0) == i)
+        def _(block=block):
+            rows_out[...] = block[...]
+
+    return rows_out[...]
+
+
+def give_part(part, part_refs):
+    for i, out in enumerate(part_refs):
+
+        @pl.when(pl.program_id(0) == i)
+        def _(out=out):
+            out[...] = part.astype(bf16)
+
+
+def feed_kernel(count, held, *refs):
+    block_refs, (in_w, down_w) = refs[:count], refs[count : count + 2]
+    outs = refs[count + 2 + held :]
+    rows_out, gate_out, up_out, hidden_out = outs[:4]
+    units = down_w.shape[0]
+    both = product(take_rows(block_refs, rows_out), in_w[...])
+    gate, up = both[:, :units], both[:, units:]
+    hidden = (gate * jax.nn.sigmoid(gate) * up).astype(bf16)
+    gate_out[...], up_out[...], hidden_out[...] = gate.astype(bf16), up.astype(bf16), hidden
+    give_part(product(hidden, down_w[...]), outs[4:])
+
+
+def feed_back_kernel(count, held, *refs):
+    block_refs, (in_w, down_w) = refs[:count], refs[count : count + 2]
+    gate_in, up_in = refs[count + 2 : count + 4]
+    rows_out, grads_out = refs[count + 4 + held : count + 6 + held]
+    units = down_w.shape[0]
+    hidden_grad = product_right(take_rows(block_refs, rows_out), down_w[...])
+    gate, up = gate_in[...].astype(f32), up_in[...].astype(f32)
+    sigmoid_gate = jax.nn.sigmoid(gate)
+    gate_grad = hidden_grad * up * sigmoid_gate * (1.0 + gate * (1.0 - sigmoid_gate))
+    grads_out[:, :units] = gate_grad.astype(bf16)
+    grads_out[:, units:] = (hidden_grad * gate * sigmoid_gate).astype(bf16)
+    give_part(product_right(grads_out[...], in_w[...]), refs[count + 6 + held :])
+
+
+def feed_call(kernel, name, blocks, first, length, weights, saved, widths, held):
     count, piece = len(blocks), blocks[0].shape[0]
-    rows, steps = piece * count, Steps(weights[1].shape[0])
-    inputs, outputs, scratch = specs(steps, rows, chip)
     held = list(held or ())
-    in_specs = [pl.BlockSpec((piece, D), lambda i: (0, 0))] * count + [s for s, _ in inputs]
-    first = len(in_specs)
-    part = pl.BlockSpec((piece, COLUMNS), lambda i: (0, steps.column(i)))
+    whole = pl.BlockSpec((piece, D), lambda i: (0, 0))
+
+    def rows(columns):
+        return pl.BlockSpec((piece, columns), lambda i: (first + i, 0))
+
+    in_specs = [whole] * count + [pl.BlockSpec(memory_space=pltpu.VMEM)] * 2
+    in_specs += [rows(array.shape[1]) for array in saved]
     results = pl.pallas_call(
-        functools.partial(kernel, steps.first, count, len(held)),
-        grid=(steps.count,),
-        in_specs=in_specs + [pl.BlockSpec(memory_space=pl.ANY)] * len(held),
-        out_specs=outputs + [part] * count,
-        out_shape=[jax.ShapeDtypeStruct((length, w), bf16) for w in widths]
+        functools.partial(kernel, count, len(held)),
+        grid=(count,),
+        in_specs=in_specs + [pl.BlockSpec(memory_space=pltpu.HBM)] * len(held),
+        out_specs=[rows(w) for w in widths] + [whole] * count,
+        out_shape=[pltpu.HBM((length, w), bf16) for w in widths]
         + [jax.ShapeDtypeStruct((piece, D), bf16)] * count,
-        scratch_shapes=[pltpu.VMEM((rows, D), bf16)]
-        + [pltpu.VMEM((rows, width), bf16) for width in scratch],
-        input_output_aliases={first + i: i for i in range(len(held))},
+        input_output_aliases={len(in_specs) + i: i for i in range(len(held))},
         cost_estimate=cost(1),
-        compiler_params=pltpu.CompilerParams(vmem_limit_bytes=40 << 20),
+        compiler_params=pltpu.CompilerParams(vmem_limit_bytes=24 << 20),
         name=name,
-    )(*blocks, *[array for _, array in inputs], *held)
+    )(*blocks, *weights, *saved, *held)
     return list(results[: len(widths)]), tuple(results[len(widths) :])
-
-
-def feed(blocks, chip, length, weights, held):
-    units = weights[1].shape[0]
-
-    def specs(steps, rows, chip):
-        by_unit = pl.BlockSpec((rows, UNITS), lambda i: (chip, steps.unit(i)))
-        inputs = [
-            (pl.BlockSpec((D, UNITS), lambda i: (0, steps.unit(i))), weights[0]),
-            (pl.BlockSpec((D, UNITS), lambda i: (0, steps.first + steps.unit(i))), weights[0]),
-            (pl.BlockSpec((units, COLUMNS), lambda i: (0, steps.column(i))), weights[1]),
-        ]
-        rows_out = pl.BlockSpec((rows, D // steps.first), lambda i: (chip, steps.unit(i)))
-        return inputs, [rows_out, by_unit, by_unit, by_unit], [units]
-
-    widths = (D, units, units, units)
-    return feed_call(feed_kernel, "feed", blocks, chip, length, specs, weights, widths, held)
-
-
-def feed_back(blocks, chip, length, gate_all, up_all, weights, held):
-    units = weights[1].shape[0]
-
-    def specs(steps, rows, chip):
-        by_unit = pl.BlockSpec((rows, UNITS), lambda i: (chip, steps.unit(i)))
-        inputs = [
-            (by_unit, gate_all),
-            (by_unit, up_all),
-            (pl.BlockSpec((UNITS, D), lambda i: (steps.unit(i), 0)), weights[1]),
-            (pl.BlockSpec((COLUMNS, 2 * units), lambda i: (steps.column(i), 0)), weights[0]),
-        ]
-        rows_out = pl.BlockSpec((rows, D // steps.first), lambda i: (chip, steps.unit(i)))
-        grads = pl.BlockSpec((rows, 2 * units // steps.second), lambda i: (chip, steps.column(i)))
-        return inputs, [rows_out, grads], [2 * units]
-
-    widths = (D, 2 * units)
-    return feed_call(
-        feed_back_kernel, "feed_back", blocks, chip, length, specs, weights, widths, held
-    )
-
-
-def chunk(step, size, offset=0):
-    return pl.ds(pl.multiple_of(step * size, size) + offset, size)
-
-
-def take_rows(block_refs, rows, rows_out):
-    step = pl.program_id(0)
-
-    @pl.when(step == 0)
-    def _():
-        piece = block_refs[0].shape[0]
-        for i, block in enumerate(block_refs):
-            rows[i * piece : (i + 1) * piece, :] = block[...]
-
-    size = rows_out.shape[1]
-    rows_out[...] = rows[:, chunk(step, size)]
-
-
-def give_parts(part, part_refs):
-    piece = part_refs[0].shape[0]
-    for i, out in enumerate(part_refs):
-        out[...] = part[i * piece : (i + 1) * piece].astype(bf16)
-
-
-def feed_kernel(first, count, held, *refs):
-    block_refs, (gate_w, up_w, down_w) = refs[:count], refs[count : count + 3]
-    outs = refs[count + 3 + held :]
-    rows_out, gate_out, up_out, hidden_out = outs[:4]
-    part_refs, (rows, all_hidden) = outs[4 : 4 + count], outs[4 + count :]
-    step = pl.program_id(0)
-
-    @pl.when(step < first)
-    def _():
-        take_rows(block_refs, rows, rows_out)
-        gate, up = product(rows[...], gate_w[...]), product(rows[...], up_w[...])
-        hidden = (gate * jax.nn.sigmoid(gate) * up).astype(bf16)
-        gate_out[...], up_out[...] = gate.astype(bf16), up.astype(bf16)
-        hidden_out[...] = hidden
-        all_hidden[:, chunk(step, UNITS)] = hidden
-
-    @pl.when(step >= first)
-    def _():
-        give_parts(product(all_hidden[...], down_w[...]), part_refs)
-
-
-def feed_back_kernel(first, count, held, *refs):
-    block_refs, (gate_in, up_in, down_w, in_w) = refs[:count], refs[count : count + 4]
-    outs = refs[count + 4 + held :]
-    rows_out, grads_out = outs[:2]
-    part_refs, (rows, grads) = outs[2 : 2 + count], outs[2 + count :]
-    units = grads.shape[1] // 2
-    step = pl.program_id(0)
-
-    @pl.when(step < first)
-    def _():
-        take_rows(block_refs, rows, rows_out)
-        hidden_grad = product_right(rows[...], down_w[...])
-        gate, up = gate_in[...].astype(f32), up_in[...].astype(f32)
-        sigmoid_gate = jax.nn.sigmoid(gate)
-        gate_grad = hidden_grad * up * sigmoid_gate * (1.0 + gate * (1.0 - sigmoid_gate))
-        grads[:, chunk(step, UNITS)] = gate_grad.astype(bf16)
-        grads[:, chunk(step, UNITS, units)] = (hidden_grad * gate * sigmoid_gate).astype(bf16)
-
-    @pl.when(step >= first)
-    def _():
-        size = grads_out.shape[1]
-        grads_out[...] = grads[:, chunk(step - first, size)]
-        give_parts(product_right(grads[...], in_w[...]), part_refs)
 
 
 def norm_forward(values, gain_row):
@@ -924,14 +851,18 @@
         return parts
 
     def window_of(k):
-        return 2 * line - 2 if k == 0 else 2 * line - 1 if k == line else k - 1
+        return 2 * line - 2 if k == 0 else 2 * line - 1 if k == line else 2 * (k - 1)
 
     held = {}
+    weights_here = tuple(
+        pltpu.with_memory_space_constraint(w, pltpu.VMEM) for w in (in_here, down_here)
+    )
 
     def forward_chip(k, same, other):
         blocks = [b for b in (same, other) if b is not None]
-        held["forward"], parts = feed(
-            blocks, window_of(k), length, (in_here, down_here), held.get("forward")
+        held["forward"], parts = feed_call(
+            feed_kernel, "feed", blocks, window_of(k), length, weights_here, (),
+            (D, units, units, units), held.get("forward"),
         )
         return parts
 
@@ -956,9 +887,9 @@
 
     def backward_chip(k, same, other):
         blocks = [b for b in (same, other) if b is not None]
-        held["backward"], parts = feed_back(
-            blocks, window_of(k), length, gate_all, up_all, (in_here, down_here),
-            held.get("backward"),
+        held["backward"], parts = feed_call(
+            feed_back_kernel, "feed_back", blocks, window_of(k), length, weights_here,
+            (gate_all, up_all), (D, 2 * units), held.get("backward"),
         )
         return parts
 
@@ -1009,15 +940,23 @@
     grad_down = scatter_over(grad_down, DATA)
     mixing = small_sum(mixing, CTX) / D
     projected_grad = finish(weighted, projected, factors, mixing, value_grad)
-    projected_grad, out_pieces = together(projected_grad, chips_start(out_grad, LINE))
+    out_steps = offsets(LINE)
+
+    def out_pieces(turn):
+        return [shift(pick(out_grad, place(LINE, steps)), LINE, steps) for steps in turn]
+
+    projected_grad, near = together(projected_grad, out_pieces(out_steps[:-1]))
     grad_blocks = projected_grad.reshape(line, 2, piece_len, 3 * width)
 
     later = []
 
-    def input_chip(k):
+    def input_product(k):
         rows = pick(grad_blocks, row.served(k))
         rows = jnp.concatenate([pick(rows, core), pick(rows, 1 - core)], axis=0)
-        part = product_right(rows, qkv_here).astype(bf16)
+        return product_right(rows, qkv_here).astype(bf16)
+
+    def input_chip(k):
+        part = row.tied[0][2] if k == line - 4 else input_product(k)
         part = scatter_sum(part[:piece_len], part[piece_len:])
         if not later:
             later.extend(together(part, projected_grad))
@@ -1031,7 +970,8 @@
 
     def last_grads(slot, tied):
         if slot == 1:
-            return (product_left(full_input, later[1]).astype(bf16), gain_grads)
+            grads = product_left(full_input, later[1]).astype(bf16)
+            return (grads, gain_grads, input_product(line - 4), out_pieces(out_steps[-1:]))
         if slot == 2:
             rows = jnp.zeros((5, D), f32)
             rows = lax.dynamic_update_slice(rows, tied[0][1], (0, ctx_place * width))
@@ -1048,12 +988,17 @@
     qkv_cores, gain_rows, in_pieces, grad_down = tied[line - 2]
     qkv_pieces = chips_start(by_core(*qkv_cores), LINE)
     gain_rows, qkv_pieces = together(step(sum(gain_rows), "zh"), qkv_pieces)
-    gain_rows = small_sum(sum(gain_rows), ("dl", "dh"))
+    gain_rows = sum(gain_rows)
+    if sizes_of(DATA) == (2, 2):
+        sides = [shift(gain_rows, DATA, steps) for steps in offsets(DATA)]
+        gain_rows = (sides[0] + sides[1]) + (sides[2] + sides[3])
+    else:
+        gain_rows = small_sum(gain_rows, ("dl", "dh"))
     input_grad = residual_grad + input_part
     grad_in = by_source(in_pieces, LINE)
     grad_in = collect(grad_in.reshape((owners,) + grad_in.shape[2:]), 2 * data_count)
     grad_down = grad_down.astype(f32)
-    grad_out = sum(piece.astype(f32) for piece in out_pieces)
+    grad_out = sum(piece.astype(f32) for piece in near + tied[0][3])
     grad_qkv = by_source(qkv_pieces, LINE)
     grad_qkv = collect(grad_qkv.reshape(owners, row_count, 3 * width), 3)
     live_count = jnp.sum(seq_lengths).astype(f32)

time: 1010 us -> 989 us (0.979)
  Pallas kernels: 208 us -> 172 us
  waiting for transfers between devices: 344 us -> 363 us
    pallas_call x10, Pallas kernels: 113 us -> 72.5 us  [feed_call(): pl.pallas_call(functools.partial(kernel, count, len(held)), grid=(count,)...]
    ppermute x36, waiting for transfers between devices: 215 us -> 235 us  [hop(): return lax.ppermute(value, self.axes, pairs)]
    ppermute x24 -> x27, starting transfers between devices: 47.3 us -> 50.5 us  [shift(): return lax.ppermute(value, axes, pairs)]
    ppermute x8 -> x6, starting transfers between devices: 24.1 us -> 21.3 us  [small_sum(): value = value + lax.ppermute(value, axis, [(0, 1), (1, 0)])]
    ppermute x24 -> x27, waiting for transfers between devices: 66.3 us -> 65.1 us  [shift(): return lax.ppermute(value, axes, pairs)]
    unnamed x152 -> x162, local copies, waits for them, and re-layouts: 20.6 us -> 20.7 us
  transfers between devices with their start and end apart: 111 -> 112, of which waited for: 47 -> 47; matrix products, arithmetic and copies ran while one was open for 19% -> 20% of each run, Pallas kernels for 17% -> 14%
where the time goes in v5:
time: 989 us; the launch traced here: 978 us
  waiting for transfers between devices  363 us (37%)
  starting transfers between devices  182 us (18%)
  Pallas kernels  172 us (17%)
  other arithmetic  107 us (11%)
  matrix products  68.9 us (7%)
  local copies, waits for them, and re-layouts  62.9 us (6%)
  between operations  22.8 us (2%)
    ppermute x36, waiting for transfers between devices, hop(): return lax.ppermute(value, self.axes, pairs)  235 us
    ppermute x36, starting transfers between devices, hop(): return lax.ppermute(value, self.axes, pairs)  100 us
    pallas_call x10, Pallas kernels, feed_call(): pl.pallas_call(functools.partial(kernel, count, len(held)), grid=(count,)...  72.5 us
    ppermute x27, waiting for transfers between devices, shift(): return lax.ppermute(value, axes, pairs)  65.1 us
    dot_general x4, matrix products, product_left(): lax.dot_general(left_side, right_side, (((0,), (0,)), ((), ())), preferre...  51.6 us
    ppermute x27, starting transfers between devices, shift(): return lax.ppermute(value, axes, pairs)  50.5 us
    convert_element_type x6, other arithmetic, hop_values(): values.append(value.astype(bf16))  26 us
    ppermute x3, waiting for transfers between devices, step(): return (rows, lax.ppermute(rows, axis, [(0, 1), (1, 0)]))  21.5 us
  transfers between devices with their start and end apart: 112, of which 47 were waited for; matrix products, arithmetic and copies ran while one was open for 20% of the time, Pallas kernels for 14%

profile of v5, /device:TPU:0, one launch (start us, length us, event | category | flops | bytes accessed | tf_op | source)
XLA Modules:
  0.0 977.8 jit_solution(9606029773182266766)
XLA Ops:
  53.7 5.6 spread.3
  65.0 10.2 %collective-permute-done.4 = bf16[256,2048]{1,0:T(8,128)(2,1)} collective-permute-done((bf16[256,2048]{1,0:T(8,128)(2,1)S(1)}, bf16[256,2048]{1,0:T(8,128)(2,1)}, u32[]{:S(2)}, u32[]{:S(2)}) %collective-permute-start.4) | collective-permute-done | bytes 1048608 | tf_op jit(solution)/shard_map/ppermute | solution.py:105
  86.9 8.2 collective-permute-start.9
  97.6 18.2 %collective-permute-done.10 = bf16[256,2048]{1,0:T(8,128)(2,1)} collective-permute-done((bf16[256,2048]{1,0:T(8,128)(2,1)}, bf16[256,2048]{1,0:T(8,128)(2,1)}, u32[]{:S(2)}, u32[]{:S(2)}) %collective-permute-start.10) | collective-permute-done | bytes 1048608 | tf_op jit(solution)/shard_map/ppermute | solution.py:105
  138.8 11.9 %project.1 = (f32[2048,768]{1,0:T(8,128)}, f32[2,2048]{1,0:T(2,128)S(1)}) custom-call(bf16[2048,2048]{1,0:T(8,128)(2,1)} %bitcast.34.in_ref, bf16[2048,768]{1,0:T(8,128)(2,1)S(1)} %copy-done.11), custom_call_target="tpu_custom_call" | custom-call | flops 10000000000 | bytes 30000000 | tf_op jit(solution)/shard_map/project/pallas_call | solution.py:485
  154.3 6.3 collective-permute-start.18
  172.5 6.3 turn.1
  178.8 14.8 %attend.1 = (f32[2048,256]{1,0:T(8,128)}, f32[2,1,2048]{2,1,0:T(1,128)S(1)}) custom-call(s32[4]{0:T(128)S(1)} %and_select_fusion.low_ref, s32[1,2048]{1,0:T(1,128)S(1)} %bitcast.208, bf16[2048,256]{1,0:T(8,128)(2,1)} %get-tuple-element.278.q_ref, bf16[2048,256]{1,0:T(8,128)(2,1)} %get-tuple-element.279.k_ref, bf16[2048,256]{1,0:T(8,128)(2,1)} %get-tuple-element.280.v_ref), custom_call_target="tpu_custom_call" | custom-call | flops 16000000000 | bytes 48000000 | tf_op jit(solution)/shard_map/attend/pallas_call | solution.py:327
  195.5 12.4 %collective-permute-done.23.refs_3_ = bf16[2,64,2048]{2,1,0:T(8,128)(2,1)S(1)} collective-permute-done((bf16[2,64,2048]{2,1,0:T(8,128)(2,1)}, bf16[2,64,2048]{2,1,0:T(8,128)(2,1)S(1)}, u32[]{:S(2)}, u32[]{:S(2)}) %collective-permute-start.23) | collective-permute-done | bytes 524320 | tf_op jit(solution)/shard_map/ppermute | solution.py:58
  213.8 8.2 collective-permute-start.25
  224.5 6.8 bitcast_select_fusion
  234.1 9.2 collective-permute-done.26.refs_3_
  244.6 6.2 multiply_reduce_fusion.6
  252.2 8.4 collective-permute-start.29
  261.9 19.7 %collective-permute-done.29 = bf16[256,2048]{1,0:T(8,128)(2,1)} collective-permute-done((bf16[256,2048]{1,0:T(8,128)(2,1)S(1)}, bf16[256,2048]{1,0:T(8,128)(2,1)}, u32[]{:S(2)}, u32[]{:S(2)}) %collective-permute-start.29) | collective-permute-done | bytes 1048608 | tf_op jit(solution)/shard_map/ppermute | solution.py:105
  293.5 14.3 %all-gather.11.cloned.1.call-done.refs_1_.refs_2_ = bf16[2048,2048]{1,0:T(8,128)(2,1)} async-done(((bf16[512,2048]{1,0:T(8,128)(2,1)}), bf16[2048,2048]{1,0:T(8,128)(2,1)}) %all-gather.11.cloned.1.call-update) | async-done | bytes 8388624 | tf_op jit(solution)/shard_map/all_gather | solution.py:832
  326.4 9.0 feed.6
  335.4 10.2 %feed.7 = (bf16[2048,2048]{1,0:T(8,128)(2,1)}, bf16[2048,1024]{1,0:T(8,128)(2,1)}, bf16[2048,1024]{1,0:T(8,128)(2,1)}, bf16[2048,1024]{1,0:T(8,128)(2,1)}, bf16[...) custom-call(bf16[256,2048]{1,0:T(8,128)(2,1)S(1)} %select_select_fus, ...), custom_call_target="tpu_custom_call", output_to_operand_aliasing={{0}: (4, {}), {1}: (5, {}), {2}: (6, {}), {3}: (7, {})} | custom-call | flops 1000000000 | bytes 3000000 | tf_op jit(solution)/shard_map/feed/pallas_call | solution.py:707
  357.3 9.3 feed.8
  376.9 20.9 %collective-permute-done.40 = bf16[256,2048]{1,0:T(8,128)(2,1)S(1)} collective-permute-done((bf16[256,2048]{1,0:T(8,128)(2,1)S(1)}, bf16[256,2048]{1,0:T(8,128)(2,1)S(1)}, u32[]{:S(2)}, u32[]{:S(2)}) %collective-permute-start.40) | collective-permute-done | bytes 1048608 | tf_op jit(solution)/shard_map/ppermute | solution.py:105
  405.6 20.6 %collective-permute-done.43 = bf16[256,2048]{1,0:T(8,128)(2,1)S(1)} collective-permute-done((bf16[256,2048]{1,0:T(8,128)(2,1)S(1)}, bf16[256,2048]{1,0:T(8,128)(2,1)S(1)}, u32[]{:S(2)}, u32[]{:S(2)}) %collective-permute-start.43) | collective-permute-done | bytes 1048608 | tf_op jit(solution)/shard_map/ppermute | solution.py:105
  428.4 8.6 collective-permute-start.46
  439.5 18.2 %collective-permute-done.46 = bf16[256,2048]{1,0:T(8,128)(2,1)S(1)} collective-permute-done((bf16[256,2048]{1,0:T(8,128)(2,1)S(1)}, bf16[256,2048]{1,0:T(8,128)(2,1)S(1)}, u32[]{:S(2)}, u32[]{:S(2)}) %collective-permute-start.46) | collective-permute-done | bytes 1048608 | tf_op jit(solution)/shard_map/ppermute | solution.py:105
  473.0 14.3 %collective-permute-done.49 = bf16[256,2048]{1,0:T(8,128)(2,1)S(1)} collective-permute-done((bf16[256,2048]{1,0:T(8,128)(2,1)S(1)}, bf16[256,2048]{1,0:T(8,128)(2,1)S(1)}, u32[]{:S(2)}, u32[]{:S(2)}) %collective-permute-start.49) | collective-permute-done | bytes 1048608 | tf_op jit(solution)/shard_map/ppermute | solution.py:105
  495.7 9.4 feed_back.6
  505.1 12.3 %collective-permute-done.52 = bf16[256,2048]{1,0:T(8,128)(2,1)S(1)} collective-permute-done((bf16[256,2048]{1,0:T(8,128)(2,1)S(1)}, bf16[256,2048]{1,0:T(8,128)(2,1)S(1)}, u32[]{:S(2)}, u32[]{:S(2)}) %collective-permute-start.52) | collective-permute-done | bytes 1048608 | tf_op jit(solution)/shard_map/ppermute | solution.py:105
  527.4 9.5 feed_back.7
  538.0 10.9 %collective-permute-done.55 = bf16[256,2048]{1,0:T(8,128)(2,1)S(1)} collective-permute-done((bf16[256,2048]{1,0:T(8,128)(2,1)S(1)}, bf16[256,2048]{1,0:T(8,128)(2,1)S(1)}, u32[]{:S(2)}, u32[]{:S(2)}) %collective-permute-start.55) | collective-permute-done | bytes 1048608 | tf_op jit(solution)/shard_map/ppermute | solution.py:105
  557.9 9.4 feed_back.8
  579.1 22.2 %convolution_convert_fusion.1 = bf16[2048,2048]{1,0:T(8,128)(2,1)} fusion(bf16[2048,2048]{1,0:T(8,128)(2,1)S(1)} %bitcast.214, bf16[2048,2048]{1,0:T(8,128)(2,1)} %get-tuple-element.376), kind=kOutput, calls=%fused_computation.2 | convolution fusion | flops 17184063488 | bytes 25165824 | tf_op jit(solution)/shard_map/dot_general | solution.py:266
  605.6 6.6 add_convert_fusion.12
  616.1 13.3 %convolution_convert_fusion.2 = bf16[1024,2048]{1,0:T(8,128)(2,1)} fusion(bf16[2048,1024]{1,0:T(8,128)(2,1)S(1)} %copy-done.24, bf16[2048,2048]{1,0:T(8,128)(2,1)} %get-tuple-element.383), kind=kOutput, calls=%fused_computation.4 | convolution fusion | flops 8592031744 | bytes 16777216 | tf_op jit(solution)/shard_map/dot_general | solution.py:266
  649.3 18.8 %collective-permute-done.66 = bf16[256,2048]{1,0:T(8,128)(2,1)S(1)} collective-permute-done((bf16[256,2048]{1,0:T(8,128)(2,1)S(1)}, bf16[256,2048]{1,0:T(8,128)(2,1)S(1)}, u32[]{:S(2)}, u32[]{:S(2)}) %collective-permute-start.66) | collective-permute-done | bytes 1048608 | tf_op jit(solution)/shard_map/ppermute | solution.py:105
  683.9 5.6 convolution_convert_fusion
  698.1 8.4 collective-permute-done.70.refs_2_
  706.5 9.7 collective-permute-done.71.refs_3_
  718.6 6.0 join.1
  735.8 18.5 %attend_back.1 = (f32[2048,256]{1,0:T(8,128)}, f32[2048,256]{1,0:T(8,128)}, f32[2048,256]{1,0:T(8,128)}) custom-call(s32[4]{0:T(128)S(1)} %copy-done.23, s32[1,2048]{1,0:T(1,128)S(1)} %bitcast.209, bf16[2048,256]{1,0:T(8,128)(2,1)S(1)} %copy-done.13, bf16[2048,256]{1,0:T(8,128)(2,1)S(1)} %copy-done.14, bf16[2048,256]{1,0:T(8,128)(2,1)S(1)} %copy-done.15, ...), custom_call_target="tpu_custom_call" | custom-call | flops 25999998976 | bytes 78000000 | tf_op jit(solution)/shard_map/attend_back/pallas_call | solution.py:393
  754.3 7.4 unturn.1
  761.7 10.2 %collective-permute-done.76.refs_3_ = bf16[2,64,2048]{2,1,0:T(8,128)(2,1)S(1)} collective-permute-done((bf16[2,64,2048]{2,1,0:T(8,128)(2,1)}, bf16[2,64,2048]{2,1,0:T(8,128)(2,1)S(1)}, u32[]{:S(2)}, u32[]{:S(2)}) %collective-permute-start.76) | collective-permute-done | bytes 524320 | tf_op jit(solution)/shard_map/ppermute | solution.py:58
  772.6 9.5 collective-permute-start.78
  793.9 7.2 finish.1
  804.1 10.5 %collective-permute-done.82 = bf16[64,2048]{1,0:T(8,128)(2,1)S(1)} collective-permute-done((bf16[64,2048]{1,0:T(8,128)(2,1)S(1)}, bf16[64,2048]{1,0:T(8,128)(2,1)S(1)}, u32[]{:S(2)}, u32[]{:S(2)}) %collective-permute-start.82) | collective-permute-done | bytes 262176 | tf_op jit(solution)/shard_map/ppermute | solution.py:58
  835.2 10.6 %convolution_convert_fusion.3 = bf16[2048,768]{1,0:T(8,128)(2,1)} fusion(bf16[2048,2048]{1,0:T(8,128)(2,1)} %bitcast.34.in_ref, bf16[2048,768]{1,0:T(8,128)(2,1)S(1)} %copy-done.33), kind=kOutput, calls=%fused_computation.5 | convolution fusion | flops 6444023808 | bytes 14680064 | tf_op jit(solution)/shard_map/dot_general | solution.py:266
  876.4 14.8 %collective-permute-done.89 = bf16[256,2048]{1,0:T(8,128)(2,1)} collective-permute-done((bf16[256,2048]{1,0:T(8,128)(2,1)}, bf16[256,2048]{1,0:T(8,128)(2,1)}, u32[]{:S(2)}, u32[]{:S(2)}) %collective-permute-start.89) | collective-permute-done | bytes 1048608 | tf_op jit(solution)/shard_map/ppermute | solution.py:105
  891.2 9.4 reduce-scatter.9.cloned.1.call-done
  919.0 18.5 %collective-permute-done.96 = f32[5,2048]{1,0:T(8,128)S(1)} collective-permute-done((f32[5,2048]{1,0:T(8,128)S(1)}, f32[5,2048]{1,0:T(8,128)S(1)}, u32[]{:S(2)}, u32[]{:S(2)}) %collective-permute-start.96) | collective-permute-done | bytes 40992 | tf_op jit(solution)/shard_map/ppermute | solution.py:968
  950.5 6.1 collect.3
  (504 shorter events, 412.6 us)
Async XLA Ops:
  7.2 70.2 %all-gather.5.cloned.1.call-start = ((), (), s32[]{:S(2)}) async-start(), calls=%async_computation.4 | async-start | bytes 5242880 | tf_op jit(solution)/shard_map/all_gather | solution.py:796
  7.9 129.0 %all-gather.7.cloned.1.call-start = ((), (), s32[]{:S(2)}) async-start(), calls=%async_computation.5 | async-start | bytes 3932160 | tf_op jit(solution)/shard_map/all_gather | solution.py:810
  7.9 27.7 %collective-permute-start = (bf16[256,2048]{1,0:T(8,128)(2,1)}, bf16[256,2048]{1,0:T(8,128)(2,1)S(1)}, u32[]{:S(2)}, u32[]{:S(2)}) collective-permute-start(bf16[256,2048]{1,0:T(8,128)(2,1)} %bitcast.223), channel_id=1, source_target_pairs={{0,2},{2,4},{4,6},{1,3},{3,5},{5,7},{8,10},{10,12},{12,14},{9,11},... | collective-permute-start | bytes 3145736 | tf_op jit(solution)/shard_map/ppermute | solution.py:105
  13.0 26.7 %collective-permute-start.1 = (bf16[256,2048]{1,0:T(8,128)(2,1)}, bf16[256,2048]{1,0:T(8,128)(2,1)S(1)}, u32[]{:S(2)}, u32[]{:S(2)}) collective-permute-start(bf16[256,2048]{1,0:T(8,128)(2,1)} %bitcast.224), channel_id=1, source_target_pairs={{2,0},{4,2},{6,4},{3,1},{5,3},{7,5},{10,8},{12,10},{14,12},{11,9},... | collective-permute-start | bytes 3145736 | tf_op jit(solution)/shard_map/ppermute | solution.py:105
  14.3 25.4 %collective-permute-start.2 = (bf16[256,2048]{1,0:T(8,128)(2,1)}, bf16[256,2048]{1,0:T(8,128)(2,1)}, u32[]{:S(2)}, u32[]{:S(2)}) collective-permute-start(bf16[256,2048]{1,0:T(8,128)(2,1)} %bitcast.225), channel_id=1, source_target_pairs={{0,1},{1,0},{2,3},{3,2},{4,5},{5,4},{6,7},{7,6},{8,9},{9,8},{10,11... | collective-permute-start | bytes 3145736 | tf_op jit(solution)/shard_map/ppermute | solution.py:62
  39.7 25.2 %collective-permute-start.6 = (bf16[2,64,768]{2,1,0:T(8,128)(2,1)S(1)}, bf16[2,64,768]{2,1,0:T(8,128)(2,1)S(1)}, u32[]{:S(2)}, u32[]{:S(2)}) collective-permute-start(bf16[2,64,768]{2,1,0:T(8,128)(2,1)S(1)} %get-tuple-element.533), channel_id=1, source_target_pairs={{0,2},{2,0},{4,6},{6,4},{1,3},{3,1},{5,7},{7,5},{8,10},{10,8},{12,... | collective-permute-start | bytes 589832 | tf_op jit(solution)/shard_map/ppermute | solution.py:58
  44.2 31.0 %collective-permute-start.4 = (bf16[256,2048]{1,0:T(8,128)(2,1)S(1)}, bf16[256,2048]{1,0:T(8,128)(2,1)}, u32[]{:S(2)}, u32[]{:S(2)}) collective-permute-start(bf16[256,2048]{1,0:T(8,128)(2,1)S(1)} %collective-permute-done), channel_id=1, source_target_pairs={{0,2},{2,4},{4,6},{1,3},{3,5},{5,7},{8,10},{10,12},{12,14},{9,11},... | collective-permute-start | bytes 3145736 | tf_op jit(solution)/shard_map/ppermute | solution.py:105
  47.7 29.7 %collective-permute-start.5 = (bf16[256,2048]{1,0:T(8,128)(2,1)S(1)}, bf16[256,2048]{1,0:T(8,128)(2,1)}, u32[]{:S(2)}, u32[]{:S(2)}) collective-permute-start(bf16[256,2048]{1,0:T(8,128)(2,1)S(1)} %collective-permute-done.1), channel_id=1, source_target_pairs={{2,0},{4,2},{6,4},{3,1},{5,3},{7,5},{10,8},{12,10},{14,12},{11,9},... | collective-permute-start | bytes 3145736 | tf_op jit(solution)/shard_map/ppermute | solution.py:105
  65.0 32.6 %collective-permute-start.11 = (bf16[256,2048]{1,0:T(8,128)(2,1)}, bf16[256,2048]{1,0:T(8,128)(2,1)}, u32[]{:S(2)}, u32[]{:S(2)}) collective-permute-start(bf16[256,2048]{1,0:T(8,128)(2,1)} %get-tuple-element.474), channel_id=1, source_target_pairs={{0,1},{1,0},{2,3},{3,2},{4,5},{5,4},{6,7},{7,6},{8,9},{9,8},{10,11... | collective-permute-start | bytes 3145736 | tf_op jit(solution)/shard_map/ppermute | solution.py:62
  79.4 131.4 %all-gather.9.cloned.1.call-start = ((), (), s32[]{:S(2)}) async-start(), calls=%async_computation.6 | async-start | bytes 5242880 | tf_op jit(solution)/shard_map/all_gather | solution.py:819
  85.6 30.2 %collective-permute-start.10 = (bf16[256,2048]{1,0:T(8,128)(2,1)}, bf16[256,2048]{1,0:T(8,128)(2,1)}, u32[]{:S(2)}, u32[]{:S(2)}) collective-permute-start(bf16[256,2048]{1,0:T(8,128)(2,1)} %collective-permute-done.5), channel_id=1, source_target_pairs={{2,0},{4,2},{6,4},{3,1},{5,3},{7,5},{10,8},{12,10},{14,12},{11,9},... | collective-permute-start | bytes 3145736 | tf_op jit(solution)/shard_map/ppermute | solution.py:105
  86.9 30.1 %collective-permute-start.9 = (bf16[256,2048]{1,0:T(8,128)(2,1)}, bf16[256,2048]{1,0:T(8,128)(2,1)}, u32[]{:S(2)}, u32[]{:S(2)}) collective-permute-start(bf16[256,2048]{1,0:T(8,128)(2,1)} %collective-permute-done.4), channel_id=1, source_target_pairs={{0,2},{2,4},{4,6},{1,3},{3,5},{5,7},{8,10},{10,12},{12,14},{9,11},... | collective-permute-start | bytes 3145736 | tf_op jit(solution)/shard_map/ppermute | solution.py:105
  154.0 153.7 %all-gather.11.cloned.1.call-start = ((), (), s32[]{:S(2)}) async-start(), calls=%async_computation.7 | async-start | bytes 10485760 | tf_op jit(solution)/shard_map/all_gather | solution.py:832
  167.5 28.0 %collective-permute-start.22 = (bf16[2,64,2048]{2,1,0:T(8,128)(2,1)}, bf16[2,64,2048]{2,1,0:T(8,128)(2,1)S(1)}, u32[]{:S(2)}, u32[]{:S(2)}) collective-permute-start(bf16[2,64,2048]{2,1,0:T(8,128)(2,1)} %get-tuple-element.505), channel_id=1, source_target_pairs={{0,2},{2,0},{4,6},{6,4},{1,3},{3,1},{5,7},{7,5},{8,10},{10,8},{12,... | collective-permute-start | bytes 1572872 | tf_op jit(solution)/shard_map/ppermute | solution.py:58
  169.5 38.4 %collective-permute-start.23 = (bf16[2,64,2048]{2,1,0:T(8,128)(2,1)}, bf16[2,64,2048]{2,1,0:T(8,128)(2,1)S(1)}, u32[]{:S(2)}, u32[]{:S(2)}) collective-permute-start(bf16[2,64,2048]{2,1,0:T(8,128)(2,1)} %get-tuple-element.504), channel_id=1, source_target_pairs={{0,4},{2,6},{4,0},{6,2},{1,5},{3,7},{5,1},{7,3},{8,12},{10,14},{12... | collective-permute-start | bytes 1572872 | tf_op jit(solution)/shard_map/ppermute | solution.py:58
  170.4 37.5 %collective-permute-start.24 = (bf16[2,64,2048]{2,1,0:T(8,128)(2,1)}, bf16[2,64,2048]{2,1,0:T(8,128)(2,1)S(1)}, u32[]{:S(2)}, u32[]{:S(2)}) collective-permute-start(bf16[2,64,2048]{2,1,0:T(8,128)(2,1)} %get-tuple-element.503), channel_id=1, source_target_pairs={{0,6},{2,4},{4,2},{6,0},{1,7},{3,5},{5,3},{7,1},{8,14},{10,12},{12... | collective-permute-start | bytes 1572872 | tf_op jit(solution)/shard_map/ppermute | solution.py:58
  213.2 476.3 %reduce-scatter.5.cloned.1.call-start = ((), (), s32[]{:S(2)}) async-start(), calls=%async_computation.8 | async-start | bytes 10485760 | tf_op jit(solution)/shard_map/reduce_scatter | solution.py:743
  252.2 29.4 %collective-permute-start.29 = (bf16[256,2048]{1,0:T(8,128)(2,1)S(1)}, bf16[256,2048]{1,0:T(8,128)(2,1)}, u32[]{:S(2)}, u32[]{:S(2)}) collective-permute-start(bf16[256,2048]{1,0:T(8,128)(2,1)S(1)} %fusion.7.refs_0_), channel_id=1, source_target_pairs={{0,2},{2,4},{4,6},{1,3},{3,5},{5,7},{8,10},{10,12},{12,14},{9,11},... | collective-permute-start | bytes 3145736 | tf_op jit(solution)/shard_map/ppermute | solution.py:105
  260.6 26.3 %collective-permute-start.30 = (bf16[256,2048]{1,0:T(8,128)(2,1)S(1)}, bf16[256,2048]{1,0:T(8,128)(2,1)}, u32[]{:S(2)}, u32[]{:S(2)}) collective-permute-start(bf16[256,2048]{1,0:T(8,128)(2,1)S(1)} %fusion.7.refs_0_), channel_id=1, source_target_pairs={{2,0},{4,2},{6,4},{3,1},{5,3},{7,5},{10,8},{12,10},{14,12},{11,9},... | collective-permute-start | bytes 3145736 | tf_op jit(solution)/shard_map/ppermute | solution.py:105
  288.7 28.1 %collective-permute-start.34 = (bf16[256,2048]{1,0:T(8,128)(2,1)S(1)}, bf16[256,2048]{1,0:T(8,128)(2,1)}, u32[]{:S(2)}, u32[]{:S(2)}) collective-permute-start(bf16[256,2048]{1,0:T(8,128)(2,1)S(1)} %broadcast_select_fusion.5.refs_0_), channel_id=1, source_target_pairs={{0,1},{1,0},{2,3},{3,2},{4,5},{5,4},{6,7},{7,6},{8,9},{9,8},{10,11... | collective-permute-start | bytes 3145736 | tf_op jit(solution)/shard_map/ppermute | solution.py:62
  288.8 28.0 %collective-permute-start.32 = (bf16[256,2048]{1,0:T(8,128)(2,1)}, bf16[256,2048]{1,0:T(8,128)(2,1)}, u32[]{:S(2)}, u32[]{:S(2)}) collective-permute-start(bf16[256,2048]{1,0:T(8,128)(2,1)} %collective-permute-done.29), channel_id=1, source_target_pairs={{0,2},{2,4},{4,6},{1,3},{3,5},{5,7},{8,10},{10,12},{12,14},{9,11},... | collective-permute-start | bytes 3145736 | tf_op jit(solution)/shard_map/ppermute | solution.py:105
  292.2 27.5 %collective-permute-start.33 = (bf16[256,2048]{1,0:T(8,128)(2,1)}, bf16[256,2048]{1,0:T(8,128)(2,1)}, u32[]{:S(2)}, u32[]{:S(2)}) collective-permute-start(bf16[256,2048]{1,0:T(8,128)(2,1)} %collective-permute-done.30), channel_id=1, source_target_pairs={{2,0},{4,2},{6,4},{3,1},{5,3},{7,5},{10,8},{12,10},{14,12},{11,9},... | collective-permute-start | bytes 3145736 | tf_op jit(solution)/shard_map/ppermute | solution.py:105
  324.8 27.5 %collective-permute-start.36 = (bf16[256,2048]{1,0:T(8,128)(2,1)}, bf16[256,2048]{1,0:T(8,128)(2,1)S(1)}, u32[]{:S(2)}, u32[]{:S(2)}) collective-permute-start(bf16[256,2048]{1,0:T(8,128)(2,1)} %collective-permute-done.33), channel_id=1, source_target_pairs={{2,0},{4,2},{6,4},{3,1},{5,3},{7,5},{10,8},{12,10},{14,12},{11,9},... | collective-permute-start | bytes 3145736 | tf_op jit(solution)/shard_map/ppermute | solution.py:105
  371.2 26.6 %collective-permute-start.40 = (bf16[256,2048]{1,0:T(8,128)(2,1)S(1)}, bf16[256,2048]{1,0:T(8,128)(2,1)S(1)}, u32[]{:S(2)}, u32[]{:S(2)}) collective-permute-start(bf16[256,2048]{1,0:T(8,128)(2,1)S(1)} %add_convert_fusion.23), channel_id=1, source_target_pairs={{0,2},{1,3},{8,10},{9,11},{16,18},{17,19},{24,26},{25,27}} | collective-permute-start | bytes 3145736 | tf_op jit(solution)/shard_map/ppermute | solution.py:105
  376.5 28.7 %collective-permute-start.45 = (bf16[256,2048]{1,0:T(8,128)(2,1)S(1)}, bf16[256,2048]{1,0:T(8,128)(2,1)S(1)}, u32[]{:S(2)}, u32[]{:S(2)}) collective-permute-start(bf16[256,2048]{1,0:T(8,128)(2,1)S(1)} %get-tuple-element.338), channel_id=1, source_target_pairs={{0,1},{1,0},{2,3},{3,2},{4,5},{5,4},{6,7},{7,6},{8,9},{9,8},{10,11... | collective-permute-start | bytes 3145736 | tf_op jit(solution)/shard_map/ppermute | solution.py:62
  400.0 26.3 %collective-permute-start.43 = (bf16[256,2048]{1,0:T(8,128)(2,1)S(1)}, bf16[256,2048]{1,0:T(8,128)(2,1)S(1)}, u32[]{:S(2)}, u32[]{:S(2)}) collective-permute-start(bf16[256,2048]{1,0:T(8,128)(2,1)S(1)} %get-tuple-element.502), channel_id=1, source_target_pairs={{0,2},{2,4},{1,3},{3,5},{8,10},{10,12},{9,11},{11,13},{16,18},{18,... | collective-permute-start | bytes 3145736 | tf_op jit(solution)/shard_map/ppermute | solution.py:105
  405.2 33.9 %collective-permute-start.48 = (bf16[256,2048]{1,0:T(8,128)(2,1)S(1)}, bf16[256,2048]{1,0:T(8,128)(2,1)S(1)}, u32[]{:S(2)}, u32[]{:S(2)}) collective-permute-start(bf16[256,2048]{1,0:T(8,128)(2,1)S(1)} %get-tuple-element.343), channel_id=1, source_target_pairs={{0,1},{1,0},{2,3},{3,2},{4,5},{5,4},{6,7},{7,6},{8,9},{9,8},{10,11... | collective-permute-start | bytes 3145736 | tf_op jit(solution)/shard_map/ppermute | solution.py:62
  428.4 29.3 %collective-permute-start.46 = (bf16[256,2048]{1,0:T(8,128)(2,1)S(1)}, bf16[256,2048]{1,0:T(8,128)(2,1)S(1)}, u32[]{:S(2)}, u32[]{:S(2)}) collective-permute-start(bf16[256,2048]{1,0:T(8,128)(2,1)S(1)} %get-tuple-element.500), channel_id=1, source_target_pairs={{0,2},{2,4},{4,6},{1,3},{3,5},{5,7},{8,10},{10,12},{12,14},{9,11},... | collective-permute-start | bytes 3145736 | tf_op jit(solution)/shard_map/ppermute | solution.py:105
  492.2 25.2 %collective-permute-start.52 = (bf16[256,2048]{1,0:T(8,128)(2,1)S(1)}, bf16[256,2048]{1,0:T(8,128)(2,1)S(1)}, u32[]{:S(2)}, u32[]{:S(2)}) collective-permute-start(bf16[256,2048]{1,0:T(8,128)(2,1)S(1)} %collective-permute-done.49), channel_id=1, source_target_pairs={{0,2},{2,4},{4,6},{1,3},{3,5},{5,7},{8,10},{10,12},{12,14},{9,11},... | collective-permute-start | bytes 3145736 | tf_op jit(solution)/shard_map/ppermute | solution.py:105
  494.4 27.2 %collective-permute-start.53 = (bf16[256,2048]{1,0:T(8,128)(2,1)S(1)}, bf16[256,2048]{1,0:T(8,128)(2,1)S(1)}, u32[]{:S(2)}, u32[]{:S(2)}) collective-permute-start(bf16[256,2048]{1,0:T(8,128)(2,1)S(1)} %collective-permute-done.50), channel_id=1, source_target_pairs={{2,0},{4,2},{6,4},{3,1},{5,3},{7,5},{10,8},{12,10},{14,12},{11,9},... | collective-permute-start | bytes 3145736 | tf_op jit(solution)/shard_map/ppermute | solution.py:105
  523.7 25.2 %collective-permute-start.55 = (bf16[256,2048]{1,0:T(8,128)(2,1)S(1)}, bf16[256,2048]{1,0:T(8,128)(2,1)S(1)}, u32[]{:S(2)}, u32[]{:S(2)}) collective-permute-start(bf16[256,2048]{1,0:T(8,128)(2,1)S(1)} %collective-permute-done.52), channel_id=1, source_target_pairs={{0,2},{2,4},{4,6},{1,3},{3,5},{5,7},{8,10},{10,12},{12,14},{9,11},... | collective-permute-start | bytes 3145736 | tf_op jit(solution)/shard_map/ppermute | solution.py:105
  525.9 27.2 %collective-permute-start.56 = (bf16[256,2048]{1,0:T(8,128)(2,1)S(1)}, bf16[256,2048]{1,0:T(8,128)(2,1)S(1)}, u32[]{:S(2)}, u32[]{:S(2)}) collective-permute-start(bf16[256,2048]{1,0:T(8,128)(2,1)S(1)} %collective-permute-done.53), channel_id=1, source_target_pairs={{2,0},{4,2},{6,4},{3,1},{5,3},{7,5},{10,8},{12,10},{14,12},{11,9},... | collective-permute-start | bytes 3145736 | tf_op jit(solution)/shard_map/ppermute | solution.py:105
  572.2 29.1 %collective-permute-start.62 = (bf16[256,2048]{1,0:T(8,128)(2,1)}, bf16[256,2048]{1,0:T(8,128)(2,1)}, u32[]{:S(2)}, u32[]{:S(2)}) collective-permute-start(bf16[256,2048]{1,0:T(8,128)(2,1)} %get-tuple-element.374), channel_id=1, source_target_pairs={{0,1},{1,0},{2,3},{3,2},{4,5},{5,4},{6,7},{7,6},{8,9},{9,8},{10,11... | collective-permute-start | bytes 3145736 | tf_op jit(solution)/shard_map/ppermute | solution.py:62
  573.9 29.9 %collective-permute-start.60 = (bf16[256,2048]{1,0:T(8,128)(2,1)}, bf16[256,2048]{1,0:T(8,128)(2,1)}, u32[]{:S(2)}, u32[]{:S(2)}) collective-permute-start(bf16[256,2048]{1,0:T(8,128)(2,1)} %add_convert_fusion.15), channel_id=1, source_target_pairs={{0,2},{1,3},{8,10},{9,11},{16,18},{17,19},{24,26},{25,27}} | collective-permute-start | bytes 3145736 | tf_op jit(solution)/shard_map/ppermute | solution.py:105
  577.0 26.8 %collective-permute-start.61 = (bf16[256,2048]{1,0:T(8,128)(2,1)}, bf16[256,2048]{1,0:T(8,128)(2,1)}, u32[]{:S(2)}, u32[]{:S(2)}) collective-permute-start(bf16[256,2048]{1,0:T(8,128)(2,1)} %add_convert_fusion.15), channel_id=1, source_target_pairs={{6,4},{7,5},{14,12},{15,13},{22,20},{23,21},{30,28},{31,29}} | collective-permute-start | bytes 3145736 | tf_op jit(solution)/shard_map/ppermute | solution.py:105
  603.9 185.0 %reduce-scatter.7.cloned.1.call-start = ((), (), s32[]{:S(2)}) async-start(), calls=%async_computation.9 | async-start | bytes 5242880 | tf_op jit(solution)/shard_map/reduce_scatter | solution.py:743
  605.1 42.5 %collective-permute-start.68 = (bf16[256,2048]{1,0:T(8,128)(2,1)S(1)}, bf16[256,2048]{1,0:T(8,128)(2,1)}, u32[]{:S(2)}, u32[]{:S(2)}) collective-permute-start(bf16[256,2048]{1,0:T(8,128)(2,1)S(1)} %copy-done.17), channel_id=1, source_target_pairs={{0,1},{1,0},{2,3},{3,2},{4,5},{5,4},{6,7},{7,6},{8,9},{9,8},{10,11... | collective-permute-start | bytes 3145736 | tf_op jit(solution)/shard_map/ppermute | solution.py:62
  641.3 26.7 %collective-permute-start.66 = (bf16[256,2048]{1,0:T(8,128)(2,1)S(1)}, bf16[256,2048]{1,0:T(8,128)(2,1)S(1)}, u32[]{:S(2)}, u32[]{:S(2)}) collective-permute-start(bf16[256,2048]{1,0:T(8,128)(2,1)S(1)} %get-tuple-element.496), channel_id=1, source_target_pairs={{0,2},{2,4},{4,6},{1,3},{3,5},{5,7},{8,10},{10,12},{12,14},{9,11},... | collective-permute-start | bytes 3145736 | tf_op jit(solution)/shard_map/ppermute | solution.py:105
  646.1 26.1 %collective-permute-start.67 = (bf16[256,2048]{1,0:T(8,128)(2,1)S(1)}, bf16[256,2048]{1,0:T(8,128)(2,1)S(1)}, u32[]{:S(2)}, u32[]{:S(2)}) collective-permute-start(bf16[256,2048]{1,0:T(8,128)(2,1)S(1)} %get-tuple-element.495), channel_id=1, source_target_pairs={{2,0},{4,2},{6,4},{3,1},{5,3},{7,5},{10,8},{12,10},{14,12},{11,9},... | collective-permute-start | bytes 3145736 | tf_op jit(solution)/shard_map/ppermute | solution.py:105
  725.4 151.0 %reduce-scatter.11.cloned.1.call-start = ((), (), s32[]{:S(2)}) async-start(), calls=%async_computation.11 | async-start | bytes 5242880 | tf_op jit(solution)/shard_map/reduce_scatter | solution.py:743
  728.1 33.6 %collective-permute-start.75 = (bf16[2,64,2048]{2,1,0:T(8,128)(2,1)}, bf16[2,64,2048]{2,1,0:T(8,128)(2,1)S(1)}, u32[]{:S(2)}, u32[]{:S(2)}) collective-permute-start(bf16[2,64,2048]{2,1,0:T(8,128)(2,1)} %get-tuple-element.491), channel_id=1, source_target_pairs={{0,2},{2,0},{4,6},{6,4},{1,3},{3,1},{5,7},{7,5},{8,10},{10,8},{12,... | collective-permute-start | bytes 1572872 | tf_op jit(solution)/shard_map/ppermute | solution.py:58
  733.4 38.4 %collective-permute-start.76 = (bf16[2,64,2048]{2,1,0:T(8,128)(2,1)}, bf16[2,64,2048]{2,1,0:T(8,128)(2,1)S(1)}, u32[]{:S(2)}, u32[]{:S(2)}) collective-permute-start(bf16[2,64,2048]{2,1,0:T(8,128)(2,1)} %get-tuple-element.490), channel_id=1, source_target_pairs={{0,4},{2,6},{4,0},{6,2},{1,5},{3,7},{5,1},{7,3},{8,12},{10,14},{12... | collective-permute-start | bytes 1572872 | tf_op jit(solution)/shard_map/ppermute | solution.py:58
  733.4 38.4 %collective-permute-start.77 = (bf16[2,64,2048]{2,1,0:T(8,128)(2,1)}, bf16[2,64,2048]{2,1,0:T(8,128)(2,1)S(1)}, u32[]{:S(2)}, u32[]{:S(2)}) collective-permute-start(bf16[2,64,2048]{2,1,0:T(8,128)(2,1)} %get-tuple-element.489), channel_id=1, source_target_pairs={{0,6},{2,4},{4,2},{6,0},{1,7},{3,5},{5,3},{7,1},{8,14},{10,12},{12... | collective-permute-start | bytes 1572872 | tf_op jit(solution)/shard_map/ppermute | solution.py:58
  771.9 128.8 %reduce-scatter.9.cloned.1.call-start = ((), (), s32[]{:S(2)}) async-start(), calls=%async_computation.10 | async-start | bytes 3932160 | tf_op jit(solution)/shard_map/reduce_scatter | solution.py:743
  801.1 49.1 %collective-permute-start.88 = (bf16[64,2048]{1,0:T(8,128)(2,1)}, bf16[64,2048]{1,0:T(8,128)(2,1)}, u32[]{:S(2)}, u32[]{:S(2)}) collective-permute-start(bf16[64,2048]{1,0:T(8,128)(2,1)} %get-tuple-element.509), channel_id=1, source_target_pairs={{0,6},{2,4},{4,2},{6,0},{1,7},{3,5},{5,3},{7,1},{8,14},{10,12},{12... | collective-permute-start | bytes 786440 | tf_op jit(solution)/shard_map/ppermute | solution.py:58
  863.5 27.8 %collective-permute-start.89 = (bf16[256,2048]{1,0:T(8,128)(2,1)}, bf16[256,2048]{1,0:T(8,128)(2,1)}, u32[]{:S(2)}, u32[]{:S(2)}) collective-permute-start(bf16[256,2048]{1,0:T(8,128)(2,1)} %get-tuple-element.488), channel_id=1, source_target_pairs={{0,2},{2,4},{1,3},{3,5},{8,10},{10,12},{9,11},{11,13},{16,18},{18,... | collective-permute-start | bytes 3145736 | tf_op jit(solution)/shard_map/ppermute | solution.py:105
  905.9 31.6 %collective-permute-start.93 = (bf16[256,2048]{1,0:T(8,128)(2,1)}, bf16[256,2048]{1,0:T(8,128)(2,1)S(1)}, u32[]{:S(2)}, u32[]{:S(2)}) collective-permute-start(bf16[256,2048]{1,0:T(8,128)(2,1)} %get-tuple-element.486), channel_id=1, source_target_pairs={{0,2},{2,4},{4,6},{1,3},{3,5},{5,7},{8,10},{10,12},{12,14},{9,11},... | collective-permute-start | bytes 3145736 | tf_op jit(solution)/shard_map/ppermute | solution.py:105
  909.3 28.1 %collective-permute-start.94 = (bf16[256,2048]{1,0:T(8,128)(2,1)}, bf16[256,2048]{1,0:T(8,128)(2,1)}, u32[]{:S(2)}, u32[]{:S(2)}) collective-permute-start(bf16[256,2048]{1,0:T(8,128)(2,1)} %get-tuple-element.485), channel_id=1, source_target_pairs={{2,0},{4,2},{6,4},{3,1},{5,3},{7,5},{10,8},{12,10},{14,12},{11,9},... | collective-permute-start | bytes 3145736 | tf_op jit(solution)/shard_map/ppermute | solution.py:105
  (144 other events, 2419.8 us)
Sparse Core Ops, SparseCore 0:
  9.8 55.3 all-gather.4
  79.5 48.4 all-gather.6
  154.1 56.6 all-gather.8
  213.4 94.3 all-gather.10
  604.0 84.1 reduce-scatter.4
  725.5 54.7 reduce-scatter.6
  783.2 52.6 reduce-scatter.10
  855.9 44.6 reduce-scatter.8

commit v6 on v5

--- a/solution.py
+++ b/solution.py
@@ -152,6 +152,11 @@
                 j = i + step * far
                 known = 0 <= j < self.count
                 wanted[step].append(int(np.argmax(self.order[i] == j)) if known else None)
+        used = sorted({w for side in wanted.values() for w in side if w is not None})
+        if last[1] is not None and len(used) == 2:
+            flags = [[int(w == used[1]) for w in wanted[step]] for step in (1, -1)]
+            flags = jnp.asarray(np.array(flags, dtype=np.int32))[:, self.place]
+            return combine(flags, made[used[0]], made[used[1]], last[1], last[-1])
         values = []
         for step in (1, -1):
             value = self.choose(made, wanted[step])
@@ -183,6 +188,27 @@
         return total, tied
 
 
+def combine_kernel(flag_ref, one_ref, two_ref, right_ref, left_ref, right_out, left_out):
+    for i, (last, out) in enumerate(((right_ref, right_out), (left_ref, left_out))):
+        chosen = jnp.where(flag_ref[i] == 0, one_ref[...], two_ref[...])
+        out[...] = (chosen.astype(f32) + last[...].astype(f32)).astype(bf16)
+
+
+def combine(flags, one, two, right, left):
+    rows, columns = one.shape
+    block = pl.BlockSpec((rows, columns), lambda i, flags: (0, 0))
+    return pl.pallas_call(
+        combine_kernel,
+        grid_spec=pltpu.PrefetchScalarGridSpec(
+            num_scalar_prefetch=1, grid=(1,), in_specs=[block] * 4, out_specs=[block] * 2
+        ),
+        out_shape=[jax.ShapeDtypeStruct((rows, columns), bf16)] * 2,
+        cost_estimate=cost(1),
+        compiler_params=pltpu.CompilerParams(vmem_limit_bytes=16 << 20),
+        name="combine",
+    )(flags, one, two, right, left)
+
+
 def scatter_sum(for_same, for_other):
     return (for_same.astype(f32) + swap(for_other.astype(bf16)).astype(f32)).astype(bf16)
 
@@ -288,32 +314,41 @@
     return (key_place >= starts) & (key_place <= query_place)
 
 
+def heads_of(width):
+    return [slice(h, h + HEAD_DIM) for h in range(0, width, HEAD_DIM)]
+
+
 def attend_kernel(low_ref, starts_ref, q_ref, k_ref, v_ref, out_ref, log_ref):
-    block = pl.program_id(1)
+    block = pl.program_id(0)
     bq, bk = q_ref.shape[0], BLOCK_K
-    queries, starts = q_ref[...], starts_ref[...]
+    starts, heads = starts_ref[...], heads_of(q_ref.shape[1])
 
     def step(j, carry):
-        top, total, acc = carry
         rows = pl.ds(pl.multiple_of(j * bk, bk), bk)
-        scores = product_right(k_ref[rows, :], queries) * scale_factor
-        ok = allowed_keys(scores.shape, j * bk, block * bq, starts)
-        scores = jnp.where(ok, scores, masked_score)
-        new_top = jnp.maximum(top, jnp.max(scores, axis=0, keepdims=True))
-        ratio = jnp.exp(top - new_top)
-        expanded = jnp.exp(scores - new_top)
-        total = total * ratio + jnp.sum(expanded, axis=0, keepdims=True)
-        acc = acc * ratio + product_left(v_ref[rows, :], expanded.astype(bf16))
-        return (new_top, total, acc)
+        ok = allowed_keys((bk, bq), j * bk, block * bq, starts)
+        results = []
+        for head, (top, total, acc) in zip(heads, carry):
+            scores = product_right(k_ref[rows, head], q_ref[:, head]) * scale_factor
+            scores = jnp.where(ok, scores, masked_score)
+            new_top = jnp.maximum(top, jnp.max(scores, axis=0, keepdims=True))
+            ratio = jnp.exp(top - new_top)
+            expanded = jnp.exp(scores - new_top)
+            total = total * ratio + jnp.sum(expanded, axis=0, keepdims=True)
+            acc = acc * ratio + product_left(v_ref[rows, head], expanded.astype(bf16))
+            results.append((new_top, total, acc))
+        return tuple(results)
 
     init = (
         jnp.full((1, bq), masked_score, f32),
         jnp.zeros((1, bq), f32),
         jnp.zeros((HEAD_DIM, bq), f32),
     )
-    top, total, acc = lax.fori_loop(low_ref[block], (block * bq + bq) // bk, step, init)
-    out_ref[...] = (acc / total).T
-    log_ref[0] = top + jnp.log(total)
+    final = lax.fori_loop(
+        low_ref[block], (block * bq + bq) // bk, step, tuple(init for _ in heads)
+    )
+    for h, (head, (top, total, acc)) in enumerate(zip(heads, final)):
+        out_ref[:, head] = (acc / total).T
+        log_ref[h] = top + jnp.log(total)
 
 
 def in_hbm(*arrays):
@@ -324,27 +359,21 @@
     length, width = queries.shape
     queries, keys, values = in_hbm(queries, keys, values)
     heads, bq = width // HEAD_DIM, BLOCK_Q
+    whole = pl.BlockSpec((length, width), lambda i, low: (0, 0))
+    part = pl.BlockSpec((bq, width), lambda i, low: (i, 0))
     return pl.pallas_call(
         attend_kernel,
         grid_spec=pltpu.PrefetchScalarGridSpec(
             num_scalar_prefetch=1,
-            grid=(heads, length // bq),
-            in_specs=[
-                pl.BlockSpec((1, bq), lambda h, i, low: (0, i)),
-                pl.BlockSpec((bq, HEAD_DIM), lambda h, i, low: (i, h)),
-                pl.BlockSpec((length, HEAD_DIM), lambda h, i, low: (0, h)),
-                pl.BlockSpec((length, HEAD_DIM), lambda h, i, low: (0, h)),
-            ],
-            out_specs=[
-                pl.BlockSpec((bq, HEAD_DIM), lambda h, i, low: (i, h)),
-                pl.BlockSpec((1, 1, bq), lambda h, i, low: (h, 0, i)),
-            ],
+            grid=(length // bq,),
+            in_specs=[pl.BlockSpec((1, bq), lambda i, low: (0, i)), part, whole, whole],
+            out_specs=[part, pl.BlockSpec((heads, 1, bq), lambda i, low: (0, 0, i))],
         ),
         out_shape=[
             pltpu.HBM((length, width), f32),
             jax.ShapeDtypeStruct((heads, 1, length), f32),
         ],
-        compiler_params=pltpu.CompilerParams(vmem_limit_bytes=16 << 20),
+        compiler_params=pltpu.CompilerParams(vmem_limit_bytes=24 << 20),
         cost_estimate=cost(16),
         name="attend",
     )(lows, starts, queries, keys, values)
@@ -353,61 +382,68 @@
 def attend_back_kernel(
     low_ref, starts_ref, q_ref, k_ref, v_ref, out_ref, log_ref, grad_ref, dq_ref, dk_ref, dv_ref
 ):
-    length = q_ref.shape[0]
-    bq, bk = BLOCK_Q, BLOCK_K
-    dk_ref[...] = jnp.zeros_like(dk_ref)
-    dv_ref[...] = jnp.zeros_like(dv_ref)
-
-    def query_step(i, carry):
-        queries_at = pl.ds(pl.multiple_of(i * bq, bq), bq)
-        queries, grads = q_ref[queries_at, :], grad_ref[queries_at, :]
-        starts = starts_ref[:, queries_at]
-        log_total = log_ref[0, :, queries_at]
-        inner = jnp.sum((grads.astype(f32) * out_ref[queries_at, :]).T, axis=0, keepdims=True)
-
-        def step(j, acc):
-            rows = pl.ds(pl.multiple_of(j * bk, bk), bk)
-            keys = k_ref[rows, :]
+    block = pl.program_id(0)
+    bq, bk = q_ref.shape[0], BLOCK_K
+    starts, heads = starts_ref[...], heads_of(q_ref.shape[1])
+
+    @pl.when(block == 0)
+    def _():
+        dk_ref[...] = jnp.zeros_like(dk_ref)
+        dv_ref[...] = jnp.zeros_like(dv_ref)
+
+    inner = [
+        jnp.sum((grad_ref[:, head].astype(f32) * out_ref[:, head]).T, axis=0, keepdims=True)
+        for head in heads
+    ]
+
+    def step(j, carry):
+        rows = pl.ds(pl.multiple_of(j * bk, bk), bk)
+        ok = allowed_keys((bk, bq), j * bk, block * bq, starts)
+        results = []
+        for h, (head, acc) in enumerate(zip(heads, carry)):
+            keys, queries, grads = k_ref[rows, head], q_ref[:, head], grad_ref[:, head]
             scores = product_right(keys, queries) * scale_factor
-            ok = allowed_keys(scores.shape, j * bk, i * bq, starts)
-            probs = jnp.where(ok, jnp.exp(scores - log_total), 0.0)
-            dv_ref[rows, :] += product(probs.astype(bf16), grads)
-            prob_grad = product_right(v_ref[rows, :], grads)
-            score_grad = (probs * (prob_grad - inner)).astype(bf16)
-            dk_ref[rows, :] += product(score_grad, queries) * scale_factor
-            return acc + product_left(keys, score_grad)
-
-        acc = lax.fori_loop(
-            low_ref[i], (i * bq + bq) // bk, step, jnp.zeros((HEAD_DIM, bq), f32)
-        )
-        dq_ref[queries_at, :] = (acc * scale_factor).T
-        return carry
-
-    lax.fori_loop(0, length // bq, query_step, 0)
+            probs = jnp.where(ok, jnp.exp(scores - log_ref[h]), 0.0)
+            dv_ref[rows, head] += product(probs.astype(bf16), grads)
+            prob_grad = product_right(v_ref[rows, head], grads)
+            score_grad = (probs * (prob_grad - inner[h])).astype(bf16)
+            dk_ref[rows, head] += product(score_grad, queries) * scale_factor
+            results.append(acc + product_left(keys, score_grad))
+        return tuple(results)
+
+    final = lax.fori_loop(
+        low_ref[block],
+        (block * bq + bq) // bk,
+        step,
+        tuple(jnp.zeros((HEAD_DIM, bq), f32) for _ in heads),
+    )
+    for head, acc in zip(heads, final):
+        dq_ref[:, head] = (acc * scale_factor).T
 
 
 def attend_back(lows, starts, queries, keys, values, out, log_total, grads):
     length, width = queries.shape
-    heads = width // HEAD_DIM
-    column = pl.BlockSpec((length, HEAD_DIM), lambda h, low: (0, h))
+    heads, bq = width // HEAD_DIM, BLOCK_Q
+    whole = pl.BlockSpec((length, width), lambda i, low: (0, 0))
+    part = pl.BlockSpec((bq, width), lambda i, low: (i, 0))
     return pl.pallas_call(
         attend_back_kernel,
         grid_spec=pltpu.PrefetchScalarGridSpec(
             num_scalar_prefetch=1,
-            grid=(heads,),
+            grid=(length // bq,),
             in_specs=[
-                pl.BlockSpec((1, length), lambda h, low: (0, 0)),
-                column,
-                column,
-                column,
-                column,
-                pl.BlockSpec((1, 1, length), lambda h, low: (h, 0, 0)),
-                column,
+                pl.BlockSpec((1, bq), lambda i, low: (0, i)),
+                part,
+                whole,
+                whole,
+                part,
+                pl.BlockSpec((heads, 1, bq), lambda i, low: (0, 0, i)),
+                part,
             ],
-            out_specs=[column, column, column],
+            out_specs=[part, whole, whole],
         ),
         out_shape=[pltpu.HBM((length, width), f32)] * 3,
-        compiler_params=pltpu.CompilerParams(vmem_limit_bytes=28 << 20),
+        compiler_params=pltpu.CompilerParams(vmem_limit_bytes=32 << 20),
         cost_estimate=cost(26),
         name="attend_back",
     )(lows, starts, queries, keys, values, out, log_total, grads)

time: 989 us -> 980 us (level)
  other arithmetic: 107 us -> 76.5 us
  Pallas kernels: 172 us -> 189 us
  starting transfers between devices: 182 us -> 193 us
    convert_element_type x6 -> x0, other arithmetic: 26 us -> none  [hop_values(): values.append(value.astype(bf16))]
    pallas_call x0 -> x6, Pallas kernels: none -> 16.7 us  [combine(): pl.pallas_call(combine_kernel, grid_spec=pltpu.PrefetchScalarGridSpec(num...]
    ppermute x36, starting transfers between devices: 100 us -> 110 us  [hop(): return lax.ppermute(value, self.axes, pairs)]
  transfers between devices with their start and end apart: 112 -> 112, of which waited for: 47 -> 47; matrix products, arithmetic and copies ran while one was open for 20% -> 17% of each run, Pallas kernels for 14% -> 16%
where the time goes in v6:
time: 980 us; the launch traced here: 969 us
  waiting for transfers between devices  361 us (37%)
  starting transfers between devices  193 us (20%)
  Pallas kernels  189 us (19%)
  other arithmetic  76.5 us (8%)
  matrix products  68.1 us (7%)
  local copies, waits for them, and re-layouts  59.2 us (6%)
  between operations  22.8 us (2%)
    ppermute x36, waiting for transfers between devices, hop(): return lax.ppermute(value, self.axes, pairs)  237 us
    ppermute x36, starting transfers between devices, hop(): return lax.ppermute(value, self.axes, pairs)  110 us
    pallas_call x10, Pallas kernels, feed_call(): pl.pallas_call(functools.partial(kernel, count, len(held)), grid=(count,)...  71.5 us
    ppermute x27, waiting for transfers between devices, shift(): return lax.ppermute(value, axes, pairs)  55.4 us
    ppermute x27, starting transfers between devices, shift(): return lax.ppermute(value, axes, pairs)  50.8 us
    dot_general x4, matrix products, product_left(): lax.dot_general(left_side, right_side, (((0,), (0,)), ((), ())), preferre...  50.6 us
    ppermute x3, waiting for transfers between devices, step(): return (rows, lax.ppermute(rows, axis, [(0, 1), (1, 0)]))  22.6 us
    ppermute x6, starting transfers between devices, small_sum(): value = value + lax.ppermute(value, axis, [(0, 1), (1, 0)])  21.2 us
  transfers between devices with their start and end apart: 112, of which 47 were waited for; matrix products, arithmetic and copies ran while one was open for 17% of the time, Pallas kernels for 16%

profile of v6, /device:TPU:0, one launch (start us, length us, event | category | flops | bytes accessed | tf_op | source)
XLA Modules:
  0.0 969.1 jit_solution(3441271495314947647)
XLA Ops:
  53.8 5.6 spread.3
  65.1 10.1 %collective-permute-done.4 = bf16[256,2048]{1,0:T(8,128)(2,1)} collective-permute-done((bf16[256,2048]{1,0:T(8,128)(2,1)S(1)}, bf16[256,2048]{1,0:T(8,128)(2,1)}, u32[]{:S(2)}, u32[]{:S(2)}) %collective-permute-start.4) | collective-permute-done | bytes 1048608 | tf_op jit(solution)/shard_map/ppermute | solution.py:105
  86.9 8.2 collective-permute-start.9
  97.6 18.2 %collective-permute-done.10 = bf16[256,2048]{1,0:T(8,128)(2,1)} collective-permute-done((bf16[256,2048]{1,0:T(8,128)(2,1)}, bf16[256,2048]{1,0:T(8,128)(2,1)}, u32[]{:S(2)}, u32[]{:S(2)}) %collective-permute-start.10) | collective-permute-done | bytes 1048608 | tf_op jit(solution)/shard_map/ppermute | solution.py:105
  138.8 11.9 %project.1 = (f32[2048,768]{1,0:T(8,128)}, f32[2,2048]{1,0:T(2,128)S(1)}) custom-call(bf16[2048,2048]{1,0:T(8,128)(2,1)} %bitcast.34.in_ref, bf16[2048,768]{1,0:T(8,128)(2,1)S(1)} %copy-done.15), custom_call_target="tpu_custom_call" | custom-call | flops 10000000000 | bytes 30000000 | tf_op jit(solution)/shard_map/project/pallas_call | solution.py:521
  154.3 6.3 collective-permute-start.18
  172.5 6.3 turn.1
  178.8 15.3 %attend.1 = (f32[2048,256]{1,0:T(8,128)}, f32[2,1,2048]{2,1,0:T(1,128)S(1)}) custom-call(s32[4]{0:T(128)S(1)} %and_select_fusion.low_ref, s32[1,2048]{1,0:T(1,128)S(1)} %bitcast.209, bf16[2048,256]{1,0:T(8,128)(2,1)} %get-tuple-element.290.q_ref, bf16[2048,256]{1,0:T(8,128)(2,1)} %get-tuple-element.291.k_ref, bf16[2048,256]{1,0:T(8,128)(2,1)} %get-tuple-element.292.v_ref), custom_call_target="tpu_custom_call" | custom-call | flops 16000000000 | bytes 48000000 | tf_op jit(solution)/shard_map/attend/pallas_call | solution.py:364
  196.0 11.9 %collective-permute-done.23.refs_3_ = bf16[2,64,2048]{2,1,0:T(8,128)(2,1)S(1)} collective-permute-done((bf16[2,64,2048]{2,1,0:T(8,128)(2,1)}, bf16[2,64,2048]{2,1,0:T(8,128)(2,1)S(1)}, u32[]{:S(2)}, u32[]{:S(2)}) %collective-permute-start.23) | collective-permute-done | bytes 524320 | tf_op jit(solution)/shard_map/ppermute | solution.py:58
  213.7 8.3 collective-permute-start.25
  224.5 6.7 bitcast_select_fusion
  234.1 9.2 collective-permute-done.26.refs_3_
  244.6 6.2 multiply_reduce_fusion.6
  252.2 8.4 collective-permute-start.29
  261.9 19.7 %collective-permute-done.29 = bf16[256,2048]{1,0:T(8,128)(2,1)} collective-permute-done((bf16[256,2048]{1,0:T(8,128)(2,1)S(1)}, bf16[256,2048]{1,0:T(8,128)(2,1)}, u32[]{:S(2)}, u32[]{:S(2)}) %collective-permute-start.29) | collective-permute-done | bytes 1048608 | tf_op jit(solution)/shard_map/ppermute | solution.py:105
  293.5 14.2 %all-gather.11.cloned.1.call-done.refs_1_.refs_2_ = bf16[2048,2048]{1,0:T(8,128)(2,1)} async-done(((bf16[512,2048]{1,0:T(8,128)(2,1)}), bf16[2048,2048]{1,0:T(8,128)(2,1)}) %all-gather.11.cloned.1.call-update) | async-done | bytes 8388624 | tf_op jit(solution)/shard_map/all_gather | solution.py:868
  326.4 8.8 feed.6
  335.2 10.0 %feed.7 = (bf16[2048,2048]{1,0:T(8,128)(2,1)}, bf16[2048,1024]{1,0:T(8,128)(2,1)}, bf16[2048,1024]{1,0:T(8,128)(2,1)}, bf16[2048,1024]{1,0:T(8,128)(2,1)}, bf16[...) custom-call(bf16[256,2048]{1,0:T(8,128)(2,1)S(1)} %select_select_fus, ...), custom_call_target="tpu_custom_call", output_to_operand_aliasing={{0}: (4, {}), {1}: (5, {}), {2}: (6, {}), {3}: (7, {})} | custom-call | flops 1000000000 | bytes 3000000 | tf_op jit(solution)/shard_map/feed/pallas_call | solution.py:743
  357.2 9.1 feed.8
  376.5 20.8 %collective-permute-done.40.right_ref = bf16[256,2048]{1,0:T(8,128)(2,1)S(1)} collective-permute-done((bf16[256,2048]{1,0:T(8,128)(2,1)S(1)}, bf16[256,2048]{1,0:T(8,128)(2,1)S(1)}, u32[]{:S(2)}, u32[]{:S(2)}) %collective-permute-start.40) | collective-permute-done | bytes 1048608 | tf_op jit(solution)/shard_map/ppermute | solution.py:105
  404.1 20.6 %collective-permute-done.43.right_ref = bf16[256,2048]{1,0:T(8,128)(2,1)S(1)} collective-permute-done((bf16[256,2048]{1,0:T(8,128)(2,1)S(1)}, bf16[256,2048]{1,0:T(8,128)(2,1)S(1)}, u32[]{:S(2)}, u32[]{:S(2)}) %collective-permute-start.43) | collective-permute-done | bytes 1048608 | tf_op jit(solution)/shard_map/ppermute | solution.py:105
  425.9 8.6 collective-permute-start.46
  436.8 18.3 %collective-permute-done.46 = bf16[256,2048]{1,0:T(8,128)(2,1)S(1)} collective-permute-done((bf16[256,2048]{1,0:T(8,128)(2,1)S(1)}, bf16[256,2048]{1,0:T(8,128)(2,1)S(1)}, u32[]{:S(2)}, u32[]{:S(2)}) %collective-permute-start.46) | collective-permute-done | bytes 1048608 | tf_op jit(solution)/shard_map/ppermute | solution.py:105
  470.4 14.3 %collective-permute-done.49 = bf16[256,2048]{1,0:T(8,128)(2,1)S(1)} collective-permute-done((bf16[256,2048]{1,0:T(8,128)(2,1)S(1)}, bf16[256,2048]{1,0:T(8,128)(2,1)S(1)}, u32[]{:S(2)}, u32[]{:S(2)}) %collective-permute-start.49) | collective-permute-done | bytes 1048608 | tf_op jit(solution)/shard_map/ppermute | solution.py:105
  493.2 9.3 feed_back.6
  502.5 12.4 %collective-permute-done.52 = bf16[256,2048]{1,0:T(8,128)(2,1)S(1)} collective-permute-done((bf16[256,2048]{1,0:T(8,128)(2,1)S(1)}, bf16[256,2048]{1,0:T(8,128)(2,1)S(1)}, u32[]{:S(2)}, u32[]{:S(2)}) %collective-permute-start.52) | collective-permute-done | bytes 1048608 | tf_op jit(solution)/shard_map/ppermute | solution.py:105
  524.9 9.4 feed_back.7
  534.3 12.1 %collective-permute-done.55 = bf16[256,2048]{1,0:T(8,128)(2,1)S(1)} collective-permute-done((bf16[256,2048]{1,0:T(8,128)(2,1)S(1)}, bf16[256,2048]{1,0:T(8,128)(2,1)S(1)}, u32[]{:S(2)}, u32[]{:S(2)}) %collective-permute-start.55) | collective-permute-done | bytes 1048608 | tf_op jit(solution)/shard_map/ppermute | solution.py:105
  555.4 9.3 feed_back.8
  575.6 21.3 %convolution_convert_fusion.1 = bf16[2048,2048]{1,0:T(8,128)(2,1)} fusion(bf16[2048,2048]{1,0:T(8,128)(2,1)S(1)} %bitcast.215, bf16[2048,2048]{1,0:T(8,128)(2,1)} %get-tuple-element.392), kind=kOutput, calls=%fused_computation.2 | convolution fusion | flops 17184063488 | bytes 25165824 | tf_op jit(solution)/shard_map/dot_general | solution.py:292
  607.5 13.2 %convolution_convert_fusion.2 = bf16[1024,2048]{1,0:T(8,128)(2,1)} fusion(bf16[2048,1024]{1,0:T(8,128)(2,1)S(1)} %copy-done.33, bf16[2048,2048]{1,0:T(8,128)(2,1)} %get-tuple-element.401), kind=kOutput, calls=%fused_computation.4 | convolution fusion | flops 8592031744 | bytes 16777216 | tf_op jit(solution)/shard_map/dot_general | solution.py:292
  631.4 7.4 collective-permute-start.66
  642.1 18.0 %collective-permute-done.66 = bf16[256,2048]{1,0:T(8,128)(2,1)S(1)} collective-permute-done((bf16[256,2048]{1,0:T(8,128)(2,1)S(1)}, bf16[256,2048]{1,0:T(8,128)(2,1)S(1)}, u32[]{:S(2)}, u32[]{:S(2)}) %collective-permute-start.66) | collective-permute-done | bytes 1048608 | tf_op jit(solution)/shard_map/ppermute | solution.py:105
  692.0 9.4 collective-permute-done.70.refs_2_
  701.3 9.1 collective-permute-done.71.refs_3_
  712.8 6.1 join.1
  730.2 19.1 %attend_back.1 = (f32[2048,256]{1,0:T(8,128)}, f32[2048,256]{1,0:T(8,128)}, f32[2048,256]{1,0:T(8,128)}) custom-call(s32[4]{0:T(128)S(1)} %copy-done.32, s32[1,2048]{1,0:T(1,128)S(1)} %bitcast.210, bf16[2048,256]{1,0:T(8,128)(2,1)S(1)} %copy-done.17, bf16[2048,256]{1,0:T(8,128)(2,1)S(1)} %copy-done.18, bf16[2048,256]{1,0:T(8,128)(2,1)S(1)} %copy-done.19, ...), custom_call_target="tpu_custom_call" | custom-call | flops 25999998976 | bytes 78000000 | tf_op jit(solution)/shard_map/attend_back/pallas_call | solution.py:429
  749.3 7.4 unturn.1
  756.7 9.5 collective-permute-done.76.refs_3_
  767.2 10.6 %collective-permute-start.78 = (f32[2,2048]{1,0:T(2,128)S(1)}, f32[2,2048]{1,0:T(2,128)S(1)}, u32[]{:S(2)}, u32[]{:S(2)}) collective-permute-start(f32[2,2048]{1,0:T(2,128)S(1)} %copy-done.65), channel_id=1, source_target_pairs={{0,4},{4,0},{1,5},{5,1},{2,6},{6,2},{3,7},{7,3},{8,12},{12,8},{9,1... | collective-permute-start | bytes 49160 | tf_op jit(solution)/shard_map/ppermute | solution.py:281
  789.1 7.2 finish.1
  815.6 11.3 %collective-permute-start.84 = (bf16[256,2048]{1,0:T(8,128)(2,1)S(1)}, bf16[256,2048]{1,0:T(8,128)(2,1)}, u32[]{:S(2)}, u32[]{:S(2)}) collective-permute-start(bf16[256,2048]{1,0:T(8,128)(2,1)S(1)} %add_convert_fusion.3.two_ref), channel_id=1, source_target_pairs={{0,2},{1,3},{8,10},{9,11},{16,18},{17,19},{24,26},{25,27}} | collective-permute-start | bytes 3145736 | tf_op jit(solution)/shard_map/ppermute | solution.py:105
  828.7 10.5 %convolution_convert_fusion.3 = bf16[2048,768]{1,0:T(8,128)(2,1)} fusion(bf16[2048,2048]{1,0:T(8,128)(2,1)} %bitcast.34.in_ref, bf16[2048,768]{1,0:T(8,128)(2,1)S(1)} %copy-done.42), kind=kOutput, calls=%fused_computation.5 | convolution fusion | flops 6444023808 | bytes 14680064 | tf_op jit(solution)/shard_map/dot_general | solution.py:292
  843.1 5.7 collective-permute-done.84.right_ref
  867.1 15.6 %collective-permute-done.89.right_ref = bf16[256,2048]{1,0:T(8,128)(2,1)S(1)} collective-permute-done((bf16[256,2048]{1,0:T(8,128)(2,1)}, bf16[256,2048]{1,0:T(8,128)(2,1)S(1)}, u32[]{:S(2)}, u32[]{:S(2)}) %collective-permute-start.89) | collective-permute-done | bytes 1048608 | tf_op jit(solution)/shard_map/ppermute | solution.py:105
  882.7 12.1 %reduce-scatter.9.cloned.1.call-done = bf16[512,768]{1,0:T(8,128)(2,1)} async-done(((bf16[2048,768]{1,0:T(8,128)(2,1)}), bf16[512,768]{1,0:T(8,128)(2,1)}) %reduce-scatter.9.cloned.1.call-update) | async-done | bytes 786448 | tf_op jit(solution)/shard_map/reduce_scatter | solution.py:779
  911.3 18.5 %collective-permute-done.96 = f32[5,2048]{1,0:T(8,128)S(1)} collective-permute-done((f32[5,2048]{1,0:T(8,128)S(1)}, f32[5,2048]{1,0:T(8,128)S(1)}, u32[]{:S(2)}, u32[]{:S(2)}) %collective-permute-start.96) | collective-permute-done | bytes 40992 | tf_op jit(solution)/shard_map/ppermute | solution.py:1004
  940.8 6.1 collect.3
  (504 shorter events, 398.7 us)
Async XLA Ops:
  7.2 70.2 %all-gather.5.cloned.1.call-start = ((), (), s32[]{:S(2)}) async-start(), calls=%async_computation.4 | async-start | bytes 5242880 | tf_op jit(solution)/shard_map/all_gather | solution.py:832
  7.9 129.0 %all-gather.7.cloned.1.call-start = ((), (), s32[]{:S(2)}) async-start(), calls=%async_computation.5 | async-start | bytes 3932160 | tf_op jit(solution)/shard_map/all_gather | solution.py:846
  7.9 27.7 %collective-permute-start = (bf16[256,2048]{1,0:T(8,128)(2,1)}, bf16[256,2048]{1,0:T(8,128)(2,1)S(1)}, u32[]{:S(2)}, u32[]{:S(2)}) collective-permute-start(bf16[256,2048]{1,0:T(8,128)(2,1)} %bitcast.224), channel_id=1, source_target_pairs={{0,2},{2,4},{4,6},{1,3},{3,5},{5,7},{8,10},{10,12},{12,14},{9,11},... | collective-permute-start | bytes 3145736 | tf_op jit(solution)/shard_map/ppermute | solution.py:105
  13.0 26.7 %collective-permute-start.1 = (bf16[256,2048]{1,0:T(8,128)(2,1)}, bf16[256,2048]{1,0:T(8,128)(2,1)S(1)}, u32[]{:S(2)}, u32[]{:S(2)}) collective-permute-start(bf16[256,2048]{1,0:T(8,128)(2,1)} %bitcast.225), channel_id=1, source_target_pairs={{2,0},{4,2},{6,4},{3,1},{5,3},{7,5},{10,8},{12,10},{14,12},{11,9},... | collective-permute-start | bytes 3145736 | tf_op jit(solution)/shard_map/ppermute | solution.py:105
  14.3 25.4 %collective-permute-start.2 = (bf16[256,2048]{1,0:T(8,128)(2,1)}, bf16[256,2048]{1,0:T(8,128)(2,1)}, u32[]{:S(2)}, u32[]{:S(2)}) collective-permute-start(bf16[256,2048]{1,0:T(8,128)(2,1)} %bitcast.226), channel_id=1, source_target_pairs={{0,1},{1,0},{2,3},{3,2},{4,5},{5,4},{6,7},{7,6},{8,9},{9,8},{10,11... | collective-permute-start | bytes 3145736 | tf_op jit(solution)/shard_map/ppermute | solution.py:62
  44.2 31.0 %collective-permute-start.4 = (bf16[256,2048]{1,0:T(8,128)(2,1)S(1)}, bf16[256,2048]{1,0:T(8,128)(2,1)}, u32[]{:S(2)}, u32[]{:S(2)}) collective-permute-start(bf16[256,2048]{1,0:T(8,128)(2,1)S(1)} %collective-permute-done), channel_id=1, source_target_pairs={{0,2},{2,4},{4,6},{1,3},{3,5},{5,7},{8,10},{10,12},{12,14},{9,11},... | collective-permute-start | bytes 3145736 | tf_op jit(solution)/shard_map/ppermute | solution.py:105
  47.7 29.7 %collective-permute-start.5 = (bf16[256,2048]{1,0:T(8,128)(2,1)S(1)}, bf16[256,2048]{1,0:T(8,128)(2,1)}, u32[]{:S(2)}, u32[]{:S(2)}) collective-permute-start(bf16[256,2048]{1,0:T(8,128)(2,1)S(1)} %collective-permute-done.1), channel_id=1, source_target_pairs={{2,0},{4,2},{6,4},{3,1},{5,3},{7,5},{10,8},{12,10},{14,12},{11,9},... | collective-permute-start | bytes 3145736 | tf_op jit(solution)/shard_map/ppermute | solution.py:105
  65.0 32.5 %collective-permute-start.11 = (bf16[256,2048]{1,0:T(8,128)(2,1)}, bf16[256,2048]{1,0:T(8,128)(2,1)}, u32[]{:S(2)}, u32[]{:S(2)}) collective-permute-start(bf16[256,2048]{1,0:T(8,128)(2,1)} %get-tuple-element.498), channel_id=1, source_target_pairs={{0,1},{1,0},{2,3},{3,2},{4,5},{5,4},{6,7},{7,6},{8,9},{9,8},{10,11... | collective-permute-start | bytes 3145736 | tf_op jit(solution)/shard_map/ppermute | solution.py:62
  79.4 131.3 %all-gather.9.cloned.1.call-start = ((), (), s32[]{:S(2)}) async-start(), calls=%async_computation.6 | async-start | bytes 5242880 | tf_op jit(solution)/shard_map/all_gather | solution.py:855
  85.6 30.2 %collective-permute-start.10 = (bf16[256,2048]{1,0:T(8,128)(2,1)}, bf16[256,2048]{1,0:T(8,128)(2,1)}, u32[]{:S(2)}, u32[]{:S(2)}) collective-permute-start(bf16[256,2048]{1,0:T(8,128)(2,1)} %collective-permute-done.5), channel_id=1, source_target_pairs={{2,0},{4,2},{6,4},{3,1},{5,3},{7,5},{10,8},{12,10},{14,12},{11,9},... | collective-permute-start | bytes 3145736 | tf_op jit(solution)/shard_map/ppermute | solution.py:105
  86.9 30.1 %collective-permute-start.9 = (bf16[256,2048]{1,0:T(8,128)(2,1)}, bf16[256,2048]{1,0:T(8,128)(2,1)}, u32[]{:S(2)}, u32[]{:S(2)}) collective-permute-start(bf16[256,2048]{1,0:T(8,128)(2,1)} %collective-permute-done.4), channel_id=1, source_target_pairs={{0,2},{2,4},{4,6},{1,3},{3,5},{5,7},{8,10},{10,12},{12,14},{9,11},... | collective-permute-start | bytes 3145736 | tf_op jit(solution)/shard_map/ppermute | solution.py:105
  154.0 153.7 %all-gather.11.cloned.1.call-start = ((), (), s32[]{:S(2)}) async-start(), calls=%async_computation.7 | async-start | bytes 10485760 | tf_op jit(solution)/shard_map/all_gather | solution.py:868
  167.5 28.5 %collective-permute-start.22 = (bf16[2,64,2048]{2,1,0:T(8,128)(2,1)}, bf16[2,64,2048]{2,1,0:T(8,128)(2,1)S(1)}, u32[]{:S(2)}, u32[]{:S(2)}) collective-permute-start(bf16[2,64,2048]{2,1,0:T(8,128)(2,1)} %get-tuple-element.517), channel_id=1, source_target_pairs={{0,2},{2,0},{4,6},{6,4},{1,3},{3,1},{5,7},{7,5},{8,10},{10,8},{12,... | collective-permute-start | bytes 1572872 | tf_op jit(solution)/shard_map/ppermute | solution.py:58
  169.5 38.4 %collective-permute-start.23 = (bf16[2,64,2048]{2,1,0:T(8,128)(2,1)}, bf16[2,64,2048]{2,1,0:T(8,128)(2,1)S(1)}, u32[]{:S(2)}, u32[]{:S(2)}) collective-permute-start(bf16[2,64,2048]{2,1,0:T(8,128)(2,1)} %get-tuple-element.516), channel_id=1, source_target_pairs={{0,4},{2,6},{4,0},{6,2},{1,5},{3,7},{5,1},{7,3},{8,12},{10,14},{12... | collective-permute-start | bytes 1572872 | tf_op jit(solution)/shard_map/ppermute | solution.py:58
  170.4 37.5 %collective-permute-start.24 = (bf16[2,64,2048]{2,1,0:T(8,128)(2,1)}, bf16[2,64,2048]{2,1,0:T(8,128)(2,1)S(1)}, u32[]{:S(2)}, u32[]{:S(2)}) collective-permute-start(bf16[2,64,2048]{2,1,0:T(8,128)(2,1)} %get-tuple-element.515), channel_id=1, source_target_pairs={{0,6},{2,4},{4,2},{6,0},{1,7},{3,5},{5,3},{7,1},{8,14},{10,12},{12... | collective-permute-start | bytes 1572872 | tf_op jit(solution)/shard_map/ppermute | solution.py:58
  213.2 470.2 %reduce-scatter.5.cloned.1.call-start = ((), (), s32[]{:S(2)}) async-start(), calls=%async_computation.8 | async-start | bytes 10485760 | tf_op jit(solution)/shard_map/reduce_scatter | solution.py:779
  252.2 29.4 %collective-permute-start.29 = (bf16[256,2048]{1,0:T(8,128)(2,1)S(1)}, bf16[256,2048]{1,0:T(8,128)(2,1)}, u32[]{:S(2)}, u32[]{:S(2)}) collective-permute-start(bf16[256,2048]{1,0:T(8,128)(2,1)S(1)} %fusion.7.refs_0_), channel_id=1, source_target_pairs={{0,2},{2,4},{4,6},{1,3},{3,5},{5,7},{8,10},{10,12},{12,14},{9,11},... | collective-permute-start | bytes 3145736 | tf_op jit(solution)/shard_map/ppermute | solution.py:105
  260.5 26.3 %collective-permute-start.30 = (bf16[256,2048]{1,0:T(8,128)(2,1)S(1)}, bf16[256,2048]{1,0:T(8,128)(2,1)}, u32[]{:S(2)}, u32[]{:S(2)}) collective-permute-start(bf16[256,2048]{1,0:T(8,128)(2,1)S(1)} %fusion.7.refs_0_), channel_id=1, source_target_pairs={{2,0},{4,2},{6,4},{3,1},{5,3},{7,5},{10,8},{12,10},{14,12},{11,9},... | collective-permute-start | bytes 3145736 | tf_op jit(solution)/shard_map/ppermute | solution.py:105
  288.8 28.0 %collective-permute-start.34 = (bf16[256,2048]{1,0:T(8,128)(2,1)S(1)}, bf16[256,2048]{1,0:T(8,128)(2,1)}, u32[]{:S(2)}, u32[]{:S(2)}) collective-permute-start(bf16[256,2048]{1,0:T(8,128)(2,1)S(1)} %broadcast_select_fusion.5.refs_0_), channel_id=1, source_target_pairs={{0,1},{1,0},{2,3},{3,2},{4,5},{5,4},{6,7},{7,6},{8,9},{9,8},{10,11... | collective-permute-start | bytes 3145736 | tf_op jit(solution)/shard_map/ppermute | solution.py:62
  288.9 27.9 %collective-permute-start.32 = (bf16[256,2048]{1,0:T(8,128)(2,1)}, bf16[256,2048]{1,0:T(8,128)(2,1)}, u32[]{:S(2)}, u32[]{:S(2)}) collective-permute-start(bf16[256,2048]{1,0:T(8,128)(2,1)} %collective-permute-done.29), channel_id=1, source_target_pairs={{0,2},{2,4},{4,6},{1,3},{3,5},{5,7},{8,10},{10,12},{12,14},{9,11},... | collective-permute-start | bytes 3145736 | tf_op jit(solution)/shard_map/ppermute | solution.py:105
  292.2 27.5 %collective-permute-start.33 = (bf16[256,2048]{1,0:T(8,128)(2,1)}, bf16[256,2048]{1,0:T(8,128)(2,1)}, u32[]{:S(2)}, u32[]{:S(2)}) collective-permute-start(bf16[256,2048]{1,0:T(8,128)(2,1)} %collective-permute-done.30), channel_id=1, source_target_pairs={{2,0},{4,2},{6,4},{3,1},{5,3},{7,5},{10,8},{12,10},{14,12},{11,9},... | collective-permute-start | bytes 3145736 | tf_op jit(solution)/shard_map/ppermute | solution.py:105
  324.9 27.5 %collective-permute-start.36 = (bf16[256,2048]{1,0:T(8,128)(2,1)}, bf16[256,2048]{1,0:T(8,128)(2,1)S(1)}, u32[]{:S(2)}, u32[]{:S(2)}) collective-permute-start(bf16[256,2048]{1,0:T(8,128)(2,1)} %collective-permute-done.33), channel_id=1, source_target_pairs={{2,0},{4,2},{6,4},{3,1},{5,3},{7,5},{10,8},{12,10},{14,12},{11,9},... | collective-permute-start | bytes 3145736 | tf_op jit(solution)/shard_map/ppermute | solution.py:105
  370.9 26.4 %collective-permute-start.40 = (bf16[256,2048]{1,0:T(8,128)(2,1)S(1)}, bf16[256,2048]{1,0:T(8,128)(2,1)S(1)}, u32[]{:S(2)}, u32[]{:S(2)}) collective-permute-start(bf16[256,2048]{1,0:T(8,128)(2,1)S(1)} %add_convert_fusion.11.two_ref), channel_id=1, source_target_pairs={{0,2},{1,3},{8,10},{9,11},{16,18},{17,19},{24,26},{25,27}} | collective-permute-start | bytes 3145736 | tf_op jit(solution)/shard_map/ppermute | solution.py:105
  376.1 27.6 %collective-permute-start.45 = (bf16[256,2048]{1,0:T(8,128)(2,1)S(1)}, bf16[256,2048]{1,0:T(8,128)(2,1)S(1)}, u32[]{:S(2)}, u32[]{:S(2)}) collective-permute-start(bf16[256,2048]{1,0:T(8,128)(2,1)S(1)} %get-tuple-element.352), channel_id=1, source_target_pairs={{0,1},{1,0},{2,3},{3,2},{4,5},{5,4},{6,7},{7,6},{8,9},{9,8},{10,11... | collective-permute-start | bytes 3145736 | tf_op jit(solution)/shard_map/ppermute | solution.py:62
  398.4 26.3 %collective-permute-start.43 = (bf16[256,2048]{1,0:T(8,128)(2,1)S(1)}, bf16[256,2048]{1,0:T(8,128)(2,1)S(1)}, u32[]{:S(2)}, u32[]{:S(2)}) collective-permute-start(bf16[256,2048]{1,0:T(8,128)(2,1)S(1)} %get-tuple-element.349), channel_id=1, source_target_pairs={{0,2},{2,4},{1,3},{3,5},{8,10},{10,12},{9,11},{11,13},{16,18},{18,... | collective-permute-start | bytes 3145736 | tf_op jit(solution)/shard_map/ppermute | solution.py:105
  403.6 32.8 %collective-permute-start.48 = (bf16[256,2048]{1,0:T(8,128)(2,1)S(1)}, bf16[256,2048]{1,0:T(8,128)(2,1)S(1)}, u32[]{:S(2)}, u32[]{:S(2)}) collective-permute-start(bf16[256,2048]{1,0:T(8,128)(2,1)S(1)} %get-tuple-element.359), channel_id=1, source_target_pairs={{0,1},{1,0},{2,3},{3,2},{4,5},{5,4},{6,7},{7,6},{8,9},{9,8},{10,11... | collective-permute-start | bytes 3145736 | tf_op jit(solution)/shard_map/ppermute | solution.py:62
  425.9 29.2 %collective-permute-start.46 = (bf16[256,2048]{1,0:T(8,128)(2,1)S(1)}, bf16[256,2048]{1,0:T(8,128)(2,1)S(1)}, u32[]{:S(2)}, u32[]{:S(2)}) collective-permute-start(bf16[256,2048]{1,0:T(8,128)(2,1)S(1)} %get-tuple-element.356), channel_id=1, source_target_pairs={{0,2},{2,4},{4,6},{1,3},{3,5},{5,7},{8,10},{10,12},{12,14},{9,11},... | collective-permute-start | bytes 3145736 | tf_op jit(solution)/shard_map/ppermute | solution.py:105
  491.9 27.2 %collective-permute-start.53 = (bf16[256,2048]{1,0:T(8,128)(2,1)S(1)}, bf16[256,2048]{1,0:T(8,128)(2,1)S(1)}, u32[]{:S(2)}, u32[]{:S(2)}) collective-permute-start(bf16[256,2048]{1,0:T(8,128)(2,1)S(1)} %collective-permute-done.50), channel_id=1, source_target_pairs={{2,0},{4,2},{6,4},{3,1},{5,3},{7,5},{10,8},{12,10},{14,12},{11,9},... | collective-permute-start | bytes 3145736 | tf_op jit(solution)/shard_map/ppermute | solution.py:105
  523.4 27.2 %collective-permute-start.56 = (bf16[256,2048]{1,0:T(8,128)(2,1)S(1)}, bf16[256,2048]{1,0:T(8,128)(2,1)S(1)}, u32[]{:S(2)}, u32[]{:S(2)}) collective-permute-start(bf16[256,2048]{1,0:T(8,128)(2,1)S(1)} %collective-permute-done.53), channel_id=1, source_target_pairs={{2,0},{4,2},{6,4},{3,1},{5,3},{7,5},{10,8},{12,10},{14,12},{11,9},... | collective-permute-start | bytes 3145736 | tf_op jit(solution)/shard_map/ppermute | solution.py:105
  569.7 27.3 %collective-permute-start.62 = (bf16[256,2048]{1,0:T(8,128)(2,1)}, bf16[256,2048]{1,0:T(8,128)(2,1)}, u32[]{:S(2)}, u32[]{:S(2)}) collective-permute-start(bf16[256,2048]{1,0:T(8,128)(2,1)} %get-tuple-element.390), channel_id=1, source_target_pairs={{0,1},{1,0},{2,3},{3,2},{4,5},{5,4},{6,7},{7,6},{8,9},{9,8},{10,11... | collective-permute-start | bytes 3145736 | tf_op jit(solution)/shard_map/ppermute | solution.py:62
  570.4 28.5 %collective-permute-start.60 = (bf16[256,2048]{1,0:T(8,128)(2,1)S(1)}, bf16[256,2048]{1,0:T(8,128)(2,1)}, u32[]{:S(2)}, u32[]{:S(2)}) collective-permute-start(bf16[256,2048]{1,0:T(8,128)(2,1)S(1)} %add_convert_fusion.7.two_ref), channel_id=1, source_target_pairs={{0,2},{1,3},{8,10},{9,11},{16,18},{17,19},{24,26},{25,27}} | collective-permute-start | bytes 3145736 | tf_op jit(solution)/shard_map/ppermute | solution.py:105
  573.5 25.4 %collective-permute-start.61 = (bf16[256,2048]{1,0:T(8,128)(2,1)S(1)}, bf16[256,2048]{1,0:T(8,128)(2,1)}, u32[]{:S(2)}, u32[]{:S(2)}) collective-permute-start(bf16[256,2048]{1,0:T(8,128)(2,1)S(1)} %add_convert_fusion.7.two_ref), channel_id=1, source_target_pairs={{6,4},{7,5},{14,12},{15,13},{22,20},{23,21},{30,28},{31,29}} | collective-permute-start | bytes 3145736 | tf_op jit(solution)/shard_map/ppermute | solution.py:105
  599.0 184.4 %reduce-scatter.7.cloned.1.call-start = ((), (), s32[]{:S(2)}) async-start(), calls=%async_computation.9 | async-start | bytes 5242880 | tf_op jit(solution)/shard_map/reduce_scatter | solution.py:779
  599.1 41.2 %collective-permute-start.68 = (bf16[256,2048]{1,0:T(8,128)(2,1)}, bf16[256,2048]{1,0:T(8,128)(2,1)}, u32[]{:S(2)}, u32[]{:S(2)}) collective-permute-start(bf16[256,2048]{1,0:T(8,128)(2,1)} %copy-done.20), channel_id=1, source_target_pairs={{0,1},{1,0},{2,3},{3,2},{4,5},{5,4},{6,7},{7,6},{8,9},{9,8},{10,11... | collective-permute-start | bytes 3145736 | tf_op jit(solution)/shard_map/ppermute | solution.py:62
  631.4 28.7 %collective-permute-start.66 = (bf16[256,2048]{1,0:T(8,128)(2,1)S(1)}, bf16[256,2048]{1,0:T(8,128)(2,1)S(1)}, u32[]{:S(2)}, u32[]{:S(2)}) collective-permute-start(bf16[256,2048]{1,0:T(8,128)(2,1)S(1)} %get-tuple-element.405), channel_id=1, source_target_pairs={{0,2},{2,4},{4,6},{1,3},{3,5},{5,7},{8,10},{10,12},{12,14},{9,11},... | collective-permute-start | bytes 3145736 | tf_op jit(solution)/shard_map/ppermute | solution.py:105
  638.8 25.5 %collective-permute-start.67 = (bf16[256,2048]{1,0:T(8,128)(2,1)S(1)}, bf16[256,2048]{1,0:T(8,128)(2,1)S(1)}, u32[]{:S(2)}, u32[]{:S(2)}) collective-permute-start(bf16[256,2048]{1,0:T(8,128)(2,1)S(1)} %get-tuple-element.406), channel_id=1, source_target_pairs={{2,0},{4,2},{6,4},{3,1},{5,3},{7,5},{10,8},{12,10},{14,12},{11,9},... | collective-permute-start | bytes 3145736 | tf_op jit(solution)/shard_map/ppermute | solution.py:105
  719.6 147.5 %reduce-scatter.11.cloned.1.call-start = ((), (), s32[]{:S(2)}) async-start(), calls=%async_computation.11 | async-start | bytes 5242880 | tf_op jit(solution)/shard_map/reduce_scatter | solution.py:779
  722.4 34.3 %collective-permute-start.75 = (bf16[2,64,2048]{2,1,0:T(8,128)(2,1)}, bf16[2,64,2048]{2,1,0:T(8,128)(2,1)S(1)}, u32[]{:S(2)}, u32[]{:S(2)}) collective-permute-start(bf16[2,64,2048]{2,1,0:T(8,128)(2,1)} %get-tuple-element.511), channel_id=1, source_target_pairs={{0,2},{2,0},{4,6},{6,4},{1,3},{3,1},{5,7},{7,5},{8,10},{10,8},{12,... | collective-permute-start | bytes 1572872 | tf_op jit(solution)/shard_map/ppermute | solution.py:58
  727.8 38.4 %collective-permute-start.76 = (bf16[2,64,2048]{2,1,0:T(8,128)(2,1)}, bf16[2,64,2048]{2,1,0:T(8,128)(2,1)S(1)}, u32[]{:S(2)}, u32[]{:S(2)}) collective-permute-start(bf16[2,64,2048]{2,1,0:T(8,128)(2,1)} %get-tuple-element.510), channel_id=1, source_target_pairs={{0,4},{2,6},{4,0},{6,2},{1,5},{3,7},{5,1},{7,3},{8,12},{10,14},{12... | collective-permute-start | bytes 1572872 | tf_op jit(solution)/shard_map/ppermute | solution.py:58
  728.7 37.5 %collective-permute-start.77 = (bf16[2,64,2048]{2,1,0:T(8,128)(2,1)S(1)}, bf16[2,64,2048]{2,1,0:T(8,128)(2,1)S(1)}, u32[]{:S(2)}, u32[]{:S(2)}) collective-permute-start(bf16[2,64,2048]{2,1,0:T(8,128)(2,1)S(1)} %get-tuple-element.509), channel_id=1, source_target_pairs={{0,6},{2,4},{4,2},{6,0},{1,7},{3,5},{5,3},{7,1},{8,14},{10,12},{12... | collective-permute-start | bytes 1572872 | tf_op jit(solution)/shard_map/ppermute | solution.py:58
  767.2 127.7 %reduce-scatter.9.cloned.1.call-start = ((), (), s32[]{:S(2)}) async-start(), calls=%async_computation.10 | async-start | bytes 3932160 | tf_op jit(solution)/shard_map/reduce_scatter | solution.py:779
  796.4 46.8 %collective-permute-start.88 = (bf16[64,2048]{1,0:T(8,128)(2,1)}, bf16[64,2048]{1,0:T(8,128)(2,1)}, u32[]{:S(2)}, u32[]{:S(2)}) collective-permute-start(bf16[64,2048]{1,0:T(8,128)(2,1)} %get-tuple-element.521), channel_id=1, source_target_pairs={{0,6},{2,4},{4,2},{6,0},{1,7},{3,5},{5,3},{7,1},{8,14},{10,12},{12... | collective-permute-start | bytes 786440 | tf_op jit(solution)/shard_map/ppermute | solution.py:58
  808.3 30.9 %collective-permute-start.87 = (bf16[256,2048]{1,0:T(8,128)(2,1)}, bf16[256,2048]{1,0:T(8,128)(2,1)}, u32[]{:S(2)}, u32[]{:S(2)}) collective-permute-start(bf16[256,2048]{1,0:T(8,128)(2,1)} %slice.108), channel_id=1, source_target_pairs={{0,1},{1,0},{2,3},{3,2},{4,5},{5,4},{6,7},{7,6},{8,9},{9,8},{10,11... | collective-permute-start | bytes 3145736 | tf_op jit(solution)/shard_map/ppermute | solution.py:62
  811.8 29.4 %collective-permute-start.86 = (bf16[256,2048]{1,0:T(8,128)(2,1)}, bf16[256,2048]{1,0:T(8,128)(2,1)}, u32[]{:S(2)}, u32[]{:S(2)}) collective-permute-start(bf16[256,2048]{1,0:T(8,128)(2,1)} %slice.106), channel_id=1, source_target_pairs={{0,1},{1,0},{2,3},{3,2},{4,5},{5,4},{6,7},{7,6},{8,9},{9,8},{10,11... | collective-permute-start | bytes 3145736 | tf_op jit(solution)/shard_map/ppermute | solution.py:62
  815.6 33.3 %collective-permute-start.84 = (bf16[256,2048]{1,0:T(8,128)(2,1)S(1)}, bf16[256,2048]{1,0:T(8,128)(2,1)}, u32[]{:S(2)}, u32[]{:S(2)}) collective-permute-start(bf16[256,2048]{1,0:T(8,128)(2,1)S(1)} %add_convert_fusion.3.two_ref), channel_id=1, source_target_pairs={{0,2},{1,3},{8,10},{9,11},{16,18},{17,19},{24,26},{25,27}} | collective-permute-start | bytes 3145736 | tf_op jit(solution)/shard_map/ppermute | solution.py:105
  854.9 27.9 %collective-permute-start.89 = (bf16[256,2048]{1,0:T(8,128)(2,1)}, bf16[256,2048]{1,0:T(8,128)(2,1)S(1)}, u32[]{:S(2)}, u32[]{:S(2)}) collective-permute-start(bf16[256,2048]{1,0:T(8,128)(2,1)} %get-tuple-element.441), channel_id=1, source_target_pairs={{0,2},{2,4},{1,3},{3,5},{8,10},{10,12},{9,11},{11,13},{16,18},{18,... | collective-permute-start | bytes 3145736 | tf_op jit(solution)/shard_map/ppermute | solution.py:105
  898.2 31.6 %collective-permute-start.93 = (bf16[256,2048]{1,0:T(8,128)(2,1)}, bf16[256,2048]{1,0:T(8,128)(2,1)S(1)}, u32[]{:S(2)}, u32[]{:S(2)}) collective-permute-start(bf16[256,2048]{1,0:T(8,128)(2,1)} %get-tuple-element.451), channel_id=1, source_target_pairs={{0,2},{2,4},{4,6},{1,3},{3,5},{5,7},{8,10},{10,12},{12,14},{9,11},... | collective-permute-start | bytes 3145736 | tf_op jit(solution)/shard_map/ppermute | solution.py:105
  901.7 28.2 %collective-permute-start.94 = (bf16[256,2048]{1,0:T(8,128)(2,1)}, bf16[256,2048]{1,0:T(8,128)(2,1)S(1)}, u32[]{:S(2)}, u32[]{:S(2)}) collective-permute-start(bf16[256,2048]{1,0:T(8,128)(2,1)} %get-tuple-element.452), channel_id=1, source_target_pairs={{2,0},{4,2},{6,4},{3,1},{5,3},{7,5},{10,8},{12,10},{14,12},{11,9},... | collective-permute-start | bytes 3145736 | tf_op jit(solution)/shard_map/ppermute | solution.py:105
  (144 other events, 2383.8 us)
Sparse Core Ops, SparseCore 0:
  9.8 55.4 all-gather.4
  79.5 48.4 all-gather.6
  154.1 56.6 all-gather.8
  213.3 94.3 all-gather.10
  599.1 84.1 reduce-scatter.4
  719.8 55.6 reduce-scatter.6
  778.4 52.6 reduce-scatter.10
  849.0 45.8 reduce-scatter.8

commit v7 on v6

--- a/solution.py
+++ b/solution.py
@@ -638,7 +638,7 @@
         in_specs=[
             row_block(width),
             row_block(width),
-            row_block(3 * width),
+            row_block(2 * width),
             lane_block(2),
             whole_block(2, width),
             row_block(HEAD_DIM),
@@ -674,7 +674,7 @@
         grid=(length // 512,),
         in_specs=[
             row_block(2 * width),
-            row_block(3 * width),
+            row_block(2 * width),
             lane_block(2),
             lane_block(2),
             row_block(width),

time: 980 us -> 980 us (level)
  no operation moved by 1% of the time
where the time goes in v7:
time: 980 us; the launch traced here: 969 us
  waiting for transfers between devices  362 us (37%)
  starting transfers between devices  193 us (20%)
  Pallas kernels  187 us (19%)
  other arithmetic  76.5 us (8%)
  matrix products  68.1 us (7%)
  local copies, waits for them, and re-layouts  59.2 us (6%)
  between operations  22.8 us (2%)
    ppermute x36, waiting for transfers between devices, hop(): return lax.ppermute(value, self.axes, pairs)  237 us
    ppermute x36, starting transfers between devices, hop(): return lax.ppermute(value, self.axes, pairs)  110 us
    pallas_call x10, Pallas kernels, feed_call(): pl.pallas_call(functools.partial(kernel, count, len(held)), grid=(count,)...  71.5 us
    ppermute x27, waiting for transfers between devices, shift(): return lax.ppermute(value, axes, pairs)  56.4 us
    ppermute x27, starting transfers between devices, shift(): return lax.ppermute(value, axes, pairs)  51 us
    dot_general x4, matrix products, product_left(): lax.dot_general(left_side, right_side, (((0,), (0,)), ((), ())), preferre...  50.6 us
    ppermute x3, waiting for transfers between devices, step(): return (rows, lax.ppermute(rows, axis, [(0, 1), (1, 0)]))  22.6 us
    ppermute x6, starting transfers between devices, small_sum(): value = value + lax.ppermute(value, axis, [(0, 1), (1, 0)])  21.2 us
  transfers between devices with their start and end apart: 112, of which 47 were waited for; matrix products, arithmetic and copies ran while one was open for 17% of the time, Pallas kernels for 16%

profile of v7, /device:TPU:0, one launch (start us, length us, event | category | flops | bytes accessed | tf_op | source)
XLA Modules:
  0.0 969.1 jit_solution(7566216683489137816)
XLA Ops:
  53.8 5.6 spread.3
  65.1 10.1 %collective-permute-done.4 = bf16[256,2048]{1,0:T(8,128)(2,1)} collective-permute-done((bf16[256,2048]{1,0:T(8,128)(2,1)S(1)}, bf16[256,2048]{1,0:T(8,128)(2,1)}, u32[]{:S(2)}, u32[]{:S(2)}) %collective-permute-start.4) | collective-permute-done | bytes 1048608 | tf_op jit(solution)/shard_map/ppermute | solution.py:105
  86.9 8.2 collective-permute-start.9
  97.6 18.2 %collective-permute-done.10 = bf16[256,2048]{1,0:T(8,128)(2,1)} collective-permute-done((bf16[256,2048]{1,0:T(8,128)(2,1)}, bf16[256,2048]{1,0:T(8,128)(2,1)}, u32[]{:S(2)}, u32[]{:S(2)}) %collective-permute-start.10) | collective-permute-done | bytes 1048608 | tf_op jit(solution)/shard_map/ppermute | solution.py:105
  138.8 11.9 %project.1 = (f32[2048,768]{1,0:T(8,128)}, f32[2,2048]{1,0:T(2,128)S(1)}) custom-call(bf16[2048,2048]{1,0:T(8,128)(2,1)} %bitcast.34.in_ref, bf16[2048,768]{1,0:T(8,128)(2,1)S(1)} %copy-done.15), custom_call_target="tpu_custom_call" | custom-call | flops 10000000000 | bytes 30000000 | tf_op jit(solution)/shard_map/project/pallas_call | solution.py:521
  154.3 6.3 collective-permute-start.18
  172.5 6.3 turn.1
  178.8 15.3 %attend.1 = (f32[2048,256]{1,0:T(8,128)}, f32[2,1,2048]{2,1,0:T(1,128)S(1)}) custom-call(s32[4]{0:T(128)S(1)} %and_select_fusion.low_ref, s32[1,2048]{1,0:T(1,128)S(1)} %bitcast.209, bf16[2048,256]{1,0:T(8,128)(2,1)} %get-tuple-element.290.q_ref, bf16[2048,256]{1,0:T(8,128)(2,1)} %get-tuple-element.291.k_ref, bf16[2048,256]{1,0:T(8,128)(2,1)} %get-tuple-element.292.v_ref), custom_call_target="tpu_custom_call" | custom-call | flops 16000000000 | bytes 48000000 | tf_op jit(solution)/shard_map/attend/pallas_call | solution.py:364
  196.0 11.9 %collective-permute-done.23.refs_3_ = bf16[2,64,2048]{2,1,0:T(8,128)(2,1)S(1)} collective-permute-done((bf16[2,64,2048]{2,1,0:T(8,128)(2,1)}, bf16[2,64,2048]{2,1,0:T(8,128)(2,1)S(1)}, u32[]{:S(2)}, u32[]{:S(2)}) %collective-permute-start.23) | collective-permute-done | bytes 524320 | tf_op jit(solution)/shard_map/ppermute | solution.py:58
  213.7 8.3 collective-permute-start.25
  224.5 6.7 bitcast_select_fusion
  234.1 9.2 collective-permute-done.26.refs_3_
  244.6 6.2 multiply_reduce_fusion.6
  252.2 8.4 collective-permute-start.29
  261.9 19.7 %collective-permute-done.29 = bf16[256,2048]{1,0:T(8,128)(2,1)} collective-permute-done((bf16[256,2048]{1,0:T(8,128)(2,1)S(1)}, bf16[256,2048]{1,0:T(8,128)(2,1)}, u32[]{:S(2)}, u32[]{:S(2)}) %collective-permute-start.29) | collective-permute-done | bytes 1048608 | tf_op jit(solution)/shard_map/ppermute | solution.py:105
  293.5 14.2 %all-gather.11.cloned.1.call-done.refs_1_.refs_2_ = bf16[2048,2048]{1,0:T(8,128)(2,1)} async-done(((bf16[512,2048]{1,0:T(8,128)(2,1)}), bf16[2048,2048]{1,0:T(8,128)(2,1)}) %all-gather.11.cloned.1.call-update) | async-done | bytes 8388624 | tf_op jit(solution)/shard_map/all_gather | solution.py:868
  326.4 8.8 feed.6
  335.2 10.0 %feed.7 = (bf16[2048,2048]{1,0:T(8,128)(2,1)}, bf16[2048,1024]{1,0:T(8,128)(2,1)}, bf16[2048,1024]{1,0:T(8,128)(2,1)}, bf16[2048,1024]{1,0:T(8,128)(2,1)}, bf16[...) custom-call(bf16[256,2048]{1,0:T(8,128)(2,1)S(1)} %select_select_fus, ...), custom_call_target="tpu_custom_call", output_to_operand_aliasing={{0}: (4, {}), {1}: (5, {}), {2}: (6, {}), {3}: (7, {})} | custom-call | flops 1000000000 | bytes 3000000 | tf_op jit(solution)/shard_map/feed/pallas_call | solution.py:743
  357.2 9.1 feed.8
  376.5 20.8 %collective-permute-done.40.right_ref = bf16[256,2048]{1,0:T(8,128)(2,1)S(1)} collective-permute-done((bf16[256,2048]{1,0:T(8,128)(2,1)S(1)}, bf16[256,2048]{1,0:T(8,128)(2,1)S(1)}, u32[]{:S(2)}, u32[]{:S(2)}) %collective-permute-start.40) | collective-permute-done | bytes 1048608 | tf_op jit(solution)/shard_map/ppermute | solution.py:105
  404.1 20.6 %collective-permute-done.43.right_ref = bf16[256,2048]{1,0:T(8,128)(2,1)S(1)} collective-permute-done((bf16[256,2048]{1,0:T(8,128)(2,1)S(1)}, bf16[256,2048]{1,0:T(8,128)(2,1)S(1)}, u32[]{:S(2)}, u32[]{:S(2)}) %collective-permute-start.43) | collective-permute-done | bytes 1048608 | tf_op jit(solution)/shard_map/ppermute | solution.py:105
  425.9 8.6 collective-permute-start.46
  436.8 18.3 %collective-permute-done.46 = bf16[256,2048]{1,0:T(8,128)(2,1)S(1)} collective-permute-done((bf16[256,2048]{1,0:T(8,128)(2,1)S(1)}, bf16[256,2048]{1,0:T(8,128)(2,1)S(1)}, u32[]{:S(2)}, u32[]{:S(2)}) %collective-permute-start.46) | collective-permute-done | bytes 1048608 | tf_op jit(solution)/shard_map/ppermute | solution.py:105
  470.4 14.3 %collective-permute-done.49 = bf16[256,2048]{1,0:T(8,128)(2,1)S(1)} collective-permute-done((bf16[256,2048]{1,0:T(8,128)(2,1)S(1)}, bf16[256,2048]{1,0:T(8,128)(2,1)S(1)}, u32[]{:S(2)}, u32[]{:S(2)}) %collective-permute-start.49) | collective-permute-done | bytes 1048608 | tf_op jit(solution)/shard_map/ppermute | solution.py:105
  493.2 9.3 feed_back.6
  502.5 12.4 %collective-permute-done.52 = bf16[256,2048]{1,0:T(8,128)(2,1)S(1)} collective-permute-done((bf16[256,2048]{1,0:T(8,128)(2,1)S(1)}, bf16[256,2048]{1,0:T(8,128)(2,1)S(1)}, u32[]{:S(2)}, u32[]{:S(2)}) %collective-permute-start.52) | collective-permute-done | bytes 1048608 | tf_op jit(solution)/shard_map/ppermute | solution.py:105
  524.9 9.4 feed_back.7
  534.3 12.1 %collective-permute-done.55 = bf16[256,2048]{1,0:T(8,128)(2,1)S(1)} collective-permute-done((bf16[256,2048]{1,0:T(8,128)(2,1)S(1)}, bf16[256,2048]{1,0:T(8,128)(2,1)S(1)}, u32[]{:S(2)}, u32[]{:S(2)}) %collective-permute-start.55) | collective-permute-done | bytes 1048608 | tf_op jit(solution)/shard_map/ppermute | solution.py:105
  555.4 9.3 feed_back.8
  575.6 21.3 %convolution_convert_fusion.1 = bf16[2048,2048]{1,0:T(8,128)(2,1)} fusion(bf16[2048,2048]{1,0:T(8,128)(2,1)S(1)} %bitcast.215, bf16[2048,2048]{1,0:T(8,128)(2,1)} %get-tuple-element.392), kind=kOutput, calls=%fused_computation.2 | convolution fusion | flops 17184063488 | bytes 25165824 | tf_op jit(solution)/shard_map/dot_general | solution.py:292
  607.5 13.2 %convolution_convert_fusion.2 = bf16[1024,2048]{1,0:T(8,128)(2,1)} fusion(bf16[2048,1024]{1,0:T(8,128)(2,1)S(1)} %copy-done.33, bf16[2048,2048]{1,0:T(8,128)(2,1)} %get-tuple-element.401), kind=kOutput, calls=%fused_computation.4 | convolution fusion | flops 8592031744 | bytes 16777216 | tf_op jit(solution)/shard_map/dot_general | solution.py:292
  631.4 7.4 collective-permute-start.66
  642.1 18.0 %collective-permute-done.66 = bf16[256,2048]{1,0:T(8,128)(2,1)S(1)} collective-permute-done((bf16[256,2048]{1,0:T(8,128)(2,1)S(1)}, bf16[256,2048]{1,0:T(8,128)(2,1)S(1)}, u32[]{:S(2)}, u32[]{:S(2)}) %collective-permute-start.66) | collective-permute-done | bytes 1048608 | tf_op jit(solution)/shard_map/ppermute | solution.py:105
  692.0 9.4 collective-permute-done.70.refs_2_
  701.3 9.1 collective-permute-done.71.refs_3_
  712.8 6.1 join.1
  730.2 19.1 %attend_back.1 = (f32[2048,256]{1,0:T(8,128)}, f32[2048,256]{1,0:T(8,128)}, f32[2048,256]{1,0:T(8,128)}) custom-call(s32[4]{0:T(128)S(1)} %copy-done.32, s32[1,2048]{1,0:T(1,128)S(1)} %bitcast.210, bf16[2048,256]{1,0:T(8,128)(2,1)S(1)} %copy-done.17, bf16[2048,256]{1,0:T(8,128)(2,1)S(1)} %copy-done.18, bf16[2048,256]{1,0:T(8,128)(2,1)S(1)} %copy-done.19, ...), custom_call_target="tpu_custom_call" | custom-call | flops 25999998976 | bytes 78000000 | tf_op jit(solution)/shard_map/attend_back/pallas_call | solution.py:429
  749.3 6.9 unturn.1
  756.2 10.0 %collective-permute-done.76.refs_3_ = bf16[2,64,2048]{2,1,0:T(8,128)(2,1)S(1)} collective-permute-done((bf16[2,64,2048]{2,1,0:T(8,128)(2,1)}, bf16[2,64,2048]{2,1,0:T(8,128)(2,1)S(1)}, u32[]{:S(2)}, u32[]{:S(2)}) %collective-permute-start.76) | collective-permute-done | bytes 524320 | tf_op jit(solution)/shard_map/ppermute | solution.py:58
  767.2 10.6 %collective-permute-start.78 = (f32[2,2048]{1,0:T(2,128)S(1)}, f32[2,2048]{1,0:T(2,128)S(1)}, u32[]{:S(2)}, u32[]{:S(2)}) collective-permute-start(f32[2,2048]{1,0:T(2,128)S(1)} %copy-done.65), channel_id=1, source_target_pairs={{0,4},{4,0},{1,5},{5,1},{2,6},{6,2},{3,7},{7,3},{8,12},{12,8},{9,1... | collective-permute-start | bytes 49160 | tf_op jit(solution)/shard_map/ppermute | solution.py:281
  789.1 6.6 finish.1
  815.6 11.3 %collective-permute-start.84 = (bf16[256,2048]{1,0:T(8,128)(2,1)S(1)}, bf16[256,2048]{1,0:T(8,128)(2,1)}, u32[]{:S(2)}, u32[]{:S(2)}) collective-permute-start(bf16[256,2048]{1,0:T(8,128)(2,1)S(1)} %add_convert_fusion.3.two_ref), channel_id=1, source_target_pairs={{0,2},{1,3},{8,10},{9,11},{16,18},{17,19},{24,26},{25,27}} | collective-permute-start | bytes 3145736 | tf_op jit(solution)/shard_map/ppermute | solution.py:105
  828.7 10.5 %convolution_convert_fusion.3 = bf16[2048,768]{1,0:T(8,128)(2,1)} fusion(bf16[2048,2048]{1,0:T(8,128)(2,1)} %bitcast.34.in_ref, bf16[2048,768]{1,0:T(8,128)(2,1)S(1)} %copy-done.42), kind=kOutput, calls=%fused_computation.5 | convolution fusion | flops 6444023808 | bytes 14680064 | tf_op jit(solution)/shard_map/dot_general | solution.py:292
  843.1 5.7 collective-permute-done.84.right_ref
  867.1 15.6 %collective-permute-done.89.right_ref = bf16[256,2048]{1,0:T(8,128)(2,1)S(1)} collective-permute-done((bf16[256,2048]{1,0:T(8,128)(2,1)}, bf16[256,2048]{1,0:T(8,128)(2,1)S(1)}, u32[]{:S(2)}, u32[]{:S(2)}) %collective-permute-start.89) | collective-permute-done | bytes 1048608 | tf_op jit(solution)/shard_map/ppermute | solution.py:105
  882.7 12.1 %reduce-scatter.9.cloned.1.call-done = bf16[512,768]{1,0:T(8,128)(2,1)} async-done(((bf16[2048,768]{1,0:T(8,128)(2,1)}), bf16[512,768]{1,0:T(8,128)(2,1)}) %reduce-scatter.9.cloned.1.call-update) | async-done | bytes 786448 | tf_op jit(solution)/shard_map/reduce_scatter | solution.py:779
  911.3 18.5 %collective-permute-done.96 = f32[5,2048]{1,0:T(8,128)S(1)} collective-permute-done((f32[5,2048]{1,0:T(8,128)S(1)}, f32[5,2048]{1,0:T(8,128)S(1)}, u32[]{:S(2)}, u32[]{:S(2)}) %collective-permute-start.96) | collective-permute-done | bytes 40992 | tf_op jit(solution)/shard_map/ppermute | solution.py:1004
  940.8 6.1 collect.3
  (504 shorter events, 399.4 us)
Async XLA Ops:
  7.2 70.2 %all-gather.5.cloned.1.call-start = ((), (), s32[]{:S(2)}) async-start(), calls=%async_computation.4 | async-start | bytes 5242880 | tf_op jit(solution)/shard_map/all_gather | solution.py:832
  7.9 129.0 %all-gather.7.cloned.1.call-start = ((), (), s32[]{:S(2)}) async-start(), calls=%async_computation.5 | async-start | bytes 3932160 | tf_op jit(solution)/shard_map/all_gather | solution.py:846
  7.9 27.7 %collective-permute-start = (bf16[256,2048]{1,0:T(8,128)(2,1)}, bf16[256,2048]{1,0:T(8,128)(2,1)S(1)}, u32[]{:S(2)}, u32[]{:S(2)}) collective-permute-start(bf16[256,2048]{1,0:T(8,128)(2,1)} %bitcast.224), channel_id=1, source_target_pairs={{0,2},{2,4},{4,6},{1,3},{3,5},{5,7},{8,10},{10,12},{12,14},{9,11},... | collective-permute-start | bytes 3145736 | tf_op jit(solution)/shard_map/ppermute | solution.py:105
  13.0 26.7 %collective-permute-start.1 = (bf16[256,2048]{1,0:T(8,128)(2,1)}, bf16[256,2048]{1,0:T(8,128)(2,1)S(1)}, u32[]{:S(2)}, u32[]{:S(2)}) collective-permute-start(bf16[256,2048]{1,0:T(8,128)(2,1)} %bitcast.225), channel_id=1, source_target_pairs={{2,0},{4,2},{6,4},{3,1},{5,3},{7,5},{10,8},{12,10},{14,12},{11,9},... | collective-permute-start | bytes 3145736 | tf_op jit(solution)/shard_map/ppermute | solution.py:105
  14.3 25.4 %collective-permute-start.2 = (bf16[256,2048]{1,0:T(8,128)(2,1)}, bf16[256,2048]{1,0:T(8,128)(2,1)}, u32[]{:S(2)}, u32[]{:S(2)}) collective-permute-start(bf16[256,2048]{1,0:T(8,128)(2,1)} %bitcast.226), channel_id=1, source_target_pairs={{0,1},{1,0},{2,3},{3,2},{4,5},{5,4},{6,7},{7,6},{8,9},{9,8},{10,11... | collective-permute-start | bytes 3145736 | tf_op jit(solution)/shard_map/ppermute | solution.py:62
  44.2 31.0 %collective-permute-start.4 = (bf16[256,2048]{1,0:T(8,128)(2,1)S(1)}, bf16[256,2048]{1,0:T(8,128)(2,1)}, u32[]{:S(2)}, u32[]{:S(2)}) collective-permute-start(bf16[256,2048]{1,0:T(8,128)(2,1)S(1)} %collective-permute-done), channel_id=1, source_target_pairs={{0,2},{2,4},{4,6},{1,3},{3,5},{5,7},{8,10},{10,12},{12,14},{9,11},... | collective-permute-start | bytes 3145736 | tf_op jit(solution)/shard_map/ppermute | solution.py:105
  47.7 29.7 %collective-permute-start.5 = (bf16[256,2048]{1,0:T(8,128)(2,1)S(1)}, bf16[256,2048]{1,0:T(8,128)(2,1)}, u32[]{:S(2)}, u32[]{:S(2)}) collective-permute-start(bf16[256,2048]{1,0:T(8,128)(2,1)S(1)} %collective-permute-done.1), channel_id=1, source_target_pairs={{2,0},{4,2},{6,4},{3,1},{5,3},{7,5},{10,8},{12,10},{14,12},{11,9},... | collective-permute-start | bytes 3145736 | tf_op jit(solution)/shard_map/ppermute | solution.py:105
  65.0 32.5 %collective-permute-start.11 = (bf16[256,2048]{1,0:T(8,128)(2,1)}, bf16[256,2048]{1,0:T(8,128)(2,1)}, u32[]{:S(2)}, u32[]{:S(2)}) collective-permute-start(bf16[256,2048]{1,0:T(8,128)(2,1)} %get-tuple-element.498), channel_id=1, source_target_pairs={{0,1},{1,0},{2,3},{3,2},{4,5},{5,4},{6,7},{7,6},{8,9},{9,8},{10,11... | collective-permute-start | bytes 3145736 | tf_op jit(solution)/shard_map/ppermute | solution.py:62
  79.4 131.3 %all-gather.9.cloned.1.call-start = ((), (), s32[]{:S(2)}) async-start(), calls=%async_computation.6 | async-start | bytes 5242880 | tf_op jit(solution)/shard_map/all_gather | solution.py:855
  85.6 30.2 %collective-permute-start.10 = (bf16[256,2048]{1,0:T(8,128)(2,1)}, bf16[256,2048]{1,0:T(8,128)(2,1)}, u32[]{:S(2)}, u32[]{:S(2)}) collective-permute-start(bf16[256,2048]{1,0:T(8,128)(2,1)} %collective-permute-done.5), channel_id=1, source_target_pairs={{2,0},{4,2},{6,4},{3,1},{5,3},{7,5},{10,8},{12,10},{14,12},{11,9},... | collective-permute-start | bytes 3145736 | tf_op jit(solution)/shard_map/ppermute | solution.py:105
  86.9 30.1 %collective-permute-start.9 = (bf16[256,2048]{1,0:T(8,128)(2,1)}, bf16[256,2048]{1,0:T(8,128)(2,1)}, u32[]{:S(2)}, u32[]{:S(2)}) collective-permute-start(bf16[256,2048]{1,0:T(8,128)(2,1)} %collective-permute-done.4), channel_id=1, source_target_pairs={{0,2},{2,4},{4,6},{1,3},{3,5},{5,7},{8,10},{10,12},{12,14},{9,11},... | collective-permute-start | bytes 3145736 | tf_op jit(solution)/shard_map/ppermute | solution.py:105
  154.0 153.7 %all-gather.11.cloned.1.call-start = ((), (), s32[]{:S(2)}) async-start(), calls=%async_computation.7 | async-start | bytes 10485760 | tf_op jit(solution)/shard_map/all_gather | solution.py:868
  167.5 28.5 %collective-permute-start.22 = (bf16[2,64,2048]{2,1,0:T(8,128)(2,1)}, bf16[2,64,2048]{2,1,0:T(8,128)(2,1)S(1)}, u32[]{:S(2)}, u32[]{:S(2)}) collective-permute-start(bf16[2,64,2048]{2,1,0:T(8,128)(2,1)} %get-tuple-element.517), channel_id=1, source_target_pairs={{0,2},{2,0},{4,6},{6,4},{1,3},{3,1},{5,7},{7,5},{8,10},{10,8},{12,... | collective-permute-start | bytes 1572872 | tf_op jit(solution)/shard_map/ppermute | solution.py:58
  169.5 38.4 %collective-permute-start.23 = (bf16[2,64,2048]{2,1,0:T(8,128)(2,1)}, bf16[2,64,2048]{2,1,0:T(8,128)(2,1)S(1)}, u32[]{:S(2)}, u32[]{:S(2)}) collective-permute-start(bf16[2,64,2048]{2,1,0:T(8,128)(2,1)} %get-tuple-element.516), channel_id=1, source_target_pairs={{0,4},{2,6},{4,0},{6,2},{1,5},{3,7},{5,1},{7,3},{8,12},{10,14},{12... | collective-permute-start | bytes 1572872 | tf_op jit(solution)/shard_map/ppermute | solution.py:58
  170.4 37.5 %collective-permute-start.24 = (bf16[2,64,2048]{2,1,0:T(8,128)(2,1)}, bf16[2,64,2048]{2,1,0:T(8,128)(2,1)S(1)}, u32[]{:S(2)}, u32[]{:S(2)}) collective-permute-start(bf16[2,64,2048]{2,1,0:T(8,128)(2,1)} %get-tuple-element.515), channel_id=1, source_target_pairs={{0,6},{2,4},{4,2},{6,0},{1,7},{3,5},{5,3},{7,1},{8,14},{10,12},{12... | collective-permute-start | bytes 1572872 | tf_op jit(solution)/shard_map/ppermute | solution.py:58
  213.2 470.2 %reduce-scatter.5.cloned.1.call-start = ((), (), s32[]{:S(2)}) async-start(), calls=%async_computation.8 | async-start | bytes 10485760 | tf_op jit(solution)/shard_map/reduce_scatter | solution.py:779
  252.2 29.4 %collective-permute-start.29 = (bf16[256,2048]{1,0:T(8,128)(2,1)S(1)}, bf16[256,2048]{1,0:T(8,128)(2,1)}, u32[]{:S(2)}, u32[]{:S(2)}) collective-permute-start(bf16[256,2048]{1,0:T(8,128)(2,1)S(1)} %fusion.7.refs_0_), channel_id=1, source_target_pairs={{0,2},{2,4},{4,6},{1,3},{3,5},{5,7},{8,10},{10,12},{12,14},{9,11},... | collective-permute-start | bytes 3145736 | tf_op jit(solution)/shard_map/ppermute | solution.py:105
  260.5 26.3 %collective-permute-start.30 = (bf16[256,2048]{1,0:T(8,128)(2,1)S(1)}, bf16[256,2048]{1,0:T(8,128)(2,1)}, u32[]{:S(2)}, u32[]{:S(2)}) collective-permute-start(bf16[256,2048]{1,0:T(8,128)(2,1)S(1)} %fusion.7.refs_0_), channel_id=1, source_target_pairs={{2,0},{4,2},{6,4},{3,1},{5,3},{7,5},{10,8},{12,10},{14,12},{11,9},... | collective-permute-start | bytes 3145736 | tf_op jit(solution)/shard_map/ppermute | solution.py:105
  288.8 28.0 %collective-permute-start.34 = (bf16[256,2048]{1,0:T(8,128)(2,1)S(1)}, bf16[256,2048]{1,0:T(8,128)(2,1)}, u32[]{:S(2)}, u32[]{:S(2)}) collective-permute-start(bf16[256,2048]{1,0:T(8,128)(2,1)S(1)} %broadcast_select_fusion.5.refs_0_), channel_id=1, source_target_pairs={{0,1},{1,0},{2,3},{3,2},{4,5},{5,4},{6,7},{7,6},{8,9},{9,8},{10,11... | collective-permute-start | bytes 3145736 | tf_op jit(solution)/shard_map/ppermute | solution.py:62
  288.9 27.9 %collective-permute-start.32 = (bf16[256,2048]{1,0:T(8,128)(2,1)}, bf16[256,2048]{1,0:T(8,128)(2,1)}, u32[]{:S(2)}, u32[]{:S(2)}) collective-permute-start(bf16[256,2048]{1,0:T(8,128)(2,1)} %collective-permute-done.29), channel_id=1, source_target_pairs={{0,2},{2,4},{4,6},{1,3},{3,5},{5,7},{8,10},{10,12},{12,14},{9,11},... | collective-permute-start | bytes 3145736 | tf_op jit(solution)/shard_map/ppermute | solution.py:105
  292.2 27.5 %collective-permute-start.33 = (bf16[256,2048]{1,0:T(8,128)(2,1)}, bf16[256,2048]{1,0:T(8,128)(2,1)}, u32[]{:S(2)}, u32[]{:S(2)}) collective-permute-start(bf16[256,2048]{1,0:T(8,128)(2,1)} %collective-permute-done.30), channel_id=1, source_target_pairs={{2,0},{4,2},{6,4},{3,1},{5,3},{7,5},{10,8},{12,10},{14,12},{11,9},... | collective-permute-start | bytes 3145736 | tf_op jit(solution)/shard_map/ppermute | solution.py:105
  324.9 27.5 %collective-permute-start.36 = (bf16[256,2048]{1,0:T(8,128)(2,1)}, bf16[256,2048]{1,0:T(8,128)(2,1)S(1)}, u32[]{:S(2)}, u32[]{:S(2)}) collective-permute-start(bf16[256,2048]{1,0:T(8,128)(2,1)} %collective-permute-done.33), channel_id=1, source_target_pairs={{2,0},{4,2},{6,4},{3,1},{5,3},{7,5},{10,8},{12,10},{14,12},{11,9},... | collective-permute-start | bytes 3145736 | tf_op jit(solution)/shard_map/ppermute | solution.py:105
  370.9 26.4 %collective-permute-start.40 = (bf16[256,2048]{1,0:T(8,128)(2,1)S(1)}, bf16[256,2048]{1,0:T(8,128)(2,1)S(1)}, u32[]{:S(2)}, u32[]{:S(2)}) collective-permute-start(bf16[256,2048]{1,0:T(8,128)(2,1)S(1)} %add_convert_fusion.11.two_ref), channel_id=1, source_target_pairs={{0,2},{1,3},{8,10},{9,11},{16,18},{17,19},{24,26},{25,27}} | collective-permute-start | bytes 3145736 | tf_op jit(solution)/shard_map/ppermute | solution.py:105
  376.1 27.6 %collective-permute-start.45 = (bf16[256,2048]{1,0:T(8,128)(2,1)S(1)}, bf16[256,2048]{1,0:T(8,128)(2,1)S(1)}, u32[]{:S(2)}, u32[]{:S(2)}) collective-permute-start(bf16[256,2048]{1,0:T(8,128)(2,1)S(1)} %get-tuple-element.352), channel_id=1, source_target_pairs={{0,1},{1,0},{2,3},{3,2},{4,5},{5,4},{6,7},{7,6},{8,9},{9,8},{10,11... | collective-permute-start | bytes 3145736 | tf_op jit(solution)/shard_map/ppermute | solution.py:62
  398.4 26.3 %collective-permute-start.43 = (bf16[256,2048]{1,0:T(8,128)(2,1)S(1)}, bf16[256,2048]{1,0:T(8,128)(2,1)S(1)}, u32[]{:S(2)}, u32[]{:S(2)}) collective-permute-start(bf16[256,2048]{1,0:T(8,128)(2,1)S(1)} %get-tuple-element.349), channel_id=1, source_target_pairs={{0,2},{2,4},{1,3},{3,5},{8,10},{10,12},{9,11},{11,13},{16,18},{18,... | collective-permute-start | bytes 3145736 | tf_op jit(solution)/shard_map/ppermute | solution.py:105
  403.6 32.8 %collective-permute-start.48 = (bf16[256,2048]{1,0:T(8,128)(2,1)S(1)}, bf16[256,2048]{1,0:T(8,128)(2,1)S(1)}, u32[]{:S(2)}, u32[]{:S(2)}) collective-permute-start(bf16[256,2048]{1,0:T(8,128)(2,1)S(1)} %get-tuple-element.359), channel_id=1, source_target_pairs={{0,1},{1,0},{2,3},{3,2},{4,5},{5,4},{6,7},{7,6},{8,9},{9,8},{10,11... | collective-permute-start | bytes 3145736 | tf_op jit(solution)/shard_map/ppermute | solution.py:62
  425.9 29.2 %collective-permute-start.46 = (bf16[256,2048]{1,0:T(8,128)(2,1)S(1)}, bf16[256,2048]{1,0:T(8,128)(2,1)S(1)}, u32[]{:S(2)}, u32[]{:S(2)}) collective-permute-start(bf16[256,2048]{1,0:T(8,128)(2,1)S(1)} %get-tuple-element.356), channel_id=1, source_target_pairs={{0,2},{2,4},{4,6},{1,3},{3,5},{5,7},{8,10},{10,12},{12,14},{9,11},... | collective-permute-start | bytes 3145736 | tf_op jit(solution)/shard_map/ppermute | solution.py:105
  491.9 27.2 %collective-permute-start.53 = (bf16[256,2048]{1,0:T(8,128)(2,1)S(1)}, bf16[256,2048]{1,0:T(8,128)(2,1)S(1)}, u32[]{:S(2)}, u32[]{:S(2)}) collective-permute-start(bf16[256,2048]{1,0:T(8,128)(2,1)S(1)} %collective-permute-done.50), channel_id=1, source_target_pairs={{2,0},{4,2},{6,4},{3,1},{5,3},{7,5},{10,8},{12,10},{14,12},{11,9},... | collective-permute-start | bytes 3145736 | tf_op jit(solution)/shard_map/ppermute | solution.py:105
  523.4 27.2 %collective-permute-start.56 = (bf16[256,2048]{1,0:T(8,128)(2,1)S(1)}, bf16[256,2048]{1,0:T(8,128)(2,1)S(1)}, u32[]{:S(2)}, u32[]{:S(2)}) collective-permute-start(bf16[256,2048]{1,0:T(8,128)(2,1)S(1)} %collective-permute-done.53), channel_id=1, source_target_pairs={{2,0},{4,2},{6,4},{3,1},{5,3},{7,5},{10,8},{12,10},{14,12},{11,9},... | collective-permute-start | bytes 3145736 | tf_op jit(solution)/shard_map/ppermute | solution.py:105
  569.7 27.3 %collective-permute-start.62 = (bf16[256,2048]{1,0:T(8,128)(2,1)}, bf16[256,2048]{1,0:T(8,128)(2,1)}, u32[]{:S(2)}, u32[]{:S(2)}) collective-permute-start(bf16[256,2048]{1,0:T(8,128)(2,1)} %get-tuple-element.390), channel_id=1, source_target_pairs={{0,1},{1,0},{2,3},{3,2},{4,5},{5,4},{6,7},{7,6},{8,9},{9,8},{10,11... | collective-permute-start | bytes 3145736 | tf_op jit(solution)/shard_map/ppermute | solution.py:62
  570.4 28.5 %collective-permute-start.60 = (bf16[256,2048]{1,0:T(8,128)(2,1)S(1)}, bf16[256,2048]{1,0:T(8,128)(2,1)}, u32[]{:S(2)}, u32[]{:S(2)}) collective-permute-start(bf16[256,2048]{1,0:T(8,128)(2,1)S(1)} %add_convert_fusion.7.two_ref), channel_id=1, source_target_pairs={{0,2},{1,3},{8,10},{9,11},{16,18},{17,19},{24,26},{25,27}} | collective-permute-start | bytes 3145736 | tf_op jit(solution)/shard_map/ppermute | solution.py:105
  573.5 25.4 %collective-permute-start.61 = (bf16[256,2048]{1,0:T(8,128)(2,1)S(1)}, bf16[256,2048]{1,0:T(8,128)(2,1)}, u32[]{:S(2)}, u32[]{:S(2)}) collective-permute-start(bf16[256,2048]{1,0:T(8,128)(2,1)S(1)} %add_convert_fusion.7.two_ref), channel_id=1, source_target_pairs={{6,4},{7,5},{14,12},{15,13},{22,20},{23,21},{30,28},{31,29}} | collective-permute-start | bytes 3145736 | tf_op jit(solution)/shard_map/ppermute | solution.py:105
  599.0 184.4 %reduce-scatter.7.cloned.1.call-start = ((), (), s32[]{:S(2)}) async-start(), calls=%async_computation.9 | async-start | bytes 5242880 | tf_op jit(solution)/shard_map/reduce_scatter | solution.py:779
  599.1 41.2 %collective-permute-start.68 = (bf16[256,2048]{1,0:T(8,128)(2,1)}, bf16[256,2048]{1,0:T(8,128)(2,1)}, u32[]{:S(2)}, u32[]{:S(2)}) collective-permute-start(bf16[256,2048]{1,0:T(8,128)(2,1)} %copy-done.20), channel_id=1, source_target_pairs={{0,1},{1,0},{2,3},{3,2},{4,5},{5,4},{6,7},{7,6},{8,9},{9,8},{10,11... | collective-permute-start | bytes 3145736 | tf_op jit(solution)/shard_map/ppermute | solution.py:62
  631.4 28.7 %collective-permute-start.66 = (bf16[256,2048]{1,0:T(8,128)(2,1)S(1)}, bf16[256,2048]{1,0:T(8,128)(2,1)S(1)}, u32[]{:S(2)}, u32[]{:S(2)}) collective-permute-start(bf16[256,2048]{1,0:T(8,128)(2,1)S(1)} %get-tuple-element.405), channel_id=1, source_target_pairs={{0,2},{2,4},{4,6},{1,3},{3,5},{5,7},{8,10},{10,12},{12,14},{9,11},... | collective-permute-start | bytes 3145736 | tf_op jit(solution)/shard_map/ppermute | solution.py:105
  638.8 25.5 %collective-permute-start.67 = (bf16[256,2048]{1,0:T(8,128)(2,1)S(1)}, bf16[256,2048]{1,0:T(8,128)(2,1)S(1)}, u32[]{:S(2)}, u32[]{:S(2)}) collective-permute-start(bf16[256,2048]{1,0:T(8,128)(2,1)S(1)} %get-tuple-element.406), channel_id=1, source_target_pairs={{2,0},{4,2},{6,4},{3,1},{5,3},{7,5},{10,8},{12,10},{14,12},{11,9},... | collective-permute-start | bytes 3145736 | tf_op jit(solution)/shard_map/ppermute | solution.py:105
  719.6 147.5 %reduce-scatter.11.cloned.1.call-start = ((), (), s32[]{:S(2)}) async-start(), calls=%async_computation.11 | async-start | bytes 5242880 | tf_op jit(solution)/shard_map/reduce_scatter | solution.py:779
  722.4 33.8 %collective-permute-start.75 = (bf16[2,64,2048]{2,1,0:T(8,128)(2,1)}, bf16[2,64,2048]{2,1,0:T(8,128)(2,1)S(1)}, u32[]{:S(2)}, u32[]{:S(2)}) collective-permute-start(bf16[2,64,2048]{2,1,0:T(8,128)(2,1)} %get-tuple-element.511), channel_id=1, source_target_pairs={{0,2},{2,0},{4,6},{6,4},{1,3},{3,1},{5,7},{7,5},{8,10},{10,8},{12,... | collective-permute-start | bytes 1572872 | tf_op jit(solution)/shard_map/ppermute | solution.py:58
  727.8 38.4 %collective-permute-start.76 = (bf16[2,64,2048]{2,1,0:T(8,128)(2,1)}, bf16[2,64,2048]{2,1,0:T(8,128)(2,1)S(1)}, u32[]{:S(2)}, u32[]{:S(2)}) collective-permute-start(bf16[2,64,2048]{2,1,0:T(8,128)(2,1)} %get-tuple-element.510), channel_id=1, source_target_pairs={{0,4},{2,6},{4,0},{6,2},{1,5},{3,7},{5,1},{7,3},{8,12},{10,14},{12... | collective-permute-start | bytes 1572872 | tf_op jit(solution)/shard_map/ppermute | solution.py:58
  728.7 37.5 %collective-permute-start.77 = (bf16[2,64,2048]{2,1,0:T(8,128)(2,1)S(1)}, bf16[2,64,2048]{2,1,0:T(8,128)(2,1)S(1)}, u32[]{:S(2)}, u32[]{:S(2)}) collective-permute-start(bf16[2,64,2048]{2,1,0:T(8,128)(2,1)S(1)} %get-tuple-element.509), channel_id=1, source_target_pairs={{0,6},{2,4},{4,2},{6,0},{1,7},{3,5},{5,3},{7,1},{8,14},{10,12},{12... | collective-permute-start | bytes 1572872 | tf_op jit(solution)/shard_map/ppermute | solution.py:58
  767.2 127.7 %reduce-scatter.9.cloned.1.call-start = ((), (), s32[]{:S(2)}) async-start(), calls=%async_computation.10 | async-start | bytes 3932160 | tf_op jit(solution)/shard_map/reduce_scatter | solution.py:779
  795.7 47.4 %collective-permute-start.88 = (bf16[64,2048]{1,0:T(8,128)(2,1)}, bf16[64,2048]{1,0:T(8,128)(2,1)}, u32[]{:S(2)}, u32[]{:S(2)}) collective-permute-start(bf16[64,2048]{1,0:T(8,128)(2,1)} %get-tuple-element.521), channel_id=1, source_target_pairs={{0,6},{2,4},{4,2},{6,0},{1,7},{3,5},{5,3},{7,1},{8,14},{10,12},{12... | collective-permute-start | bytes 786440 | tf_op jit(solution)/shard_map/ppermute | solution.py:58
  808.3 30.9 %collective-permute-start.87 = (bf16[256,2048]{1,0:T(8,128)(2,1)}, bf16[256,2048]{1,0:T(8,128)(2,1)}, u32[]{:S(2)}, u32[]{:S(2)}) collective-permute-start(bf16[256,2048]{1,0:T(8,128)(2,1)} %slice.108), channel_id=1, source_target_pairs={{0,1},{1,0},{2,3},{3,2},{4,5},{5,4},{6,7},{7,6},{8,9},{9,8},{10,11... | collective-permute-start | bytes 3145736 | tf_op jit(solution)/shard_map/ppermute | solution.py:62
  811.8 29.4 %collective-permute-start.86 = (bf16[256,2048]{1,0:T(8,128)(2,1)}, bf16[256,2048]{1,0:T(8,128)(2,1)}, u32[]{:S(2)}, u32[]{:S(2)}) collective-permute-start(bf16[256,2048]{1,0:T(8,128)(2,1)} %slice.106), channel_id=1, source_target_pairs={{0,1},{1,0},{2,3},{3,2},{4,5},{5,4},{6,7},{7,6},{8,9},{9,8},{10,11... | collective-permute-start | bytes 3145736 | tf_op jit(solution)/shard_map/ppermute | solution.py:62
  815.6 33.3 %collective-permute-start.84 = (bf16[256,2048]{1,0:T(8,128)(2,1)S(1)}, bf16[256,2048]{1,0:T(8,128)(2,1)}, u32[]{:S(2)}, u32[]{:S(2)}) collective-permute-start(bf16[256,2048]{1,0:T(8,128)(2,1)S(1)} %add_convert_fusion.3.two_ref), channel_id=1, source_target_pairs={{0,2},{1,3},{8,10},{9,11},{16,18},{17,19},{24,26},{25,27}} | collective-permute-start | bytes 3145736 | tf_op jit(solution)/shard_map/ppermute | solution.py:105
  854.9 27.9 %collective-permute-start.89 = (bf16[256,2048]{1,0:T(8,128)(2,1)}, bf16[256,2048]{1,0:T(8,128)(2,1)S(1)}, u32[]{:S(2)}, u32[]{:S(2)}) collective-permute-start(bf16[256,2048]{1,0:T(8,128)(2,1)} %get-tuple-element.441), channel_id=1, source_target_pairs={{0,2},{2,4},{1,3},{3,5},{8,10},{10,12},{9,11},{11,13},{16,18},{18,... | collective-permute-start | bytes 3145736 | tf_op jit(solution)/shard_map/ppermute | solution.py:105
  898.2 31.6 %collective-permute-start.93 = (bf16[256,2048]{1,0:T(8,128)(2,1)}, bf16[256,2048]{1,0:T(8,128)(2,1)S(1)}, u32[]{:S(2)}, u32[]{:S(2)}) collective-permute-start(bf16[256,2048]{1,0:T(8,128)(2,1)} %get-tuple-element.451), channel_id=1, source_target_pairs={{0,2},{2,4},{4,6},{1,3},{3,5},{5,7},{8,10},{10,12},{12,14},{9,11},... | collective-permute-start | bytes 3145736 | tf_op jit(solution)/shard_map/ppermute | solution.py:105
  901.7 28.2 %collective-permute-start.94 = (bf16[256,2048]{1,0:T(8,128)(2,1)}, bf16[256,2048]{1,0:T(8,128)(2,1)S(1)}, u32[]{:S(2)}, u32[]{:S(2)}) collective-permute-start(bf16[256,2048]{1,0:T(8,128)(2,1)} %get-tuple-element.452), channel_id=1, source_target_pairs={{2,0},{4,2},{6,4},{3,1},{5,3},{7,5},{10,8},{12,10},{14,12},{11,9},... | collective-permute-start | bytes 3145736 | tf_op jit(solution)/shard_map/ppermute | solution.py:105
  (144 other events, 2384.3 us)
Sparse Core Ops, SparseCore 0:
  9.8 55.4 all-gather.4
  79.5 48.4 all-gather.6
  154.1 56.6 all-gather.8
  213.3 94.3 all-gather.10
  599.1 84.1 reduce-scatter.4
  719.8 55.6 reduce-scatter.6
  778.4 52.6 reduce-scatter.10
  849.0 45.8 reduce-scatter.8
